TPU v7x, 32 devices: a whole 2x2x4 slice. The times are simulated.
32 devices in a mesh: mem: 4 (over y, core), sub: 8 (over z, x).
Axes of the slice: x: 2, y: 2, z: 4, core: 2. Of those that a mesh axis runs over, the one named last changes fastest.
Arguments:
- prior_sample_array: float32 [80, 8, 24, 512], P('mem', 'sub'), may hold values from -6 to 6
- courant_x: float32 [8, 512], P('sub'), may hold values from -0.3 to 0.3
- courant_y: float32 [8, 512], P('sub'), may hold values from -0.3 to 0.3
- diffusion: float32 [8, 512], P('sub'), may hold values from 0.02 to 0.09
- obs_cell: int32 [4, 128], replicated, may hold values from 0 to 4095
- obs_value: float32 [4, 128], replicated, may hold values from -6 to 6
- obs_error: float32 [4, 128], replicated, may hold values from 0.2 to 1
- obs_weight: float32 [4, 128, 24], replicated, may hold values from -1.25 to 1.25
- taper_radius: float32 [4, 128], replicated, may hold values from 64 to 256
Outputs:
- analysis: float32 [80, 8, 24, 512], P(None, 'sub', None, 'mem')
All inputs are finite; a program needn't handle non-finite values.
Results may differ from a plain program's by a relative error of at most 0.0003.
Values sent between devices are 32-bit elements; how exact they have to be, the bound alone decides.
No kernel may reach another device: no remote copies, remote signals or barrier semaphores. Data moves between devices by JAX's collectives and lax.ppermute only.
A program may use at most 64 MiB of HBM per device.

v0:
```python
import jax
import jax.numpy as jnp
from jax import lax
from jax.sharding import PartitionSpec as P

highest = lax.Precision.HIGHEST


def padded_2(shard, sides, width):
    for axis, dim in sides:
        size, length = (lax.axis_size(axis), shard.shape[dim])
        up = [(i, (i + 1) % size) for i in range(size - 1)]
        down = [(j, i) for i, j in up]
        last = lax.slice_in_dim(shard, length - width, length, axis=dim)
        first = lax.slice_in_dim(shard, 0, width, axis=dim)
        before = lax.ppermute(last, axis, up)
        after = lax.ppermute(first, axis, down)
        shard = jnp.concatenate([before, shard, after], axis=dim)
    return shard


def gaspari(delta_row, delta_col, cutoff_radius, width):
    cyclic_shifted = (delta_col + width // 2) % width - width // 2
    row_dist = delta_row.astype(jnp.float32)
    col_dist = cyclic_shifted.astype(jnp.float32)
    ratio = jnp.sqrt(row_dist * row_dist + col_dist * col_dist) / cutoff_radius
    inner = (((-0.25 * ratio + 0.5) * ratio + 0.625) * ratio - 5.0 / 3.0) * ratio * ratio + 1.0
    bounded = jnp.maximum(ratio, 1.0)
    outer = (
        ((((ratio / 12.0 - 0.5) * ratio + 0.625) * ratio + 5.0 / 3.0) * ratio - 5.0) * ratio
        + 4.0
        - 2.0 / (3.0 * bounded)
    )
    return jnp.where(ratio <= 1.0, inner, jnp.where(ratio < 2.0, outer, 0.0))


def carried_quantity(
    center,
    west_cells,
    east_cells,
    north_cells,
    southern_neighbours,
    flow_x,
    meridional_velocity,
    mixing,
):
    result = (
        center
        - jnp.maximum(flow_x, 0.0) * (center - west_cells)
        - jnp.minimum(flow_x, 0.0) * (east_cells - center)
    )
    result = (
        result
        - jnp.maximum(meridional_velocity, 0.0) * (center - southern_neighbours)
        - jnp.minimum(meridional_velocity, 0.0) * (north_cells - center)
    )
    return result + mixing * (
        east_cells + west_cells + north_cells + southern_neighbours - 4.0 * center
    )


def obs_factors(obs_prior, obs_value, obs_error):
    members = obs_prior.shape[1]
    average = jnp.mean(obs_prior, axis=1)
    anomaly = obs_prior - average[:, None]
    covariance = jnp.dot(anomaly, anomaly.T, precision=highest) / (members - 1) + jnp.diag(
        obs_error
    )
    factor = jnp.linalg.cholesky(covariance)
    innovation = (obs_value - average)[:, None]
    midpoint_values = lax.linalg.triangular_solve(factor, innovation, left_side=True, lower=True)
    solved = lax.linalg.triangular_solve(
        factor, midpoint_values, left_side=True, lower=True, transpose_a=True
    )
    shifted = factor + jnp.diag(jnp.sqrt(obs_error))
    reduced = lax.linalg.triangular_solve(shifted, anomaly, left_side=True, lower=True)
    squared = lax.linalg.triangular_solve(
        factor, reduced, left_side=True, lower=True, transpose_a=True
    )
    return (anomaly, solved - squared)


def local_prior(existing_grid_values, obs_rows, obs_cols, weights, row_start, col_start):
    rows_dev = existing_grid_values.shape[1]
    cols_dev = existing_grid_values.shape[3]
    local_rows = obs_rows - row_start
    local_cols = obs_cols - col_start
    owned = (
        (local_rows >= 0) & (local_rows < rows_dev) & (local_cols >= 0) & (local_cols < cols_dev)
    )
    picked = existing_grid_values[
        :, jnp.clip(local_rows, 0, rows_dev - 1), :, jnp.clip(local_cols, 0, cols_dev - 1)
    ]
    values = jnp.einsum("kmc,kc->km", picked, weights, precision=highest)
    return jnp.where(owned[:, None], values, 0.0)


def apply_update(existing_grid_values, obs_anomaly, coeffs, taper_cells, members):
    average = jnp.mean(existing_grid_values, axis=0)
    anomaly = existing_grid_values - average[None]
    cross_cov = jnp.einsum("mrcx,km->rcxk", anomaly, obs_anomaly, precision=highest) / (members - 1)
    gain = cross_cov * taper_cells[:, None, :, :]
    return existing_grid_values + jnp.einsum("rcxk,km->mrcx", gain, coeffs, precision=highest)


def shards(
    prior_sample_array,
    courant_x,
    courant_y,
    diffusion,
    obs_cell,
    obs_value,
    obs_error,
    obs_weight,
    taper_radius,
):
    width = courant_x.shape[1]
    rows_dev = prior_sample_array.shape[1]
    cols_dev = width // lax.axis_size("mem")
    members = prior_sample_array.shape[0] * lax.axis_size("mem")
    col_start = lax.axis_index("mem") * cols_dev
    row_start = lax.axis_index("sub") * rows_dev
    padded = padded_2(prior_sample_array, (("sub", 1),), 1)
    propagated_grids = carried_quantity(
        prior_sample_array,
        jnp.roll(prior_sample_array, 1, axis=3),
        jnp.roll(prior_sample_array, -1, axis=3),
        padded[:, 2:],
        padded[:, :-2],
        courant_x[:, None, :],
        courant_y[:, None, :],
        diffusion[:, None, :],
    )
    existing_grid_values = lax.all_to_all(
        propagated_grids, "mem", split_axis=3, concat_axis=0, tiled=True
    )
    row_ids = row_start + jnp.arange(rows_dev, dtype=jnp.int32)
    col_ids = col_start + jnp.arange(cols_dev, dtype=jnp.int32)
    obs_rows = obs_cell // width
    obs_cols = obs_cell % width
    batches = obs_cell.shape[0]

    def taper_cells(batch_index):
        return gaspari(
            row_ids[:, None, None] - obs_rows[batch_index][None, None, :],
            col_ids[None, :, None] - obs_cols[batch_index][None, None, :],
            taper_radius[batch_index][None, None, :],
            width,
        )

    for batch_index in range(batches):
        obs_prior = lax.psum(
            local_prior(
                existing_grid_values,
                obs_rows[batch_index],
                obs_cols[batch_index],
                obs_weight[batch_index],
                row_start,
                col_start,
            ),
            ("mem", "sub"),
        )
        obs_anomaly, coeffs = obs_factors(obs_prior, obs_value[batch_index], obs_error[batch_index])
        existing_grid_values = apply_update(
            existing_grid_values, obs_anomaly, coeffs, taper_cells(batch_index), members
        )
    return existing_grid_values


def solution(mesh):
    return jax.shard_map(
        shards,
        mesh=mesh,
        in_specs=(
            P("mem", "sub", None, None),
            P("sub", None),
            P("sub", None),
            P("sub", None),
            P(),
            P(),
            P(),
            P(),
            P(),
        ),
        out_specs=P(None, "sub", None, "mem"),
        check_vma=False,
    )
```

profile of v0, /device:TPU:0, one launch (start us, length us, event | category | flops | bytes accessed | tf_op | source)
XLA Modules:
  0.0 428.4 jit_solution(3687478982285887635)
XLA Ops:
  0.0 5.9 %collective-permute-start = (f32[20,1,24,512]{3,2,1,0:T(8,128)}, f32[20,1,24,512]{3,2,1,0:T(8,128)}, u32[]{:S(2)}, u32[]{:S(2)}) collective-permute-start(f32[20,1,24,512]{3,2,1,0:T(8,128)} %param.18), channel_id=1, source_target_pairs={{0,1},{1,2},{2,3},{3,4},{4,5},{5,6},{6,7},{8,9},{9,10},{10,11},{11... | collective-permute-start | bytes 2949128 | tf_op jit(solution)/shard_map/ppermute | solution.py:16
  14.5 32.9 %collective-permute-done = f32[20,1,24,512]{3,2,1,0:T(8,128)} collective-permute-done((f32[20,1,24,512]{3,2,1,0:T(8,128)}, f32[20,1,24,512]{3,2,1,0:T(8,128)}, u32[]{:S(2)}, u32[]{:S(2)}) %collective-permute-start) | collective-permute-done | bytes 983072 | tf_op jit(solution)/shard_map/ppermute | solution.py:16
  50.7 4.3 copy.87
  54.9 6.5 %reshape.1524 = f32[4,1,61440]{2,1,0:T(1,128)} reshape(f32[512,1,20,24]{3,2,1,0:T(8,128)} %bitcast.330) | data formatting | bytes 1966080
  61.5 3.8 all-to-all-start
  68.1 10.9 %all-to-all-done = f32[4,1,61440]{2,1,0:T(1,128)S(1)} async-done(((f32[4,1,61440]{2,1,0:T(1,128)}), f32[4,1,61440]{2,1,0:T(1,128)S(1)}, u32[]{:S(2)}, u32[]{:S(2)}) %all-to-all-start) | async-done | bytes 983072 | tf_op jit(solution)/shard_map/all_to_all | solution.py:134
  83.0 6.0 %reshape.1525 = f32[512,1,20,24]{3,2,1,0:T(8,128)} reshape(f32[4,61440]{1,0:T(4,128)S(1)} %reduce.20) | data formatting | bytes 1966080
  89.1 5.6 %copy.88 = f32[20,1,24,512]{3,1,2,0:T(1,128)S(1)} copy(f32[20,1,24,512]{2,0,1,3:T(8,128)} %bitcast.331) | data formatting | bytes 1966080 | tf_op jit(solution)/shard_map/all_to_all | solution.py:134
  98.9 42.1 %psum.28 = f32[128,80]{0,1:T(8,128)S(1)} all-reduce(f32[128,80]{0,1:T(8,128)S(1)} %broadcast_select_fusion.3), channel_id=1, replica_groups=mesh['mem'=4,'sub'=8] {'mem','sub'}, use_global_device_ids=true, to_apply=%region_0.1 | all-reduce | flops 10240 | bytes 81920 | tf_op jit(solution)/shard_map/psum | solution.py:152
  142.9 11.7 %cholesky.74 = f32[128,128]{1,0:T(8,128)S(1)} custom-call(f32[128,128]{1,0:T(8,128)S(1)} %copy.93), custom_call_target="Cholesky" | custom-call | tf_op jit(solution)/shard_map/jit(cholesky)/cholesky | solution.py:69
  156.0 9.8 %custom-call.36 = f32[1,128,128]{1,2,0:T(8,128)S(1)} custom-call(f32[1,128,128]{2,1,0:T(8,128)S(1)} %get-tuple-element.21), custom_call_target="InvertDiagBlocksLowerTriangular" | custom-call | tf_op jit(solution)/shard_map/triangular_solve/custom-call.3 | solution.py:76
  166.0 9.8 %custom-call.35 = f32[1,128,128]{1,2,0:T(8,128)S(1)} custom-call(f32[1,128,128]{2,1,0:T(8,128)S(1)} %get-tuple-element.20), custom_call_target="InvertDiagBlocksLowerTriangular" | custom-call | tf_op jit(solution)/shard_map/triangular_solve/custom-call.2 | solution.py:72
  184.3 40.4 %psum.29 = f32[128,80]{0,1:T(8,128)S(1)} all-reduce(f32[128,80]{0,1:T(8,128)S(1)} %broadcast_select_fusion.2), channel_id=1, replica_groups=mesh['mem'=4,'sub'=8] {'mem','sub'}, use_global_device_ids=true, to_apply=%region_5.11 | all-reduce | flops 10240 | bytes 81920 | tf_op jit(solution)/shard_map/psum | solution.py:152
  225.2 11.7 %cholesky.85 = f32[128,128]{1,0:T(8,128)S(1)} custom-call(f32[128,128]{1,0:T(8,128)S(1)} %copy.98), custom_call_target="Cholesky" | custom-call | tf_op jit(solution)/shard_map/jit(cholesky)/cholesky | solution.py:69
  238.4 9.8 %custom-call.40 = f32[1,128,128]{1,2,0:T(8,128)S(1)} custom-call(f32[1,128,128]{2,1,0:T(8,128)S(1)} %get-tuple-element.19), custom_call_target="InvertDiagBlocksLowerTriangular" | custom-call | tf_op jit(solution)/shard_map/triangular_solve/custom-call.3 | solution.py:76
  248.4 9.8 %custom-call.39 = f32[1,128,128]{1,2,0:T(8,128)S(1)} custom-call(f32[1,128,128]{2,1,0:T(8,128)S(1)} %get-tuple-element.18), custom_call_target="InvertDiagBlocksLowerTriangular" | custom-call | tf_op jit(solution)/shard_map/triangular_solve/custom-call.2 | solution.py:72
  266.1 40.3 %psum.30 = f32[128,80]{0,1:T(8,128)S(1)} all-reduce(f32[128,80]{0,1:T(8,128)S(1)} %broadcast_select_fusion.1), channel_id=1, replica_groups=mesh['mem'=4,'sub'=8] {'mem','sub'}, use_global_device_ids=true, to_apply=%region_8.14 | all-reduce | flops 10240 | bytes 81920 | tf_op jit(solution)/shard_map/psum | solution.py:152
  307.0 11.7 %cholesky.96 = f32[128,128]{1,0:T(8,128)S(1)} custom-call(f32[128,128]{1,0:T(8,128)S(1)} %copy.101), custom_call_target="Cholesky" | custom-call | tf_op jit(solution)/shard_map/jit(cholesky)/cholesky | solution.py:69
  320.2 9.8 %custom-call.44 = f32[1,128,128]{1,2,0:T(8,128)S(1)} custom-call(f32[1,128,128]{2,1,0:T(8,128)S(1)} %get-tuple-element.17), custom_call_target="InvertDiagBlocksLowerTriangular" | custom-call | tf_op jit(solution)/shard_map/triangular_solve/custom-call.3 | solution.py:76
  330.2 9.8 %custom-call.43 = f32[1,128,128]{1,2,0:T(8,128)S(1)} custom-call(f32[1,128,128]{2,1,0:T(8,128)S(1)} %get-tuple-element.16), custom_call_target="InvertDiagBlocksLowerTriangular" | custom-call | tf_op jit(solution)/shard_map/triangular_solve/custom-call.2 | solution.py:72
  347.7 40.6 %psum.31 = f32[128,80]{0,1:T(8,128)S(1)} all-reduce(f32[128,80]{0,1:T(8,128)S(1)} %broadcast_select_fusion), channel_id=1, replica_groups=mesh['mem'=4,'sub'=8] {'mem','sub'}, use_global_device_ids=true, to_apply=%region_11.17 | all-reduce | flops 10240 | bytes 81920 | tf_op jit(solution)/shard_map/psum | solution.py:152
  388.8 11.7 %cholesky.107 = f32[128,128]{1,0:T(8,128)S(1)} custom-call(f32[128,128]{1,0:T(8,128)S(1)} %copy.104), custom_call_target="Cholesky" | custom-call | tf_op jit(solution)/shard_map/jit(cholesky)/cholesky | solution.py:69
  402.1 9.8 %custom-call.48 = f32[1,128,128]{1,2,0:T(8,128)S(1)} custom-call(f32[1,128,128]{2,1,0:T(8,128)S(1)} %get-tuple-element.15), custom_call_target="InvertDiagBlocksLowerTriangular" | custom-call | tf_op jit(solution)/shard_map/triangular_solve/custom-call.3 | solution.py:76
  412.1 9.8 %custom-call.47 = f32[1,128,128]{1,2,0:T(8,128)S(1)} custom-call(f32[1,128,128]{2,1,0:T(8,128)S(1)} %get-tuple-element.14), custom_call_target="InvertDiagBlocksLowerTriangular" | custom-call | tf_op jit(solution)/shard_map/triangular_solve/custom-call.2 | solution.py:72
  (169 shorter events, 62.6 us)
Async XLA Ops:
  0.0 14.1 %copy-start.8 = (f32[20,1,24,512]{3,2,1,0:T(8,128)S(1)}, f32[20,1,24,512]{3,2,1,0:T(8,128)}, u32[]{:S(2)}) copy-start(f32[20,1,24,512]{3,2,1,0:T(8,128)} %param.18) | copy-start | bytes 2949124
  0.0 47.4 %collective-permute-start = (f32[20,1,24,512]{3,2,1,0:T(8,128)}, f32[20,1,24,512]{3,2,1,0:T(8,128)}, u32[]{:S(2)}, u32[]{:S(2)}) collective-permute-start(f32[20,1,24,512]{3,2,1,0:T(8,128)} %param.18), channel_id=1, source_target_pairs={{0,1},{1,2},{2,3},{3,4},{4,5},{5,6},{6,7},{8,9},{9,10},{10,11},{11... | collective-permute-start | bytes 2949128 | tf_op jit(solution)/shard_map/ppermute | solution.py:16
  5.9 41.4 %collective-permute-start.1 = (f32[20,1,24,512]{3,2,1,0:T(8,128)}, f32[20,1,24,512]{3,2,1,0:T(8,128)S(1)}, u32[]{:S(2)}, u32[]{:S(2)}) collective-permute-start(f32[20,1,24,512]{3,2,1,0:T(8,128)} %param.18), channel_id=1, source_target_pairs={{1,0},{2,1},{3,2},{4,3},{5,4},{6,5},{7,6},{9,8},{10,9},{11,10},{12... | collective-permute-start | bytes 2949128 | tf_op jit(solution)/shard_map/ppermute | solution.py:17
  14.1 34.2 %copy-start.15 = (f32[1,512]{1,0:T(1,128)S(1)}, f32[1,512]{1,0:T(1,128)}, u32[]{:S(2)}) copy-start(f32[1,512]{1,0:T(1,128)} %param.21) | copy-start | bytes 6148
  61.5 6.1 %copy-start.28 = (f32[4,128]{1,0:T(4,128)S(1)}, f32[4,128]{1,0:T(4,128)}, u32[]{:S(2)}) copy-start(f32[4,128]{1,0:T(4,128)} %param.26) | copy-start | bytes 6148
  61.5 17.5 %all-to-all-start = ((f32[4,1,61440]{2,1,0:T(1,128)}), f32[4,1,61440]{2,1,0:T(1,128)S(1)}, u32[]{:S(2)}, u32[]{:S(2)}) async-start(f32[4,1,61440]{2,1,0:T(1,128)} %reshape.1524), calls=%async_computation | async-start | bytes 1966080 | tf_op jit(solution)/shard_map/all_to_all | solution.py:134
  94.7 0.9 copy-start.9
  95.6 1.0 copy-start.6
  97.4 1.5 copy-start.19
  97.4 45.0 %copy-start.27 = (f32[128]{0:T(128)S(1)}, f32[128]{0:T(128)}, u32[]{:S(2)}) copy-start(f32[128]{0:T(128)} %get-tuple-element.52) | copy-start | bytes 1540
  97.4 57.9 %copy-start.26 = (f32[128]{0:T(128)S(1)}, f32[128]{0:T(128)}, u32[]{:S(2)}) copy-start(f32[128]{0:T(128)} %get-tuple-element.49) | copy-start | bytes 1540
  98.8 77.1 %copy-start.13 = (f32[4,128]{1,0:T(4,128)S(1)}, f32[4,128]{1,0:T(4,128)}, u32[]{:S(2)}) copy-start(f32[4,128]{1,0:T(4,128)} %param.23) | copy-start | bytes 6148
  98.8 77.4 %copy-start.7 = (f32[4,20,1,24,128]{4,3,1,0,2:T(8,128)S(1)}, f32[4,20,1,24,128]{4,3,1,0,2:T(8,128)}, u32[]{:S(2)}) copy-start(f32[4,20,1,24,128]{4,3,1,0,2:T(8,128)} %copy-done.6) | copy-start | bytes 2949124
  183.6 41.1 %copy-start.25 = (f32[128]{0:T(128)S(1)}, f32[128]{0:T(128)}, u32[]{:S(2)}) copy-start(f32[128]{0:T(128)} %get-tuple-element.51) | copy-start | bytes 1540
  183.6 54.1 %copy-start.24 = (f32[128]{0:T(128)S(1)}, f32[128]{0:T(128)}, u32[]{:S(2)}) copy-start(f32[128]{0:T(128)} %get-tuple-element.48) | copy-start | bytes 1540
  183.6 75.0 %copy-start.12 = (f32[24,128]{1,0:T(8,128)S(1)}, f32[24,128]{1,0:T(8,128)}, u32[]{:S(2)}) copy-start(f32[24,128]{1,0:T(8,128)} %get-tuple-element.64) | copy-start | bytes 36868
  183.6 75.0 %copy-start.3 = (f32[80,24,128]{2,0,1:T(8,128)S(1)}, f32[80,24,128]{2,0,1:T(8,128)}, u32[]{:S(2)}) copy-start(f32[80,24,128]{2,0,1:T(8,128)} %copy-done.2) | copy-start | bytes 2949124
  265.5 41.0 %copy-start.23 = (f32[128]{0:T(128)S(1)}, f32[128]{0:T(128)}, u32[]{:S(2)}) copy-start(f32[128]{0:T(128)} %get-tuple-element.53) | copy-start | bytes 1540
  265.5 54.0 %copy-start.22 = (f32[128]{0:T(128)S(1)}, f32[128]{0:T(128)}, u32[]{:S(2)}) copy-start(f32[128]{0:T(128)} %get-tuple-element.47) | copy-start | bytes 1540
  265.5 74.9 %copy-start.5 = (f32[80,24,128]{2,0,1:T(8,128)S(1)}, f32[80,24,128]{2,0,1:T(8,128)}, u32[]{:S(2)}) copy-start(f32[80,24,128]{2,0,1:T(8,128)} %copy-done.4) | copy-start | bytes 2949124
  347.0 41.3 %copy-start.21 = (f32[128]{0:T(128)S(1)}, f32[128]{0:T(128)}, u32[]{:S(2)}) copy-start(f32[128]{0:T(128)} %get-tuple-element.50) | copy-start | bytes 1540
  347.0 54.3 %copy-start.20 = (f32[128]{0:T(128)S(1)}, f32[128]{0:T(128)}, u32[]{:S(2)}) copy-start(f32[128]{0:T(128)} %get-tuple-element.46) | copy-start | bytes 1540
  347.0 74.9 %copy-start.14 = (f32[4,128]{1,0:T(4,128)S(1)}, f32[4,128]{1,0:T(4,128)}, u32[]{:S(2)}) copy-start(f32[4,128]{1,0:T(4,128)} %param.23) | copy-start | bytes 6148
  347.0 75.3 %copy-start.1 = (f32[80,24,128]{2,0,1:T(8,128)S(1)}, f32[80,24,128]{2,0,1:T(8,128)}, u32[]{:S(2)}) copy-start(f32[80,24,128]{2,0,1:T(8,128)} %copy-done) | copy-start | bytes 2949124
  (8 other events, 6.6 us)
where the time goes:
time: 432 us; the launch traced here: 428 us
  blocking collectives  163 us (38%)
  other arithmetic  145 us (34%)
  waiting for transfers between devices  43.8 us (10%)
  local copies, waits for them, and re-layouts  41.1 us (10%)
  matrix products  23.1 us (5%)
  starting transfers between devices  11 us (3%)
    psum x4, blocking collectives, shards(): lax.psum(local_prior(existing_grid_values, obs_rows[batch_index], obs_col...  163 us
    another operation x12, other arithmetic, obs_factors(): factor = jnp.linalg.cholesky(covariance)  49.7 us
    another operation x8, other arithmetic, obs_factors(): lax.linalg.triangular_solve(factor, midpoint_values, left_side=True, lowe...  42.2 us
    another operation x4, other arithmetic, obs_factors(): lax.linalg.triangular_solve(shifted, anomaly, left_side=True, lower=True)  39.2 us
    ppermute x1, waiting for transfers between devices, padded_2(): before = lax.ppermute(last, axis, up)  32.9 us
    unnamed x64, local copies, waits for them, and re-layouts  17.7 us
    all_to_all x1, waiting for transfers between devices, shards(): lax.all_to_all(propagated_grids, 'mem', split_axis=3, concat_axis=0, tile...  10.9 us
    dot_general x4, matrix products, apply_update(): jnp.einsum('mrcx,km->rcxk', anomaly, obs_anomaly, precision=highest)  10.5 us
  transfers between devices with their start and end apart: 3, of which 2 were waited for; matrix products, arithmetic and copies ran while one was open for 2% of the time, Pallas kernels for 0%

commit v1 on v0

v1 whole, which is shorter than its diff:
```python
import jax
import jax.numpy as jnp
from jax import lax
from jax.experimental import pallas as pl
from jax.experimental.pallas import tpu as pltpu
from jax.sharding import PartitionSpec as P

highest = lax.Precision.HIGHEST
f32 = jnp.float32
bf16 = jnp.bfloat16
TILE = (8, 128)


def dot(a, b, ca, cb, precision=highest):
    return lax.dot_general(
        a, b, (((ca,), (cb,)), ((), ())), precision=precision, preferred_element_type=f32
    )


def narrow(a, b, ca, cb):
    return dot(a, b, ca, cb, None)


def split2(x):
    hi = x.astype(bf16)
    return hi, (x - hi.astype(f32)).astype(bf16)


def split3(x):
    hi = x.astype(bf16)
    rest = x - hi.astype(f32)
    mid = rest.astype(bf16)
    return hi, mid, (rest - mid.astype(f32)).astype(bf16)


def call(kernel, out_shapes, name, operands, scalars=(), scratch=()):
    specs = [pl.BlockSpec(memory_space=pltpu.SMEM) for _ in scalars]
    specs += [pl.BlockSpec(memory_space=pltpu.VMEM) for _ in operands]
    return pl.pallas_call(
        kernel,
        in_specs=specs,
        out_specs=[pl.BlockSpec(memory_space=pltpu.VMEM) for _ in out_shapes],
        out_shape=[jax.ShapeDtypeStruct(s, f32) for s in out_shapes],
        scratch_shapes=list(scratch),
        compiler_params=pltpu.CompilerParams(vmem_limit_bytes=48 * 2**20),
        name=name,
    )(*scalars, *operands)


def rows_cols(cells, width):
    if width & (width - 1) == 0:
        shift = width.bit_length() - 1
        return cells >> shift, cells & (width - 1)
    return cells // width, cells % width


def to_columns(rows):
    n = rows.shape[0]
    return jnp.concatenate([rows, jnp.zeros((128 - n, 128), f32)], 0).T


def gaspari(delta_row, delta_col, cutoff_radius, width):
    half = width // 2
    folded = jnp.where(delta_col >= half, delta_col - width, delta_col)
    folded = jnp.where(delta_col < -half, delta_col + width, folded)
    ratio = jnp.sqrt(delta_row * delta_row + folded * folded) / cutoff_radius
    inner = (((-0.25 * ratio + 0.5) * ratio + 0.625) * ratio - 5.0 / 3.0) * ratio * ratio + 1.0
    bounded = jnp.maximum(ratio, 1.0)
    outer = (
        ((((ratio / 12.0 - 0.5) * ratio + 0.625) * ratio + 5.0 / 3.0) * ratio - 5.0) * ratio
        + 4.0
        - 2.0 / (3.0 * bounded)
    )
    return jnp.where(ratio <= 1.0, inner, jnp.where(ratio < 2.0, outer, 0.0))


def taper_kernel(width, batches, nobs, cols_dev):
    def kernel(place_ref, cell_ref, radius_ref, obs_taper_ref, cell_taper_ref):
        row_here = place_ref[0].astype(f32)
        col_here = place_ref[1] * cols_dev
        row_i, col_i = rows_cols(cell_ref[...], width)
        rows = row_i.astype(f32)
        cols = col_i.astype(f32)
        table = to_columns(jnp.concatenate([rows, cols, radius_ref[...]], 0))
        lane = lax.broadcasted_iota(jnp.int32, (1, cols_dev), 1)
        cell_cols = (lane + col_here).astype(f32)
        slot = 0
        for b in range(batches):
            row_j = table[:, b : b + 1]
            col_j = table[:, batches + b : batches + b + 1]
            radius = table[:, 2 * batches + b : 2 * batches + b + 1]
            cell_taper_ref[b] = gaspari(row_here - row_j, cell_cols - col_j, radius, width)
            for e in range(b + 1, batches):
                obs_taper_ref[slot] = gaspari(
                    rows[e : e + 1, :] - row_j, cols[e : e + 1, :] - col_j, radius, width
                )
                slot += 1

    return kernel


def observe_kernel(width, comps, batches, nobs, blocks, edge_rows):
    def kernel(q_ref, cx_ref, cy_ref, d_ref, cell_ref, weight_ref, own_ref, raw_ref, send_ref):
        q = q_ref[...]
        count = q.shape[0]
        cx, cy, d = cx_ref[...], cy_ref[...], d_ref[...]
        west = pltpu.roll(q, 1, 1)
        east = pltpu.roll(q, width - 1, 1)
        mine = q - jnp.maximum(cx, 0.0) * (q - west) - jnp.minimum(cx, 0.0) * (east - q)
        mine = mine - jnp.maximum(cy, 0.0) * q + jnp.minimum(cy, 0.0) * q
        mine = mine + d * (east + west - 4.0 * q)
        _, col = rows_cols(cell_ref[...], width)
        place = lax.broadcasted_iota(jnp.int32, (width, nobs), 0)
        pieces = split2(mine) + split2(q)
        stacked = jnp.concatenate(pieces, 0)
        for b in range(batches):
            pick = (place == col[b : b + 1, :]).astype(f32).astype(bf16)
            found = narrow(stacked, pick, 1, 0)
            w = jnp.concatenate(
                [weight_ref[b], jnp.zeros((nobs, 128 - comps), f32)], 1
            ).T[:comps]
            own = found[:count] + found[count : 2 * count]
            raw = found[2 * count : 3 * count] + found[3 * count :]
            at = slice(b * nobs, (b + 1) * nobs)
            own_ref[:, at] = jnp.sum(own.reshape(-1, comps, nobs) * w[None], axis=1)
            raw_ref[:, at] = jnp.sum(raw.reshape(-1, comps, nobs) * w[None], axis=1)
        cols_dev = width // blocks
        which = lax.broadcasted_iota(jnp.int32, (2 * blocks, width), 0)
        spot = lax.broadcasted_iota(jnp.int32, (2 * blocks, width), 1)
        start = (which >> 1) * cols_dev
        wanted = jnp.where(which & 1 == 0, start - 1, start + cols_dev)
        wanted = jnp.where(wanted < 0, wanted + width, wanted)
        wanted = jnp.where(wanted >= width, wanted - width, wanted)
        pick = (spot == wanted).astype(f32).astype(bf16)
        edges = sum(narrow(pick, part, 1, 1) for part in split3(q)[::-1])
        chunks = -(-count // 128)
        if chunks * 128 > count:
            edges = jnp.concatenate([edges, jnp.zeros((2 * blocks, chunks * 128 - count), f32)], 1)
        for i in range(blocks):
            at = slice(i * cols_dev, (i + 1) * cols_dev)
            send_ref[i, :count, :] = q[:, at]
            rows = [edges[2 * i : 2 * i + 2, j * 128 : (j + 1) * 128] for j in range(chunks)]
            if edge_rows > 2 * chunks:
                rows.append(jnp.zeros((edge_rows - 2 * chunks, 128), f32))
            send_ref[i, count:, :] = jnp.concatenate(rows, 0)

    return kernel


def join_kernel(width, batches, nobs):
    def kernel(place_ref, own_ref, raw_ref, above_ref, below_ref, cell_ref, out_ref):
        here = place_ref[0]
        row, col = rows_cols(cell_ref[...], width)
        place = lax.broadcasted_iota(jnp.int32, (width, nobs), 0)
        parts = split3(jnp.concatenate([above_ref[...], below_ref[...]], 0))
        stacked = jnp.concatenate([p.astype(f32) for p in parts] + [jnp.zeros((2, width), f32)], 0)
        stacked = stacked.astype(bf16)
        for b in range(batches):
            pick = (place == col[b : b + 1, :]).astype(f32).astype(bf16)
            found = narrow(stacked, pick, 1, 0)
            coef = found[0:2] + found[2:4] + found[4:6]
            r = row[b : b + 1, :]
            factor = jnp.where(r == here + 1, coef[0:1], jnp.where(r == here - 1, coef[1:2], 0.0))
            at = slice(b * nobs, (b + 1) * nobs)
            out_ref[:, at] = jnp.where(r == here, own_ref[:, at], factor * raw_ref[:, at])

    return kernel


def lane_spread(x, j):
    return jnp.take_along_axis(x, jnp.full(x.shape, j, jnp.int32), axis=1)


def row_spread(x, i):
    return jnp.broadcast_to(x[i : i + 1, :], x.shape)


def factored(cov, sides, error, members):
    tiles = cov.shape[0] // 8
    lane = lax.broadcasted_iota(jnp.int32, TILE, 1)
    sub = lax.broadcasted_iota(jnp.int32, TILE, 0)
    T = [cov[8 * q : 8 * q + 8, :] for q in range(tiles)]
    V = [sides[8 * q : 8 * q + 8, :] for q in range(tiles)]
    deviation = jnp.broadcast_to(jnp.sqrt(error), TILE)
    is_member = lane < members
    inverse, solved = [], []
    for p in range(tiles):
        block = (lane >= 8 * p) & (lane < 8 * p + 8)
        columns = [lane_spread(T[p], 8 * p + c) for c in range(8)]
        s = [[row_spread(columns[c], a) if a >= c else None for c in range(8)] for a in range(8)]
        joined = jnp.where(block, (lane - 8 * p == sub).astype(f32), T[p])
        R = [row_spread(joined, c) for c in range(8)]
        Z = [row_spread(V[p], c) for c in range(8)]
        rd, rs = [None] * 8, [None] * 8
        m = [[None] * 8 for _ in range(8)]
        for c in range(8):
            rd[c] = 1.0 / s[c][c]
            rs[c] = lax.rsqrt(s[c][c])
            root = s[c][c] * rs[c]
            spread = lane_spread(deviation, 8 * p + c)
            Z[c] = Z[c] * jnp.where(is_member, root / (root + spread), 1.0)
            for a in range(c + 1, 8):
                m[a][c] = s[a][c] * rd[c]
            for a in range(c + 1, 8):
                for e in range(c + 1, a + 1):
                    s[a][e] = s[a][e] - (s[a][c] * s[e][c]) * rd[c]
                R[a] = R[a] - m[a][c] * R[c]
                Z[a] = Z[a] - m[a][c] * Z[c]
        X, U = [None] * 8, [None] * 8
        for a in range(7, -1, -1):
            x, u = rd[a] * R[a], rd[a] * Z[a]
            for c in range(a + 1, 8):
                x = x - m[c][a] * X[c]
                u = u - m[c][a] * U[c]
            X[a], U[a] = x, u
        low, side = R[0] * rs[0], Z[0] * rs[0]
        for c in range(1, 8):
            low = jnp.where(sub == c, R[c] * rs[c], low)
            side = jnp.where(sub == c, Z[c] * rs[c], side)
        inverse.append(jnp.where(lane < 8 * p + 8, low, 0.0))
        solved.append(side)
        for q in range(p + 1, tiles):
            t, v = jnp.where(block, 0.0, T[q]), V[q]
            for c in range(8):
                column = lane_spread(T[q], 8 * p + c)
                t = t - column * X[c]
                v = v - column * U[c]
            T[q], V[q] = t, v
    return jnp.concatenate(inverse, 0), jnp.concatenate(solved, 0)


def coefficients(observed, value, error):
    members, nobs = observed.shape
    mean = jnp.sum(observed, axis=0, keepdims=True) / members
    anomaly = observed - mean
    row = lax.broadcasted_iota(jnp.int32, (nobs, nobs), 0)
    col = lax.broadcasted_iota(jnp.int32, (nobs, nobs), 1)
    cov = dot(anomaly, anomaly, 0, 0) / (members - 1) + jnp.where(row == col, error, 0.0)
    sides = jnp.concatenate(
        [anomaly, value - mean, jnp.zeros((nobs - members - 1, nobs), f32)], 0
    ).T
    inverse, solved = factored(cov, sides, error, members)
    back = dot(solved, inverse, 0, 0)
    return anomaly, back[members : members + 1] - back[:members]


def chain_kernel(batches, nobs):
    def kernel(y_ref, value_ref, error_ref, taper_ref, anomaly_ref, coeff_ref):
        members = y_ref.shape[0]
        Y = [y_ref[:, nobs * b : nobs * (b + 1)] for b in range(batches)]
        slot = 0
        for b in range(batches):
            anomaly, coeff = coefficients(Y[b], value_ref[b : b + 1, :], error_ref[b : b + 1, :])
            anomaly_ref[b] = anomaly
            coeff_ref[b] = coeff
            for e in range(b + 1, batches):
                spread = Y[e] - jnp.sum(Y[e], axis=0, keepdims=True) / members
                gain = dot(anomaly, spread, 0, 0) / (members - 1) * taper_ref[slot]
                Y[e] = Y[e] + dot(coeff, gain, 1, 0)
                slot += 1

    return kernel


def update_kernel(width, comps, batches, members, cols_dev, count, group):
    def kernel(
        place_ref, own_ref, north_ref, south_ref, cx_ref, cy_ref, d_ref,
        anomaly_ref, coeff_ref, taper_ref, out_ref, grid_ref,
    ):
        start = pl.multiple_of(place_ref[1] * cols_dev, cols_dev)
        cx = cx_ref[:, pl.ds(start, cols_dev)]
        cy = cy_ref[:, pl.ds(start, cols_dev)]
        d = d_ref[:, pl.ds(start, cols_dev)]
        lane = lax.broadcasted_iota(jnp.int32, (1, cols_dev), 1)
        for s in range(own_ref.shape[0]):
            outer = to_columns(own_ref[s, count:, :])
            for j in range(-(-count // 128)):
                size = min(128, count - 128 * j)
                at = slice(128 * j, 128 * j + size)
                q, north, south = own_ref[s, at, :], north_ref[s, at, :], south_ref[s, at, :]
                west = jnp.where(lane == 0, outer[:size, 2 * j : 2 * j + 1], pltpu.roll(q, 1, 1))
                east = jnp.where(
                    lane == cols_dev - 1,
                    outer[:size, 2 * j + 1 : 2 * j + 2],
                    pltpu.roll(q, cols_dev - 1, 1),
                )
                x = q - jnp.maximum(cx, 0.0) * (q - west) - jnp.minimum(cx, 0.0) * (east - q)
                x = x - jnp.maximum(cy, 0.0) * (q - south) - jnp.minimum(cy, 0.0) * (north - q)
                x = x + d * (east + west + north + south - 4.0 * q)
                grid_ref[pl.ds(s * count + 128 * j, size), :] = x
        left, right, tapers = [], [], []
        nobs = anomaly_ref.shape[2]
        fill = -3 * members % 128
        blank = jnp.zeros((fill, group * cols_dev), bf16)
        for b in range(batches):
            hi, lo = split2(anomaly_ref[b])
            left.append(jnp.concatenate([hi, lo, hi, jnp.zeros((fill, nobs), bf16)], 0))
            hi, lo = split2(coeff_ref[b])
            right.append(jnp.concatenate([hi, hi, lo], 1))
            tapers.append(jnp.tile(taper_ref[b] / (members - 1), (1, group)))
        for first in range(0, comps, group):
            x = jnp.concatenate(
                [grid_ref[pl.ds(first + i, members, comps), :] for i in range(group)], 1
            )
            for b in range(batches):
                spread = x - jnp.sum(x, axis=0, keepdims=True) / members
                hi, lo = split2(spread)
                gain = narrow(left[b], jnp.concatenate([hi, hi, lo, blank], 0), 0, 0) * tapers[b]
                hi, lo = split2(gain)
                x = x + narrow(right[b], jnp.concatenate([hi, lo, hi], 0), 1, 0)
            for i in range(group):
                out_ref[pl.ds(first + i, members, comps), :] = x[:, i * cols_dev : (i + 1) * cols_dev]

    return kernel


def summed(x, axis):
    size = lax.axis_size(axis)
    if size & (size - 1):
        return lax.psum(x, axis)
    step = 1
    while step < size:
        x = x + lax.ppermute(x, axis, [(i, i ^ step) for i in range(size)])
        step *= 2
    return x


def shards(
    prior_sample_array,
    courant_x,
    courant_y,
    diffusion,
    obs_cell,
    obs_value,
    obs_error,
    obs_weight,
    taper_radius,
):
    local, rows_dev, comps, width = prior_sample_array.shape
    blocks = lax.axis_size("mem")
    bands = lax.axis_size("sub")
    cols_dev = width // blocks
    members = local * blocks
    batches, nobs = obs_cell.shape
    count = local * comps
    edge_rows = -(-(2 * -(-count // 128)) // 8) * 8
    assert rows_dev == 1 and cols_dev == 128 and nobs == 128
    place = jnp.stack([lax.axis_index("sub"), lax.axis_index("mem")]).astype(jnp.int32)
    up = [(i, i + 1) for i in range(bands - 1)]
    down = [(i + 1, i) for i in range(bands - 1)]

    above = lax.ppermute(jnp.maximum(courant_y, 0.0) + diffusion, "sub", down)
    below = lax.ppermute(diffusion - jnp.minimum(courant_y, 0.0), "sub", up)
    own, raw, send = call(
        observe_kernel(width, comps, batches, nobs, blocks, edge_rows),
        [(local, batches * nobs)] * 2 + [(blocks, count + edge_rows, cols_dev)],
        "observe",
        (
            prior_sample_array.reshape(count, width),
            courant_x,
            courant_y,
            diffusion,
            obs_cell,
            obs_weight,
        ),
    )
    grid = lax.all_to_all(send, "mem", 0, 0)
    (partial,) = call(
        join_kernel(width, batches, nobs),
        [(local, batches * nobs)],
        "join",
        (own, raw, above, below, obs_cell),
        (place,),
    )
    observed = lax.all_gather(summed(partial, "sub"), "mem", tiled=True)
    north = lax.ppermute(grid, "sub", down)
    south = lax.ppermute(grid, "sub", up)
    obs_taper, cell_taper = call(
        taper_kernel(width, batches, nobs, cols_dev),
        [(batches * (batches - 1) // 2, nobs, nobs), (batches, nobs, cols_dev)],
        "tapers",
        (obs_cell, taper_radius),
        (place,),
    )
    anomaly, coeff = call(
        chain_kernel(batches, nobs),
        [(batches, members, nobs)] * 2,
        "chain",
        (observed, obs_value, obs_error, obs_taper),
    )
    (out,) = call(
        update_kernel(width, comps, batches, members, cols_dev, count, 4),
        [(members * comps, cols_dev)],
        "update",
        (grid, north, south, courant_x, courant_y, diffusion, anomaly, coeff, cell_taper),
        (place,),
        (pltpu.VMEM((members * comps, cols_dev), f32),),
    )
    return out.reshape(members, rows_dev, comps, cols_dev)


def solution(mesh):
    return jax.shard_map(
        shards,
        mesh=mesh,
        in_specs=(
            P("mem", "sub", None, None),
            P("sub", None),
            P("sub", None),
            P("sub", None),
            P(),
            P(),
            P(),
            P(),
            P(),
        ),
        out_specs=P(None, "sub", None, "mem"),
        check_vma=False,
    )
```

time: 432 us -> 127 us (0.29)
  other arithmetic: 145 us -> 0.11 us
  blocking collectives: 163 us -> 24.2 us
  Pallas kernels: 0 us -> 37.1 us
  local copies, waits for them, and re-layouts: 41.1 us -> 5.86 us
  matrix products: 23.1 us -> 0 us
  starting transfers between devices: 11 us -> 19.3 us
    psum x4 -> x0, blocking collectives: 163 us -> none  [shards(): lax.psum(local_prior(existing_grid_values, obs_rows[batch_index], obs_col...]
    another operation x24 -> x1, other arithmetic: 131 us -> 0.08 us  [shards(): jnp.stack([lax.axis_index('sub'), lax.axis_index('mem')]).astype(jnp.int32)]
    pallas_call x0 -> x5, Pallas kernels: none -> 37.1 us  [call(): pl.pallas_call(kernel, in_specs=specs, out_specs=[pl.BlockSpec(memory_spa...]
    dot_general x12 -> x0, matrix products: 20 us -> none  [the longest x4 10.5 us: apply_update(): jnp.einsum('mrcx,km->rcxk', anomaly, obs_anomaly, precision=highest)]
    all_to_all x0 -> x1, blocking collectives: none -> 18 us  [shards(): grid = lax.all_to_all(send, 'mem', 0, 0)]
    ppermute x2 -> x7, starting transfers between devices: 7.21 us -> 19.3 us  [the longest x3 8.71 us: summed(): x = x + lax.ppermute(x, axis, [(i, i ^ step) for i in range(size)])]
    unnamed x64 -> x32, local copies, waits for them, and re-layouts: 17.7 us -> 5.86 us
    all_to_all x1 -> x0, waiting for transfers between devices: 10.9 us -> none  [shards(): lax.all_to_all(propagated_grids, 'mem', split_axis=3, concat_axis=0, tile...]
  transfers between devices with their start and end apart: 3 -> 7, of which waited for: 2 -> 3; matrix products, arithmetic and copies ran while one was open for 2% -> 1% of each run, Pallas kernels for 0% -> 18%
where the time goes in v1:
time: 127 us; the launch traced here: 126 us
  waiting for transfers between devices  39.5 us (31%)
  Pallas kernels  37.1 us (29%)
  blocking collectives  24.2 us (19%)
  starting transfers between devices  19.3 us (15%)
  local copies, waits for them, and re-layouts  5.86 us (5%)
    pallas_call x5, Pallas kernels, call(): pl.pallas_call(kernel, in_specs=specs, out_specs=[pl.BlockSpec(memory_spa...  37.1 us
    ppermute x1, waiting for transfers between devices, shards(): below = lax.ppermute(diffusion - jnp.minimum(courant_y, 0.0), 'sub', up)  35.4 us
    all_to_all x1, blocking collectives, shards(): grid = lax.all_to_all(send, 'mem', 0, 0)  18 us
    ppermute x3, starting transfers between devices, summed(): x = x + lax.ppermute(x, axis, [(i, i ^ step) for i in range(size)])  8.71 us
    all_gather x1, blocking collectives, shards(): observed = lax.all_gather(summed(partial, 'sub'), 'mem', tiled=True)  6.24 us
    unnamed x32, local copies, waits for them, and re-layouts  5.86 us
    ppermute x1, starting transfers between devices, shards(): below = lax.ppermute(diffusion - jnp.minimum(courant_y, 0.0), 'sub', up)  4.55 us
    ppermute x3, waiting for transfers between devices, summed(): x = x + lax.ppermute(x, axis, [(i, i ^ step) for i in range(size)])  4.14 us
  transfers between devices with their start and end apart: 7, of which 3 were waited for; matrix products, arithmetic and copies ran while one was open for 1% of the time, Pallas kernels for 18%

profile of v1, /device:TPU:0, one launch (start us, length us, event | category | flops | bytes accessed | tf_op | source)
XLA Modules:
  0.0 126.3 jit_solution(11309792964375272489)
XLA Ops:
  0.0 1.0 copy.14.weight_ref
  1.0 1.2 copy-done
  2.2 2.8 %observe.1 = (f32[20,512]{1,0:T(8,128)S(1)}, f32[20,512]{1,0:T(8,128)S(1)}, f32[4,488,128]{2,1,0:T(8,128)S(1)}) custom-call(f32[480,512]{1,0:T(8,128)S(1)} %bitcast.8, f32[1,512]{1,0:T(1,128)S(1)} %copy-done.8, f32[1,512]{1,0:T(1,128)S(1)} %copy-done.3, f32[1,512]{1,0:T(1,128)S(1)} %copy-done.5, s32[4,128]{1,0:T(4,128)S(1)} %copy-done.7, ...), custom_call_target="tpu_custom_call" | custom-call | tf_op jit(solution)/shard_map/observe/pallas_call | solution.py:39
  5.1 18.0 %all_to_all.5.own_ref = f32[4,488,128]{2,1,0:T(8,128)S(1)} all-to-all(f32[4,488,128]{2,1,0:T(8,128)S(1)} %get-tuple-element.12), channel_id=1, replica_groups=mesh['mem'=4,'sub'=8] {'mem'}, dimensions={0} | all-to-all | bytes 1998848 | tf_op jit(solution)/shard_map/all_to_all | solution.py:367
  23.1 3.4 %collective-permute-start.1 = (f32[4,488,128]{2,1,0:T(8,128)S(1)}, f32[4,488,128]{2,1,0:T(8,128)S(1)}, u32[]{:S(2)}, u32[]{:S(2)}) collective-permute-start(f32[4,488,128]{2,1,0:T(8,128)S(1)} %all_to_all.5.own_ref), channel_id=1, source_target_pairs={{0,1},{1,2},{2,3},{3,4},{4,5},{5,6},{6,7},{8,9},{9,10},{10,11},{11... | collective-permute-start | bytes 2998280 | tf_op jit(solution)/shard_map/ppermute | solution.py:377
  26.5 1.3 %collective-permute-start = (f32[4,488,128]{2,1,0:T(8,128)S(1)}, f32[4,488,128]{2,1,0:T(8,128)S(1)}, u32[]{:S(2)}, u32[]{:S(2)}) collective-permute-start(f32[4,488,128]{2,1,0:T(8,128)S(1)} %all_to_all.5.own_ref), channel_id=1, source_target_pairs={{1,0},{2,1},{3,2},{4,3},{5,4},{6,5},{7,6},{9,8},{10,9},{11,10},{12... | collective-permute-start | bytes 2998280 | tf_op jit(solution)/shard_map/ppermute | solution.py:376
  27.8 4.5 %collective-permute-start.3 = (f32[1,512]{1,0:T(1,128)S(1)}, f32[1,512]{1,0:T(1,128)S(1)}, u32[]{:S(2)}, u32[]{:S(2)}) collective-permute-start(f32[1,512]{1,0:T(1,128)S(1)} %get-tuple-element.19), channel_id=1, source_target_pairs={{0,1},{1,2},{2,3},{3,4},{4,5},{5,6},{6,7},{8,9},{9,10},{10,11},{11... | collective-permute-start | bytes 6152 | tf_op jit(solution)/shard_map/ppermute | solution.py:353
  32.4 1.3 %collective-permute-start.2 = (f32[1,512]{1,0:T(1,128)S(1)}, f32[1,512]{1,0:T(1,128)S(1)}, u32[]{:S(2)}, u32[]{:S(2)}) collective-permute-start(f32[1,512]{1,0:T(1,128)S(1)} %get-tuple-element.20), channel_id=1, source_target_pairs={{1,0},{2,1},{3,2},{4,3},{5,4},{6,5},{7,6},{9,8},{10,9},{11,10},{12... | collective-permute-start | bytes 6152 | tf_op jit(solution)/shard_map/ppermute | solution.py:352
  33.8 35.4 %collective-permute-done.3.below_ref = f32[1,512]{1,0:T(1,128)S(1)} collective-permute-done((f32[1,512]{1,0:T(1,128)S(1)}, f32[1,512]{1,0:T(1,128)S(1)}, u32[]{:S(2)}, u32[]{:S(2)}) %collective-permute-start.3) | collective-permute-done | bytes 2080 | tf_op jit(solution)/shard_map/ppermute | solution.py:353
  69.2 0.7 join.1
  69.9 2.5 %collective-permute-start.4 = (f32[20,512]{1,0:T(8,128)S(1)}, f32[20,512]{1,0:T(8,128)S(1)}, u32[]{:S(2)}, u32[]{:S(2)}) collective-permute-start(f32[20,512]{1,0:T(8,128)S(1)} %join.1), channel_id=1, source_target_pairs={{0,1},{1,0},{2,3},{3,2},{4,5},{5,4},{6,7},{7,6},{8,9},{9,8},{10,11... | collective-permute-start | bytes 122888 | tf_op jit(solution)/shard_map/ppermute | solution.py:323
  72.5 2.1 %collective-permute-done.4 = f32[20,512]{1,0:T(8,128)S(1)} collective-permute-done((f32[20,512]{1,0:T(8,128)S(1)}, f32[20,512]{1,0:T(8,128)S(1)}, u32[]{:S(2)}, u32[]{:S(2)}) %collective-permute-start.4) | collective-permute-done | bytes 40992 | tf_op jit(solution)/shard_map/ppermute | solution.py:323
  74.5 3.1 %collective-permute-start.5 = (f32[20,512]{1,0:T(8,128)S(1)}, f32[20,512]{1,0:T(8,128)S(1)}, u32[]{:S(2)}, u32[]{:S(2)}) collective-permute-start(f32[20,512]{1,0:T(8,128)S(1)} %add.13), channel_id=1, source_target_pairs={{0,2},{1,3},{2,0},{3,1},{4,6},{5,7},{6,4},{7,5},{8,10},{9,11},{10,... | collective-permute-start | bytes 122888 | tf_op jit(solution)/shard_map/ppermute | solution.py:323
  77.6 2.1 %collective-permute-done.5 = f32[20,512]{1,0:T(8,128)S(1)} collective-permute-done((f32[20,512]{1,0:T(8,128)S(1)}, f32[20,512]{1,0:T(8,128)S(1)}, u32[]{:S(2)}, u32[]{:S(2)}) %collective-permute-start.5) | collective-permute-done | bytes 40992 | tf_op jit(solution)/shard_map/ppermute | solution.py:323
  79.7 3.1 %collective-permute-start.6 = (f32[20,512]{1,0:T(8,128)S(1)}, f32[20,512]{1,0:T(8,128)S(1)}, u32[]{:S(2)}, u32[]{:S(2)}) collective-permute-start(f32[20,512]{1,0:T(8,128)S(1)} %add.14), channel_id=1, source_target_pairs={{0,4},{1,5},{2,6},{3,7},{4,0},{5,1},{6,2},{7,3},{8,12},{9,13},{10,... | collective-permute-start | bytes 122888 | tf_op jit(solution)/shard_map/ppermute | solution.py:323
  82.8 1.7 %tapers.1 = (f32[6,128,128]{2,1,0:T(8,128)S(1)}, f32[4,128,128]{2,1,0:T(8,128)S(1)}) custom-call(s32[2]{0:T(128)S(1)} %pad_add_fusion.place_ref, s32[4,128]{1,0:T(4,128)S(1)} %copy-done.7, f32[4,128]{1,0:T(4,128)S(1)} %copy-done.14), custom_call_target="tpu_custom_call" | custom-call | tf_op jit(solution)/shard_map/tapers/pallas_call | solution.py:39
  84.5 0.7 copy-done.1
  85.2 6.2 %all-gather = f32[4,20,512]{2,1,0:T(8,128)} all-gather(f32[1,20,512]{2,1,0:T(8,128)S(1)} %add_bitcast_fusion), channel_id=1, replica_groups=mesh['mem'=4,'sub'=8] {'mem'}, dimensions={0}, use_global_device_ids=true | all-gather | bytes 204800 | tf_op jit(solution)/shard_map/all_gather | solution.py:375
  91.4 0.9 reshape.9.y_ref
  92.4 0.7 copy-done.12
  93.1 0.7 copy-done.13
  93.8 20.7 %chain.1 = (f32[4,80,128]{2,1,0:T(8,128)S(1)}, f32[4,80,128]{2,1,0:T(8,128)S(1)}) custom-call(f32[80,512]{1,0:T(8,128)S(1)} %reshape.9.y_ref, f32[4,128]{1,0:T(4,128)S(1)} %copy-done.12, f32[4,128]{1,0:T(4,128)S(1)} %copy-done.13, f32[6,128,128]{2,1,0:T(8,128)S(1)} %get-tuple-element.15.taper_ref), custom_call_target="tpu_custom_call" | custom-call | tf_op jit(solution)/shard_map/chain/pallas_call | solution.py:39
  114.5 0.6 copy-done.6
  115.1 11.2 %update.1 = f32[1920,128]{1,0:T(8,128)} custom-call(s32[2]{0:T(128)S(1)} %copy-done.11, f32[4,488,128]{2,1,0:T(8,128)S(1)} %all_to_all.5.own_ref, f32[4,488,128]{2,1,0:T(8,128)S(1)} %collective-permute-done.north_ref, f32[4,488,128]{2,1,0:T(8,128)S(1)} %collective-permute-done.1.south_ref, f32[1,512]{1,0:T(1,128)S(1)} %copy-done.9, f32[1,512]{1,0:T(1,128)S(1)} %copy-done.4, ...), custom_call_target="tpu_custom_call" | custom-call | tf_op jit(solution)/shard_map/update/pallas_call | solution.py:39
  (34 shorter events, 0.2 us)
Async XLA Ops:
  0.0 1.0 copy-start.3
  0.0 1.0 copy-start.5
  0.0 1.0 copy-start.7
  0.0 1.0 copy-start.8
  1.0 1.2 copy-start
  23.1 91.4 %collective-permute-start.1 = (f32[4,488,128]{2,1,0:T(8,128)S(1)}, f32[4,488,128]{2,1,0:T(8,128)S(1)}, u32[]{:S(2)}, u32[]{:S(2)}) collective-permute-start(f32[4,488,128]{2,1,0:T(8,128)S(1)} %all_to_all.5.own_ref), channel_id=1, source_target_pairs={{0,1},{1,2},{2,3},{3,4},{4,5},{5,6},{6,7},{8,9},{9,10},{10,11},{11... | collective-permute-start | bytes 2998280 | tf_op jit(solution)/shard_map/ppermute | solution.py:377
  26.5 87.9 %collective-permute-start = (f32[4,488,128]{2,1,0:T(8,128)S(1)}, f32[4,488,128]{2,1,0:T(8,128)S(1)}, u32[]{:S(2)}, u32[]{:S(2)}) collective-permute-start(f32[4,488,128]{2,1,0:T(8,128)S(1)} %all_to_all.5.own_ref), channel_id=1, source_target_pairs={{1,0},{2,1},{3,2},{4,3},{5,4},{6,5},{7,6},{9,8},{10,9},{11,10},{12... | collective-permute-start | bytes 2998280 | tf_op jit(solution)/shard_map/ppermute | solution.py:376
  27.8 41.3 %collective-permute-start.3 = (f32[1,512]{1,0:T(1,128)S(1)}, f32[1,512]{1,0:T(1,128)S(1)}, u32[]{:S(2)}, u32[]{:S(2)}) collective-permute-start(f32[1,512]{1,0:T(1,128)S(1)} %get-tuple-element.19), channel_id=1, source_target_pairs={{0,1},{1,2},{2,3},{3,4},{4,5},{5,6},{6,7},{8,9},{9,10},{10,11},{11... | collective-permute-start | bytes 6152 | tf_op jit(solution)/shard_map/ppermute | solution.py:353
  32.4 36.8 %collective-permute-start.2 = (f32[1,512]{1,0:T(1,128)S(1)}, f32[1,512]{1,0:T(1,128)S(1)}, u32[]{:S(2)}, u32[]{:S(2)}) collective-permute-start(f32[1,512]{1,0:T(1,128)S(1)} %get-tuple-element.20), channel_id=1, source_target_pairs={{1,0},{2,1},{3,2},{4,3},{5,4},{6,5},{7,6},{9,8},{10,9},{11,10},{12... | collective-permute-start | bytes 6152 | tf_op jit(solution)/shard_map/ppermute | solution.py:352
  33.8 49.0 %copy-start.10 = (s32[2]{0:T(128)}, s32[2]{0:T(128)S(1)}, u32[]{:S(2)}) copy-start(s32[2]{0:T(128)S(1)} %pad_add_fusion.place_ref) | copy-start | bytes 28
  69.9 4.6 %collective-permute-start.4 = (f32[20,512]{1,0:T(8,128)S(1)}, f32[20,512]{1,0:T(8,128)S(1)}, u32[]{:S(2)}, u32[]{:S(2)}) collective-permute-start(f32[20,512]{1,0:T(8,128)S(1)} %join.1), channel_id=1, source_target_pairs={{0,1},{1,0},{2,3},{3,2},{4,5},{5,4},{6,7},{7,6},{8,9},{9,8},{10,11... | collective-permute-start | bytes 122888 | tf_op jit(solution)/shard_map/ppermute | solution.py:323
  74.5 8.3 %copy-start.14 = (f32[4,128]{1,0:T(4,128)S(1)}, f32[4,128]{1,0:T(4,128)}, u32[]{:S(2)}) copy-start(f32[4,128]{1,0:T(4,128)} %radius_ref.1) | copy-start | bytes 6148
  74.5 5.1 %collective-permute-start.5 = (f32[20,512]{1,0:T(8,128)S(1)}, f32[20,512]{1,0:T(8,128)S(1)}, u32[]{:S(2)}, u32[]{:S(2)}) collective-permute-start(f32[20,512]{1,0:T(8,128)S(1)} %add.13), channel_id=1, source_target_pairs={{0,2},{1,3},{2,0},{3,1},{4,6},{5,7},{6,4},{7,5},{8,10},{9,11},{10,... | collective-permute-start | bytes 122888 | tf_op jit(solution)/shard_map/ppermute | solution.py:323
  79.7 5.5 %collective-permute-start.6 = (f32[20,512]{1,0:T(8,128)S(1)}, f32[20,512]{1,0:T(8,128)S(1)}, u32[]{:S(2)}, u32[]{:S(2)}) collective-permute-start(f32[20,512]{1,0:T(8,128)S(1)} %add.14), channel_id=1, source_target_pairs={{0,4},{1,5},{2,6},{3,7},{4,0},{5,1},{6,2},{7,3},{8,12},{9,13},{10,... | collective-permute-start | bytes 122888 | tf_op jit(solution)/shard_map/ppermute | solution.py:323
  84.5 0.7 copy-start.1
  92.4 0.7 copy-start.12
  93.1 0.7 copy-start.13
  93.8 20.7 %copy-start.2 = (f32[4,128,128]{2,1,0:T(8,128)S(1)}, f32[4,128,128]{2,1,0:T(8,128)}, u32[]{:S(2)}) copy-start(f32[4,128,128]{2,1,0:T(8,128)} %copy-done.1) | copy-start | bytes 786436
  93.8 20.7 %copy-start.9 = (f32[1,512]{1,0:T(1,128)S(1)}, f32[1,512]{1,0:T(1,128)}, u32[]{:S(2)}) copy-start(f32[1,512]{1,0:T(1,128)} %cx_ref.3) | copy-start | bytes 6148
  114.4 0.7 copy-start.6
  114.5 0.7 copy-start.4
  114.5 0.7 copy-start.11

commit v2 on v1

--- a/solution.py
+++ b/solution.py
@@ -244,58 +244,76 @@
     return anomaly, back[members : members + 1] - back[:members]
 
 
-def chain_kernel(batches, nobs):
-    def kernel(y_ref, value_ref, error_ref, taper_ref, anomaly_ref, coeff_ref):
-        members = y_ref.shape[0]
-        Y = [y_ref[:, nobs * b : nobs * (b + 1)] for b in range(batches)]
-        slot = 0
-        for b in range(batches):
+def chain_kernel(part, batches, nobs):
+    def kernel(y_ref, value_ref, error_ref, taper_ref, anomaly_ref, coeff_ref, *later_ref):
+        if len(y_ref.shape) == 3:
+            observed = jnp.concatenate([y_ref[i] for i in range(y_ref.shape[0])], 0)
+        else:
+            observed = y_ref[...]
+        members = observed.shape[0]
+        first = batches - observed.shape[1] // nobs
+        Y = {b: observed[:, nobs * (b - first) : nobs * (b - first + 1)] for b in range(first, batches)}
+        for b in part:
             anomaly, coeff = coefficients(Y[b], value_ref[b : b + 1, :], error_ref[b : b + 1, :])
-            anomaly_ref[b] = anomaly
-            coeff_ref[b] = coeff
+            anomaly_ref[b - first] = anomaly
+            coeff_ref[b - first] = coeff
             for e in range(b + 1, batches):
+                slot = b * batches - b * (b + 1) // 2 + e - b - 1
                 spread = Y[e] - jnp.sum(Y[e], axis=0, keepdims=True) / members
                 gain = dot(anomaly, spread, 0, 0) / (members - 1) * taper_ref[slot]
                 Y[e] = Y[e] + dot(coeff, gain, 1, 0)
-                slot += 1
+        for e in range(part[-1] + 1, batches):
+            at = e - part[-1] - 1
+            later_ref[0][:, nobs * at : nobs * (at + 1)] = Y[e]
 
     return kernel
 
 
 def update_kernel(width, comps, batches, members, cols_dev, count, group):
     def kernel(
-        place_ref, own_ref, north_ref, south_ref, cx_ref, cy_ref, d_ref,
-        anomaly_ref, coeff_ref, taper_ref, out_ref, grid_ref,
+        place_ref, own_ref, near_ref, far_ref, cx_ref, cy_ref, d_ref,
+        taper_ref, *refs,
     ):
+        *pair_refs, out_ref, grid_ref = refs
+        pairs = [
+            (pair_refs[i][k], pair_refs[i + 1][k])
+            for i in range(0, len(pair_refs), 2)
+            for k in range(pair_refs[i].shape[0])
+        ]
         start = pl.multiple_of(place_ref[1] * cols_dev, cols_dev)
         cx = cx_ref[:, pl.ds(start, cols_dev)]
         cy = cy_ref[:, pl.ds(start, cols_dev)]
         d = d_ref[:, pl.ds(start, cols_dev)]
         lane = lax.broadcasted_iota(jnp.int32, (1, cols_dev), 1)
+        even = jnp.full((1, cols_dev), place_ref[0] & 1, jnp.int32) == 0
+        from_south, from_north = jnp.maximum(cy, 0.0), -jnp.minimum(cy, 0.0)
+        from_near = jnp.where(even, from_north, from_south)
+        from_far = jnp.where(even, from_south, from_north)
+        from_west, from_east = jnp.maximum(cx, 0.0), -jnp.minimum(cx, 0.0)
         for s in range(own_ref.shape[0]):
             outer = to_columns(own_ref[s, count:, :])
             for j in range(-(-count // 128)):
                 size = min(128, count - 128 * j)
                 at = slice(128 * j, 128 * j + size)
-                q, north, south = own_ref[s, at, :], north_ref[s, at, :], south_ref[s, at, :]
+                q, near, far = own_ref[s, at, :], near_ref[s, at, :], far_ref[s, at, :]
                 west = jnp.where(lane == 0, outer[:size, 2 * j : 2 * j + 1], pltpu.roll(q, 1, 1))
                 east = jnp.where(
                     lane == cols_dev - 1,
                     outer[:size, 2 * j + 1 : 2 * j + 2],
                     pltpu.roll(q, cols_dev - 1, 1),
                 )
-                x = q - jnp.maximum(cx, 0.0) * (q - west) - jnp.minimum(cx, 0.0) * (east - q)
-                x = x - jnp.maximum(cy, 0.0) * (q - south) - jnp.minimum(cy, 0.0) * (north - q)
-                x = x + d * (east + west + north + south - 4.0 * q)
+                x = q - from_west * (q - west) - from_east * (q - east)
+                x = x - from_near * (q - near) - from_far * (q - far)
+                x = x + d * (east + west + near + far - 4.0 * q)
                 grid_ref[pl.ds(s * count + 128 * j, size), :] = x
         left, right, tapers = [], [], []
-        nobs = anomaly_ref.shape[2]
+        nobs = taper_ref.shape[1]
         fill = -3 * members % 128
         blank = jnp.zeros((fill, group * cols_dev), bf16)
         for b in range(batches):
-            hi, lo = split2(anomaly_ref[b])
+            hi, lo = split2(pairs[b][0])
             left.append(jnp.concatenate([hi, lo, hi, jnp.zeros((fill, nobs), bf16)], 0))
-            hi, lo = split2(coeff_ref[b])
+            hi, lo = split2(pairs[b][1])
             right.append(jnp.concatenate([hi, hi, lo], 1))
             tapers.append(jnp.tile(taper_ref[b] / (members - 1), (1, group)))
         for first in range(0, comps, group):
@@ -344,7 +362,7 @@
     batches, nobs = obs_cell.shape
     count = local * comps
     edge_rows = -(-(2 * -(-count // 128)) // 8) * 8
-    assert rows_dev == 1 and cols_dev == 128 and nobs == 128
+    assert bands % 2 == 0 and rows_dev == 1 and cols_dev == 128 and nobs == 128
     place = jnp.stack([lax.axis_index("sub"), lax.axis_index("mem")]).astype(jnp.int32)
     up = [(i, i + 1) for i in range(bands - 1)]
     down = [(i + 1, i) for i in range(bands - 1)]
@@ -364,7 +382,7 @@
             obs_weight,
         ),
     )
-    grid = lax.all_to_all(send, "mem", 0, 0)
+    grid = lax.all_to_all(send.reshape(blocks, 1, -1), "mem", 0, 0).reshape(send.shape)
     (partial,) = call(
         join_kernel(width, batches, nobs),
         [(local, batches * nobs)],
@@ -372,9 +390,6 @@
         (own, raw, above, below, obs_cell),
         (place,),
     )
-    observed = lax.all_gather(summed(partial, "sub"), "mem", tiled=True)
-    north = lax.ppermute(grid, "sub", down)
-    south = lax.ppermute(grid, "sub", up)
     obs_taper, cell_taper = call(
         taper_kernel(width, batches, nobs, cols_dev),
         [(batches * (batches - 1) // 2, nobs, nobs), (batches, nobs, cols_dev)],
@@ -382,17 +397,33 @@
         (obs_cell, taper_radius),
         (place,),
     )
-    anomaly, coeff = call(
-        chain_kernel(batches, nobs),
-        [(batches, members, nobs)] * 2,
-        "chain",
-        (observed, obs_value, obs_error, obs_taper),
+    reduced = summed(partial, "sub")
+    reduced, grid = lax.optimization_barrier((reduced, grid))
+    observed = lax.all_gather(reduced, "mem")
+    near = lax.ppermute(grid, "sub", [(i, i ^ 1) for i in range(bands)])
+    pairs = []
+    half = batches // 2
+    for part in (range(half), range(half, batches)):
+        outs = call(
+            chain_kernel(part, batches, nobs),
+            [(len(part), members, nobs)] * 2
+            + [(members, (batches - part[-1] - 1) * nobs)] * (part[-1] + 1 < batches),
+            "chain",
+            (observed, obs_value, obs_error, obs_taper),
+        )
+        pairs += outs[:2]
+        if part[-1] + 1 < batches:
+            observed, near = lax.optimization_barrier((outs[2], near))
+    far = lax.ppermute(
+        near,
+        "sub",
+        [(i, i + 2) for i in range(0, bands - 2, 2)] + [(i, i - 2) for i in range(3, bands, 2)],
     )
     (out,) = call(
         update_kernel(width, comps, batches, members, cols_dev, count, 4),
         [(members * comps, cols_dev)],
         "update",
-        (grid, north, south, courant_x, courant_y, diffusion, anomaly, coeff, cell_taper),
+        (grid, near, far, courant_x, courant_y, diffusion, cell_taper, *pairs),
         (place,),
         (pltpu.VMEM((members * comps, cols_dev), f32),),
     )

time: 127 us -> 92 us (0.72)
  blocking collectives: 24.2 us -> 5.95 us
  waiting for transfers between devices: 39.5 us -> 22.7 us
  local copies, waits for them, and re-layouts: 5.86 us -> 2.2 us
  starting transfers between devices: 19.3 us -> 22.7 us
    ppermute x1, waiting for transfers between devices: 35.4 us -> 0.01 us  [shards(): below = lax.ppermute(diffusion - jnp.minimum(courant_y, 0.0), 'sub', up)]
    all_to_all x1 -> x0, blocking collectives: 18 us -> none  [shards(): grid = lax.all_to_all(send, 'mem', 0, 0)]
    ppermute x2, waiting for transfers between devices: 0.01 us -> 11.8 us  [the longest x1 11.8 us: shards(): lax.ppermute(near, 'sub', [(i, i + 2) for i in range(0, bands - 2, 2)] +...]
    all_to_all x0 -> x1, starting transfers between devices: none -> 4.24 us  [shards(): lax.all_to_all(send.reshape(blocks, 1, -1), 'mem', 0, 0).reshape(send.shape)]
    ppermute x1, waiting for transfers between devices: 0.01 us -> 4.1 us  [shards(): above = lax.ppermute(jnp.maximum(courant_y, 0.0) + diffusion, 'sub', down)]
    unnamed x32 -> x17, local copies, waits for them, and re-layouts: 5.86 us -> 2.2 us
    ppermute x3, waiting for transfers between devices: 4.14 us -> 6.75 us  [summed(): x = x + lax.ppermute(x, axis, [(i, i ^ step) for i in range(size)])]
    ppermute x3, starting transfers between devices: 8.71 us -> 7.04 us  [summed(): x = x + lax.ppermute(x, axis, [(i, i ^ step) for i in range(size)])]
  transfers between devices with their start and end apart: 7 -> 8, of which waited for: 3 -> 5; matrix products, arithmetic and copies ran while one was open for 1% -> 0% of each run, Pallas kernels for 18% -> 25%
where the time goes in v2:
time: 92 us; the launch traced here: 91.7 us
  Pallas kernels  37.9 us (41%)
  starting transfers between devices  22.7 us (25%)
  waiting for transfers between devices  22.7 us (25%)
  blocking collectives  5.95 us (6%)
  local copies, waits for them, and re-layouts  2.2 us (2%)
    pallas_call x6, Pallas kernels, call(): pl.pallas_call(kernel, in_specs=specs, out_specs=[pl.BlockSpec(memory_spa...  37.9 us
    ppermute x1, waiting for transfers between devices, shards(): lax.ppermute(near, 'sub', [(i, i + 2) for i in range(0, bands - 2, 2)] +...  11.8 us
    ppermute x3, starting transfers between devices, summed(): x = x + lax.ppermute(x, axis, [(i, i ^ step) for i in range(size)])  7.04 us
    ppermute x3, waiting for transfers between devices, summed(): x = x + lax.ppermute(x, axis, [(i, i ^ step) for i in range(size)])  6.75 us
    all_gather x1, blocking collectives, shards(): observed = lax.all_gather(reduced, 'mem')  5.95 us
    all_to_all x1, starting transfers between devices, shards(): lax.all_to_all(send.reshape(blocks, 1, -1), 'mem', 0, 0).reshape(send.shape)  4.24 us
    ppermute x1, starting transfers between devices, shards(): below = lax.ppermute(diffusion - jnp.minimum(courant_y, 0.0), 'sub', up)  4.13 us
    ppermute x1, waiting for transfers between devices, shards(): above = lax.ppermute(jnp.maximum(courant_y, 0.0) + diffusion, 'sub', down)  4.1 us
  transfers between devices with their start and end apart: 8, of which 5 were waited for; matrix products, arithmetic and copies ran while one was open for 0% of the time, Pallas kernels for 25%

profile of v2, /device:TPU:0, one launch (start us, length us, event | category | flops | bytes accessed | tf_op | source)
XLA Modules:
  0.0 91.7 jit_solution(16834750016774357135)
XLA Ops:
  0.0 1.0 %copy.12.weight_ref = f32[4,128,24]{2,1,0:T(8,128)S(1)} copy(f32[4,128,24]{1,2,0:T(8,128)} %param.16) | data formatting | bytes 98304 | tf_op args[7]
  1.0 1.2 %copy-done = f32[20,1,24,512]{3,2,1,0:T(8,128)S(1)} copy-done((f32[20,1,24,512]{3,2,1,0:T(8,128)S(1)}, f32[20,1,24,512]{3,2,1,0:T(8,128)}, u32[]{:S(2)}) %copy-start) | copy-done | bytes 983064
  2.2 3.8 %observe.1 = (f32[20,512]{1,0:T(8,128)S(1)}, f32[20,512]{1,0:T(8,128)S(1)}, f32[4,488,128]{2,1,0:T(8,128)}) custom-call(f32[480,512]{1,0:T(8,128)S(1)} %bitcast.11, f32[1,512]{1,0:T(1,128)S(1)} %copy-done.4, f32[1,512]{1,0:T(1,128)S(1)} %copy-done.1, f32[1,512]{1,0:T(1,128)S(1)} %copy-done.2, s32[4,128]{1,0:T(4,128)S(1)} %copy-done.3, ...), custom_call_target="tpu_custom_call" | custom-call | tf_op jit(solution)/shard_map/observe/pallas_call | solution.py:39
  6.1 4.2 %all-to-all-start = ((f32[4,1,62464]{2,1,0:T(1,128)}), f32[4,1,62464]{2,1,0:T(1,128)S(1)}, u32[]{:S(2)}, u32[]{:S(2)}) async-start(f32[4,1,62464]{2,1,0:T(1,128)} %bitcast.3), calls=%async_computation | async-start | bytes 1998848 | tf_op jit(solution)/shard_map/all_to_all | solution.py:385
  10.3 4.1 %collective-permute-start.1 = (f32[1,512]{1,0:T(1,128)S(1)}, f32[1,512]{1,0:T(1,128)S(1)}, u32[]{:S(2)}, u32[]{:S(2)}) collective-permute-start(f32[1,512]{1,0:T(1,128)S(1)} %get-tuple-element.33), channel_id=1, source_target_pairs={{0,1},{1,2},{2,3},{3,4},{4,5},{5,6},{6,7},{8,9},{9,10},{10,11},{11... | collective-permute-start | bytes 6152 | tf_op jit(solution)/shard_map/ppermute | solution.py:371
  14.5 1.3 %collective-permute-start = (f32[1,512]{1,0:T(1,128)S(1)}, f32[1,512]{1,0:T(1,128)S(1)}, u32[]{:S(2)}, u32[]{:S(2)}) collective-permute-start(f32[1,512]{1,0:T(1,128)S(1)} %get-tuple-element.34), channel_id=1, source_target_pairs={{1,0},{2,1},{3,2},{4,3},{5,4},{6,5},{7,6},{9,8},{10,9},{11,10},{12... | collective-permute-start | bytes 6152 | tf_op jit(solution)/shard_map/ppermute | solution.py:370
  15.8 0.1 pad_add_fusion.place_ref
  15.8 4.1 %collective-permute-done.above_ref = f32[1,512]{1,0:T(1,128)S(1)} collective-permute-done((f32[1,512]{1,0:T(1,128)S(1)}, f32[1,512]{1,0:T(1,128)S(1)}, u32[]{:S(2)}, u32[]{:S(2)}) %collective-permute-start) | collective-permute-done | bytes 2080 | tf_op jit(solution)/shard_map/ppermute | solution.py:370
  19.9 0.7 join.1
  20.7 2.5 %collective-permute-start.2 = (f32[20,512]{1,0:T(8,128)S(1)}, f32[20,512]{1,0:T(8,128)S(1)}, u32[]{:S(2)}, u32[]{:S(2)}) collective-permute-start(f32[20,512]{1,0:T(8,128)S(1)} %join.1), channel_id=1, source_target_pairs={{0,1},{1,0},{2,3},{3,2},{4,5},{5,4},{6,7},{7,6},{8,9},{9,8},{10,11... | collective-permute-start | bytes 122888 | tf_op jit(solution)/shard_map/ppermute | solution.py:341
  23.2 2.1 %collective-permute-done.2 = f32[20,512]{1,0:T(8,128)S(1)} collective-permute-done((f32[20,512]{1,0:T(8,128)S(1)}, f32[20,512]{1,0:T(8,128)S(1)}, u32[]{:S(2)}, u32[]{:S(2)}) %collective-permute-start.2) | collective-permute-done | bytes 40992 | tf_op jit(solution)/shard_map/ppermute | solution.py:341
  25.3 1.6 %collective-permute-start.3 = (f32[20,512]{1,0:T(8,128)S(1)}, f32[20,512]{1,0:T(8,128)S(1)}, u32[]{:S(2)}, u32[]{:S(2)}) collective-permute-start(f32[20,512]{1,0:T(8,128)S(1)} %add.13), channel_id=1, source_target_pairs={{0,2},{1,3},{2,0},{3,1},{4,6},{5,7},{6,4},{7,5},{8,10},{9,11},{10,... | collective-permute-start | bytes 122888 | tf_op jit(solution)/shard_map/ppermute | solution.py:341
  26.9 2.5 %collective-permute-done.3 = f32[20,512]{1,0:T(8,128)S(1)} collective-permute-done((f32[20,512]{1,0:T(8,128)S(1)}, f32[20,512]{1,0:T(8,128)S(1)}, u32[]{:S(2)}, u32[]{:S(2)}) %collective-permute-start.3) | collective-permute-done | bytes 40992 | tf_op jit(solution)/shard_map/ppermute | solution.py:341
  29.4 2.9 %collective-permute-start.4 = (f32[20,512]{1,0:T(8,128)S(1)}, f32[20,512]{1,0:T(8,128)S(1)}, u32[]{:S(2)}, u32[]{:S(2)}) collective-permute-start(f32[20,512]{1,0:T(8,128)S(1)} %add.14), channel_id=1, source_target_pairs={{0,4},{1,5},{2,6},{3,7},{4,0},{5,1},{6,2},{7,3},{8,12},{9,13},{10,... | collective-permute-start | bytes 122888 | tf_op jit(solution)/shard_map/ppermute | solution.py:341
  32.3 2.2 %collective-permute-done.4 = f32[20,512]{1,0:T(8,128)S(1)} collective-permute-done((f32[20,512]{1,0:T(8,128)S(1)}, f32[20,512]{1,0:T(8,128)S(1)}, u32[]{:S(2)}, u32[]{:S(2)}) %collective-permute-start.4) | collective-permute-done | bytes 40992 | tf_op jit(solution)/shard_map/ppermute | solution.py:341
  34.5 2.2 %collective-permute-start.5 = (f32[4,488,128]{2,1,0:T(8,128)S(1)}, f32[4,488,128]{2,1,0:T(8,128)S(1)}, u32[]{:S(2)}, u32[]{:S(2)}) collective-permute-start(f32[4,488,128]{2,1,0:T(8,128)S(1)} %bitcast.9), channel_id=1, source_target_pairs={{0,1},{1,0},{2,3},{3,2},{4,5},{5,4},{6,7},{7,6},{8,9},{9,8},{10,11... | collective-permute-start | bytes 2998280 | tf_op jit(solution)/shard_map/ppermute | solution.py:403
  36.7 1.7 %tapers.1 = (f32[6,128,128]{2,1,0:T(8,128)S(1)}, f32[4,128,128]{2,1,0:T(8,128)S(1)}) custom-call(s32[2]{0:T(128)S(1)} %pad_add_fusion.place_ref, s32[4,128]{1,0:T(4,128)S(1)} %copy-done.3, f32[4,128]{1,0:T(4,128)S(1)} %copy-done.7), custom_call_target="tpu_custom_call" | custom-call | tf_op jit(solution)/shard_map/tapers/pallas_call | solution.py:39
  38.4 0.0 copy-start.5
  38.4 6.0 %all-gather.1.y_ref = f32[4,20,512]{2,1,0:T(8,128)S(1)} all-gather(f32[1,20,512]{2,1,0:T(8,128)S(1)} %bitcast.12), channel_id=2, replica_groups=mesh['mem'=4,'sub'=8] {'mem'}, dimensions={0}, use_global_device_ids=true | all-gather | bytes 204800 | tf_op jit(solution)/shard_map/all_gather | solution.py:402
  44.4 10.7 %chain.2 = (f32[2,80,128]{2,1,0:T(8,128)S(1)}, f32[2,80,128]{2,1,0:T(8,128)S(1)}, f32[80,256]{1,0:T(8,128)S(1)}) custom-call(f32[4,20,512]{2,1,0:T(8,128)S(1)} %all-gather.1.y_ref, f32[4,128]{1,0:T(4,128)S(1)} %copy-done.5, f32[4,128]{1,0:T(4,128)S(1)} %copy-done.6, f32[6,128,128]{2,1,0:T(8,128)S(1)} %get-tuple-element.24.taper_ref), custom_call_target="tpu_custom_call" | custom-call | tf_op jit(solution)/shard_map/chain/pallas_call | solution.py:39
  55.1 3.8 %collective-permute-start.6 = (f32[4,488,128]{2,1,0:T(8,128)S(1)}, f32[4,488,128]{2,1,0:T(8,128)S(1)}, u32[]{:S(2)}, u32[]{:S(2)}) collective-permute-start(f32[4,488,128]{2,1,0:T(8,128)S(1)} %collective-permute-done.5.near_ref), channel_id=1, source_target_pairs={{0,2},{2,4},{4,6},{3,1},{5,3},{7,5},{8,10},{10,12},{12,14},{11,9},... | collective-permute-start | bytes 2998280 | tf_op jit(solution)/shard_map/ppermute | solution.py:417
  58.9 9.7 %chain.3 = (f32[2,80,128]{2,1,0:T(8,128)S(1)}, f32[2,80,128]{2,1,0:T(8,128)S(1)}) custom-call(f32[80,256]{1,0:T(8,128)S(1)} %get-tuple-element.30.y_ref, f32[4,128]{1,0:T(4,128)S(1)} %copy-done.5, f32[4,128]{1,0:T(4,128)S(1)} %copy-done.6, f32[6,128,128]{2,1,0:T(8,128)S(1)} %get-tuple-element.24.taper_ref), custom_call_target="tpu_custom_call" | custom-call | tf_op jit(solution)/shard_map/chain/pallas_call | solution.py:39
  68.7 11.8 %collective-permute-done.6.far_ref = f32[4,488,128]{2,1,0:T(8,128)S(1)} collective-permute-done((f32[4,488,128]{2,1,0:T(8,128)S(1)}, f32[4,488,128]{2,1,0:T(8,128)S(1)}, u32[]{:S(2)}, u32[]{:S(2)}) %collective-permute-start.6) | collective-permute-done | bytes 999456 | tf_op jit(solution)/shard_map/ppermute | solution.py:417
  80.5 11.2 %update.1 = f32[1920,128]{1,0:T(8,128)} custom-call(s32[2]{0:T(128)S(1)} %pad_add_fusion.place_ref, f32[4,488,128]{2,1,0:T(8,128)S(1)} %bitcast.10, f32[4,488,128]{2,1,0:T(8,128)S(1)} %collective-permute-done.5.near_ref, f32[4,488,128]{2,1,0:T(8,128)S(1)} %collective-permute-done.6.far_ref, f32[1,512]{1,0:T(1,128)S(1)} %copy-done.4, f32[1,512]{1,0:T(1,128)S(1)} %copy-done.1, ...), custom_call_target="tpu_custom_call" | custom-call | tf_op jit(solution)/shard_map/update/pallas_call | solution.py:39
  (21 shorter events, 0.1 us)
Async XLA Ops:
  0.0 1.0 %copy-start.1 = (f32[1,512]{1,0:T(1,128)S(1)}, f32[1,512]{1,0:T(1,128)}, u32[]{:S(2)}) copy-start(f32[1,512]{1,0:T(1,128)} %cy_ref.3) | copy-start | bytes 6148
  0.0 1.0 %copy-start.2 = (f32[1,512]{1,0:T(1,128)S(1)}, f32[1,512]{1,0:T(1,128)}, u32[]{:S(2)}) copy-start(f32[1,512]{1,0:T(1,128)} %d_ref.3) | copy-start | bytes 6148
  0.0 1.0 %copy-start.3 = (s32[4,128]{1,0:T(4,128)S(1)}, s32[4,128]{1,0:T(4,128)}, u32[]{:S(2)}) copy-start(s32[4,128]{1,0:T(4,128)} %cell_ref.5) | copy-start | bytes 6148
  0.0 1.0 %copy-start.4 = (f32[1,512]{1,0:T(1,128)S(1)}, f32[1,512]{1,0:T(1,128)}, u32[]{:S(2)}) copy-start(f32[1,512]{1,0:T(1,128)} %cx_ref.3) | copy-start | bytes 6148
  1.0 1.2 %copy-start = (f32[20,1,24,512]{3,2,1,0:T(8,128)S(1)}, f32[20,1,24,512]{3,2,1,0:T(8,128)}, u32[]{:S(2)}) copy-start(f32[20,1,24,512]{3,2,1,0:T(8,128)} %param.9) | copy-start | bytes 2949124
  6.1 28.4 %all-to-all-start = ((f32[4,1,62464]{2,1,0:T(1,128)}), f32[4,1,62464]{2,1,0:T(1,128)S(1)}, u32[]{:S(2)}, u32[]{:S(2)}) async-start(f32[4,1,62464]{2,1,0:T(1,128)} %bitcast.3), calls=%async_computation | async-start | bytes 1998848 | tf_op jit(solution)/shard_map/all_to_all | solution.py:385
  10.3 5.5 %collective-permute-start.1 = (f32[1,512]{1,0:T(1,128)S(1)}, f32[1,512]{1,0:T(1,128)S(1)}, u32[]{:S(2)}, u32[]{:S(2)}) collective-permute-start(f32[1,512]{1,0:T(1,128)S(1)} %get-tuple-element.33), channel_id=1, source_target_pairs={{0,1},{1,2},{2,3},{3,4},{4,5},{5,6},{6,7},{8,9},{9,10},{10,11},{11... | collective-permute-start | bytes 6152 | tf_op jit(solution)/shard_map/ppermute | solution.py:371
  14.5 5.5 %collective-permute-start = (f32[1,512]{1,0:T(1,128)S(1)}, f32[1,512]{1,0:T(1,128)S(1)}, u32[]{:S(2)}, u32[]{:S(2)}) collective-permute-start(f32[1,512]{1,0:T(1,128)S(1)} %get-tuple-element.34), channel_id=1, source_target_pairs={{1,0},{2,1},{3,2},{4,3},{5,4},{6,5},{7,6},{9,8},{10,9},{11,10},{12... | collective-permute-start | bytes 6152 | tf_op jit(solution)/shard_map/ppermute | solution.py:370
  20.7 4.6 %collective-permute-start.2 = (f32[20,512]{1,0:T(8,128)S(1)}, f32[20,512]{1,0:T(8,128)S(1)}, u32[]{:S(2)}, u32[]{:S(2)}) collective-permute-start(f32[20,512]{1,0:T(8,128)S(1)} %join.1), channel_id=1, source_target_pairs={{0,1},{1,0},{2,3},{3,2},{4,5},{5,4},{6,7},{7,6},{8,9},{9,8},{10,11... | collective-permute-start | bytes 122888 | tf_op jit(solution)/shard_map/ppermute | solution.py:341
  25.3 4.2 %collective-permute-start.3 = (f32[20,512]{1,0:T(8,128)S(1)}, f32[20,512]{1,0:T(8,128)S(1)}, u32[]{:S(2)}, u32[]{:S(2)}) collective-permute-start(f32[20,512]{1,0:T(8,128)S(1)} %add.13), channel_id=1, source_target_pairs={{0,2},{1,3},{2,0},{3,1},{4,6},{5,7},{6,4},{7,5},{8,10},{9,11},{10,... | collective-permute-start | bytes 122888 | tf_op jit(solution)/shard_map/ppermute | solution.py:341
  29.4 5.1 %collective-permute-start.4 = (f32[20,512]{1,0:T(8,128)S(1)}, f32[20,512]{1,0:T(8,128)S(1)}, u32[]{:S(2)}, u32[]{:S(2)}) collective-permute-start(f32[20,512]{1,0:T(8,128)S(1)} %add.14), channel_id=1, source_target_pairs={{0,4},{1,5},{2,6},{3,7},{4,0},{5,1},{6,2},{7,3},{8,12},{9,13},{10,... | collective-permute-start | bytes 122888 | tf_op jit(solution)/shard_map/ppermute | solution.py:341
  34.5 2.2 %copy-start.7 = (f32[4,128]{1,0:T(4,128)S(1)}, f32[4,128]{1,0:T(4,128)}, u32[]{:S(2)}) copy-start(f32[4,128]{1,0:T(4,128)} %radius_ref.1) | copy-start | bytes 6148
  34.5 20.6 %collective-permute-start.5 = (f32[4,488,128]{2,1,0:T(8,128)S(1)}, f32[4,488,128]{2,1,0:T(8,128)S(1)}, u32[]{:S(2)}, u32[]{:S(2)}) collective-permute-start(f32[4,488,128]{2,1,0:T(8,128)S(1)} %bitcast.9), channel_id=1, source_target_pairs={{0,1},{1,0},{2,3},{3,2},{4,5},{5,4},{6,7},{7,6},{8,9},{9,8},{10,11... | collective-permute-start | bytes 2998280 | tf_op jit(solution)/shard_map/ppermute | solution.py:403
  38.4 6.0 %copy-start.5 = (f32[4,128]{1,0:T(4,128)S(1)}, f32[4,128]{1,0:T(4,128)}, u32[]{:S(2)}) copy-start(f32[4,128]{1,0:T(4,128)} %value_ref.3) | copy-start | bytes 6148
  38.4 6.0 %copy-start.6 = (f32[4,128]{1,0:T(4,128)S(1)}, f32[4,128]{1,0:T(4,128)}, u32[]{:S(2)}) copy-start(f32[4,128]{1,0:T(4,128)} %error_ref.3) | copy-start | bytes 6148
  55.1 25.3 %collective-permute-start.6 = (f32[4,488,128]{2,1,0:T(8,128)S(1)}, f32[4,488,128]{2,1,0:T(8,128)S(1)}, u32[]{:S(2)}, u32[]{:S(2)}) collective-permute-start(f32[4,488,128]{2,1,0:T(8,128)S(1)} %collective-permute-done.5.near_ref), channel_id=1, source_target_pairs={{0,2},{2,4},{4,6},{3,1},{5,3},{7,5},{8,10},{10,12},{12,14},{11,9},... | collective-permute-start | bytes 2998280 | tf_op jit(solution)/shard_map/ppermute | solution.py:417

commit v3 on v2

--- a/solution.py
+++ b/solution.py
@@ -33,7 +33,7 @@
     return hi, mid, (rest - mid.astype(f32)).astype(bf16)
 
 
-def call(kernel, out_shapes, name, operands, scalars=(), scratch=()):
+def call(kernel, out_shapes, name, operands, scalars=(), scratch=(), cost=None):
     specs = [pl.BlockSpec(memory_space=pltpu.SMEM) for _ in scalars]
     specs += [pl.BlockSpec(memory_space=pltpu.VMEM) for _ in operands]
     return pl.pallas_call(
@@ -43,6 +43,7 @@
         out_shape=[jax.ShapeDtypeStruct(s, f32) for s in out_shapes],
         scratch_shapes=list(scratch),
         compiler_params=pltpu.CompilerParams(vmem_limit_bytes=48 * 2**20),
+        cost_estimate=cost,
         name=name,
     )(*scalars, *operands)
 
@@ -99,8 +100,9 @@
     return kernel
 
 
-def observe_kernel(width, comps, batches, nobs, blocks, edge_rows):
-    def kernel(q_ref, cx_ref, cy_ref, d_ref, cell_ref, weight_ref, own_ref, raw_ref, send_ref):
+def observe_kernel(width, comps, batches, nobs, blocks, edge_rows, local):
+    def kernel(place_ref, q_ref, cx_ref, cy_ref, d_ref, cell_ref, weight_ref, share_ref, send_ref):
+        here = place_ref[0]
         q = q_ref[...]
         count = q.shape[0]
         cx, cy, d = cx_ref[...], cy_ref[...], d_ref[...]
@@ -109,21 +111,32 @@
         mine = q - jnp.maximum(cx, 0.0) * (q - west) - jnp.minimum(cx, 0.0) * (east - q)
         mine = mine - jnp.maximum(cy, 0.0) * q + jnp.minimum(cy, 0.0) * q
         mine = mine + d * (east + west - 4.0 * q)
-        _, col = rows_cols(cell_ref[...], width)
+        from_south, from_north = jnp.maximum(cy, 0.0) + d, d - jnp.minimum(cy, 0.0)
+        even = jnp.full((1, width), here & 1, jnp.int32) == 0
+        near = jnp.where(even, from_north, from_south)
+        far = jnp.where(even, from_south, from_north)
+        scales = [part.astype(f32) for part in split3(jnp.concatenate([near, far], 0))]
+        scales = jnp.concatenate(scales + [jnp.zeros((10, width), f32)], 0).astype(bf16)
+        row, col = rows_cols(cell_ref[...], width)
         place = lax.broadcasted_iota(jnp.int32, (width, nobs), 0)
-        pieces = split2(mine) + split2(q)
-        stacked = jnp.concatenate(pieces, 0)
+        stacked = jnp.concatenate(split2(mine) + split2(q) + (scales,), 0)
         for b in range(batches):
             pick = (place == col[b : b + 1, :]).astype(f32).astype(bf16)
             found = narrow(stacked, pick, 1, 0)
-            w = jnp.concatenate(
-                [weight_ref[b], jnp.zeros((nobs, 128 - comps), f32)], 1
-            ).T[:comps]
             own = found[:count] + found[count : 2 * count]
-            raw = found[2 * count : 3 * count] + found[3 * count :]
-            at = slice(b * nobs, (b + 1) * nobs)
-            own_ref[:, at] = jnp.sum(own.reshape(-1, comps, nobs) * w[None], axis=1)
-            raw_ref[:, at] = jnp.sum(raw.reshape(-1, comps, nobs) * w[None], axis=1)
+            raw = found[2 * count : 3 * count] + found[3 * count : 4 * count]
+            scale = found[4 * count : 4 * count + 2]
+            scale = scale + found[4 * count + 2 : 4 * count + 4]
+            scale = scale + found[4 * count + 4 : 4 * count + 6]
+            away = row[b : b + 1, :] - here
+            owned, beside = away == 0, (away == 1) | (away == -1)
+            value = jnp.where(owned, own, jnp.where(beside, raw, 0.0))
+            value = jnp.sum(value.reshape(-1, comps, nobs) * weight_ref[b][None], axis=1)
+            fill = share_ref.shape[0] - local - 2
+            share = [value, jnp.where(owned, scale, 1.0)]
+            if fill:
+                share.append(jnp.zeros((fill, nobs), f32))
+            share_ref[:, b * nobs : (b + 1) * nobs] = jnp.concatenate(share, 0)
         cols_dev = width // blocks
         which = lax.broadcasted_iota(jnp.int32, (2 * blocks, width), 0)
         spot = lax.broadcasted_iota(jnp.int32, (2 * blocks, width), 1)
@@ -147,22 +160,18 @@
     return kernel
 
 
-def join_kernel(width, batches, nobs):
-    def kernel(place_ref, own_ref, raw_ref, above_ref, below_ref, cell_ref, out_ref):
-        here = place_ref[0]
-        row, col = rows_cols(cell_ref[...], width)
-        place = lax.broadcasted_iota(jnp.int32, (width, nobs), 0)
-        parts = split3(jnp.concatenate([above_ref[...], below_ref[...]], 0))
-        stacked = jnp.concatenate([p.astype(f32) for p in parts] + [jnp.zeros((2, width), f32)], 0)
-        stacked = stacked.astype(bf16)
-        for b in range(batches):
-            pick = (place == col[b : b + 1, :]).astype(f32).astype(bf16)
-            found = narrow(stacked, pick, 1, 0)
-            coef = found[0:2] + found[2:4] + found[4:6]
-            r = row[b : b + 1, :]
-            factor = jnp.where(r == here + 1, coef[0:1], jnp.where(r == here - 1, coef[1:2], 0.0))
-            at = slice(b * nobs, (b + 1) * nobs)
-            out_ref[:, at] = jnp.where(r == here, own_ref[:, at], factor * raw_ref[:, at])
+def join_kernel(local, first, last):
+    def kernel(mine_ref, other_ref, out_ref):
+        mine, other = mine_ref[...], other_ref[...]
+        at = local
+        value = mine[:local] * other[at : at + 1] + other[:local] * mine[at : at + 1]
+        if last:
+            out_ref[...] = value
+        else:
+            at = local + 1 if first else local
+            scale = mine[at : at + 1] * other[at : at + 1]
+            blank = jnp.zeros((out_ref.shape[0] - local - 1, value.shape[1]), f32)
+            out_ref[...] = jnp.concatenate([value, scale, blank], 0)
 
     return kernel
 
@@ -271,7 +280,7 @@
 
 def update_kernel(width, comps, batches, members, cols_dev, count, group):
     def kernel(
-        place_ref, own_ref, near_ref, far_ref, cx_ref, cy_ref, d_ref,
+        place_ref, own_ref, near_a, near_b, far_a, far_b, cx_ref, cy_ref, d_ref,
         taper_ref, *refs,
     ):
         *pair_refs, out_ref, grid_ref = refs
@@ -291,11 +300,13 @@
         from_far = jnp.where(even, from_south, from_north)
         from_west, from_east = jnp.maximum(cx, 0.0), -jnp.minimum(cx, 0.0)
         for s in range(own_ref.shape[0]):
+            middle = near_a.shape[0]
+            near_ref, far_ref = (near_a, far_a) if s < middle else (near_b, far_b)
             outer = to_columns(own_ref[s, count:, :])
             for j in range(-(-count // 128)):
                 size = min(128, count - 128 * j)
                 at = slice(128 * j, 128 * j + size)
-                q, near, far = own_ref[s, at, :], near_ref[s, at, :], far_ref[s, at, :]
+                q, near, far = own_ref[s, at, :], near_ref[s % middle, at, :], far_ref[s % middle, at, :]
                 west = jnp.where(lane == 0, outer[:size, 2 * j : 2 * j + 1], pltpu.roll(q, 1, 1))
                 east = jnp.where(
                     lane == cols_dev - 1,
@@ -332,17 +343,6 @@
     return kernel
 
 
-def summed(x, axis):
-    size = lax.axis_size(axis)
-    if size & (size - 1):
-        return lax.psum(x, axis)
-    step = 1
-    while step < size:
-        x = x + lax.ppermute(x, axis, [(i, i ^ step) for i in range(size)])
-        step *= 2
-    return x
-
-
 def shards(
     prior_sample_array,
     courant_x,
@@ -362,16 +362,13 @@
     batches, nobs = obs_cell.shape
     count = local * comps
     edge_rows = -(-(2 * -(-count // 128)) // 8) * 8
-    assert bands % 2 == 0 and rows_dev == 1 and cols_dev == 128 and nobs == 128
+    assert bands & (bands - 1) == 0 and bands > 1 and rows_dev == 1 and batches > 2 and cols_dev == 128 and nobs == 128
     place = jnp.stack([lax.axis_index("sub"), lax.axis_index("mem")]).astype(jnp.int32)
-    up = [(i, i + 1) for i in range(bands - 1)]
-    down = [(i + 1, i) for i in range(bands - 1)]
-
-    above = lax.ppermute(jnp.maximum(courant_y, 0.0) + diffusion, "sub", down)
-    below = lax.ppermute(diffusion - jnp.minimum(courant_y, 0.0), "sub", up)
-    own, raw, send = call(
-        observe_kernel(width, comps, batches, nobs, blocks, edge_rows),
-        [(local, batches * nobs)] * 2 + [(blocks, count + edge_rows, cols_dev)],
+
+    share_rows = -(-(local + 2) // 8) * 8
+    share, send = call(
+        observe_kernel(width, comps, batches, nobs, blocks, edge_rows, local),
+        [(share_rows, batches * nobs), (blocks, count + edge_rows, cols_dev)],
         "observe",
         (
             prior_sample_array.reshape(count, width),
@@ -379,17 +376,11 @@
             courant_y,
             diffusion,
             obs_cell,
-            obs_weight,
+            obs_weight.transpose(0, 2, 1),
         ),
+        (place,),
     )
     grid = lax.all_to_all(send.reshape(blocks, 1, -1), "mem", 0, 0).reshape(send.shape)
-    (partial,) = call(
-        join_kernel(width, batches, nobs),
-        [(local, batches * nobs)],
-        "join",
-        (own, raw, above, below, obs_cell),
-        (place,),
-    )
     obs_taper, cell_taper = call(
         taper_kernel(width, batches, nobs, cols_dev),
         [(batches * (batches - 1) // 2, nobs, nobs), (batches, nobs, cols_dev)],
@@ -397,33 +388,48 @@
         (obs_cell, taper_radius),
         (place,),
     )
-    reduced = summed(partial, "sub")
-    reduced, grid = lax.optimization_barrier((reduced, grid))
-    observed = lax.all_gather(reduced, "mem")
-    near = lax.ppermute(grid, "sub", [(i, i ^ 1) for i in range(bands)])
-    pairs = []
-    half = batches // 2
-    for part in (range(half), range(half, batches)):
+    step = 1
+    while step < bands:
+        other = lax.ppermute(share, "sub", [(i, i ^ step) for i in range(bands)])
+        if step == 1:
+            other, obs_taper, cell_taper = lax.optimization_barrier((other, obs_taper, cell_taper))
+        last = 2 * step == bands
+        (share,) = call(
+            join_kernel(local, step == 1, last),
+            [(local if last else share_rows, batches * nobs)],
+            "join",
+            (share, other),
+        )
+        step *= 2
+    share, grid = lax.optimization_barrier((share, grid))
+    swap = [(i, i ^ 1) for i in range(bands)]
+    onward = [(i, i + 2) for i in range(0, bands - 2, 2)] + [(i, i - 2) for i in range(3, bands, 2)]
+    middle = blocks // 2
+    near = [lax.ppermute(part, "sub", swap) for part in (grid[:middle], grid[middle:])]
+    observed = lax.all_gather(share, "mem")
+    pairs, far = [], []
+    for i, part in enumerate((range(1), range(1, 2), range(2, batches))):
+        if i != 1:
+            at = i // 2
+            observed, near[at] = lax.optimization_barrier((observed, near[at]))
+            if at:
+                observed, far[0] = lax.optimization_barrier((observed, far[0]))
+            far.append(lax.ppermute(near[at], "sub", onward))
         outs = call(
             chain_kernel(part, batches, nobs),
             [(len(part), members, nobs)] * 2
             + [(members, (batches - part[-1] - 1) * nobs)] * (part[-1] + 1 < batches),
             "chain",
             (observed, obs_value, obs_error, obs_taper),
+            cost=pl.CostEstimate(flops=1000, bytes_accessed=1000, transcendentals=0),
         )
         pairs += outs[:2]
-        if part[-1] + 1 < batches:
-            observed, near = lax.optimization_barrier((outs[2], near))
-    far = lax.ppermute(
-        near,
-        "sub",
-        [(i, i + 2) for i in range(0, bands - 2, 2)] + [(i, i - 2) for i in range(3, bands, 2)],
-    )
+        observed = outs[-1]
     (out,) = call(
         update_kernel(width, comps, batches, members, cols_dev, count, 4),
         [(members * comps, cols_dev)],
         "update",
-        (grid, near, far, courant_x, courant_y, diffusion, cell_taper, *pairs),
+        (grid, *near, *far, courant_x, courant_y, diffusion, cell_taper, *pairs),
         (place,),
         (pltpu.VMEM((members * comps, cols_dev), f32),),
     )

time: 92 us -> 80.1 us (0.87)
  waiting for transfers between devices: 22.7 us -> 11.5 us
    ppermute x7, waiting for transfers between devices: 22.7 us -> 11.4 us  [the longest x2 6.45 us: shards(): lax.ppermute(part, 'sub', swap)]
    ppermute x7, starting transfers between devices: 18.4 us -> 17.4 us  [the longest x2 7.95 us: shards(): far.append(lax.ppermute(near[at], 'sub', onward))]
    unnamed x17 -> x18, local copies, waits for them, and re-layouts: 2.2 us -> 2.69 us
    pallas_call x6 -> x9, Pallas kernels: 37.9 us -> 37.8 us  [call(): pl.pallas_call(kernel, in_specs=specs, out_specs=[pl.BlockSpec(memory_spa...]
  transfers between devices with their start and end apart: 8 -> 8, of which waited for: 5 -> 5; matrix products, arithmetic and copies ran while one was open for 0% -> 0% of each run, Pallas kernels for 25% -> 28%
where the time goes in v3:
time: 80.1 us; the launch traced here: 79.8 us
  Pallas kernels  37.8 us (47%)
  starting transfers between devices  21.8 us (27%)
  waiting for transfers between devices  11.5 us (14%)
  blocking collectives  5.72 us (7%)
  local copies, waits for them, and re-layouts  2.76 us (3%)
    pallas_call x9, Pallas kernels, call(): pl.pallas_call(kernel, in_specs=specs, out_specs=[pl.BlockSpec(memory_spa...  37.8 us
    ppermute x2, starting transfers between devices, shards(): far.append(lax.ppermute(near[at], 'sub', onward))  7.95 us
    ppermute x3, starting transfers between devices, shards(): other = lax.ppermute(share, 'sub', [(i, i ^ step) for i in range(bands)])  7.17 us
    ppermute x2, waiting for transfers between devices, shards(): lax.ppermute(part, 'sub', swap)  6.45 us
    all_gather x1, blocking collectives, shards(): observed = lax.all_gather(share, 'mem')  5.72 us
    ppermute x3, waiting for transfers between devices, shards(): other = lax.ppermute(share, 'sub', [(i, i ^ step) for i in range(bands)])  4.95 us
    all_to_all x1, starting transfers between devices, shards(): lax.all_to_all(send.reshape(blocks, 1, -1), 'mem', 0, 0).reshape(send.shape)  4.37 us
    unnamed x18, local copies, waits for them, and re-layouts  2.69 us
  transfers between devices with their start and end apart: 8, of which 5 were waited for; matrix products, arithmetic and copies ran while one was open for 0% of the time, Pallas kernels for 28%

profile of v3, /device:TPU:0, one launch (start us, length us, event | category | flops | bytes accessed | tf_op | source)
XLA Modules:
  0.0 79.8 jit_solution(10636494019740819743)
XLA Ops:
  0.0 0.1 pad_add_fusion.place_ref
  0.1 0.6 copy-done.7
  0.8 1.2 %copy-done = f32[20,1,24,512]{3,2,1,0:T(8,128)S(1)} copy-done((f32[20,1,24,512]{3,2,1,0:T(8,128)S(1)}, f32[20,1,24,512]{3,2,1,0:T(8,128)}, u32[]{:S(2)}) %copy-start) | copy-done | bytes 983064
  2.0 0.8 copy-done.1
  2.8 4.4 %observe.1 = (f32[24,512]{1,0:T(8,128)S(1)}, f32[4,488,128]{2,1,0:T(8,128)}) custom-call(s32[2]{0:T(128)S(1)} %pad_add_fusion.place_ref, f32[480,512]{1,0:T(8,128)S(1)} %bitcast.12, f32[1,512]{1,0:T(1,128)S(1)} %copy-done.4, f32[1,512]{1,0:T(1,128)S(1)} %copy-done.5, f32[1,512]{1,0:T(1,128)S(1)} %copy-done.6, s32[4,128]{1,0:T(4,128)S(1)} %copy-done.7, ...), custom_call_target="tpu_custom_call" | custom-call | tf_op jit(solution)/shard_map/observe/pallas_call | solution.py:39
  7.2 4.4 %all-to-all-start = ((f32[4,1,62464]{2,1,0:T(1,128)}), f32[4,1,62464]{2,1,0:T(1,128)S(1)}, u32[]{:S(2)}, u32[]{:S(2)}) async-start(f32[4,1,62464]{2,1,0:T(1,128)} %bitcast.4), calls=%async_computation | async-start | bytes 1998848 | tf_op jit(solution)/shard_map/all_to_all | solution.py:383
  11.6 2.3 %collective-permute-start = (f32[24,512]{1,0:T(8,128)S(1)}, f32[24,512]{1,0:T(8,128)S(1)}, u32[]{:S(2)}, u32[]{:S(2)}) collective-permute-start(f32[24,512]{1,0:T(8,128)S(1)} %get-tuple-element.28.mine_ref), channel_id=1, source_target_pairs={{0,1},{1,0},{2,3},{3,2},{4,5},{5,4},{6,7},{7,6},{8,9},{9,8},{10,11... | collective-permute-start | bytes 147464 | tf_op jit(solution)/shard_map/ppermute | solution.py:393
  13.9 1.7 %tapers.1 = (f32[6,128,128]{2,1,0:T(8,128)S(1)}, f32[4,128,128]{2,1,0:T(8,128)S(1)}) custom-call(s32[2]{0:T(128)S(1)} %pad_add_fusion.place_ref, s32[4,128]{1,0:T(4,128)S(1)} %copy-done.7, f32[4,128]{1,0:T(4,128)S(1)} %copy-done.8), custom_call_target="tpu_custom_call" | custom-call | tf_op jit(solution)/shard_map/tapers/pallas_call | solution.py:39
  15.5 0.6 collective-permute-done.other_ref
  16.2 1.9 %collective-permute-start.1 = (f32[24,512]{1,0:T(8,128)S(1)}, f32[24,512]{1,0:T(8,128)S(1)}, u32[]{:S(2)}, u32[]{:S(2)}) collective-permute-start(f32[24,512]{1,0:T(8,128)S(1)} %join.3.mine_ref), channel_id=1, source_target_pairs={{0,2},{1,3},{2,0},{3,1},{4,6},{5,7},{6,4},{7,5},{8,10},{9,11},{10,... | collective-permute-start | bytes 147464 | tf_op jit(solution)/shard_map/ppermute | solution.py:393
  18.1 2.2 %collective-permute-done.1.other_ref = f32[24,512]{1,0:T(8,128)S(1)} collective-permute-done((f32[24,512]{1,0:T(8,128)S(1)}, f32[24,512]{1,0:T(8,128)S(1)}, u32[]{:S(2)}, u32[]{:S(2)}) %collective-permute-start.1) | collective-permute-done | bytes 49184 | tf_op jit(solution)/shard_map/ppermute | solution.py:393
  20.3 2.9 %collective-permute-start.2 = (f32[24,512]{1,0:T(8,128)S(1)}, f32[24,512]{1,0:T(8,128)S(1)}, u32[]{:S(2)}, u32[]{:S(2)}) collective-permute-start(f32[24,512]{1,0:T(8,128)S(1)} %join.4.mine_ref), channel_id=1, source_target_pairs={{0,4},{1,5},{2,6},{3,7},{4,0},{5,1},{6,2},{7,3},{8,12},{9,13},{10,... | collective-permute-start | bytes 147464 | tf_op jit(solution)/shard_map/ppermute | solution.py:393
  23.3 2.1 %collective-permute-done.2.other_ref = f32[24,512]{1,0:T(8,128)S(1)} collective-permute-done((f32[24,512]{1,0:T(8,128)S(1)}, f32[24,512]{1,0:T(8,128)S(1)}, u32[]{:S(2)}, u32[]{:S(2)}) %collective-permute-start.2) | collective-permute-done | bytes 49184 | tf_op jit(solution)/shard_map/ppermute | solution.py:393
  25.4 0.1 all-to-all-done
  25.6 2.3 %collective-permute-start.3 = (f32[2,488,128]{2,1,0:T(8,128)S(1)}, f32[2,488,128]{2,1,0:T(8,128)S(1)}, u32[]{:S(2)}, u32[]{:S(2)}) collective-permute-start(f32[2,488,128]{2,1,0:T(8,128)S(1)} %get-tuple-element.52), channel_id=1, source_target_pairs={{0,1},{1,0},{2,3},{3,2},{4,5},{5,4},{6,7},{7,6},{8,9},{9,8},{10,11... | collective-permute-start | bytes 1499144 | tf_op jit(solution)/shard_map/ppermute | solution.py:408
  27.8 0.1 collective-permute-start.4
  27.9 5.7 %all-gather.1.y_ref = f32[4,20,512]{2,1,0:T(8,128)S(1)} all-gather(f32[1,20,512]{2,1,0:T(8,128)S(1)} %bitcast.13), channel_id=2, replica_groups=mesh['mem'=4,'sub'=8] {'mem'}, dimensions={0}, use_global_device_ids=true | all-gather | bytes 204800 | tf_op jit(solution)/shard_map/all_gather | solution.py:409
  33.6 6.4 %collective-permute-done.3.near_a = f32[2,488,128]{2,1,0:T(8,128)S(1)} collective-permute-done((f32[2,488,128]{2,1,0:T(8,128)S(1)}, f32[2,488,128]{2,1,0:T(8,128)S(1)}, u32[]{:S(2)}, u32[]{:S(2)}) %collective-permute-start.3) | collective-permute-done | bytes 499744 | tf_op jit(solution)/shard_map/ppermute | solution.py:408
  40.1 4.2 %collective-permute-start.5 = (f32[2,488,128]{2,1,0:T(8,128)S(1)}, f32[2,488,128]{2,1,0:T(8,128)S(1)}, u32[]{:S(2)}, u32[]{:S(2)}) collective-permute-start(f32[2,488,128]{2,1,0:T(8,128)S(1)} %collective-permute-done.3.near_a), channel_id=1, source_target_pairs={{0,2},{2,4},{4,6},{3,1},{5,3},{7,5},{8,10},{10,12},{12,14},{11,9},... | collective-permute-start | bytes 1499144 | tf_op jit(solution)/shard_map/ppermute | solution.py:417
  44.3 5.4 %chain.3 = (f32[1,80,128]{2,1,0:T(8,128)S(1)}, f32[1,80,128]{2,1,0:T(8,128)S(1)}, f32[80,384]{1,0:T(8,128)S(1)}) custom-call(f32[4,20,512]{2,1,0:T(8,128)S(1)} %all-gather.1.y_ref, f32[4,128]{1,0:T(4,128)S(1)} %copy-done.2, f32[4,128]{1,0:T(4,128)S(1)} %copy-done.3, f32[6,128,128]{2,1,0:T(8,128)S(1)} %get-tuple-element.37.taper_ref), custom_call_target="tpu_custom_call" | custom-call | flops 1000 | bytes 1000 | tf_op jit(solution)/shard_map/chain/pallas_call | solution.py:39
  49.8 5.3 %chain.4 = (f32[1,80,128]{2,1,0:T(8,128)S(1)}, f32[1,80,128]{2,1,0:T(8,128)S(1)}, f32[80,256]{1,0:T(8,128)S(1)}) custom-call(f32[80,384]{1,0:T(8,128)S(1)} %get-tuple-element.38.y_ref, f32[4,128]{1,0:T(4,128)S(1)} %copy-done.2, f32[4,128]{1,0:T(4,128)S(1)} %copy-done.3, f32[6,128,128]{2,1,0:T(8,128)S(1)} %get-tuple-element.37.taper_ref), custom_call_target="tpu_custom_call" | custom-call | flops 1000 | bytes 1000 | tf_op jit(solution)/shard_map/chain/pallas_call | solution.py:39
  55.1 3.7 %collective-permute-start.6 = (f32[2,488,128]{2,1,0:T(8,128)S(1)}, f32[2,488,128]{2,1,0:T(8,128)S(1)}, u32[]{:S(2)}, u32[]{:S(2)}) collective-permute-start(f32[2,488,128]{2,1,0:T(8,128)S(1)} %collective-permute-done.4.near_b), channel_id=1, source_target_pairs={{0,2},{2,4},{4,6},{3,1},{5,3},{7,5},{8,10},{10,12},{12,14},{11,9},... | collective-permute-start | bytes 1499144 | tf_op jit(solution)/shard_map/ppermute | solution.py:417
  58.8 9.7 %chain.5 = (f32[2,80,128]{2,1,0:T(8,128)S(1)}, f32[2,80,128]{2,1,0:T(8,128)S(1)}) custom-call(f32[80,256]{1,0:T(8,128)S(1)} %get-tuple-element.48.y_ref, f32[4,128]{1,0:T(4,128)S(1)} %copy-done.2, f32[4,128]{1,0:T(4,128)S(1)} %copy-done.3, f32[6,128,128]{2,1,0:T(8,128)S(1)} %get-tuple-element.37.taper_ref), custom_call_target="tpu_custom_call" | custom-call | flops 1000 | bytes 1000 | tf_op jit(solution)/shard_map/chain/pallas_call | solution.py:39
  68.5 11.2 %update.1 = f32[1920,128]{1,0:T(8,128)} custom-call(s32[2]{0:T(128)S(1)} %pad_add_fusion.place_ref, f32[4,488,128]{2,1,0:T(8,128)S(1)} %bitcast.11, f32[2,488,128]{2,1,0:T(8,128)S(1)} %collective-permute-done.3.near_a, f32[2,488,128]{2,1,0:T(8,128)S(1)} %collective-permute-done.4.near_b, f32[2,488,128]{2,1,0:T(8,128)S(1)} %collective-permute-done.5.far_a, ...), custom_call_target="tpu_custom_call" | custom-call | tf_op jit(solution)/shard_map/update/pallas_call | solution.py:39
  (22 shorter events, 0.2 us)
Async XLA Ops:
  0.0 0.7 copy-start.7
  0.0 0.7 copy-start.6
  0.0 0.7 copy-start.5
  0.1 0.7 copy-start.4
  0.8 1.2 %copy-start = (f32[20,1,24,512]{3,2,1,0:T(8,128)S(1)}, f32[20,1,24,512]{3,2,1,0:T(8,128)}, u32[]{:S(2)}) copy-start(f32[20,1,24,512]{3,2,1,0:T(8,128)} %param.9) | copy-start | bytes 2949124
  2.0 0.8 %copy-start.1 = (f32[4,128,24]{1,2,0:T(8,128)S(1)}, f32[4,128,24]{1,2,0:T(8,128)}, u32[]{:S(2)}) copy-start(f32[4,128,24]{1,2,0:T(8,128)} %param.16) | copy-start | bytes 147460
  7.2 6.7 %copy-start.8 = (f32[4,128]{1,0:T(4,128)S(1)}, f32[4,128]{1,0:T(4,128)}, u32[]{:S(2)}) copy-start(f32[4,128]{1,0:T(4,128)} %radius_ref.1) | copy-start | bytes 6148
  7.2 18.3 %all-to-all-start = ((f32[4,1,62464]{2,1,0:T(1,128)}), f32[4,1,62464]{2,1,0:T(1,128)S(1)}, u32[]{:S(2)}, u32[]{:S(2)}) async-start(f32[4,1,62464]{2,1,0:T(1,128)} %bitcast.4), calls=%async_computation | async-start | bytes 1998848 | tf_op jit(solution)/shard_map/all_to_all | solution.py:383
  11.6 4.6 %collective-permute-start = (f32[24,512]{1,0:T(8,128)S(1)}, f32[24,512]{1,0:T(8,128)S(1)}, u32[]{:S(2)}, u32[]{:S(2)}) collective-permute-start(f32[24,512]{1,0:T(8,128)S(1)} %get-tuple-element.28.mine_ref), channel_id=1, source_target_pairs={{0,1},{1,0},{2,3},{3,2},{4,5},{5,4},{6,7},{7,6},{8,9},{9,8},{10,11... | collective-permute-start | bytes 147464 | tf_op jit(solution)/shard_map/ppermute | solution.py:393
  16.2 4.2 %collective-permute-start.1 = (f32[24,512]{1,0:T(8,128)S(1)}, f32[24,512]{1,0:T(8,128)S(1)}, u32[]{:S(2)}, u32[]{:S(2)}) collective-permute-start(f32[24,512]{1,0:T(8,128)S(1)} %join.3.mine_ref), channel_id=1, source_target_pairs={{0,2},{1,3},{2,0},{3,1},{4,6},{5,7},{6,4},{7,5},{8,10},{9,11},{10,... | collective-permute-start | bytes 147464 | tf_op jit(solution)/shard_map/ppermute | solution.py:393
  20.3 5.1 %collective-permute-start.2 = (f32[24,512]{1,0:T(8,128)S(1)}, f32[24,512]{1,0:T(8,128)S(1)}, u32[]{:S(2)}, u32[]{:S(2)}) collective-permute-start(f32[24,512]{1,0:T(8,128)S(1)} %join.4.mine_ref), channel_id=1, source_target_pairs={{0,4},{1,5},{2,6},{3,7},{4,0},{5,1},{6,2},{7,3},{8,12},{9,13},{10,... | collective-permute-start | bytes 147464 | tf_op jit(solution)/shard_map/ppermute | solution.py:393
  25.6 14.5 %collective-permute-start.3 = (f32[2,488,128]{2,1,0:T(8,128)S(1)}, f32[2,488,128]{2,1,0:T(8,128)S(1)}, u32[]{:S(2)}, u32[]{:S(2)}) collective-permute-start(f32[2,488,128]{2,1,0:T(8,128)S(1)} %get-tuple-element.52), channel_id=1, source_target_pairs={{0,1},{1,0},{2,3},{3,2},{4,5},{5,4},{6,7},{7,6},{8,9},{9,8},{10,11... | collective-permute-start | bytes 1499144 | tf_op jit(solution)/shard_map/ppermute | solution.py:408
  27.8 27.3 %collective-permute-start.4 = (f32[2,488,128]{2,1,0:T(8,128)S(1)}, f32[2,488,128]{2,1,0:T(8,128)S(1)}, u32[]{:S(2)}, u32[]{:S(2)}) collective-permute-start(f32[2,488,128]{2,1,0:T(8,128)S(1)} %get-tuple-element.51), channel_id=1, source_target_pairs={{0,1},{1,0},{2,3},{3,2},{4,5},{5,4},{6,7},{7,6},{8,9},{9,8},{10,11... | collective-permute-start | bytes 1499144 | tf_op jit(solution)/shard_map/ppermute | solution.py:408
  27.9 16.4 %copy-start.2 = (f32[4,128]{1,0:T(4,128)S(1)}, f32[4,128]{1,0:T(4,128)}, u32[]{:S(2)}) copy-start(f32[4,128]{1,0:T(4,128)} %value_ref.5) | copy-start | bytes 6148
  27.9 16.4 %copy-start.3 = (f32[4,128]{1,0:T(4,128)S(1)}, f32[4,128]{1,0:T(4,128)}, u32[]{:S(2)}) copy-start(f32[4,128]{1,0:T(4,128)} %error_ref.5) | copy-start | bytes 6148
  40.1 18.7 %collective-permute-start.5 = (f32[2,488,128]{2,1,0:T(8,128)S(1)}, f32[2,488,128]{2,1,0:T(8,128)S(1)}, u32[]{:S(2)}, u32[]{:S(2)}) collective-permute-start(f32[2,488,128]{2,1,0:T(8,128)S(1)} %collective-permute-done.3.near_a), channel_id=1, source_target_pairs={{0,2},{2,4},{4,6},{3,1},{5,3},{7,5},{8,10},{10,12},{12,14},{11,9},... | collective-permute-start | bytes 1499144 | tf_op jit(solution)/shard_map/ppermute | solution.py:417
  55.1 13.5 %collective-permute-start.6 = (f32[2,488,128]{2,1,0:T(8,128)S(1)}, f32[2,488,128]{2,1,0:T(8,128)S(1)}, u32[]{:S(2)}, u32[]{:S(2)}) collective-permute-start(f32[2,488,128]{2,1,0:T(8,128)S(1)} %collective-permute-done.4.near_b), channel_id=1, source_target_pairs={{0,2},{2,4},{4,6},{3,1},{5,3},{7,5},{8,10},{10,12},{12,14},{11,9},... | collective-permute-start | bytes 1499144 | tf_op jit(solution)/shard_map/ppermute | solution.py:417

commit v4 on v3

--- a/solution.py
+++ b/solution.py
@@ -118,37 +118,46 @@
         scales = [part.astype(f32) for part in split3(jnp.concatenate([near, far], 0))]
         scales = jnp.concatenate(scales + [jnp.zeros((10, width), f32)], 0).astype(bf16)
         row, col = rows_cols(cell_ref[...], width)
-        place = lax.broadcasted_iota(jnp.int32, (width, nobs), 0)
-        stacked = jnp.concatenate(split2(mine) + split2(q) + (scales,), 0)
-        for b in range(batches):
-            pick = (place == col[b : b + 1, :]).astype(f32).astype(bf16)
-            found = narrow(stacked, pick, 1, 0)
-            own = found[:count] + found[count : 2 * count]
-            raw = found[2 * count : 3 * count] + found[3 * count : 4 * count]
-            scale = found[4 * count : 4 * count + 2]
-            scale = scale + found[4 * count + 2 : 4 * count + 4]
-            scale = scale + found[4 * count + 4 : 4 * count + 6]
-            away = row[b : b + 1, :] - here
-            owned, beside = away == 0, (away == 1) | (away == -1)
-            value = jnp.where(owned, own, jnp.where(beside, raw, 0.0))
-            value = jnp.sum(value.reshape(-1, comps, nobs) * weight_ref[b][None], axis=1)
-            fill = share_ref.shape[0] - local - 2
-            share = [value, jnp.where(owned, scale, 1.0)]
-            if fill:
-                share.append(jnp.zeros((fill, nobs), f32))
-            share_ref[:, b * nobs : (b + 1) * nobs] = jnp.concatenate(share, 0)
+        row = jnp.concatenate([row[b : b + 1] for b in range(batches)], 1)
+        col = jnp.concatenate([col[b : b + 1] for b in range(batches)], 1)
+        away = row - here
+        owned, beside = away == 0, (away == 1) | (away == -1)
+        place = lax.broadcasted_iota(jnp.int32, (width, batches * nobs), 0)
+        own_pick = (place == jnp.where(owned, col, -1)).astype(f32).astype(bf16)
+        raw_pick = (place == jnp.where(beside, col, -1)).astype(f32).astype(bf16)
+        q_parts = split3(q)
+        value = narrow(
+            jnp.concatenate(split2(mine) + q_parts[:2], 1),
+            jnp.concatenate([own_pick, own_pick, raw_pick, raw_pick], 0),
+            1,
+            0,
+        )
+        weight = jnp.concatenate([weight_ref[b] for b in range(batches)], 1)
+        value = jnp.sum(value.reshape(-1, comps, batches * nobs) * weight[None], axis=1)
+        scale = narrow(scales, own_pick, 1, 0)
+        scale = scale[0:2] + scale[2:4] + scale[4:6]
+        share = [value, jnp.where(owned, scale, 1.0)]
+        fill = share_ref.shape[0] - local - 2
+        if fill:
+            share.append(jnp.zeros((fill, batches * nobs), f32))
+        share_ref[...] = jnp.concatenate(share, 0)
         cols_dev = width // blocks
-        which = lax.broadcasted_iota(jnp.int32, (2 * blocks, width), 0)
-        spot = lax.broadcasted_iota(jnp.int32, (2 * blocks, width), 1)
+        lanes = -(-2 * blocks // 128) * 128
+        which = lax.broadcasted_iota(jnp.int32, (width, lanes), 1)
+        spot = lax.broadcasted_iota(jnp.int32, (width, lanes), 0)
         start = (which >> 1) * cols_dev
         wanted = jnp.where(which & 1 == 0, start - 1, start + cols_dev)
         wanted = jnp.where(wanted < 0, wanted + width, wanted)
-        wanted = jnp.where(wanted >= width, wanted - width, wanted)
+        wanted = jnp.where(wanted == width, 0, wanted)
         pick = (spot == wanted).astype(f32).astype(bf16)
-        edges = sum(narrow(pick, part, 1, 1) for part in split3(q)[::-1])
+        edges = narrow(
+            jnp.concatenate(q_parts, 1), jnp.concatenate([pick, pick, pick], 0), 1, 0
+        )
+        room = -count % 128
+        if room:
+            edges = jnp.concatenate([edges, jnp.zeros((room, lanes), f32)], 0)
+        edges = edges.T
         chunks = -(-count // 128)
-        if chunks * 128 > count:
-            edges = jnp.concatenate([edges, jnp.zeros((2 * blocks, chunks * 128 - count), f32)], 1)
         for i in range(blocks):
             at = slice(i * cols_dev, (i + 1) * cols_dev)
             send_ref[i, :count, :] = q[:, at]
@@ -184,7 +193,7 @@
     return jnp.broadcast_to(x[i : i + 1, :], x.shape)
 
 
-def factored(cov, sides, error, members):
+def factored(cov, sides, error, members, span=4):
     tiles = cov.shape[0] // 8
     lane = lax.broadcasted_iota(jnp.int32, TILE, 1)
     sub = lax.broadcasted_iota(jnp.int32, TILE, 0)
@@ -192,7 +201,7 @@
     V = [sides[8 * q : 8 * q + 8, :] for q in range(tiles)]
     deviation = jnp.broadcast_to(jnp.sqrt(error), TILE)
     is_member = lane < members
-    inverse, solved = [], []
+    inverse, solved, finished = [], [], []
     for p in range(tiles):
         block = (lane >= 8 * p) & (lane < 8 * p + 8)
         columns = [lane_spread(T[p], 8 * p + c) for c in range(8)]
@@ -228,14 +237,41 @@
             side = jnp.where(sub == c, Z[c] * rs[c], side)
         inverse.append(jnp.where(lane < 8 * p + 8, low, 0.0))
         solved.append(side)
-        for q in range(p + 1, tiles):
+        finished.append((low, side))
+        edge = (p // span + 1) * span
+        for q in range(p + 1, edge):
             t, v = jnp.where(block, 0.0, T[q]), V[q]
             for c in range(8):
                 column = lane_spread(T[q], 8 * p + c)
                 t = t - column * X[c]
                 v = v - column * U[c]
             T[q], V[q] = t, v
+        if p + 1 == edge and edge < tiles:
+            rows = finished[edge - span : edge]
+            upper = jnp.concatenate([low for low, _ in rows], 0)
+            keep = [
+                jnp.where((lane < 8 * (edge - span + i + 1)) | (lane >= 8 * edge), low, 0.0)
+                for i, (low, _) in enumerate(rows)
+            ]
+            side_rows = jnp.concatenate([side for _, side in rows], 0)
+            taken = products(upper, jnp.concatenate([jnp.concatenate(keep, 0), side_rows], 1))
+            inside = (lane >= 8 * (edge - span)) & (lane < 8 * edge)
+            for q in range(edge, tiles):
+                at = slice(8 * q, 8 * q + 8)
+                T[q] = jnp.where(inside, 0.0, T[q]) - taken[at, :128]
+                V[q] = V[q] - taken[at, 128:]
     return jnp.concatenate(inverse, 0), jnp.concatenate(solved, 0)
+
+
+def products(a, b):
+    ah, am, al = split3(a)
+    bh, bm, bl = split3(b)
+    return narrow(
+        jnp.concatenate([al, am, ah, am, ah, ah], 0),
+        jnp.concatenate([bh, bm, bl, bh, bm, bh], 0),
+        0,
+        0,
+    )
 
 
 def coefficients(observed, value, error):
@@ -244,12 +280,12 @@
     anomaly = observed - mean
     row = lax.broadcasted_iota(jnp.int32, (nobs, nobs), 0)
     col = lax.broadcasted_iota(jnp.int32, (nobs, nobs), 1)
-    cov = dot(anomaly, anomaly, 0, 0) / (members - 1) + jnp.where(row == col, error, 0.0)
+    cov = products(anomaly, anomaly) / (members - 1) + jnp.where(row == col, error, 0.0)
     sides = jnp.concatenate(
         [anomaly, value - mean, jnp.zeros((nobs - members - 1, nobs), f32)], 0
     ).T
     inverse, solved = factored(cov, sides, error, members)
-    back = dot(solved, inverse, 0, 0)
+    back = products(solved, inverse)
     return anomaly, back[members : members + 1] - back[:members]
 
 
@@ -266,11 +302,25 @@
             anomaly, coeff = coefficients(Y[b], value_ref[b : b + 1, :], error_ref[b : b + 1, :])
             anomaly_ref[b - first] = anomaly
             coeff_ref[b - first] = coeff
-            for e in range(b + 1, batches):
-                slot = b * batches - b * (b + 1) // 2 + e - b - 1
-                spread = Y[e] - jnp.sum(Y[e], axis=0, keepdims=True) / members
-                gain = dot(anomaly, spread, 0, 0) / (members - 1) * taper_ref[slot]
-                Y[e] = Y[e] + dot(coeff, gain, 1, 0)
+            after = range(b + 1, batches)
+            if after:
+                slot = b * batches - b * (b + 1) // 2
+                later = jnp.concatenate([Y[e] for e in after], 1)
+                spread = later - jnp.sum(later, axis=0, keepdims=True) / members
+                taper = jnp.concatenate([taper_ref[slot + i] for i in range(len(after))], 1)
+                hi, lo = split2(anomaly)
+                fill = -3 * members % 128
+                left = jnp.concatenate([hi, lo, hi, jnp.zeros((fill, nobs), bf16)], 0)
+                hi, lo = split2(spread)
+                blank = jnp.zeros((fill, later.shape[1]), bf16)
+                gain = narrow(left, jnp.concatenate([hi, hi, lo, blank], 0), 0, 0)
+                gain = gain / (members - 1) * taper
+                coeff_hi, coeff_lo = split2(coeff)
+                hi, lo = split2(gain)
+                left = jnp.concatenate([coeff_hi, coeff_hi, coeff_lo], 1)
+                later = later + narrow(left, jnp.concatenate([hi, lo, hi], 0), 1, 0)
+                for i, e in enumerate(after):
+                    Y[e] = later[:, nobs * i : nobs * (i + 1)]
         for e in range(part[-1] + 1, batches):
             at = e - part[-1] - 1
             later_ref[0][:, nobs * at : nobs * (at + 1)] = Y[e]
@@ -362,7 +412,7 @@
     batches, nobs = obs_cell.shape
     count = local * comps
     edge_rows = -(-(2 * -(-count // 128)) // 8) * 8
-    assert bands & (bands - 1) == 0 and bands > 1 and rows_dev == 1 and batches > 2 and cols_dev == 128 and nobs == 128
+    assert bands & (bands - 1) == 0 and bands > 1 and rows_dev == 1 and batches == 4 and cols_dev == 128 and nobs == 128
     place = jnp.stack([lax.axis_index("sub"), lax.axis_index("mem")]).astype(jnp.int32)
 
     share_rows = -(-(local + 2) // 8) * 8
@@ -408,13 +458,13 @@
     near = [lax.ppermute(part, "sub", swap) for part in (grid[:middle], grid[middle:])]
     observed = lax.all_gather(share, "mem")
     pairs, far = [], []
-    for i, part in enumerate((range(1), range(1, 2), range(2, batches))):
-        if i != 1:
-            at = i // 2
-            observed, near[at] = lax.optimization_barrier((observed, near[at]))
-            if at:
-                observed, far[0] = lax.optimization_barrier((observed, far[0]))
-            far.append(lax.ppermute(near[at], "sub", onward))
+    for b in range(batches):
+        part = range(b, b + 1)
+        if b == 3:
+            observed, far[0] = lax.optimization_barrier((observed, far[0]))
+        if b in (1, 2):
+            observed, near[b - 1] = lax.optimization_barrier((observed, near[b - 1]))
+            far.append(lax.ppermute(near[b - 1], "sub", onward))
         outs = call(
             chain_kernel(part, batches, nobs),
             [(len(part), members, nobs)] * 2
@@ -426,7 +476,7 @@
         pairs += outs[:2]
         observed = outs[-1]
     (out,) = call(
-        update_kernel(width, comps, batches, members, cols_dev, count, 4),
+        update_kernel(width, comps, batches, members, cols_dev, count, comps),
         [(members * comps, cols_dev)],
         "update",
         (grid, *near, *far, courant_x, courant_y, diffusion, cell_taper, *pairs),

time: 80.1 us -> 70.2 us (0.88)
  Pallas kernels: 37.8 us -> 29.5 us
  waiting for transfers between devices: 11.5 us -> 9.85 us
    pallas_call x9 -> x10, Pallas kernels: 37.8 us -> 29.5 us  [call(): pl.pallas_call(kernel, in_specs=specs, out_specs=[pl.BlockSpec(memory_spa...]
    ppermute x2, waiting for transfers between devices: 6.45 us -> 3.2 us  [shards(): lax.ppermute(part, 'sub', swap)]
    ppermute x2, waiting for transfers between devices: 0.01 us -> 1.62 us  [shards(): far.append(lax.ppermute(near[b - 1], 'sub', onward))]
  transfers between devices with their start and end apart: 8 -> 8, of which waited for: 5 -> 7; matrix products, arithmetic and copies ran while one was open for 0% -> 0% of each run, Pallas kernels for 28% -> 27%
where the time goes in v4:
time: 70.2 us; the launch traced here: 69.8 us
  Pallas kernels  29.5 us (42%)
  starting transfers between devices  21.9 us (31%)
  waiting for transfers between devices  9.85 us (14%)
  blocking collectives  5.72 us (8%)
  local copies, waits for them, and re-layouts  2.76 us (4%)
    pallas_call x10, Pallas kernels, call(): pl.pallas_call(kernel, in_specs=specs, out_specs=[pl.BlockSpec(memory_spa...  29.5 us
    ppermute x2, starting transfers between devices, shards(): far.append(lax.ppermute(near[b - 1], 'sub', onward))  8 us
    ppermute x3, starting transfers between devices, shards(): other = lax.ppermute(share, 'sub', [(i, i ^ step) for i in range(bands)])  7.17 us
    all_gather x1, blocking collectives, shards(): observed = lax.all_gather(share, 'mem')  5.72 us
    ppermute x3, waiting for transfers between devices, shards(): other = lax.ppermute(share, 'sub', [(i, i ^ step) for i in range(bands)])  4.94 us
    all_to_all x1, starting transfers between devices, shards(): lax.all_to_all(send.reshape(blocks, 1, -1), 'mem', 0, 0).reshape(send.shape)  4.37 us
    ppermute x2, waiting for transfers between devices, shards(): lax.ppermute(part, 'sub', swap)  3.2 us
    unnamed x18, local copies, waits for them, and re-layouts  2.69 us
  transfers between devices with their start and end apart: 8, of which 7 were waited for; matrix products, arithmetic and copies ran while one was open for 0% of the time, Pallas kernels for 27%

profile of v4, /device:TPU:0, one launch (start us, length us, event | category | flops | bytes accessed | tf_op | source)
XLA Modules:
  0.0 69.8 jit_solution(4201067637333817884)
XLA Ops:
  0.1 0.6 copy-done.7
  0.8 1.2 %copy-done = f32[20,1,24,512]{3,2,1,0:T(8,128)S(1)} copy-done((f32[20,1,24,512]{3,2,1,0:T(8,128)S(1)}, f32[20,1,24,512]{3,2,1,0:T(8,128)}, u32[]{:S(2)}) %copy-start) | copy-done | bytes 983064
  2.0 0.8 %copy-done.1 = f32[4,128,24]{1,2,0:T(8,128)S(1)} copy-done((f32[4,128,24]{1,2,0:T(8,128)S(1)}, f32[4,128,24]{1,2,0:T(8,128)}, u32[]{:S(2)}) %copy-start.1) | copy-done | bytes 49176
  2.8 3.8 %observe.1 = (f32[24,512]{1,0:T(8,128)S(1)}, f32[4,488,128]{2,1,0:T(8,128)}) custom-call(s32[2]{0:T(128)S(1)} %pad_add_fusion.place_ref, f32[480,512]{1,0:T(8,128)S(1)} %bitcast.12, f32[1,512]{1,0:T(1,128)S(1)} %copy-done.4, f32[1,512]{1,0:T(1,128)S(1)} %copy-done.5, f32[1,512]{1,0:T(1,128)S(1)} %copy-done.6, s32[4,128]{1,0:T(4,128)S(1)} %copy-done.7, ...), custom_call_target="tpu_custom_call" | custom-call | tf_op jit(solution)/shard_map/observe/pallas_call | solution.py:39
  6.6 4.4 %all-to-all-start = ((f32[4,1,62464]{2,1,0:T(1,128)}), f32[4,1,62464]{2,1,0:T(1,128)S(1)}, u32[]{:S(2)}, u32[]{:S(2)}) async-start(f32[4,1,62464]{2,1,0:T(1,128)} %bitcast.4), calls=%async_computation | async-start | bytes 1998848 | tf_op jit(solution)/shard_map/all_to_all | solution.py:433
  10.9 2.3 %collective-permute-start = (f32[24,512]{1,0:T(8,128)S(1)}, f32[24,512]{1,0:T(8,128)S(1)}, u32[]{:S(2)}, u32[]{:S(2)}) collective-permute-start(f32[24,512]{1,0:T(8,128)S(1)} %get-tuple-element.31.mine_ref), channel_id=1, source_target_pairs={{0,1},{1,0},{2,3},{3,2},{4,5},{5,4},{6,7},{7,6},{8,9},{9,8},{10,11... | collective-permute-start | bytes 147464 | tf_op jit(solution)/shard_map/ppermute | solution.py:443
  13.2 1.7 %tapers.1 = (f32[6,128,128]{2,1,0:T(8,128)S(1)}, f32[4,128,128]{2,1,0:T(8,128)S(1)}) custom-call(s32[2]{0:T(128)S(1)} %pad_add_fusion.place_ref, s32[4,128]{1,0:T(4,128)S(1)} %copy-done.7, f32[4,128]{1,0:T(4,128)S(1)} %copy-done.8), custom_call_target="tpu_custom_call" | custom-call | tf_op jit(solution)/shard_map/tapers/pallas_call | solution.py:39
  14.9 0.6 collective-permute-done.other_ref
  15.6 1.9 %collective-permute-start.1 = (f32[24,512]{1,0:T(8,128)S(1)}, f32[24,512]{1,0:T(8,128)S(1)}, u32[]{:S(2)}, u32[]{:S(2)}) collective-permute-start(f32[24,512]{1,0:T(8,128)S(1)} %join.3.mine_ref), channel_id=1, source_target_pairs={{0,2},{1,3},{2,0},{3,1},{4,6},{5,7},{6,4},{7,5},{8,10},{9,11},{10,... | collective-permute-start | bytes 147464 | tf_op jit(solution)/shard_map/ppermute | solution.py:443
  17.5 2.2 %collective-permute-done.1.other_ref = f32[24,512]{1,0:T(8,128)S(1)} collective-permute-done((f32[24,512]{1,0:T(8,128)S(1)}, f32[24,512]{1,0:T(8,128)S(1)}, u32[]{:S(2)}, u32[]{:S(2)}) %collective-permute-start.1) | collective-permute-done | bytes 49184 | tf_op jit(solution)/shard_map/ppermute | solution.py:443
  19.7 2.9 %collective-permute-start.2 = (f32[24,512]{1,0:T(8,128)S(1)}, f32[24,512]{1,0:T(8,128)S(1)}, u32[]{:S(2)}, u32[]{:S(2)}) collective-permute-start(f32[24,512]{1,0:T(8,128)S(1)} %join.4.mine_ref), channel_id=1, source_target_pairs={{0,4},{1,5},{2,6},{3,7},{4,0},{5,1},{6,2},{7,3},{8,12},{9,13},{10,... | collective-permute-start | bytes 147464 | tf_op jit(solution)/shard_map/ppermute | solution.py:443
  22.7 2.1 %collective-permute-done.2.other_ref = f32[24,512]{1,0:T(8,128)S(1)} collective-permute-done((f32[24,512]{1,0:T(8,128)S(1)}, f32[24,512]{1,0:T(8,128)S(1)}, u32[]{:S(2)}, u32[]{:S(2)}) %collective-permute-start.2) | collective-permute-done | bytes 49184 | tf_op jit(solution)/shard_map/ppermute | solution.py:443
  24.9 2.3 %collective-permute-start.3 = (f32[2,488,128]{2,1,0:T(8,128)S(1)}, f32[2,488,128]{2,1,0:T(8,128)S(1)}, u32[]{:S(2)}, u32[]{:S(2)}) collective-permute-start(f32[2,488,128]{2,1,0:T(8,128)S(1)} %get-tuple-element.58), channel_id=1, source_target_pairs={{0,1},{1,0},{2,3},{3,2},{4,5},{5,4},{6,7},{7,6},{8,9},{9,8},{10,11... | collective-permute-start | bytes 1499144 | tf_op jit(solution)/shard_map/ppermute | solution.py:458
  27.3 5.7 %all-gather.1.y_ref = f32[4,20,512]{2,1,0:T(8,128)S(1)} all-gather(f32[1,20,512]{2,1,0:T(8,128)S(1)} %bitcast.13), channel_id=2, replica_groups=mesh['mem'=4,'sub'=8] {'mem'}, dimensions={0}, use_global_device_ids=true | all-gather | bytes 204800 | tf_op jit(solution)/shard_map/all_gather | solution.py:459
  33.0 4.4 %chain.4 = (f32[1,80,128]{2,1,0:T(8,128)S(1)}, f32[1,80,128]{2,1,0:T(8,128)S(1)}, f32[80,384]{1,0:T(8,128)S(1)}) custom-call(f32[4,20,512]{2,1,0:T(8,128)S(1)} %all-gather.1.y_ref, f32[4,128]{1,0:T(4,128)S(1)} %copy-done.2, f32[4,128]{1,0:T(4,128)S(1)} %copy-done.3, f32[6,128,128]{2,1,0:T(8,128)S(1)} %get-tuple-element.38.taper_ref), custom_call_target="tpu_custom_call" | custom-call | flops 1000 | bytes 1000 | tf_op jit(solution)/shard_map/chain/pallas_call | solution.py:39
  37.4 2.0 %collective-permute-done.3.near_a = f32[2,488,128]{2,1,0:T(8,128)S(1)} collective-permute-done((f32[2,488,128]{2,1,0:T(8,128)S(1)}, f32[2,488,128]{2,1,0:T(8,128)S(1)}, u32[]{:S(2)}, u32[]{:S(2)}) %collective-permute-start.3) | collective-permute-done | bytes 499744 | tf_op jit(solution)/shard_map/ppermute | solution.py:458
  39.5 4.1 %collective-permute-start.5 = (f32[2,488,128]{2,1,0:T(8,128)S(1)}, f32[2,488,128]{2,1,0:T(8,128)S(1)}, u32[]{:S(2)}, u32[]{:S(2)}) collective-permute-start(f32[2,488,128]{2,1,0:T(8,128)S(1)} %collective-permute-done.3.near_a), channel_id=1, source_target_pairs={{0,2},{2,4},{4,6},{3,1},{5,3},{7,5},{8,10},{10,12},{12,14},{11,9},... | collective-permute-start | bytes 1499144 | tf_op jit(solution)/shard_map/ppermute | solution.py:467
  43.5 4.4 %chain.5 = (f32[1,80,128]{2,1,0:T(8,128)S(1)}, f32[1,80,128]{2,1,0:T(8,128)S(1)}, f32[80,256]{1,0:T(8,128)S(1)}) custom-call(f32[80,384]{1,0:T(8,128)S(1)} %get-tuple-element.41.y_ref, f32[4,128]{1,0:T(4,128)S(1)} %copy-done.2, f32[4,128]{1,0:T(4,128)S(1)} %copy-done.3, f32[6,128,128]{2,1,0:T(8,128)S(1)} %get-tuple-element.38.taper_ref), custom_call_target="tpu_custom_call" | custom-call | flops 1000 | bytes 1000 | tf_op jit(solution)/shard_map/chain/pallas_call | solution.py:39
  47.9 1.2 %collective-permute-done.4.near_b = f32[2,488,128]{2,1,0:T(8,128)S(1)} collective-permute-done((f32[2,488,128]{2,1,0:T(8,128)S(1)}, f32[2,488,128]{2,1,0:T(8,128)S(1)}, u32[]{:S(2)}, u32[]{:S(2)}) %collective-permute-start.4) | collective-permute-done | bytes 499744 | tf_op jit(solution)/shard_map/ppermute | solution.py:458
  49.1 3.9 %collective-permute-start.6 = (f32[2,488,128]{2,1,0:T(8,128)S(1)}, f32[2,488,128]{2,1,0:T(8,128)S(1)}, u32[]{:S(2)}, u32[]{:S(2)}) collective-permute-start(f32[2,488,128]{2,1,0:T(8,128)S(1)} %collective-permute-done.4.near_b), channel_id=1, source_target_pairs={{0,2},{2,4},{4,6},{3,1},{5,3},{7,5},{8,10},{10,12},{12,14},{11,9},... | collective-permute-start | bytes 1499144 | tf_op jit(solution)/shard_map/ppermute | solution.py:467
  53.0 4.4 %chain.6 = (f32[1,80,128]{2,1,0:T(8,128)S(1)}, f32[1,80,128]{2,1,0:T(8,128)S(1)}, f32[80,128]{1,0:T(8,128)S(1)}) custom-call(f32[80,256]{1,0:T(8,128)S(1)} %get-tuple-element.44.y_ref, f32[4,128]{1,0:T(4,128)S(1)} %copy-done.2, f32[4,128]{1,0:T(4,128)S(1)} %copy-done.3, f32[6,128,128]{2,1,0:T(8,128)S(1)} %get-tuple-element.38.taper_ref), custom_call_target="tpu_custom_call" | custom-call | flops 1000 | bytes 1000 | tf_op jit(solution)/shard_map/chain/pallas_call | solution.py:39
  57.4 4.2 %chain.7 = (f32[1,80,128]{2,1,0:T(8,128)S(1)}, f32[1,80,128]{2,1,0:T(8,128)S(1)}) custom-call(f32[80,128]{1,0:T(8,128)S(1)} %get-tuple-element.54.y_ref, f32[4,128]{1,0:T(4,128)S(1)} %copy-done.2, f32[4,128]{1,0:T(4,128)S(1)} %copy-done.3, f32[6,128,128]{2,1,0:T(8,128)S(1)} %get-tuple-element.38.taper_ref), custom_call_target="tpu_custom_call" | custom-call | flops 1000 | bytes 1000 | tf_op jit(solution)/shard_map/chain/pallas_call | solution.py:39
  61.6 1.6 %collective-permute-done.6.far_b = f32[2,488,128]{2,1,0:T(8,128)S(1)} collective-permute-done((f32[2,488,128]{2,1,0:T(8,128)S(1)}, f32[2,488,128]{2,1,0:T(8,128)S(1)}, u32[]{:S(2)}, u32[]{:S(2)}) %collective-permute-start.6) | collective-permute-done | bytes 499744 | tf_op jit(solution)/shard_map/ppermute | solution.py:467
  63.2 6.6 %update.1 = f32[1920,128]{1,0:T(8,128)} custom-call(s32[2]{0:T(128)S(1)} %pad_add_fusion.place_ref, f32[4,488,128]{2,1,0:T(8,128)S(1)} %bitcast.11, f32[2,488,128]{2,1,0:T(8,128)S(1)} %collective-permute-done.3.near_a, f32[2,488,128]{2,1,0:T(8,128)S(1)} %collective-permute-done.4.near_b, f32[2,488,128]{2,1,0:T(8,128)S(1)} %collective-permute-done.5.far_a, ...), custom_call_target="tpu_custom_call" | custom-call | tf_op jit(solution)/shard_map/update/pallas_call | solution.py:39
  (23 shorter events, 0.4 us)
Async XLA Ops:
  0.0 0.7 copy-start.7
  0.0 0.7 copy-start.6
  0.0 0.7 %copy-start.5 = (f32[1,512]{1,0:T(1,128)S(1)}, f32[1,512]{1,0:T(1,128)}, u32[]{:S(2)}) copy-start(f32[1,512]{1,0:T(1,128)} %cy_ref.3) | copy-start | bytes 6148
  0.1 0.7 copy-start.4
  0.8 1.2 %copy-start = (f32[20,1,24,512]{3,2,1,0:T(8,128)S(1)}, f32[20,1,24,512]{3,2,1,0:T(8,128)}, u32[]{:S(2)}) copy-start(f32[20,1,24,512]{3,2,1,0:T(8,128)} %param.9) | copy-start | bytes 2949124
  2.0 0.8 %copy-start.1 = (f32[4,128,24]{1,2,0:T(8,128)S(1)}, f32[4,128,24]{1,2,0:T(8,128)}, u32[]{:S(2)}) copy-start(f32[4,128,24]{1,2,0:T(8,128)} %param.16) | copy-start | bytes 147460
  6.6 6.7 %copy-start.8 = (f32[4,128]{1,0:T(4,128)S(1)}, f32[4,128]{1,0:T(4,128)}, u32[]{:S(2)}) copy-start(f32[4,128]{1,0:T(4,128)} %radius_ref.1) | copy-start | bytes 6148
  6.6 18.3 %all-to-all-start = ((f32[4,1,62464]{2,1,0:T(1,128)}), f32[4,1,62464]{2,1,0:T(1,128)S(1)}, u32[]{:S(2)}, u32[]{:S(2)}) async-start(f32[4,1,62464]{2,1,0:T(1,128)} %bitcast.4), calls=%async_computation | async-start | bytes 1998848 | tf_op jit(solution)/shard_map/all_to_all | solution.py:433
  10.9 4.6 %collective-permute-start = (f32[24,512]{1,0:T(8,128)S(1)}, f32[24,512]{1,0:T(8,128)S(1)}, u32[]{:S(2)}, u32[]{:S(2)}) collective-permute-start(f32[24,512]{1,0:T(8,128)S(1)} %get-tuple-element.31.mine_ref), channel_id=1, source_target_pairs={{0,1},{1,0},{2,3},{3,2},{4,5},{5,4},{6,7},{7,6},{8,9},{9,8},{10,11... | collective-permute-start | bytes 147464 | tf_op jit(solution)/shard_map/ppermute | solution.py:443
  15.6 4.2 %collective-permute-start.1 = (f32[24,512]{1,0:T(8,128)S(1)}, f32[24,512]{1,0:T(8,128)S(1)}, u32[]{:S(2)}, u32[]{:S(2)}) collective-permute-start(f32[24,512]{1,0:T(8,128)S(1)} %join.3.mine_ref), channel_id=1, source_target_pairs={{0,2},{1,3},{2,0},{3,1},{4,6},{5,7},{6,4},{7,5},{8,10},{9,11},{10,... | collective-permute-start | bytes 147464 | tf_op jit(solution)/shard_map/ppermute | solution.py:443
  19.7 5.1 %collective-permute-start.2 = (f32[24,512]{1,0:T(8,128)S(1)}, f32[24,512]{1,0:T(8,128)S(1)}, u32[]{:S(2)}, u32[]{:S(2)}) collective-permute-start(f32[24,512]{1,0:T(8,128)S(1)} %join.4.mine_ref), channel_id=1, source_target_pairs={{0,4},{1,5},{2,6},{3,7},{4,0},{5,1},{6,2},{7,3},{8,12},{9,13},{10,... | collective-permute-start | bytes 147464 | tf_op jit(solution)/shard_map/ppermute | solution.py:443
  24.9 14.5 %collective-permute-start.3 = (f32[2,488,128]{2,1,0:T(8,128)S(1)}, f32[2,488,128]{2,1,0:T(8,128)S(1)}, u32[]{:S(2)}, u32[]{:S(2)}) collective-permute-start(f32[2,488,128]{2,1,0:T(8,128)S(1)} %get-tuple-element.58), channel_id=1, source_target_pairs={{0,1},{1,0},{2,3},{3,2},{4,5},{5,4},{6,7},{7,6},{8,9},{9,8},{10,11... | collective-permute-start | bytes 1499144 | tf_op jit(solution)/shard_map/ppermute | solution.py:458
  27.2 21.9 %collective-permute-start.4 = (f32[2,488,128]{2,1,0:T(8,128)S(1)}, f32[2,488,128]{2,1,0:T(8,128)S(1)}, u32[]{:S(2)}, u32[]{:S(2)}) collective-permute-start(f32[2,488,128]{2,1,0:T(8,128)S(1)} %get-tuple-element.57), channel_id=1, source_target_pairs={{0,1},{1,0},{2,3},{3,2},{4,5},{5,4},{6,7},{7,6},{8,9},{9,8},{10,11... | collective-permute-start | bytes 1499144 | tf_op jit(solution)/shard_map/ppermute | solution.py:458
  27.3 5.7 %copy-start.2 = (f32[4,128]{1,0:T(4,128)S(1)}, f32[4,128]{1,0:T(4,128)}, u32[]{:S(2)}) copy-start(f32[4,128]{1,0:T(4,128)} %value_ref.7) | copy-start | bytes 6148
  27.3 5.7 %copy-start.3 = (f32[4,128]{1,0:T(4,128)S(1)}, f32[4,128]{1,0:T(4,128)}, u32[]{:S(2)}) copy-start(f32[4,128]{1,0:T(4,128)} %error_ref.7) | copy-start | bytes 6148
  39.5 18.0 %collective-permute-start.5 = (f32[2,488,128]{2,1,0:T(8,128)S(1)}, f32[2,488,128]{2,1,0:T(8,128)S(1)}, u32[]{:S(2)}, u32[]{:S(2)}) collective-permute-start(f32[2,488,128]{2,1,0:T(8,128)S(1)} %collective-permute-done.3.near_a), channel_id=1, source_target_pairs={{0,2},{2,4},{4,6},{3,1},{5,3},{7,5},{8,10},{10,12},{12,14},{11,9},... | collective-permute-start | bytes 1499144 | tf_op jit(solution)/shard_map/ppermute | solution.py:467
  49.1 14.1 %collective-permute-start.6 = (f32[2,488,128]{2,1,0:T(8,128)S(1)}, f32[2,488,128]{2,1,0:T(8,128)S(1)}, u32[]{:S(2)}, u32[]{:S(2)}) collective-permute-start(f32[2,488,128]{2,1,0:T(8,128)S(1)} %collective-permute-done.4.near_b), channel_id=1, source_target_pairs={{0,2},{2,4},{4,6},{3,1},{5,3},{7,5},{8,10},{10,12},{12,14},{11,9},... | collective-permute-start | bytes 1499144 | tf_op jit(solution)/shard_map/ppermute | solution.py:467

commit v5 on v4

--- a/solution.py
+++ b/solution.py
@@ -33,9 +33,9 @@
     return hi, mid, (rest - mid.astype(f32)).astype(bf16)
 
 
-def call(kernel, out_shapes, name, operands, scalars=(), scratch=(), cost=None):
+def call(kernel, out_shapes, name, operands, scalars=(), scratch=(), space=pltpu.VMEM):
     specs = [pl.BlockSpec(memory_space=pltpu.SMEM) for _ in scalars]
-    specs += [pl.BlockSpec(memory_space=pltpu.VMEM) for _ in operands]
+    specs += [pl.BlockSpec(memory_space=space) for _ in operands]
     return pl.pallas_call(
         kernel,
         in_specs=specs,
@@ -43,7 +43,6 @@
         out_shape=[jax.ShapeDtypeStruct(s, f32) for s in out_shapes],
         scratch_shapes=list(scratch),
         compiler_params=pltpu.CompilerParams(vmem_limit_bytes=48 * 2**20),
-        cost_estimate=cost,
         name=name,
     )(*scalars, *operands)
 
@@ -100,17 +99,20 @@
     return kernel
 
 
-def observe_kernel(width, comps, batches, nobs, blocks, edge_rows, local):
-    def kernel(place_ref, q_ref, cx_ref, cy_ref, d_ref, cell_ref, weight_ref, share_ref, send_ref):
+def share_kernel(width, comps, batches, nobs, local):
+    def kernel(place_ref, *refs):
+        sources, (share_ref, *fetched, arrived) = refs[:6], refs[6:]
+        q_ref, cx_ref, cy_ref, d_ref, cell_ref, weight_ref = fetched
+        copies = [
+            pltpu.make_async_copy(source, target, arrived.at[i])
+            for i, (source, target) in enumerate(zip(sources, fetched))
+        ]
+        for copy in copies:
+            copy.start()
         here = place_ref[0]
-        q = q_ref[...]
-        count = q.shape[0]
+        for copy in copies[1:]:
+            copy.wait()
         cx, cy, d = cx_ref[...], cy_ref[...], d_ref[...]
-        west = pltpu.roll(q, 1, 1)
-        east = pltpu.roll(q, width - 1, 1)
-        mine = q - jnp.maximum(cx, 0.0) * (q - west) - jnp.minimum(cx, 0.0) * (east - q)
-        mine = mine - jnp.maximum(cy, 0.0) * q + jnp.minimum(cy, 0.0) * q
-        mine = mine + d * (east + west - 4.0 * q)
         from_south, from_north = jnp.maximum(cy, 0.0) + d, d - jnp.minimum(cy, 0.0)
         even = jnp.full((1, width), here & 1, jnp.int32) == 0
         near = jnp.where(even, from_north, from_south)
@@ -125,9 +127,15 @@
         place = lax.broadcasted_iota(jnp.int32, (width, batches * nobs), 0)
         own_pick = (place == jnp.where(owned, col, -1)).astype(f32).astype(bf16)
         raw_pick = (place == jnp.where(beside, col, -1)).astype(f32).astype(bf16)
-        q_parts = split3(q)
+        copies[0].wait()
+        q = q_ref[...]
+        west = pltpu.roll(q, 1, 1)
+        east = pltpu.roll(q, width - 1, 1)
+        mine = q - jnp.maximum(cx, 0.0) * (q - west) - jnp.minimum(cx, 0.0) * (east - q)
+        mine = mine - jnp.maximum(cy, 0.0) * q + jnp.minimum(cy, 0.0) * q
+        mine = mine + d * (east + west - 4.0 * q)
         value = narrow(
-            jnp.concatenate(split2(mine) + q_parts[:2], 1),
+            jnp.concatenate(split2(mine) + split2(q), 1),
             jnp.concatenate([own_pick, own_pick, raw_pick, raw_pick], 0),
             1,
             0,
@@ -141,6 +149,15 @@
         if fill:
             share.append(jnp.zeros((fill, batches * nobs), f32))
         share_ref[...] = jnp.concatenate(share, 0)
+
+    return kernel
+
+
+def send_kernel(width, blocks, edge_rows):
+    def kernel(q_ref, send_ref):
+        q = q_ref[...]
+        count = q.shape[0]
+        q_parts = split3(q)
         cols_dev = width // blocks
         lanes = -(-2 * blocks // 128) * 128
         which = lax.broadcasted_iota(jnp.int32, (width, lanes), 1)
@@ -289,12 +306,17 @@
     return anomaly, back[members : members + 1] - back[:members]
 
 
-def chain_kernel(part, batches, nobs):
-    def kernel(y_ref, value_ref, error_ref, taper_ref, anomaly_ref, coeff_ref, *later_ref):
-        if len(y_ref.shape) == 3:
-            observed = jnp.concatenate([y_ref[i] for i in range(y_ref.shape[0])], 0)
-        else:
-            observed = y_ref[...]
+def chain_kernel(part, batches, nobs, pieces):
+    def kernel(place_ref, *refs):
+        y_refs, refs = refs[:pieces], refs[pieces:]
+        value_ref, error_ref, taper_ref, anomaly_ref, coeff_ref, *later_ref = refs
+        blocks = [ref[...] for ref in y_refs]
+        step = 1
+        while step < pieces:
+            odd = jnp.full(blocks[0].shape, place_ref[1] & step, jnp.int32) != 0
+            blocks = [jnp.where(odd, blocks[k ^ step], blocks[k]) for k in range(pieces)]
+            step *= 2
+        observed = jnp.concatenate(blocks, 0) if pieces > 1 else blocks[0]
         members = observed.shape[0]
         first = batches - observed.shape[1] // nobs
         Y = {b: observed[:, nobs * (b - first) : nobs * (b - first + 1)] for b in range(first, batches)}
@@ -412,25 +434,29 @@
     batches, nobs = obs_cell.shape
     count = local * comps
     edge_rows = -(-(2 * -(-count // 128)) // 8) * 8
-    assert bands & (bands - 1) == 0 and bands > 1 and rows_dev == 1 and batches == 4 and cols_dev == 128 and nobs == 128
+    assert bands & (bands - 1) == 0 and bands > 2 and blocks & (blocks - 1) == 0 and rows_dev == 1 and batches == 4 and cols_dev == 128 and nobs == 128
     place = jnp.stack([lax.axis_index("sub"), lax.axis_index("mem")]).astype(jnp.int32)
 
     share_rows = -(-(local + 2) // 8) * 8
-    share, send = call(
-        observe_kernel(width, comps, batches, nobs, blocks, edge_rows, local),
-        [(share_rows, batches * nobs), (blocks, count + edge_rows, cols_dev)],
-        "observe",
-        (
-            prior_sample_array.reshape(count, width),
-            courant_x,
-            courant_y,
-            diffusion,
-            obs_cell,
-            obs_weight.transpose(0, 2, 1),
-        ),
+    prior = prior_sample_array.reshape(count, width)
+    (send,) = call(
+        send_kernel(width, blocks, edge_rows),
+        [(blocks, count + edge_rows, cols_dev)],
+        "send",
+        (prior,),
+    )
+    grid = lax.all_to_all(send.reshape(blocks, 1, -1), "mem", 0, 0).reshape(send.shape)
+    sources = (prior, courant_x, courant_y, diffusion, obs_cell, obs_weight.transpose(0, 2, 1))
+    (place, send) = lax.optimization_barrier((place, send))
+    (share,) = call(
+        share_kernel(width, comps, batches, nobs, local),
+        [(share_rows, batches * nobs)],
+        "share",
+        sources,
         (place,),
-    )
-    grid = lax.all_to_all(send.reshape(blocks, 1, -1), "mem", 0, 0).reshape(send.shape)
+        [pltpu.VMEM(x.shape, x.dtype) for x in sources] + [pltpu.SemaphoreType.DMA((6,))],
+        pl.ANY,
+    )
     obs_taper, cell_taper = call(
         taper_kernel(width, batches, nobs, cols_dev),
         [(batches * (batches - 1) // 2, nobs, nobs), (batches, nobs, cols_dev)],
@@ -450,31 +476,38 @@
             "join",
             (share, other),
         )
+        if 4 * step == bands:
+            share, grid = lax.optimization_barrier((share, grid))
         step *= 2
-    share, grid = lax.optimization_barrier((share, grid))
     swap = [(i, i ^ 1) for i in range(bands)]
     onward = [(i, i + 2) for i in range(0, bands - 2, 2)] + [(i, i - 2) for i in range(3, bands, 2)]
     middle = blocks // 2
     near = [lax.ppermute(part, "sub", swap) for part in (grid[:middle], grid[middle:])]
-    observed = lax.all_gather(share, "mem")
+    observed = {0: share}
+    step = blocks // 2
+    while step:
+        to = [(i, i ^ step) for i in range(blocks)]
+        observed.update({k ^ step: lax.ppermute(x, "mem", to) for k, x in observed.items()})
+        step //= 2
+    observed = [observed[k] for k in range(blocks)]
     pairs, far = [], []
     for b in range(batches):
         part = range(b, b + 1)
-        if b == 3:
-            observed, far[0] = lax.optimization_barrier((observed, far[0]))
-        if b in (1, 2):
-            observed, near[b - 1] = lax.optimization_barrier((observed, near[b - 1]))
-            far.append(lax.ppermute(near[b - 1], "sub", onward))
+        if b == 2:
+            *observed, far[0] = lax.optimization_barrier((*observed, far[0]))
+        if b < 2:
+            *observed, near[b] = lax.optimization_barrier((*observed, near[b]))
+            far.append(lax.ppermute(near[b], "sub", onward))
         outs = call(
-            chain_kernel(part, batches, nobs),
+            chain_kernel(part, batches, nobs, len(observed)),
             [(len(part), members, nobs)] * 2
             + [(members, (batches - part[-1] - 1) * nobs)] * (part[-1] + 1 < batches),
             "chain",
-            (observed, obs_value, obs_error, obs_taper),
-            cost=pl.CostEstimate(flops=1000, bytes_accessed=1000, transcendentals=0),
+            (*observed, obs_value, obs_error, obs_taper),
+            (place,),
         )
         pairs += outs[:2]
-        observed = outs[-1]
+        observed = outs[2:]
     (out,) = call(
         update_kernel(width, comps, batches, members, cols_dev, count, comps),
         [(members * comps, cols_dev)],

time: 70.2 us -> 70.8 us (level)
  blocking collectives: 5.72 us -> 0 us
  waiting for transfers between devices: 9.85 us -> 13.4 us
  Pallas kernels: 29.5 us -> 32.5 us
  local copies, waits for them, and re-layouts: 2.76 us -> 1.9 us
    all_gather x1 -> x0, blocking collectives: 5.72 us -> none  [shards(): observed = lax.all_gather(share, 'mem')]
    ppermute x2 -> x5, waiting for transfers between devices: 1.62 us -> 4.71 us  [the longest x3 4.7 us: shards(): lax.ppermute(x, 'mem', to)]
    pallas_call x10 -> x11, Pallas kernels: 29.5 us -> 32.5 us  [call(): pl.pallas_call(kernel, in_specs=specs, out_specs=[pl.BlockSpec(memory_spa...]
    all_to_all x1, waiting for transfers between devices: 0.09 us -> 1.4 us  [shards(): lax.all_to_all(send.reshape(blocks, 1, -1), 'mem', 0, 0).reshape(send.shape)]
    ppermute x2, waiting for transfers between devices: 3.2 us -> 2.24 us  [shards(): lax.ppermute(part, 'sub', swap)]
    unnamed x18 -> x20, local copies, waits for them, and re-layouts: 2.69 us -> 1.83 us
    ppermute x2 -> x5, starting transfers between devices: 8 us -> 8.68 us  [the longest x2 8 us: shards(): far.append(lax.ppermute(near[b], 'sub', onward))]
  transfers between devices with their start and end apart: 8 -> 11, of which waited for: 7 -> 8; matrix products, arithmetic and copies ran while one was open for 0% -> 0% of each run, Pallas kernels for 27% -> 34%
where the time goes in v5:
time: 70.8 us; the launch traced here: 70.6 us
  Pallas kernels  32.5 us (46%)
  starting transfers between devices  22.6 us (32%)
  waiting for transfers between devices  13.4 us (19%)
  local copies, waits for them, and re-layouts  1.9 us (3%)
    pallas_call x11, Pallas kernels, call(): pl.pallas_call(kernel, in_specs=specs, out_specs=[pl.BlockSpec(memory_spa...  32.5 us
    ppermute x2, starting transfers between devices, shards(): far.append(lax.ppermute(near[b], 'sub', onward))  8 us
    ppermute x3, starting transfers between devices, shards(): other = lax.ppermute(share, 'sub', [(i, i ^ step) for i in range(bands)])  7.2 us
    ppermute x3, waiting for transfers between devices, shards(): other = lax.ppermute(share, 'sub', [(i, i ^ step) for i in range(bands)])  5.01 us
    ppermute x3, waiting for transfers between devices, shards(): lax.ppermute(x, 'mem', to)  4.7 us
    all_to_all x1, starting transfers between devices, shards(): lax.all_to_all(send.reshape(blocks, 1, -1), 'mem', 0, 0).reshape(send.shape)  4.38 us
    ppermute x2, starting transfers between devices, shards(): lax.ppermute(part, 'sub', swap)  2.35 us
    ppermute x2, waiting for transfers between devices, shards(): lax.ppermute(part, 'sub', swap)  2.24 us
  transfers between devices with their start and end apart: 11, of which 8 were waited for; matrix products, arithmetic and copies ran while one was open for 0% of the time, Pallas kernels for 34%

profile of v5, /device:TPU:0, one launch (start us, length us, event | category | flops | bytes accessed | tf_op | source)
XLA Modules:
  0.0 70.6 jit_solution(3242532645993913073)
XLA Ops:
  0.0 1.2 %copy-done = f32[20,1,24,512]{3,2,1,0:T(8,128)S(1)} copy-done((f32[20,1,24,512]{3,2,1,0:T(8,128)S(1)}, f32[20,1,24,512]{3,2,1,0:T(8,128)}, u32[]{:S(2)}) %copy-start) | copy-done | bytes 983064
  1.2 1.6 %send.1 = f32[4,488,128]{2,1,0:T(8,128)} custom-call(f32[480,512]{1,0:T(8,128)S(1)} %bitcast.11), custom_call_target="tpu_custom_call" | custom-call | tf_op jit(solution)/shard_map/send/pallas_call | solution.py:39
  2.8 4.4 %all-to-all-start = ((f32[4,1,62464]{2,1,0:T(1,128)}), f32[4,1,62464]{2,1,0:T(1,128)S(1)}, u32[]{:S(2)}, u32[]{:S(2)}) async-start(f32[4,1,62464]{2,1,0:T(1,128)} %bitcast.4), calls=%async_computation | async-start | bytes 1998848 | tf_op jit(solution)/shard_map/all_to_all | solution.py:448
  7.9 3.0 %share.1.mine_ref = f32[24,512]{1,0:T(8,128)S(1)} custom-call(s32[2]{0:T(128)S(1)} %pad_add_fusion.place_ref, f32[480,512]{1,0:T(8,128)S(1)} %bitcast.12, f32[1,512]{1,0:T(1,128)S(1)} %copy-done.5, f32[1,512]{1,0:T(1,128)S(1)} %copy-done.6, f32[1,512]{1,0:T(1,128)S(1)} %copy-done.7, s32[4,128]{1,0:T(4,128)S(1)} %copy-done.8, f32[4,24,128]{2,1,0:T(8,128)S(1)} %bitcast.13), custom_call_target="tpu_custom_call" | custom-call | tf_op jit(solution)/shard_map/share/pallas_call | solution.py:39
  10.9 2.3 %collective-permute-start = (f32[24,512]{1,0:T(8,128)S(1)}, f32[24,512]{1,0:T(8,128)S(1)}, u32[]{:S(2)}, u32[]{:S(2)}) collective-permute-start(f32[24,512]{1,0:T(8,128)S(1)} %share.1.mine_ref), channel_id=1, source_target_pairs={{0,1},{1,0},{2,3},{3,2},{4,5},{5,4},{6,7},{7,6},{8,9},{9,8},{10,11... | collective-permute-start | bytes 147464 | tf_op jit(solution)/shard_map/ppermute | solution.py:469
  13.2 1.7 %tapers.1 = (f32[6,128,128]{2,1,0:T(8,128)S(1)}, f32[4,128,128]{2,1,0:T(8,128)S(1)}) custom-call(s32[2]{0:T(128)S(1)} %pad_add_fusion.place_ref, s32[4,128]{1,0:T(4,128)S(1)} %copy-done.8, f32[4,128]{1,0:T(4,128)S(1)} %copy-done.9), custom_call_target="tpu_custom_call" | custom-call | tf_op jit(solution)/shard_map/tapers/pallas_call | solution.py:39
  14.9 0.7 collective-permute-done.other_ref
  15.6 1.9 %collective-permute-start.1 = (f32[24,512]{1,0:T(8,128)S(1)}, f32[24,512]{1,0:T(8,128)S(1)}, u32[]{:S(2)}, u32[]{:S(2)}) collective-permute-start(f32[24,512]{1,0:T(8,128)S(1)} %join.3.mine_ref), channel_id=1, source_target_pairs={{0,2},{1,3},{2,0},{3,1},{4,6},{5,7},{6,4},{7,5},{8,10},{9,11},{10,... | collective-permute-start | bytes 147464 | tf_op jit(solution)/shard_map/ppermute | solution.py:469
  17.5 2.3 %collective-permute-done.1.other_ref = f32[24,512]{1,0:T(8,128)S(1)} collective-permute-done((f32[24,512]{1,0:T(8,128)S(1)}, f32[24,512]{1,0:T(8,128)S(1)}, u32[]{:S(2)}, u32[]{:S(2)}) %collective-permute-start.1) | collective-permute-done | bytes 49184 | tf_op jit(solution)/shard_map/ppermute | solution.py:469
  19.8 1.4 %all-to-all-done = f32[4,1,62464]{2,1,0:T(1,128)S(1)} async-done(((f32[4,1,62464]{2,1,0:T(1,128)}), f32[4,1,62464]{2,1,0:T(1,128)S(1)}, u32[]{:S(2)}, u32[]{:S(2)}) %all-to-all-start) | async-done | bytes 999456 | tf_op jit(solution)/shard_map/all_to_all | solution.py:448
  21.2 2.3 %collective-permute-start.6 = (f32[2,488,128]{2,1,0:T(8,128)S(1)}, f32[2,488,128]{2,1,0:T(8,128)S(1)}, u32[]{:S(2)}, u32[]{:S(2)}) collective-permute-start(f32[2,488,128]{2,1,0:T(8,128)S(1)} %get-tuple-element.62), channel_id=1, source_target_pairs={{0,1},{1,0},{2,3},{3,2},{4,5},{5,4},{6,7},{7,6},{8,9},{9,8},{10,11... | collective-permute-start | bytes 1499144 | tf_op jit(solution)/shard_map/ppermute | solution.py:485
  23.6 3.0 %collective-permute-start.2 = (f32[24,512]{1,0:T(8,128)S(1)}, f32[24,512]{1,0:T(8,128)S(1)}, u32[]{:S(2)}, u32[]{:S(2)}) collective-permute-start(f32[24,512]{1,0:T(8,128)S(1)} %join.4.mine_ref), channel_id=1, source_target_pairs={{0,4},{1,5},{2,6},{3,7},{4,0},{5,1},{6,2},{7,3},{8,12},{9,13},{10,... | collective-permute-start | bytes 147464 | tf_op jit(solution)/shard_map/ppermute | solution.py:469
  26.6 2.1 %collective-permute-done.2.other_ref = f32[24,512]{1,0:T(8,128)S(1)} collective-permute-done((f32[24,512]{1,0:T(8,128)S(1)}, f32[24,512]{1,0:T(8,128)S(1)}, u32[]{:S(2)}, u32[]{:S(2)}) %collective-permute-start.2) | collective-permute-done | bytes 49184 | tf_op jit(solution)/shard_map/ppermute | solution.py:469
  28.7 0.7 collective-permute-start.4
  29.4 3.5 %collective-permute-done.4.refs_2_ = f32[20,512]{1,0:T(8,128)S(1)} collective-permute-done((f32[20,512]{1,0:T(8,128)S(1)}, f32[20,512]{1,0:T(8,128)S(1)}, u32[]{:S(2)}, u32[]{:S(2)}) %collective-permute-start.4) | collective-permute-done | bytes 40992 | tf_op jit(solution)/shard_map/ppermute | solution.py:490
  32.8 1.2 %collective-permute-done.5.refs_3_ = f32[20,512]{1,0:T(8,128)S(1)} collective-permute-done((f32[20,512]{1,0:T(8,128)S(1)}, f32[20,512]{1,0:T(8,128)S(1)}, u32[]{:S(2)}, u32[]{:S(2)}) %collective-permute-start.5) | collective-permute-done | bytes 40992 | tf_op jit(solution)/shard_map/ppermute | solution.py:490
  34.1 1.7 %collective-permute-done.6.near_a = f32[2,488,128]{2,1,0:T(8,128)S(1)} collective-permute-done((f32[2,488,128]{2,1,0:T(8,128)S(1)}, f32[2,488,128]{2,1,0:T(8,128)S(1)}, u32[]{:S(2)}, u32[]{:S(2)}) %collective-permute-start.6) | collective-permute-done | bytes 499744 | tf_op jit(solution)/shard_map/ppermute | solution.py:485
  35.7 4.1 %collective-permute-start.8 = (f32[2,488,128]{2,1,0:T(8,128)S(1)}, f32[2,488,128]{2,1,0:T(8,128)S(1)}, u32[]{:S(2)}, u32[]{:S(2)}) collective-permute-start(f32[2,488,128]{2,1,0:T(8,128)S(1)} %collective-permute-done.6.near_a), channel_id=1, source_target_pairs={{0,2},{2,4},{4,6},{3,1},{5,3},{7,5},{8,10},{10,12},{12,14},{11,9},... | collective-permute-start | bytes 1499144 | tf_op jit(solution)/shard_map/ppermute | solution.py:500
  39.8 5.0 %chain.4 = (f32[1,80,128]{2,1,0:T(8,128)S(1)}, f32[1,80,128]{2,1,0:T(8,128)S(1)}, f32[80,384]{1,0:T(8,128)S(1)}) custom-call(s32[2]{0:T(128)S(1)} %pad_add_fusion.place_ref, f32[20,512]{1,0:T(8,128)S(1)} %join.5.refs_0_, f32[20,512]{1,0:T(8,128)S(1)} %collective-permute-done.3.refs_1_, f32[20,512]{1,0:T(8,128)S(1)} %collective-permute-done.4.refs_2_, ...), custom_call_target="tpu_custom_call" | custom-call | tf_op jit(solution)/shard_map/chain/pallas_call | solution.py:39
  45.4 3.9 %collective-permute-start.9 = (f32[2,488,128]{2,1,0:T(8,128)S(1)}, f32[2,488,128]{2,1,0:T(8,128)S(1)}, u32[]{:S(2)}, u32[]{:S(2)}) collective-permute-start(f32[2,488,128]{2,1,0:T(8,128)S(1)} %collective-permute-done.7.near_b), channel_id=1, source_target_pairs={{0,2},{2,4},{4,6},{3,1},{5,3},{7,5},{8,10},{10,12},{12,14},{11,9},... | collective-permute-start | bytes 1499144 | tf_op jit(solution)/shard_map/ppermute | solution.py:500
  49.3 4.9 %chain.5 = (f32[1,80,128]{2,1,0:T(8,128)S(1)}, f32[1,80,128]{2,1,0:T(8,128)S(1)}, f32[80,256]{1,0:T(8,128)S(1)}) custom-call(s32[2]{0:T(128)S(1)} %pad_add_fusion.place_ref, f32[80,384]{1,0:T(8,128)S(1)} %get-tuple-element.47.refs_0_, f32[4,128]{1,0:T(4,128)S(1)} %copy-done.3, f32[4,128]{1,0:T(4,128)S(1)} %copy-done.4, ...), custom_call_target="tpu_custom_call" | custom-call | tf_op jit(solution)/shard_map/chain/pallas_call | solution.py:39
  54.3 4.9 %chain.6 = (f32[1,80,128]{2,1,0:T(8,128)S(1)}, f32[1,80,128]{2,1,0:T(8,128)S(1)}, f32[80,128]{1,0:T(8,128)S(1)}) custom-call(s32[2]{0:T(128)S(1)} %pad_add_fusion.place_ref, f32[80,256]{1,0:T(8,128)S(1)} %get-tuple-element.55.refs_0_, f32[4,128]{1,0:T(4,128)S(1)} %copy-done.3, f32[4,128]{1,0:T(4,128)S(1)} %copy-done.4, ...), custom_call_target="tpu_custom_call" | custom-call | tf_op jit(solution)/shard_map/chain/pallas_call | solution.py:39
  59.2 4.7 %chain.7 = (f32[1,80,128]{2,1,0:T(8,128)S(1)}, f32[1,80,128]{2,1,0:T(8,128)S(1)}) custom-call(s32[2]{0:T(128)S(1)} %pad_add_fusion.place_ref, f32[80,128]{1,0:T(8,128)S(1)} %get-tuple-element.58.refs_0_, f32[4,128]{1,0:T(4,128)S(1)} %copy-done.3, f32[4,128]{1,0:T(4,128)S(1)} %copy-done.4, f32[6,128,128]{2,1,0:T(8,128)S(1)} %get-tuple-element.44.refs_6_.refs_3_), custom_call_target="tpu_custom_call" | custom-call | tf_op jit(solution)/shard_map/chain/pallas_call | solution.py:39
  63.9 6.6 %update.1 = f32[1920,128]{1,0:T(8,128)} custom-call(s32[2]{0:T(128)S(1)} %pad_add_fusion.place_ref, f32[4,488,128]{2,1,0:T(8,128)S(1)} %bitcast.10, f32[2,488,128]{2,1,0:T(8,128)S(1)} %collective-permute-done.6.near_a, f32[2,488,128]{2,1,0:T(8,128)S(1)} %collective-permute-done.7.near_b, f32[2,488,128]{2,1,0:T(8,128)S(1)} %collective-permute-done.8.far_a, ...), custom_call_target="tpu_custom_call" | custom-call | tf_op jit(solution)/shard_map/update/pallas_call | solution.py:39
  (31 shorter events, 1.5 us)
Async XLA Ops:
  0.0 1.2 %copy-start = (f32[20,1,24,512]{3,2,1,0:T(8,128)S(1)}, f32[20,1,24,512]{3,2,1,0:T(8,128)}, u32[]{:S(2)}) copy-start(f32[20,1,24,512]{3,2,1,0:T(8,128)} %param.9) | copy-start | bytes 2949124
  2.8 4.5 %copy-start.1 = (f32[20,1,24,512]{3,2,1,0:T(8,128)S(1)}, f32[20,1,24,512]{3,2,1,0:T(8,128)}, u32[]{:S(2)}) copy-start(f32[20,1,24,512]{3,2,1,0:T(8,128)} %param.9) | copy-start | bytes 2949124
  2.8 4.5 %copy-start.2 = (f32[4,128,24]{1,2,0:T(8,128)S(1)}, f32[4,128,24]{1,2,0:T(8,128)}, u32[]{:S(2)}) copy-start(f32[4,128,24]{1,2,0:T(8,128)} %param.16) | copy-start | bytes 147460
  2.8 4.5 %copy-start.7 = (f32[1,512]{1,0:T(1,128)S(1)}, f32[1,512]{1,0:T(1,128)}, u32[]{:S(2)}) copy-start(f32[1,512]{1,0:T(1,128)} %d_ref.1) | copy-start | bytes 6148
  2.8 4.5 %copy-start.8 = (s32[4,128]{1,0:T(4,128)S(1)}, s32[4,128]{1,0:T(4,128)}, u32[]{:S(2)}) copy-start(s32[4,128]{1,0:T(4,128)} %cell_ref.1) | copy-start | bytes 6148
  2.8 18.3 %all-to-all-start = ((f32[4,1,62464]{2,1,0:T(1,128)}), f32[4,1,62464]{2,1,0:T(1,128)S(1)}, u32[]{:S(2)}, u32[]{:S(2)}) async-start(f32[4,1,62464]{2,1,0:T(1,128)} %bitcast.4), calls=%async_computation | async-start | bytes 1998848 | tf_op jit(solution)/shard_map/all_to_all | solution.py:448
  7.2 0.7 copy-start.6
  7.2 0.7 copy-start.5
  7.9 5.3 %copy-start.9 = (f32[4,128]{1,0:T(4,128)S(1)}, f32[4,128]{1,0:T(4,128)}, u32[]{:S(2)}) copy-start(f32[4,128]{1,0:T(4,128)} %radius_ref.1) | copy-start | bytes 6148
  10.9 4.7 %collective-permute-start = (f32[24,512]{1,0:T(8,128)S(1)}, f32[24,512]{1,0:T(8,128)S(1)}, u32[]{:S(2)}, u32[]{:S(2)}) collective-permute-start(f32[24,512]{1,0:T(8,128)S(1)} %share.1.mine_ref), channel_id=1, source_target_pairs={{0,1},{1,0},{2,3},{3,2},{4,5},{5,4},{6,7},{7,6},{8,9},{9,8},{10,11... | collective-permute-start | bytes 147464 | tf_op jit(solution)/shard_map/ppermute | solution.py:469
  15.6 4.2 %collective-permute-start.1 = (f32[24,512]{1,0:T(8,128)S(1)}, f32[24,512]{1,0:T(8,128)S(1)}, u32[]{:S(2)}, u32[]{:S(2)}) collective-permute-start(f32[24,512]{1,0:T(8,128)S(1)} %join.3.mine_ref), channel_id=1, source_target_pairs={{0,2},{1,3},{2,0},{3,1},{4,6},{5,7},{6,4},{7,5},{8,10},{9,11},{10,... | collective-permute-start | bytes 147464 | tf_op jit(solution)/shard_map/ppermute | solution.py:469
  21.2 14.5 %collective-permute-start.6 = (f32[2,488,128]{2,1,0:T(8,128)S(1)}, f32[2,488,128]{2,1,0:T(8,128)S(1)}, u32[]{:S(2)}, u32[]{:S(2)}) collective-permute-start(f32[2,488,128]{2,1,0:T(8,128)S(1)} %get-tuple-element.62), channel_id=1, source_target_pairs={{0,1},{1,0},{2,3},{3,2},{4,5},{5,4},{6,7},{7,6},{8,9},{9,8},{10,11... | collective-permute-start | bytes 1499144 | tf_op jit(solution)/shard_map/ppermute | solution.py:485
  23.5 16.3 %copy-start.3 = (f32[4,128]{1,0:T(4,128)S(1)}, f32[4,128]{1,0:T(4,128)}, u32[]{:S(2)}) copy-start(f32[4,128]{1,0:T(4,128)} %refs_1_.7) | copy-start | bytes 6148
  23.5 16.3 %copy-start.4 = (f32[4,128]{1,0:T(4,128)S(1)}, f32[4,128]{1,0:T(4,128)}, u32[]{:S(2)}) copy-start(f32[4,128]{1,0:T(4,128)} %refs_2_.7) | copy-start | bytes 6148
  23.5 21.9 %collective-permute-start.7 = (f32[2,488,128]{2,1,0:T(8,128)S(1)}, f32[2,488,128]{2,1,0:T(8,128)S(1)}, u32[]{:S(2)}, u32[]{:S(2)}) collective-permute-start(f32[2,488,128]{2,1,0:T(8,128)S(1)} %get-tuple-element.61), channel_id=1, source_target_pairs={{0,1},{1,0},{2,3},{3,2},{4,5},{5,4},{6,7},{7,6},{8,9},{9,8},{10,11... | collective-permute-start | bytes 1499144 | tf_op jit(solution)/shard_map/ppermute | solution.py:485
  23.6 5.1 %collective-permute-start.2 = (f32[24,512]{1,0:T(8,128)S(1)}, f32[24,512]{1,0:T(8,128)S(1)}, u32[]{:S(2)}, u32[]{:S(2)}) collective-permute-start(f32[24,512]{1,0:T(8,128)S(1)} %join.4.mine_ref), channel_id=1, source_target_pairs={{0,4},{1,5},{2,6},{3,7},{4,0},{5,1},{6,2},{7,3},{8,12},{9,13},{10,... | collective-permute-start | bytes 147464 | tf_op jit(solution)/shard_map/ppermute | solution.py:469
  28.7 4.2 %collective-permute-start.4 = (f32[20,512]{1,0:T(8,128)S(1)}, f32[20,512]{1,0:T(8,128)S(1)}, u32[]{:S(2)}, u32[]{:S(2)}) collective-permute-start(f32[20,512]{1,0:T(8,128)S(1)} %join.5.refs_0_), channel_id=1, source_target_pairs={{0,16},{8,24},{16,0},{24,8},{1,17},{9,25},{17,1},{25,9},{2,18},{10... | collective-permute-start | bytes 122888 | tf_op jit(solution)/shard_map/ppermute | solution.py:490
  29.4 3.5 %collective-permute-start.3 = (f32[20,512]{1,0:T(8,128)S(1)}, f32[20,512]{1,0:T(8,128)S(1)}, u32[]{:S(2)}, u32[]{:S(2)}) collective-permute-start(f32[20,512]{1,0:T(8,128)S(1)} %join.5.refs_0_), channel_id=1, source_target_pairs={{0,8},{8,0},{16,24},{24,16},{1,9},{9,1},{17,25},{25,17},{2,10},{10... | collective-permute-start | bytes 122888 | tf_op jit(solution)/shard_map/ppermute | solution.py:490
  32.8 1.2 %collective-permute-start.5 = (f32[20,512]{1,0:T(8,128)S(1)}, f32[20,512]{1,0:T(8,128)S(1)}, u32[]{:S(2)}, u32[]{:S(2)}) collective-permute-start(f32[20,512]{1,0:T(8,128)S(1)} %collective-permute-done.4.refs_2_), channel_id=1, source_target_pairs={{0,8},{8,0},{16,24},{24,16},{1,9},{9,1},{17,25},{25,17},{2,10},{10... | collective-permute-start | bytes 122888 | tf_op jit(solution)/shard_map/ppermute | solution.py:490
  35.7 18.5 %collective-permute-start.8 = (f32[2,488,128]{2,1,0:T(8,128)S(1)}, f32[2,488,128]{2,1,0:T(8,128)S(1)}, u32[]{:S(2)}, u32[]{:S(2)}) collective-permute-start(f32[2,488,128]{2,1,0:T(8,128)S(1)} %collective-permute-done.6.near_a), channel_id=1, source_target_pairs={{0,2},{2,4},{4,6},{3,1},{5,3},{7,5},{8,10},{10,12},{12,14},{11,9},... | collective-permute-start | bytes 1499144 | tf_op jit(solution)/shard_map/ppermute | solution.py:500
  45.4 18.5 %collective-permute-start.9 = (f32[2,488,128]{2,1,0:T(8,128)S(1)}, f32[2,488,128]{2,1,0:T(8,128)S(1)}, u32[]{:S(2)}, u32[]{:S(2)}) collective-permute-start(f32[2,488,128]{2,1,0:T(8,128)S(1)} %collective-permute-done.7.near_b), channel_id=1, source_target_pairs={{0,2},{2,4},{4,6},{3,1},{5,3},{7,5},{8,10},{10,12},{12,14},{11,9},... | collective-permute-start | bytes 1499144 | tf_op jit(solution)/shard_map/ppermute | solution.py:500

commit v6 on v5

--- a/solution.py
+++ b/solution.py
@@ -33,9 +33,8 @@
     return hi, mid, (rest - mid.astype(f32)).astype(bf16)
 
 
-def call(kernel, out_shapes, name, operands, scalars=(), scratch=(), space=pltpu.VMEM):
-    specs = [pl.BlockSpec(memory_space=pltpu.SMEM) for _ in scalars]
-    specs += [pl.BlockSpec(memory_space=space) for _ in operands]
+def call(kernel, out_shapes, name, operands, scratch=(), space=pltpu.VMEM):
+    specs = [pl.BlockSpec(memory_space=space) for _ in operands]
     return pl.pallas_call(
         kernel,
         in_specs=specs,
@@ -44,7 +43,7 @@
         scratch_shapes=list(scratch),
         compiler_params=pltpu.CompilerParams(vmem_limit_bytes=48 * 2**20),
         name=name,
-    )(*scalars, *operands)
+    )(*operands)
 
 
 def rows_cols(cells, width):
@@ -75,9 +74,9 @@
 
 
 def taper_kernel(width, batches, nobs, cols_dev):
-    def kernel(place_ref, cell_ref, radius_ref, obs_taper_ref, cell_taper_ref):
-        row_here = place_ref[0].astype(f32)
-        col_here = place_ref[1] * cols_dev
+    def kernel(cell_ref, radius_ref, obs_taper_ref, cell_taper_ref):
+        row_here = lax.axis_index("sub").astype(f32)
+        col_here = lax.axis_index("mem") * cols_dev
         row_i, col_i = rows_cols(cell_ref[...], width)
         rows = row_i.astype(f32)
         cols = col_i.astype(f32)
@@ -100,7 +99,7 @@
 
 
 def share_kernel(width, comps, batches, nobs, local):
-    def kernel(place_ref, *refs):
+    def kernel(*refs):
         sources, (share_ref, *fetched, arrived) = refs[:6], refs[6:]
         q_ref, cx_ref, cy_ref, d_ref, cell_ref, weight_ref = fetched
         copies = [
@@ -109,7 +108,7 @@
         ]
         for copy in copies:
             copy.start()
-        here = place_ref[0]
+        here = lax.axis_index("sub")
         for copy in copies[1:]:
             copy.wait()
         cx, cy, d = cx_ref[...], cy_ref[...], d_ref[...]
@@ -257,11 +256,18 @@
         finished.append((low, side))
         edge = (p // span + 1) * span
         for q in range(p + 1, edge):
+            column = [lane_spread(T[q], 8 * p + c) for c in range(8)]
+            left, right = X, U
+            if q == p + 1:
+                for c in range(8):
+                    for a in range(c):
+                        column[c] = column[c] - m[c][a] * column[a]
+                column = [column[c] * rd[c] for c in range(8)]
+                left, right = R, Z
             t, v = jnp.where(block, 0.0, T[q]), V[q]
             for c in range(8):
-                column = lane_spread(T[q], 8 * p + c)
-                t = t - column * X[c]
-                v = v - column * U[c]
+                t = t - column[c] * left[c]
+                v = v - column[c] * right[c]
             T[q], V[q] = t, v
         if p + 1 == edge and edge < tiles:
             rows = finished[edge - span : edge]
@@ -307,13 +313,13 @@
 
 
 def chain_kernel(part, batches, nobs, pieces):
-    def kernel(place_ref, *refs):
+    def kernel(*refs):
         y_refs, refs = refs[:pieces], refs[pieces:]
         value_ref, error_ref, taper_ref, anomaly_ref, coeff_ref, *later_ref = refs
         blocks = [ref[...] for ref in y_refs]
         step = 1
         while step < pieces:
-            odd = jnp.full(blocks[0].shape, place_ref[1] & step, jnp.int32) != 0
+            odd = jnp.full(blocks[0].shape, lax.axis_index("mem") & step, jnp.int32) != 0
             blocks = [jnp.where(odd, blocks[k ^ step], blocks[k]) for k in range(pieces)]
             step *= 2
         observed = jnp.concatenate(blocks, 0) if pieces > 1 else blocks[0]
@@ -352,7 +358,7 @@
 
 def update_kernel(width, comps, batches, members, cols_dev, count, group):
     def kernel(
-        place_ref, own_ref, near_a, near_b, far_a, far_b, cx_ref, cy_ref, d_ref,
+        own_ref, near_a, near_b, far_a, far_b, cx_ref, cy_ref, d_ref,
         taper_ref, *refs,
     ):
         *pair_refs, out_ref, grid_ref = refs
@@ -361,12 +367,12 @@
             for i in range(0, len(pair_refs), 2)
             for k in range(pair_refs[i].shape[0])
         ]
-        start = pl.multiple_of(place_ref[1] * cols_dev, cols_dev)
+        start = pl.multiple_of(lax.axis_index("mem") * cols_dev, cols_dev)
         cx = cx_ref[:, pl.ds(start, cols_dev)]
         cy = cy_ref[:, pl.ds(start, cols_dev)]
         d = d_ref[:, pl.ds(start, cols_dev)]
         lane = lax.broadcasted_iota(jnp.int32, (1, cols_dev), 1)
-        even = jnp.full((1, cols_dev), place_ref[0] & 1, jnp.int32) == 0
+        even = jnp.full((1, cols_dev), lax.axis_index("sub") & 1, jnp.int32) == 0
         from_south, from_north = jnp.maximum(cy, 0.0), -jnp.minimum(cy, 0.0)
         from_near = jnp.where(even, from_north, from_south)
         from_far = jnp.where(even, from_south, from_north)
@@ -435,7 +441,6 @@
     count = local * comps
     edge_rows = -(-(2 * -(-count // 128)) // 8) * 8
     assert bands & (bands - 1) == 0 and bands > 2 and blocks & (blocks - 1) == 0 and rows_dev == 1 and batches == 4 and cols_dev == 128 and nobs == 128
-    place = jnp.stack([lax.axis_index("sub"), lax.axis_index("mem")]).astype(jnp.int32)
 
     share_rows = -(-(local + 2) // 8) * 8
     prior = prior_sample_array.reshape(count, width)
@@ -446,14 +451,13 @@
         (prior,),
     )
     grid = lax.all_to_all(send.reshape(blocks, 1, -1), "mem", 0, 0).reshape(send.shape)
-    sources = (prior, courant_x, courant_y, diffusion, obs_cell, obs_weight.transpose(0, 2, 1))
-    (place, send) = lax.optimization_barrier((place, send))
+    held_x, send = lax.optimization_barrier((courant_x, send))
+    sources = (prior, held_x, courant_y, diffusion, obs_cell, obs_weight.transpose(0, 2, 1))
     (share,) = call(
         share_kernel(width, comps, batches, nobs, local),
         [(share_rows, batches * nobs)],
         "share",
         sources,
-        (place,),
         [pltpu.VMEM(x.shape, x.dtype) for x in sources] + [pltpu.SemaphoreType.DMA((6,))],
         pl.ANY,
     )
@@ -462,7 +466,6 @@
         [(batches * (batches - 1) // 2, nobs, nobs), (batches, nobs, cols_dev)],
         "tapers",
         (obs_cell, taper_radius),
-        (place,),
     )
     step = 1
     while step < bands:
@@ -504,7 +507,6 @@
             + [(members, (batches - part[-1] - 1) * nobs)] * (part[-1] + 1 < batches),
             "chain",
             (*observed, obs_value, obs_error, obs_taper),
-            (place,),
         )
         pairs += outs[:2]
         observed = outs[2:]
@@ -513,7 +515,6 @@
         [(members * comps, cols_dev)],
         "update",
         (grid, *near, *far, courant_x, courant_y, diffusion, cell_taper, *pairs),
-        (place,),
         (pltpu.VMEM((members * comps, cols_dev), f32),),
     )
     return out.reshape(members, rows_dev, comps, cols_dev)

time: 70.8 us -> 67.1 us (0.948)
  Pallas kernels: 32.5 us -> 26.6 us
  waiting for transfers between devices: 13.4 us -> 16.1 us
    pallas_call x11, Pallas kernels: 32.5 us -> 26.6 us  [call(): pl.pallas_call(kernel, in_specs=specs, out_specs=[pl.BlockSpec(memory_spa...]
    all_to_all x1, waiting for transfers between devices: 1.4 us -> 2.59 us  [shards(): lax.all_to_all(send.reshape(blocks, 1, -1), 'mem', 0, 0).reshape(send.shape)]
    ppermute x2, waiting for transfers between devices: 2.24 us -> 3.27 us  [shards(): lax.ppermute(part, 'sub', swap)]
  transfers between devices with their start and end apart: 11 -> 11, of which waited for: 8 -> 8; matrix products, arithmetic and copies ran while one was open for 0% -> 0% of each run, Pallas kernels for 34% -> 28%
where the time goes in v6:
time: 67.1 us; the launch traced here: 66.8 us
  Pallas kernels  26.6 us (40%)
  starting transfers between devices  22.6 us (34%)
  waiting for transfers between devices  16.1 us (24%)
  local copies, waits for them, and re-layouts  1.31 us (2%)
    pallas_call x11, Pallas kernels, call(): pl.pallas_call(kernel, in_specs=specs, out_specs=[pl.BlockSpec(memory_spa...  26.6 us
    ppermute x2, starting transfers between devices, shards(): far.append(lax.ppermute(near[b], 'sub', onward))  8 us
    ppermute x3, starting transfers between devices, shards(): other = lax.ppermute(share, 'sub', [(i, i ^ step) for i in range(bands)])  7.22 us
    ppermute x3, waiting for transfers between devices, shards(): other = lax.ppermute(share, 'sub', [(i, i ^ step) for i in range(bands)])  5.53 us
    ppermute x3, waiting for transfers between devices, shards(): lax.ppermute(x, 'mem', to)  4.7 us
    all_to_all x1, starting transfers between devices, shards(): lax.all_to_all(send.reshape(blocks, 1, -1), 'mem', 0, 0).reshape(send.shape)  4.38 us
    ppermute x2, waiting for transfers between devices, shards(): lax.ppermute(part, 'sub', swap)  3.27 us
    all_to_all x1, waiting for transfers between devices, shards(): lax.all_to_all(send.reshape(blocks, 1, -1), 'mem', 0, 0).reshape(send.shape)  2.59 us
  transfers between devices with their start and end apart: 11, of which 8 were waited for; matrix products, arithmetic and copies ran while one was open for 0% of the time, Pallas kernels for 28%

profile of v6, /device:TPU:0, one launch (start us, length us, event | category | flops | bytes accessed | tf_op | source)
XLA Modules:
  0.0 66.8 jit_solution(8004971783289586623)
XLA Ops:
  0.0 1.2 %copy-done = f32[20,1,24,512]{3,2,1,0:T(8,128)S(1)} copy-done((f32[20,1,24,512]{3,2,1,0:T(8,128)S(1)}, f32[20,1,24,512]{3,2,1,0:T(8,128)}, u32[]{:S(2)}) %copy-start) | copy-done | bytes 983064
  1.2 1.6 %send.1 = f32[4,488,128]{2,1,0:T(8,128)} custom-call(f32[480,512]{1,0:T(8,128)S(1)} %bitcast.9), custom_call_target="tpu_custom_call" | custom-call | tf_op jit(solution)/shard_map/send/pallas_call | solution.py:38
  2.9 4.4 %all-to-all-start = ((f32[4,1,62464]{2,1,0:T(1,128)}), f32[4,1,62464]{2,1,0:T(1,128)S(1)}, u32[]{:S(2)}, u32[]{:S(2)}) async-start(f32[4,1,62464]{2,1,0:T(1,128)} %bitcast.2), calls=%async_computation | async-start | bytes 1998848 | tf_op jit(solution)/shard_map/all_to_all | solution.py:453
  7.3 2.4 %share.1.mine_ref = f32[24,512]{1,0:T(8,128)S(1)} custom-call(f32[480,512]{1,0:T(8,128)S(1)} %bitcast.10, f32[1,512]{1,0:T(1,128)S(1)} %copy-done.5, f32[1,512]{1,0:T(1,128)S(1)} %copy-done.6, f32[1,512]{1,0:T(1,128)S(1)} %copy-done.7, s32[4,128]{1,0:T(4,128)S(1)} %copy-done.8, f32[4,24,128]{2,1,0:T(8,128)S(1)} %bitcast.11), custom_call_target="tpu_custom_call" | custom-call | tf_op jit(solution)/shard_map/share/pallas_call | solution.py:38
  9.7 2.3 %collective-permute-start = (f32[24,512]{1,0:T(8,128)S(1)}, f32[24,512]{1,0:T(8,128)S(1)}, u32[]{:S(2)}, u32[]{:S(2)}) collective-permute-start(f32[24,512]{1,0:T(8,128)S(1)} %share.1.mine_ref), channel_id=1, source_target_pairs={{0,1},{1,0},{2,3},{3,2},{4,5},{5,4},{6,7},{7,6},{8,9},{9,8},{10,11... | collective-permute-start | bytes 147464 | tf_op jit(solution)/shard_map/ppermute | solution.py:472
  12.1 1.1 %tapers.1 = (f32[6,128,128]{2,1,0:T(8,128)S(1)}, f32[4,128,128]{2,1,0:T(8,128)S(1)}) custom-call(s32[4,128]{1,0:T(4,128)S(1)} %copy-done.8, f32[4,128]{1,0:T(4,128)S(1)} %copy-done.9), custom_call_target="tpu_custom_call" | custom-call | tf_op jit(solution)/shard_map/tapers/pallas_call | solution.py:38
  13.2 1.2 %collective-permute-done.other_ref = f32[24,512]{1,0:T(8,128)S(1)} collective-permute-done((f32[24,512]{1,0:T(8,128)S(1)}, f32[24,512]{1,0:T(8,128)S(1)}, u32[]{:S(2)}, u32[]{:S(2)}) %collective-permute-start) | collective-permute-done | bytes 49184 | tf_op jit(solution)/shard_map/ppermute | solution.py:472
  14.4 1.9 %collective-permute-start.1 = (f32[24,512]{1,0:T(8,128)S(1)}, f32[24,512]{1,0:T(8,128)S(1)}, u32[]{:S(2)}, u32[]{:S(2)}) collective-permute-start(f32[24,512]{1,0:T(8,128)S(1)} %join.3.mine_ref), channel_id=1, source_target_pairs={{0,2},{1,3},{2,0},{3,1},{4,6},{5,7},{6,4},{7,5},{8,10},{9,11},{10,... | collective-permute-start | bytes 147464 | tf_op jit(solution)/shard_map/ppermute | solution.py:472
  16.3 2.3 %collective-permute-done.1.other_ref = f32[24,512]{1,0:T(8,128)S(1)} collective-permute-done((f32[24,512]{1,0:T(8,128)S(1)}, f32[24,512]{1,0:T(8,128)S(1)}, u32[]{:S(2)}, u32[]{:S(2)}) %collective-permute-start.1) | collective-permute-done | bytes 49184 | tf_op jit(solution)/shard_map/ppermute | solution.py:472
  18.6 2.6 %all-to-all-done = f32[4,1,62464]{2,1,0:T(1,128)S(1)} async-done(((f32[4,1,62464]{2,1,0:T(1,128)}), f32[4,1,62464]{2,1,0:T(1,128)S(1)}, u32[]{:S(2)}, u32[]{:S(2)}) %all-to-all-start) | async-done | bytes 999456 | tf_op jit(solution)/shard_map/all_to_all | solution.py:453
  21.3 2.3 %collective-permute-start.6 = (f32[2,488,128]{2,1,0:T(8,128)S(1)}, f32[2,488,128]{2,1,0:T(8,128)S(1)}, u32[]{:S(2)}, u32[]{:S(2)}) collective-permute-start(f32[2,488,128]{2,1,0:T(8,128)S(1)} %get-tuple-element.62), channel_id=1, source_target_pairs={{0,1},{1,0},{2,3},{3,2},{4,5},{5,4},{6,7},{7,6},{8,9},{9,8},{10,11... | collective-permute-start | bytes 1499144 | tf_op jit(solution)/shard_map/ppermute | solution.py:488
  23.6 3.0 %collective-permute-start.2 = (f32[24,512]{1,0:T(8,128)S(1)}, f32[24,512]{1,0:T(8,128)S(1)}, u32[]{:S(2)}, u32[]{:S(2)}) collective-permute-start(f32[24,512]{1,0:T(8,128)S(1)} %join.4.mine_ref), channel_id=1, source_target_pairs={{0,4},{1,5},{2,6},{3,7},{4,0},{5,1},{6,2},{7,3},{8,12},{9,13},{10,... | collective-permute-start | bytes 147464 | tf_op jit(solution)/shard_map/ppermute | solution.py:472
  26.6 2.1 %collective-permute-done.2.other_ref = f32[24,512]{1,0:T(8,128)S(1)} collective-permute-done((f32[24,512]{1,0:T(8,128)S(1)}, f32[24,512]{1,0:T(8,128)S(1)}, u32[]{:S(2)}, u32[]{:S(2)}) %collective-permute-start.2) | collective-permute-done | bytes 49184 | tf_op jit(solution)/shard_map/ppermute | solution.py:472
  29.4 3.5 %collective-permute-done.4.refs_2_ = f32[20,512]{1,0:T(8,128)S(1)} collective-permute-done((f32[20,512]{1,0:T(8,128)S(1)}, f32[20,512]{1,0:T(8,128)S(1)}, u32[]{:S(2)}, u32[]{:S(2)}) %collective-permute-start.4) | collective-permute-done | bytes 40992 | tf_op jit(solution)/shard_map/ppermute | solution.py:493
  32.9 1.2 %collective-permute-done.5.refs_3_ = f32[20,512]{1,0:T(8,128)S(1)} collective-permute-done((f32[20,512]{1,0:T(8,128)S(1)}, f32[20,512]{1,0:T(8,128)S(1)}, u32[]{:S(2)}, u32[]{:S(2)}) %collective-permute-start.5) | collective-permute-done | bytes 40992 | tf_op jit(solution)/shard_map/ppermute | solution.py:493
  34.1 1.7 %collective-permute-done.6.near_a = f32[2,488,128]{2,1,0:T(8,128)S(1)} collective-permute-done((f32[2,488,128]{2,1,0:T(8,128)S(1)}, f32[2,488,128]{2,1,0:T(8,128)S(1)}, u32[]{:S(2)}, u32[]{:S(2)}) %collective-permute-start.6) | collective-permute-done | bytes 499744 | tf_op jit(solution)/shard_map/ppermute | solution.py:488
  35.8 4.1 %collective-permute-start.8 = (f32[2,488,128]{2,1,0:T(8,128)S(1)}, f32[2,488,128]{2,1,0:T(8,128)S(1)}, u32[]{:S(2)}, u32[]{:S(2)}) collective-permute-start(f32[2,488,128]{2,1,0:T(8,128)S(1)} %collective-permute-done.6.near_a), channel_id=1, source_target_pairs={{0,2},{2,4},{4,6},{3,1},{5,3},{7,5},{8,10},{10,12},{12,14},{11,9},... | collective-permute-start | bytes 1499144 | tf_op jit(solution)/shard_map/ppermute | solution.py:503
  39.9 3.9 %chain.4 = (f32[1,80,128]{2,1,0:T(8,128)S(1)}, f32[1,80,128]{2,1,0:T(8,128)S(1)}, f32[80,384]{1,0:T(8,128)S(1)}) custom-call(f32[20,512]{1,0:T(8,128)S(1)} %join.5.refs_0_, f32[20,512]{1,0:T(8,128)S(1)} %collective-permute-done.3.refs_1_, f32[20,512]{1,0:T(8,128)S(1)} %collective-permute-done.4.refs_2_, f32[20,512]{1,0:T(8,128)S(1)} %collective-permute-done.5.refs_3_, ...), custom_call_target="tpu_custom_call" | custom-call | tf_op jit(solution)/shard_map/chain/pallas_call | solution.py:38
  43.8 1.6 %collective-permute-done.7.near_b = f32[2,488,128]{2,1,0:T(8,128)S(1)} collective-permute-done((f32[2,488,128]{2,1,0:T(8,128)S(1)}, f32[2,488,128]{2,1,0:T(8,128)S(1)}, u32[]{:S(2)}, u32[]{:S(2)}) %collective-permute-start.7) | collective-permute-done | bytes 499744 | tf_op jit(solution)/shard_map/ppermute | solution.py:488
  45.4 3.9 %collective-permute-start.9 = (f32[2,488,128]{2,1,0:T(8,128)S(1)}, f32[2,488,128]{2,1,0:T(8,128)S(1)}, u32[]{:S(2)}, u32[]{:S(2)}) collective-permute-start(f32[2,488,128]{2,1,0:T(8,128)S(1)} %collective-permute-done.7.near_b), channel_id=1, source_target_pairs={{0,2},{2,4},{4,6},{3,1},{5,3},{7,5},{8,10},{10,12},{12,14},{11,9},... | collective-permute-start | bytes 1499144 | tf_op jit(solution)/shard_map/ppermute | solution.py:503
  49.3 3.9 %chain.5 = (f32[1,80,128]{2,1,0:T(8,128)S(1)}, f32[1,80,128]{2,1,0:T(8,128)S(1)}, f32[80,256]{1,0:T(8,128)S(1)}) custom-call(f32[80,384]{1,0:T(8,128)S(1)} %get-tuple-element.47.refs_0_, f32[4,128]{1,0:T(4,128)S(1)} %copy-done.3, f32[4,128]{1,0:T(4,128)S(1)} %copy-done.4, f32[6,128,128]{2,1,0:T(8,128)S(1)} %get-tuple-element.44.refs_6_.refs_3_), custom_call_target="tpu_custom_call" | custom-call | tf_op jit(solution)/shard_map/chain/pallas_call | solution.py:38
  53.2 3.9 %chain.6 = (f32[1,80,128]{2,1,0:T(8,128)S(1)}, f32[1,80,128]{2,1,0:T(8,128)S(1)}, f32[80,128]{1,0:T(8,128)S(1)}) custom-call(f32[80,256]{1,0:T(8,128)S(1)} %get-tuple-element.55.refs_0_, f32[4,128]{1,0:T(4,128)S(1)} %copy-done.3, f32[4,128]{1,0:T(4,128)S(1)} %copy-done.4, f32[6,128,128]{2,1,0:T(8,128)S(1)} %get-tuple-element.44.refs_6_.refs_3_), custom_call_target="tpu_custom_call" | custom-call | tf_op jit(solution)/shard_map/chain/pallas_call | solution.py:38
  57.1 3.7 %chain.7 = (f32[1,80,128]{2,1,0:T(8,128)S(1)}, f32[1,80,128]{2,1,0:T(8,128)S(1)}) custom-call(f32[80,128]{1,0:T(8,128)S(1)} %get-tuple-element.58.refs_0_, f32[4,128]{1,0:T(4,128)S(1)} %copy-done.3, f32[4,128]{1,0:T(4,128)S(1)} %copy-done.4, f32[6,128,128]{2,1,0:T(8,128)S(1)} %get-tuple-element.44.refs_6_.refs_3_), custom_call_target="tpu_custom_call" | custom-call | tf_op jit(solution)/shard_map/chain/pallas_call | solution.py:38
  60.8 6.0 %update.1 = f32[1920,128]{1,0:T(8,128)} custom-call(f32[4,488,128]{2,1,0:T(8,128)S(1)} %bitcast.8, f32[2,488,128]{2,1,0:T(8,128)S(1)} %collective-permute-done.6.near_a, f32[2,488,128]{2,1,0:T(8,128)S(1)} %collective-permute-done.7.near_b, f32[2,488,128]{2,1,0:T(8,128)S(1)} %collective-permute-done.8.far_a, f32[2,488,128]{2,1,0:T(8,128)S(1)} %collective-permute-done.9.far_b, ...), custom_call_target="tpu_custom_call" | custom-call | tf_op jit(solution)/shard_map/update/pallas_call | solution.py:38
  (30 shorter events, 0.9 us)
Async XLA Ops:
  0.0 1.2 %copy-start = (f32[20,1,24,512]{3,2,1,0:T(8,128)S(1)}, f32[20,1,24,512]{3,2,1,0:T(8,128)}, u32[]{:S(2)}) copy-start(f32[20,1,24,512]{3,2,1,0:T(8,128)} %param.9) | copy-start | bytes 2949124
  2.8 4.4 %copy-start.1 = (f32[20,1,24,512]{3,2,1,0:T(8,128)S(1)}, f32[20,1,24,512]{3,2,1,0:T(8,128)}, u32[]{:S(2)}) copy-start(f32[20,1,24,512]{3,2,1,0:T(8,128)} %param.9) | copy-start | bytes 2949124
  2.8 4.4 %copy-start.2 = (f32[4,128,24]{1,2,0:T(8,128)S(1)}, f32[4,128,24]{1,2,0:T(8,128)}, u32[]{:S(2)}) copy-start(f32[4,128,24]{1,2,0:T(8,128)} %param.16) | copy-start | bytes 147460
  2.8 4.4 %copy-start.5 = (f32[1,512]{1,0:T(1,128)S(1)}, f32[1,512]{1,0:T(1,128)}, u32[]{:S(2)}) copy-start(f32[1,512]{1,0:T(1,128)} %cx_ref.1) | copy-start | bytes 6148
  2.8 4.4 %copy-start.6 = (f32[1,512]{1,0:T(1,128)S(1)}, f32[1,512]{1,0:T(1,128)}, u32[]{:S(2)}) copy-start(f32[1,512]{1,0:T(1,128)} %cy_ref.1) | copy-start | bytes 6148
  2.8 4.4 %copy-start.7 = (f32[1,512]{1,0:T(1,128)S(1)}, f32[1,512]{1,0:T(1,128)}, u32[]{:S(2)}) copy-start(f32[1,512]{1,0:T(1,128)} %d_ref.1) | copy-start | bytes 6148
  2.9 4.4 %copy-start.8 = (s32[4,128]{1,0:T(4,128)S(1)}, s32[4,128]{1,0:T(4,128)}, u32[]{:S(2)}) copy-start(s32[4,128]{1,0:T(4,128)} %cell_ref.1) | copy-start | bytes 6148
  2.9 18.3 %all-to-all-start = ((f32[4,1,62464]{2,1,0:T(1,128)}), f32[4,1,62464]{2,1,0:T(1,128)S(1)}, u32[]{:S(2)}, u32[]{:S(2)}) async-start(f32[4,1,62464]{2,1,0:T(1,128)} %bitcast.2), calls=%async_computation | async-start | bytes 1998848 | tf_op jit(solution)/shard_map/all_to_all | solution.py:453
  7.3 4.8 %copy-start.9 = (f32[4,128]{1,0:T(4,128)S(1)}, f32[4,128]{1,0:T(4,128)}, u32[]{:S(2)}) copy-start(f32[4,128]{1,0:T(4,128)} %radius_ref.1) | copy-start | bytes 6148
  9.7 4.7 %collective-permute-start = (f32[24,512]{1,0:T(8,128)S(1)}, f32[24,512]{1,0:T(8,128)S(1)}, u32[]{:S(2)}, u32[]{:S(2)}) collective-permute-start(f32[24,512]{1,0:T(8,128)S(1)} %share.1.mine_ref), channel_id=1, source_target_pairs={{0,1},{1,0},{2,3},{3,2},{4,5},{5,4},{6,7},{7,6},{8,9},{9,8},{10,11... | collective-permute-start | bytes 147464 | tf_op jit(solution)/shard_map/ppermute | solution.py:472
  14.4 4.2 %collective-permute-start.1 = (f32[24,512]{1,0:T(8,128)S(1)}, f32[24,512]{1,0:T(8,128)S(1)}, u32[]{:S(2)}, u32[]{:S(2)}) collective-permute-start(f32[24,512]{1,0:T(8,128)S(1)} %join.3.mine_ref), channel_id=1, source_target_pairs={{0,2},{1,3},{2,0},{3,1},{4,6},{5,7},{6,4},{7,5},{8,10},{9,11},{10,... | collective-permute-start | bytes 147464 | tf_op jit(solution)/shard_map/ppermute | solution.py:472
  21.3 14.5 %collective-permute-start.6 = (f32[2,488,128]{2,1,0:T(8,128)S(1)}, f32[2,488,128]{2,1,0:T(8,128)S(1)}, u32[]{:S(2)}, u32[]{:S(2)}) collective-permute-start(f32[2,488,128]{2,1,0:T(8,128)S(1)} %get-tuple-element.62), channel_id=1, source_target_pairs={{0,1},{1,0},{2,3},{3,2},{4,5},{5,4},{6,7},{7,6},{8,9},{9,8},{10,11... | collective-permute-start | bytes 1499144 | tf_op jit(solution)/shard_map/ppermute | solution.py:488
  23.5 16.3 %copy-start.3 = (f32[4,128]{1,0:T(4,128)S(1)}, f32[4,128]{1,0:T(4,128)}, u32[]{:S(2)}) copy-start(f32[4,128]{1,0:T(4,128)} %refs_1_.6) | copy-start | bytes 6148
  23.5 16.3 %copy-start.4 = (f32[4,128]{1,0:T(4,128)S(1)}, f32[4,128]{1,0:T(4,128)}, u32[]{:S(2)}) copy-start(f32[4,128]{1,0:T(4,128)} %refs_2_.7) | copy-start | bytes 6148
  23.5 21.9 %collective-permute-start.7 = (f32[2,488,128]{2,1,0:T(8,128)S(1)}, f32[2,488,128]{2,1,0:T(8,128)S(1)}, u32[]{:S(2)}, u32[]{:S(2)}) collective-permute-start(f32[2,488,128]{2,1,0:T(8,128)S(1)} %get-tuple-element.61), channel_id=1, source_target_pairs={{0,1},{1,0},{2,3},{3,2},{4,5},{5,4},{6,7},{7,6},{8,9},{9,8},{10,11... | collective-permute-start | bytes 1499144 | tf_op jit(solution)/shard_map/ppermute | solution.py:488
  23.6 5.1 %collective-permute-start.2 = (f32[24,512]{1,0:T(8,128)S(1)}, f32[24,512]{1,0:T(8,128)S(1)}, u32[]{:S(2)}, u32[]{:S(2)}) collective-permute-start(f32[24,512]{1,0:T(8,128)S(1)} %join.4.mine_ref), channel_id=1, source_target_pairs={{0,4},{1,5},{2,6},{3,7},{4,0},{5,1},{6,2},{7,3},{8,12},{9,13},{10,... | collective-permute-start | bytes 147464 | tf_op jit(solution)/shard_map/ppermute | solution.py:472
  28.7 4.2 %collective-permute-start.4 = (f32[20,512]{1,0:T(8,128)S(1)}, f32[20,512]{1,0:T(8,128)S(1)}, u32[]{:S(2)}, u32[]{:S(2)}) collective-permute-start(f32[20,512]{1,0:T(8,128)S(1)} %join.5.refs_0_), channel_id=1, source_target_pairs={{0,16},{8,24},{16,0},{24,8},{1,17},{9,25},{17,1},{25,9},{2,18},{10... | collective-permute-start | bytes 122888 | tf_op jit(solution)/shard_map/ppermute | solution.py:493
  29.4 3.5 %collective-permute-start.3 = (f32[20,512]{1,0:T(8,128)S(1)}, f32[20,512]{1,0:T(8,128)S(1)}, u32[]{:S(2)}, u32[]{:S(2)}) collective-permute-start(f32[20,512]{1,0:T(8,128)S(1)} %join.5.refs_0_), channel_id=1, source_target_pairs={{0,8},{8,0},{16,24},{24,16},{1,9},{9,1},{17,25},{25,17},{2,10},{10... | collective-permute-start | bytes 122888 | tf_op jit(solution)/shard_map/ppermute | solution.py:493
  32.9 1.2 %collective-permute-start.5 = (f32[20,512]{1,0:T(8,128)S(1)}, f32[20,512]{1,0:T(8,128)S(1)}, u32[]{:S(2)}, u32[]{:S(2)}) collective-permute-start(f32[20,512]{1,0:T(8,128)S(1)} %collective-permute-done.4.refs_2_), channel_id=1, source_target_pairs={{0,8},{8,0},{16,24},{24,16},{1,9},{9,1},{17,25},{25,17},{2,10},{10... | collective-permute-start | bytes 122888 | tf_op jit(solution)/shard_map/ppermute | solution.py:493
  35.8 17.5 %collective-permute-start.8 = (f32[2,488,128]{2,1,0:T(8,128)S(1)}, f32[2,488,128]{2,1,0:T(8,128)S(1)}, u32[]{:S(2)}, u32[]{:S(2)}) collective-permute-start(f32[2,488,128]{2,1,0:T(8,128)S(1)} %collective-permute-done.6.near_a), channel_id=1, source_target_pairs={{0,2},{2,4},{4,6},{3,1},{5,3},{7,5},{8,10},{10,12},{12,14},{11,9},... | collective-permute-start | bytes 1499144 | tf_op jit(solution)/shard_map/ppermute | solution.py:503
  45.4 15.4 %collective-permute-start.9 = (f32[2,488,128]{2,1,0:T(8,128)S(1)}, f32[2,488,128]{2,1,0:T(8,128)S(1)}, u32[]{:S(2)}, u32[]{:S(2)}) collective-permute-start(f32[2,488,128]{2,1,0:T(8,128)S(1)} %collective-permute-done.7.near_b), channel_id=1, source_target_pairs={{0,2},{2,4},{4,6},{3,1},{5,3},{7,5},{8,10},{10,12},{12,14},{11,9},... | collective-permute-start | bytes 1499144 | tf_op jit(solution)/shard_map/ppermute | solution.py:503

commit v7 on v6

--- a/solution.py
+++ b/solution.py
@@ -153,7 +153,8 @@
 
 
 def send_kernel(width, blocks, edge_rows):
-    def kernel(q_ref, send_ref):
+    def kernel(q_ref, *send_refs):
+        here = lax.axis_index("mem")
         q = q_ref[...]
         count = q.shape[0]
         q_parts = split3(q)
@@ -161,7 +162,7 @@
         lanes = -(-2 * blocks // 128) * 128
         which = lax.broadcasted_iota(jnp.int32, (width, lanes), 1)
         spot = lax.broadcasted_iota(jnp.int32, (width, lanes), 0)
-        start = (which >> 1) * cols_dev
+        start = ((which >> 1) ^ here) * cols_dev
         wanted = jnp.where(which & 1 == 0, start - 1, start + cols_dev)
         wanted = jnp.where(wanted < 0, wanted + width, wanted)
         wanted = jnp.where(wanted == width, 0, wanted)
@@ -174,13 +175,13 @@
             edges = jnp.concatenate([edges, jnp.zeros((room, lanes), f32)], 0)
         edges = edges.T
         chunks = -(-count // 128)
-        for i in range(blocks):
-            at = slice(i * cols_dev, (i + 1) * cols_dev)
-            send_ref[i, :count, :] = q[:, at]
+        for i, send_ref in enumerate(send_refs):
+            first = pl.multiple_of((here ^ i) * cols_dev, cols_dev)
+            send_ref[:count, :] = q_ref[:, pl.ds(first, cols_dev)]
             rows = [edges[2 * i : 2 * i + 2, j * 128 : (j + 1) * 128] for j in range(chunks)]
             if edge_rows > 2 * chunks:
                 rows.append(jnp.zeros((edge_rows - 2 * chunks, 128), f32))
-            send_ref[i, count:, :] = jnp.concatenate(rows, 0)
+            send_ref[count:, :] = jnp.concatenate(rows, 0)
 
     return kernel
 
@@ -356,12 +357,12 @@
     return kernel
 
 
-def update_kernel(width, comps, batches, members, cols_dev, count, group):
+def update_kernel(width, comps, batches, members, cols_dev, count, blocks, group):
     def kernel(
-        own_ref, near_a, near_b, far_a, far_b, cx_ref, cy_ref, d_ref,
-        taper_ref, *refs,
+        *refs,
     ):
-        *pair_refs, out_ref, grid_ref = refs
+        own_refs, near_refs, far_refs = (refs[i * blocks : (i + 1) * blocks] for i in range(3))
+        cx_ref, cy_ref, d_ref, taper_ref, *pair_refs, out_ref, grid_ref = refs[3 * blocks :]
         pairs = [
             (pair_refs[i][k], pair_refs[i + 1][k])
             for i in range(0, len(pair_refs), 2)
@@ -377,14 +378,13 @@
         from_near = jnp.where(even, from_north, from_south)
         from_far = jnp.where(even, from_south, from_north)
         from_west, from_east = jnp.maximum(cx, 0.0), -jnp.minimum(cx, 0.0)
-        for s in range(own_ref.shape[0]):
-            middle = near_a.shape[0]
-            near_ref, far_ref = (near_a, far_a) if s < middle else (near_b, far_b)
-            outer = to_columns(own_ref[s, count:, :])
+        for s, (own_ref, near_ref, far_ref) in enumerate(zip(own_refs, near_refs, far_refs)):
+            base = pl.multiple_of((lax.axis_index("mem") ^ s) * count, 8)
+            outer = to_columns(own_ref[count:, :])
             for j in range(-(-count // 128)):
                 size = min(128, count - 128 * j)
                 at = slice(128 * j, 128 * j + size)
-                q, near, far = own_ref[s, at, :], near_ref[s % middle, at, :], far_ref[s % middle, at, :]
+                q, near, far = own_ref[at, :], near_ref[at, :], far_ref[at, :]
                 west = jnp.where(lane == 0, outer[:size, 2 * j : 2 * j + 1], pltpu.roll(q, 1, 1))
                 east = jnp.where(
                     lane == cols_dev - 1,
@@ -394,7 +394,7 @@
                 x = q - from_west * (q - west) - from_east * (q - east)
                 x = x - from_near * (q - near) - from_far * (q - far)
                 x = x + d * (east + west + near + far - 4.0 * q)
-                grid_ref[pl.ds(s * count + 128 * j, size), :] = x
+                grid_ref[pl.ds(base + 128 * j, size), :] = x
         left, right, tapers = [], [], []
         nobs = taper_ref.shape[1]
         fill = -3 * members % 128
@@ -444,14 +444,16 @@
 
     share_rows = -(-(local + 2) // 8) * 8
     prior = prior_sample_array.reshape(count, width)
-    (send,) = call(
+    sends = call(
         send_kernel(width, blocks, edge_rows),
-        [(blocks, count + edge_rows, cols_dev)],
+        [(count + edge_rows, cols_dev)] * blocks,
         "send",
         (prior,),
     )
-    grid = lax.all_to_all(send.reshape(blocks, 1, -1), "mem", 0, 0).reshape(send.shape)
-    held_x, send = lax.optimization_barrier((courant_x, send))
+    grid = [sends[0]] + [
+        lax.ppermute(sends[k], "mem", [(i, i ^ k) for i in range(blocks)]) for k in range(1, blocks)
+    ]
+    held_x, *sends = lax.optimization_barrier((courant_x, *sends))
     sources = (prior, held_x, courant_y, diffusion, obs_cell, obs_weight.transpose(0, 2, 1))
     (share,) = call(
         share_kernel(width, comps, batches, nobs, local),
@@ -467,6 +469,11 @@
         "tapers",
         (obs_cell, taper_radius),
     )
+    swap = [(i, i ^ 1) for i in range(bands)]
+    onward = [(i, i + 2) for i in range(0, bands - 2, 2)] + [(i, i - 2) for i in range(3, bands, 2)]
+    middle = blocks // 2
+    parts = (slice(0, middle), slice(middle, blocks))
+    near, far = [], []
     step = 1
     while step < bands:
         other = lax.ppermute(share, "sub", [(i, i ^ step) for i in range(bands)])
@@ -479,13 +486,13 @@
             "join",
             (share, other),
         )
-        if 4 * step == bands:
-            share, grid = lax.optimization_barrier((share, grid))
+        if step in (1, 2):
+            part = parts[step // 2]
+            share, *grid[part] = lax.optimization_barrier((share, *grid[part]))
+            near += [lax.ppermute(x, "sub", swap) for x in grid[part]]
         step *= 2
-    swap = [(i, i ^ 1) for i in range(bands)]
-    onward = [(i, i + 2) for i in range(0, bands - 2, 2)] + [(i, i - 2) for i in range(3, bands, 2)]
-    middle = blocks // 2
-    near = [lax.ppermute(part, "sub", swap) for part in (grid[:middle], grid[middle:])]
+    share, *near[:middle] = lax.optimization_barrier((share, *near[:middle]))
+    far += [lax.ppermute(x, "sub", onward) for x in near[:middle]]
     observed = {0: share}
     step = blocks // 2
     while step:
@@ -493,14 +500,16 @@
         observed.update({k ^ step: lax.ppermute(x, "mem", to) for k, x in observed.items()})
         step //= 2
     observed = [observed[k] for k in range(blocks)]
-    pairs, far = [], []
+    pairs = []
     for b in range(batches):
         part = range(b, b + 1)
+        if b == 0:
+            held = lax.optimization_barrier((*observed, *near[middle:]))
+            observed, near[middle:] = held[: len(observed)], held[len(observed) :]
+            far += [lax.ppermute(x, "sub", onward) for x in near[middle:]]
         if b == 2:
-            *observed, far[0] = lax.optimization_barrier((*observed, far[0]))
-        if b < 2:
-            *observed, near[b] = lax.optimization_barrier((*observed, near[b]))
-            far.append(lax.ppermute(near[b], "sub", onward))
+            held = lax.optimization_barrier((*observed, *far[:middle]))
+            observed, far[:middle] = held[: len(observed)], held[len(observed) :]
         outs = call(
             chain_kernel(part, batches, nobs, len(observed)),
             [(len(part), members, nobs)] * 2
@@ -511,10 +520,10 @@
         pairs += outs[:2]
         observed = outs[2:]
     (out,) = call(
-        update_kernel(width, comps, batches, members, cols_dev, count, comps),
+        update_kernel(width, comps, batches, members, cols_dev, count, blocks, comps),
         [(members * comps, cols_dev)],
         "update",
-        (grid, *near, *far, courant_x, courant_y, diffusion, cell_taper, *pairs),
+        (*grid, *near, *far, courant_x, courant_y, diffusion, cell_taper, *pairs),
         (pltpu.VMEM((members * comps, cols_dev), f32),),
     )
     return out.reshape(members, rows_dev, comps, cols_dev)

time: 67.1 us -> 65.5 us (0.976)
  waiting for transfers between devices: 16.1 us -> 10.4 us
  starting transfers between devices: 22.6 us -> 26.7 us
    ppermute x4 -> x11, starting transfers between devices: 10.3 us -> 19.9 us  [the longest x2 6.95 us: shards(): far += [lax.ppermute(x, 'sub', onward) for x in near[:middle]]]
    all_to_all x1 -> x0, starting transfers between devices: 4.38 us -> none  [shards(): lax.all_to_all(send.reshape(blocks, 1, -1), 'mem', 0, 0).reshape(send.shape)]
    all_to_all x1 -> x0, waiting for transfers between devices: 2.59 us -> none  [shards(): lax.all_to_all(send.reshape(blocks, 1, -1), 'mem', 0, 0).reshape(send.shape)]
    ppermute x4 -> x11, waiting for transfers between devices: 3.28 us -> 1.08 us  [the longest x4 1.06 us: shards(): near += [lax.ppermute(x, 'sub', swap) for x in grid[part]]]
    ppermute x3, waiting for transfers between devices: 4.7 us -> 2.95 us  [shards(): lax.ppermute(x, 'mem', to)]
    ppermute x3, starting transfers between devices: 7.22 us -> 5.71 us  [shards(): other = lax.ppermute(share, 'sub', [(i, i ^ step) for i in range(bands)])]
    ppermute x3, waiting for transfers between devices: 5.53 us -> 6.38 us  [shards(): other = lax.ppermute(share, 'sub', [(i, i ^ step) for i in range(bands)])]
    unnamed x20 -> x18, local copies, waits for them, and re-layouts: 1.24 us -> 1.85 us
  transfers between devices with their start and end apart: 11 -> 17, of which waited for: 8 -> 5; matrix products, arithmetic and copies ran while one was open for 0% -> 0% of each run, Pallas kernels for 28% -> 29%
where the time goes in v7:
time: 65.5 us; the launch traced here: 65.3 us
  starting transfers between devices  26.7 us (41%)
  Pallas kernels  26.1 us (40%)
  waiting for transfers between devices  10.4 us (16%)
  local copies, waits for them, and re-layouts  1.85 us (3%)
    pallas_call x11, Pallas kernels, call(): pl.pallas_call(kernel, in_specs=specs, out_specs=[pl.BlockSpec(memory_spa...  26.1 us
    ppermute x2, starting transfers between devices, shards(): far += [lax.ppermute(x, 'sub', onward) for x in near[:middle]]  6.95 us
    ppermute x3, waiting for transfers between devices, shards(): other = lax.ppermute(share, 'sub', [(i, i ^ step) for i in range(bands)])  6.38 us
    ppermute x3, starting transfers between devices, shards(): other = lax.ppermute(share, 'sub', [(i, i ^ step) for i in range(bands)])  5.71 us
    ppermute x2, starting transfers between devices, shards(): far += [lax.ppermute(x, 'sub', onward) for x in near[middle:]]  5.59 us
    ppermute x4, starting transfers between devices, shards(): near += [lax.ppermute(x, 'sub', swap) for x in grid[part]]  4.18 us
    ppermute x3, starting transfers between devices, shards(): lax.ppermute(sends[k], 'mem', [(i, i ^ k) for i in range(blocks)])  3.15 us
    ppermute x3, waiting for transfers between devices, shards(): lax.ppermute(x, 'mem', to)  2.95 us
  transfers between devices with their start and end apart: 17, of which 5 were waited for; matrix products, arithmetic and copies ran while one was open for 0% of the time, Pallas kernels for 29%

profile of v7, /device:TPU:0, one launch (start us, length us, event | category | flops | bytes accessed | tf_op | source)
XLA Modules:
  0.0 65.3 jit_solution(16833606145188229202)
XLA Ops:
  0.0 1.2 %copy-done = f32[20,1,24,512]{3,2,1,0:T(8,128)S(1)} copy-done((f32[20,1,24,512]{3,2,1,0:T(8,128)S(1)}, f32[20,1,24,512]{3,2,1,0:T(8,128)}, u32[]{:S(2)}) %copy-start) | copy-done | bytes 983064
  2.4 2.6 %collective-permute-start.3 = (f32[488,128]{1,0:T(8,128)S(1)}, f32[488,128]{1,0:T(8,128)S(1)}, u32[]{:S(2)}, u32[]{:S(2)}) collective-permute-start(f32[488,128]{1,0:T(8,128)S(1)} %get-tuple-element.46), channel_id=1, source_target_pairs={{0,16},{8,24},{16,0},{24,8},{1,17},{9,25},{17,1},{25,9},{2,18},{10... | collective-permute-start | bytes 749576 | tf_op jit(solution)/shard_map/ppermute | solution.py:454
  5.7 2.4 %share.1.mine_ref = f32[24,512]{1,0:T(8,128)S(1)} custom-call(f32[480,512]{1,0:T(8,128)S(1)} %bitcast.6, f32[1,512]{1,0:T(1,128)S(1)} %copy-done.4, f32[1,512]{1,0:T(1,128)S(1)} %copy-done.5, f32[1,512]{1,0:T(1,128)S(1)} %copy-done.6, s32[4,128]{1,0:T(4,128)S(1)} %copy-done.7, f32[4,24,128]{2,1,0:T(8,128)S(1)} %bitcast.7), custom_call_target="tpu_custom_call" | custom-call | tf_op jit(solution)/shard_map/share/pallas_call | solution.py:38
  8.1 1.6 %collective-permute-start = (f32[24,512]{1,0:T(8,128)S(1)}, f32[24,512]{1,0:T(8,128)S(1)}, u32[]{:S(2)}, u32[]{:S(2)}) collective-permute-start(f32[24,512]{1,0:T(8,128)S(1)} %share.1.mine_ref), channel_id=1, source_target_pairs={{0,1},{1,0},{2,3},{3,2},{4,5},{5,4},{6,7},{7,6},{8,9},{9,8},{10,11... | collective-permute-start | bytes 147464 | tf_op jit(solution)/shard_map/ppermute | solution.py:479
  9.7 1.1 %tapers.1 = (f32[6,128,128]{2,1,0:T(8,128)S(1)}, f32[4,128,128]{2,1,0:T(8,128)S(1)}) custom-call(s32[4,128]{1,0:T(4,128)S(1)} %copy-done.7, f32[4,128]{1,0:T(4,128)S(1)} %copy-done.8), custom_call_target="tpu_custom_call" | custom-call | tf_op jit(solution)/shard_map/tapers/pallas_call | solution.py:38
  10.8 1.5 %collective-permute-done.other_ref = f32[24,512]{1,0:T(8,128)S(1)} collective-permute-done((f32[24,512]{1,0:T(8,128)S(1)}, f32[24,512]{1,0:T(8,128)S(1)}, u32[]{:S(2)}, u32[]{:S(2)}) %collective-permute-start) | collective-permute-done | bytes 49184 | tf_op jit(solution)/shard_map/ppermute | solution.py:479
  12.3 1.6 %collective-permute-start.6 = (f32[488,128]{1,0:T(8,128)S(1)}, f32[488,128]{1,0:T(8,128)S(1)}, u32[]{:S(2)}, u32[]{:S(2)}) collective-permute-start(f32[488,128]{1,0:T(8,128)S(1)} %get-tuple-element.52.refs_0_), channel_id=1, source_target_pairs={{0,1},{1,0},{2,3},{3,2},{4,5},{5,4},{6,7},{7,6},{8,9},{9,8},{10,11... | collective-permute-start | bytes 749576 | tf_op jit(solution)/shard_map/ppermute | solution.py:492
  14.4 1.6 %collective-permute-start.2 = (f32[24,512]{1,0:T(8,128)S(1)}, f32[24,512]{1,0:T(8,128)S(1)}, u32[]{:S(2)}, u32[]{:S(2)}) collective-permute-start(f32[24,512]{1,0:T(8,128)S(1)} %join.3.mine_ref), channel_id=1, source_target_pairs={{0,2},{1,3},{2,0},{3,1},{4,6},{5,7},{6,4},{7,5},{8,10},{9,11},{10,... | collective-permute-start | bytes 147464 | tf_op jit(solution)/shard_map/ppermute | solution.py:479
  16.0 2.5 %collective-permute-done.2.other_ref = f32[24,512]{1,0:T(8,128)S(1)} collective-permute-done((f32[24,512]{1,0:T(8,128)S(1)}, f32[24,512]{1,0:T(8,128)S(1)}, u32[]{:S(2)}, u32[]{:S(2)}) %collective-permute-start.2) | collective-permute-done | bytes 49184 | tf_op jit(solution)/shard_map/ppermute | solution.py:479
  18.5 1.6 %collective-permute-start.11 = (f32[488,128]{1,0:T(8,128)S(1)}, f32[488,128]{1,0:T(8,128)S(1)}, u32[]{:S(2)}, u32[]{:S(2)}) collective-permute-start(f32[488,128]{1,0:T(8,128)S(1)} %collective-permute-done.3.refs_2_), channel_id=1, source_target_pairs={{0,1},{1,0},{2,3},{3,2},{4,5},{5,4},{6,7},{7,6},{8,9},{9,8},{10,11... | collective-permute-start | bytes 749576 | tf_op jit(solution)/shard_map/ppermute | solution.py:492
  20.6 2.6 %collective-permute-start.5 = (f32[24,512]{1,0:T(8,128)S(1)}, f32[24,512]{1,0:T(8,128)S(1)}, u32[]{:S(2)}, u32[]{:S(2)}) collective-permute-start(f32[24,512]{1,0:T(8,128)S(1)} %join.4.mine_ref), channel_id=1, source_target_pairs={{0,4},{1,5},{2,6},{3,7},{4,0},{5,1},{6,2},{7,3},{8,12},{9,13},{10,... | collective-permute-start | bytes 147464 | tf_op jit(solution)/shard_map/ppermute | solution.py:479
  23.2 2.4 %collective-permute-done.5.other_ref = f32[24,512]{1,0:T(8,128)S(1)} collective-permute-done((f32[24,512]{1,0:T(8,128)S(1)}, f32[24,512]{1,0:T(8,128)S(1)}, u32[]{:S(2)}, u32[]{:S(2)}) %collective-permute-start.5) | collective-permute-done | bytes 49184 | tf_op jit(solution)/shard_map/ppermute | solution.py:479
  25.6 1.1 %collective-permute-done.7.refs_5_ = f32[488,128]{1,0:T(8,128)S(1)} collective-permute-done((f32[488,128]{1,0:T(8,128)S(1)}, f32[488,128]{1,0:T(8,128)S(1)}, u32[]{:S(2)}, u32[]{:S(2)}) %collective-permute-start.7) | collective-permute-done | bytes 249888 | tf_op jit(solution)/shard_map/ppermute | solution.py:492
  26.7 1.1 %collective-permute-start.9 = (f32[20,512]{1,0:T(8,128)S(1)}, f32[20,512]{1,0:T(8,128)S(1)}, u32[]{:S(2)}, u32[]{:S(2)}) collective-permute-start(f32[20,512]{1,0:T(8,128)S(1)} %join.5.refs_0_), channel_id=1, source_target_pairs={{0,16},{8,24},{16,0},{24,8},{1,17},{9,25},{17,1},{25,9},{2,18},{10... | collective-permute-start | bytes 122888 | tf_op jit(solution)/shard_map/ppermute | solution.py:500
  27.8 2.9 %collective-permute-done.9.refs_2_ = f32[20,512]{1,0:T(8,128)S(1)} collective-permute-done((f32[20,512]{1,0:T(8,128)S(1)}, f32[20,512]{1,0:T(8,128)S(1)}, u32[]{:S(2)}, u32[]{:S(2)}) %collective-permute-start.9) | collective-permute-done | bytes 40992 | tf_op jit(solution)/shard_map/ppermute | solution.py:500
  30.8 3.5 %collective-permute-start.13 = (f32[488,128]{1,0:T(8,128)S(1)}, f32[488,128]{1,0:T(8,128)S(1)}, u32[]{:S(2)}, u32[]{:S(2)}) collective-permute-start(f32[488,128]{1,0:T(8,128)S(1)} %collective-permute-done.6.refs_4_), channel_id=1, source_target_pairs={{0,2},{2,4},{4,6},{3,1},{5,3},{7,5},{8,10},{10,12},{12,14},{11,9},... | collective-permute-start | bytes 749576 | tf_op jit(solution)/shard_map/ppermute | solution.py:495
  34.3 3.5 %collective-permute-start.14 = (f32[488,128]{1,0:T(8,128)S(1)}, f32[488,128]{1,0:T(8,128)S(1)}, u32[]{:S(2)}, u32[]{:S(2)}) collective-permute-start(f32[488,128]{1,0:T(8,128)S(1)} %collective-permute-done.7.refs_5_), channel_id=1, source_target_pairs={{0,2},{2,4},{4,6},{3,1},{5,3},{7,5},{8,10},{10,12},{12,14},{11,9},... | collective-permute-start | bytes 749576 | tf_op jit(solution)/shard_map/ppermute | solution.py:495
  37.8 3.5 %collective-permute-start.15 = (f32[488,128]{1,0:T(8,128)S(1)}, f32[488,128]{1,0:T(8,128)S(1)}, u32[]{:S(2)}, u32[]{:S(2)}) collective-permute-start(f32[488,128]{1,0:T(8,128)S(1)} %collective-permute-done.11.refs_6_), channel_id=1, source_target_pairs={{0,2},{2,4},{4,6},{3,1},{5,3},{7,5},{8,10},{10,12},{12,14},{11,9},... | collective-permute-start | bytes 749576 | tf_op jit(solution)/shard_map/ppermute | solution.py:509
  41.3 2.1 %collective-permute-start.16 = (f32[488,128]{1,0:T(8,128)S(1)}, f32[488,128]{1,0:T(8,128)S(1)}, u32[]{:S(2)}, u32[]{:S(2)}) collective-permute-start(f32[488,128]{1,0:T(8,128)S(1)} %collective-permute-done.12.refs_7_), channel_id=1, source_target_pairs={{0,2},{2,4},{4,6},{3,1},{5,3},{7,5},{8,10},{10,12},{12,14},{11,9},... | collective-permute-start | bytes 749576 | tf_op jit(solution)/shard_map/ppermute | solution.py:509
  43.4 3.9 %chain.4 = (f32[1,80,128]{2,1,0:T(8,128)S(1)}, f32[1,80,128]{2,1,0:T(8,128)S(1)}, f32[80,384]{1,0:T(8,128)S(1)}) custom-call(f32[20,512]{1,0:T(8,128)S(1)} %join.5.refs_0_, f32[20,512]{1,0:T(8,128)S(1)} %collective-permute-done.8.refs_1_, f32[20,512]{1,0:T(8,128)S(1)} %collective-permute-done.9.refs_2_, f32[20,512]{1,0:T(8,128)S(1)} %collective-permute-done.10.refs_3_, ...), custom_call_target="tpu_custom_call" | custom-call | tf_op jit(solution)/shard_map/chain/pallas_call | solution.py:38
  47.4 3.9 %chain.5 = (f32[1,80,128]{2,1,0:T(8,128)S(1)}, f32[1,80,128]{2,1,0:T(8,128)S(1)}, f32[80,256]{1,0:T(8,128)S(1)}) custom-call(f32[80,384]{1,0:T(8,128)S(1)} %get-tuple-element.68.refs_0_, f32[4,128]{1,0:T(4,128)S(1)} %copy-done.2, f32[4,128]{1,0:T(4,128)S(1)} %copy-done.3, f32[6,128,128]{2,1,0:T(8,128)S(1)} %get-tuple-element.67.refs_6_.refs_3_), custom_call_target="tpu_custom_call" | custom-call | tf_op jit(solution)/shard_map/chain/pallas_call | solution.py:38
  51.3 3.9 %chain.6 = (f32[1,80,128]{2,1,0:T(8,128)S(1)}, f32[1,80,128]{2,1,0:T(8,128)S(1)}, f32[80,128]{1,0:T(8,128)S(1)}) custom-call(f32[80,256]{1,0:T(8,128)S(1)} %get-tuple-element.77.refs_0_, f32[4,128]{1,0:T(4,128)S(1)} %copy-done.2, f32[4,128]{1,0:T(4,128)S(1)} %copy-done.3, f32[6,128,128]{2,1,0:T(8,128)S(1)} %get-tuple-element.67.refs_6_.refs_3_), custom_call_target="tpu_custom_call" | custom-call | tf_op jit(solution)/shard_map/chain/pallas_call | solution.py:38
  55.1 3.7 %chain.7 = (f32[1,80,128]{2,1,0:T(8,128)S(1)}, f32[1,80,128]{2,1,0:T(8,128)S(1)}) custom-call(f32[80,128]{1,0:T(8,128)S(1)} %get-tuple-element.80.refs_0_, f32[4,128]{1,0:T(4,128)S(1)} %copy-done.2, f32[4,128]{1,0:T(4,128)S(1)} %copy-done.3, f32[6,128,128]{2,1,0:T(8,128)S(1)} %get-tuple-element.67.refs_6_.refs_3_), custom_call_target="tpu_custom_call" | custom-call | tf_op jit(solution)/shard_map/chain/pallas_call | solution.py:38
  58.8 6.4 %update.1 = f32[1920,128]{1,0:T(8,128)} custom-call(f32[488,128]{1,0:T(8,128)S(1)} %get-tuple-element.52.refs_0_, f32[488,128]{1,0:T(8,128)S(1)} %collective-permute-done.1.refs_1_, f32[488,128]{1,0:T(8,128)S(1)} %collective-permute-done.3.refs_2_, f32[488,128]{1,0:T(8,128)S(1)} %collective-permute-done.4.refs_3_, ...), custom_call_target="tpu_custom_call" | custom-call | tf_op jit(solution)/shard_map/update/pallas_call | solution.py:38
  (39 shorter events, 3.0 us)
Async XLA Ops:
  0.0 1.2 %copy-start = (f32[20,1,24,512]{3,2,1,0:T(8,128)S(1)}, f32[20,1,24,512]{3,2,1,0:T(8,128)}, u32[]{:S(2)}) copy-start(f32[20,1,24,512]{3,2,1,0:T(8,128)} %param.9) | copy-start | bytes 2949124
  1.2 3.8 %copy-start.1 = (f32[4,128,24]{1,2,0:T(8,128)S(1)}, f32[4,128,24]{1,2,0:T(8,128)}, u32[]{:S(2)}) copy-start(f32[4,128,24]{1,2,0:T(8,128)} %param.16) | copy-start | bytes 147460
  1.2 3.8 %copy-start.6 = (f32[1,512]{1,0:T(1,128)S(1)}, f32[1,512]{1,0:T(1,128)}, u32[]{:S(2)}) copy-start(f32[1,512]{1,0:T(1,128)} %refs_14_.1) | copy-start | bytes 6148
  1.2 3.8 %copy-start.7 = (s32[4,128]{1,0:T(4,128)S(1)}, s32[4,128]{1,0:T(4,128)}, u32[]{:S(2)}) copy-start(s32[4,128]{1,0:T(4,128)} %cell_ref.1) | copy-start | bytes 6148
  1.9 10.4 %collective-permute-start.1 = (f32[488,128]{1,0:T(8,128)S(1)}, f32[488,128]{1,0:T(8,128)S(1)}, u32[]{:S(2)}, u32[]{:S(2)}) collective-permute-start(f32[488,128]{1,0:T(8,128)S(1)} %get-tuple-element.45), channel_id=1, source_target_pairs={{0,8},{8,0},{16,24},{24,16},{1,9},{9,1},{17,25},{25,17},{2,10},{10... | collective-permute-start | bytes 749576 | tf_op jit(solution)/shard_map/ppermute | solution.py:454
  2.4 16.1 %collective-permute-start.3 = (f32[488,128]{1,0:T(8,128)S(1)}, f32[488,128]{1,0:T(8,128)S(1)}, u32[]{:S(2)}, u32[]{:S(2)}) collective-permute-start(f32[488,128]{1,0:T(8,128)S(1)} %get-tuple-element.46), channel_id=1, source_target_pairs={{0,16},{8,24},{16,0},{24,8},{1,17},{9,25},{17,1},{25,9},{2,18},{10... | collective-permute-start | bytes 749576 | tf_op jit(solution)/shard_map/ppermute | solution.py:454
  5.0 13.6 %collective-permute-start.4 = (f32[488,128]{1,0:T(8,128)S(1)}, f32[488,128]{1,0:T(8,128)S(1)}, u32[]{:S(2)}, u32[]{:S(2)}) collective-permute-start(f32[488,128]{1,0:T(8,128)S(1)} %get-tuple-element.47), channel_id=1, source_target_pairs={{0,24},{8,16},{16,8},{24,0},{1,25},{9,17},{17,9},{25,1},{2,26},{10... | collective-permute-start | bytes 749576 | tf_op jit(solution)/shard_map/ppermute | solution.py:454
  5.7 4.0 %copy-start.8 = (f32[4,128]{1,0:T(4,128)S(1)}, f32[4,128]{1,0:T(4,128)}, u32[]{:S(2)}) copy-start(f32[4,128]{1,0:T(4,128)} %radius_ref.1) | copy-start | bytes 6148
  8.1 4.2 %collective-permute-start = (f32[24,512]{1,0:T(8,128)S(1)}, f32[24,512]{1,0:T(8,128)S(1)}, u32[]{:S(2)}, u32[]{:S(2)}) collective-permute-start(f32[24,512]{1,0:T(8,128)S(1)} %share.1.mine_ref), channel_id=1, source_target_pairs={{0,1},{1,0},{2,3},{3,2},{4,5},{5,4},{6,7},{7,6},{8,9},{9,8},{10,11... | collective-permute-start | bytes 147464 | tf_op jit(solution)/shard_map/ppermute | solution.py:479
  12.3 13.3 %collective-permute-start.6 = (f32[488,128]{1,0:T(8,128)S(1)}, f32[488,128]{1,0:T(8,128)S(1)}, u32[]{:S(2)}, u32[]{:S(2)}) collective-permute-start(f32[488,128]{1,0:T(8,128)S(1)} %get-tuple-element.52.refs_0_), channel_id=1, source_target_pairs={{0,1},{1,0},{2,3},{3,2},{4,5},{5,4},{6,7},{7,6},{8,9},{9,8},{10,11... | collective-permute-start | bytes 749576 | tf_op jit(solution)/shard_map/ppermute | solution.py:492
  13.8 12.8 %collective-permute-start.7 = (f32[488,128]{1,0:T(8,128)S(1)}, f32[488,128]{1,0:T(8,128)S(1)}, u32[]{:S(2)}, u32[]{:S(2)}) collective-permute-start(f32[488,128]{1,0:T(8,128)S(1)} %collective-permute-done.1.refs_1_), channel_id=1, source_target_pairs={{0,1},{1,0},{2,3},{3,2},{4,5},{5,4},{6,7},{7,6},{8,9},{9,8},{10,11... | collective-permute-start | bytes 749576 | tf_op jit(solution)/shard_map/ppermute | solution.py:492
  14.4 4.1 %collective-permute-start.2 = (f32[24,512]{1,0:T(8,128)S(1)}, f32[24,512]{1,0:T(8,128)S(1)}, u32[]{:S(2)}, u32[]{:S(2)}) collective-permute-start(f32[24,512]{1,0:T(8,128)S(1)} %join.3.mine_ref), channel_id=1, source_target_pairs={{0,2},{1,3},{2,0},{3,1},{4,6},{5,7},{6,4},{7,5},{8,10},{9,11},{10,... | collective-permute-start | bytes 147464 | tf_op jit(solution)/shard_map/ppermute | solution.py:479
  18.5 24.9 %copy-start.2 = (f32[4,128]{1,0:T(4,128)S(1)}, f32[4,128]{1,0:T(4,128)}, u32[]{:S(2)}) copy-start(f32[4,128]{1,0:T(4,128)} %refs_1_.6) | copy-start | bytes 6148
  18.5 24.9 %copy-start.3 = (f32[4,128]{1,0:T(4,128)S(1)}, f32[4,128]{1,0:T(4,128)}, u32[]{:S(2)}) copy-start(f32[4,128]{1,0:T(4,128)} %refs_2_.7) | copy-start | bytes 6148
  18.5 19.2 %collective-permute-start.11 = (f32[488,128]{1,0:T(8,128)S(1)}, f32[488,128]{1,0:T(8,128)S(1)}, u32[]{:S(2)}, u32[]{:S(2)}) collective-permute-start(f32[488,128]{1,0:T(8,128)S(1)} %collective-permute-done.3.refs_2_), channel_id=1, source_target_pairs={{0,1},{1,0},{2,3},{3,2},{4,5},{5,4},{6,7},{7,6},{8,9},{9,8},{10,11... | collective-permute-start | bytes 749576 | tf_op jit(solution)/shard_map/ppermute | solution.py:492
  20.1 17.7 %collective-permute-start.12 = (f32[488,128]{1,0:T(8,128)S(1)}, f32[488,128]{1,0:T(8,128)S(1)}, u32[]{:S(2)}, u32[]{:S(2)}) collective-permute-start(f32[488,128]{1,0:T(8,128)S(1)} %collective-permute-done.4.refs_3_), channel_id=1, source_target_pairs={{0,1},{1,0},{2,3},{3,2},{4,5},{5,4},{6,7},{7,6},{8,9},{9,8},{10,11... | collective-permute-start | bytes 749576 | tf_op jit(solution)/shard_map/ppermute | solution.py:492
  20.6 5.0 %collective-permute-start.5 = (f32[24,512]{1,0:T(8,128)S(1)}, f32[24,512]{1,0:T(8,128)S(1)}, u32[]{:S(2)}, u32[]{:S(2)}) collective-permute-start(f32[24,512]{1,0:T(8,128)S(1)} %join.4.mine_ref), channel_id=1, source_target_pairs={{0,4},{1,5},{2,6},{3,7},{4,0},{5,1},{6,2},{7,3},{8,12},{9,13},{10,... | collective-permute-start | bytes 147464 | tf_op jit(solution)/shard_map/ppermute | solution.py:479
  26.7 4.1 %collective-permute-start.9 = (f32[20,512]{1,0:T(8,128)S(1)}, f32[20,512]{1,0:T(8,128)S(1)}, u32[]{:S(2)}, u32[]{:S(2)}) collective-permute-start(f32[20,512]{1,0:T(8,128)S(1)} %join.5.refs_0_), channel_id=1, source_target_pairs={{0,16},{8,24},{16,0},{24,8},{1,17},{9,25},{17,1},{25,9},{2,18},{10... | collective-permute-start | bytes 122888 | tf_op jit(solution)/shard_map/ppermute | solution.py:500
  27.8 6.4 %collective-permute-start.8 = (f32[20,512]{1,0:T(8,128)S(1)}, f32[20,512]{1,0:T(8,128)S(1)}, u32[]{:S(2)}, u32[]{:S(2)}) collective-permute-start(f32[20,512]{1,0:T(8,128)S(1)} %join.5.refs_0_), channel_id=1, source_target_pairs={{0,8},{8,0},{16,24},{24,16},{1,9},{9,1},{17,25},{25,17},{2,10},{10... | collective-permute-start | bytes 122888 | tf_op jit(solution)/shard_map/ppermute | solution.py:500
  30.8 7.0 %collective-permute-start.10 = (f32[20,512]{1,0:T(8,128)S(1)}, f32[20,512]{1,0:T(8,128)S(1)}, u32[]{:S(2)}, u32[]{:S(2)}) collective-permute-start(f32[20,512]{1,0:T(8,128)S(1)} %collective-permute-done.9.refs_2_), channel_id=1, source_target_pairs={{0,8},{8,0},{16,24},{24,16},{1,9},{9,1},{17,25},{25,17},{2,10},{10... | collective-permute-start | bytes 122888 | tf_op jit(solution)/shard_map/ppermute | solution.py:500
  30.8 20.5 %collective-permute-start.13 = (f32[488,128]{1,0:T(8,128)S(1)}, f32[488,128]{1,0:T(8,128)S(1)}, u32[]{:S(2)}, u32[]{:S(2)}) collective-permute-start(f32[488,128]{1,0:T(8,128)S(1)} %collective-permute-done.6.refs_4_), channel_id=1, source_target_pairs={{0,2},{2,4},{4,6},{3,1},{5,3},{7,5},{8,10},{10,12},{12,14},{11,9},... | collective-permute-start | bytes 749576 | tf_op jit(solution)/shard_map/ppermute | solution.py:495
  34.3 17.0 %collective-permute-start.14 = (f32[488,128]{1,0:T(8,128)S(1)}, f32[488,128]{1,0:T(8,128)S(1)}, u32[]{:S(2)}, u32[]{:S(2)}) collective-permute-start(f32[488,128]{1,0:T(8,128)S(1)} %collective-permute-done.7.refs_5_), channel_id=1, source_target_pairs={{0,2},{2,4},{4,6},{3,1},{5,3},{7,5},{8,10},{10,12},{12,14},{11,9},... | collective-permute-start | bytes 749576 | tf_op jit(solution)/shard_map/ppermute | solution.py:495
  37.8 21.0 %collective-permute-start.15 = (f32[488,128]{1,0:T(8,128)S(1)}, f32[488,128]{1,0:T(8,128)S(1)}, u32[]{:S(2)}, u32[]{:S(2)}) collective-permute-start(f32[488,128]{1,0:T(8,128)S(1)} %collective-permute-done.11.refs_6_), channel_id=1, source_target_pairs={{0,2},{2,4},{4,6},{3,1},{5,3},{7,5},{8,10},{10,12},{12,14},{11,9},... | collective-permute-start | bytes 749576 | tf_op jit(solution)/shard_map/ppermute | solution.py:509
  41.3 17.5 %collective-permute-start.16 = (f32[488,128]{1,0:T(8,128)S(1)}, f32[488,128]{1,0:T(8,128)S(1)}, u32[]{:S(2)}, u32[]{:S(2)}) collective-permute-start(f32[488,128]{1,0:T(8,128)S(1)} %collective-permute-done.12.refs_7_), channel_id=1, source_target_pairs={{0,2},{2,4},{4,6},{3,1},{5,3},{7,5},{8,10},{10,12},{12,14},{11,9},... | collective-permute-start | bytes 749576 | tf_op jit(solution)/shard_map/ppermute | solution.py:509
  (2 other events, 1.4 us)

commit v8 on v7

--- a/solution.py
+++ b/solution.py
@@ -357,12 +357,15 @@
     return kernel
 
 
-def update_kernel(width, comps, batches, members, cols_dev, count, blocks, group):
+def update_kernel(width, comps, batches, members, cols_dev, count, blocks, bands, group):
     def kernel(
         *refs,
     ):
-        own_refs, near_refs, far_refs = (refs[i * blocks : (i + 1) * blocks] for i in range(3))
-        cx_ref, cy_ref, d_ref, taper_ref, *pair_refs, out_ref, grid_ref = refs[3 * blocks :]
+        own_refs, halos, refs = refs[:blocks], refs[blocks : blocks + 4], refs[blocks + 4 :]
+        near_refs, far_refs = (
+            [ref.at[i] for ref in halos[at : at + 2] for i in range(ref.shape[0])] for at in (0, 2)
+        )
+        cx_ref, cy_ref, d_ref, taper_ref, *pair_refs, out_ref, grid_ref = refs
         pairs = [
             (pair_refs[i][k], pair_refs[i + 1][k])
             for i in range(0, len(pair_refs), 2)
@@ -373,7 +376,9 @@
         cy = cy_ref[:, pl.ds(start, cols_dev)]
         d = d_ref[:, pl.ds(start, cols_dev)]
         lane = lax.broadcasted_iota(jnp.int32, (1, cols_dev), 1)
-        even = jnp.full((1, cols_dev), lax.axis_index("sub") & 1, jnp.int32) == 0
+        band = jnp.full((1, cols_dev), lax.axis_index("sub"), jnp.int32)
+        even = band & 1 == 0
+        outermost = (band == 0) | (band == bands - 1)
         from_south, from_north = jnp.maximum(cy, 0.0), -jnp.minimum(cy, 0.0)
         from_near = jnp.where(even, from_north, from_south)
         from_far = jnp.where(even, from_south, from_north)
@@ -384,7 +389,8 @@
             for j in range(-(-count // 128)):
                 size = min(128, count - 128 * j)
                 at = slice(128 * j, 128 * j + size)
-                q, near, far = own_ref[at, :], near_ref[at, :], far_ref[at, :]
+                q, near = own_ref[at, :], near_ref[at, :]
+                far = jnp.where(outermost, 0.0, far_ref[at, :])
                 west = jnp.where(lane == 0, outer[:size, 2 * j : 2 * j + 1], pltpu.roll(q, 1, 1))
                 east = jnp.where(
                     lane == cols_dev - 1,
@@ -471,6 +477,8 @@
     )
     swap = [(i, i ^ 1) for i in range(bands)]
     onward = [(i, i + 2) for i in range(0, bands - 2, 2)] + [(i, i - 2) for i in range(3, bands, 2)]
+    around = onward + [(bands - 2, 0), (1, bands - 1)]
+    across = onward + [(1, 0), (bands - 2, bands - 1)]
     middle = blocks // 2
     parts = (slice(0, middle), slice(middle, blocks))
     near, far = [], []
@@ -489,10 +497,10 @@
         if step in (1, 2):
             part = parts[step // 2]
             share, *grid[part] = lax.optimization_barrier((share, *grid[part]))
-            near += [lax.ppermute(x, "sub", swap) for x in grid[part]]
+            near.append(lax.ppermute(jnp.stack(grid[part]), "sub", swap))
         step *= 2
-    share, *near[:middle] = lax.optimization_barrier((share, *near[:middle]))
-    far += [lax.ppermute(x, "sub", onward) for x in near[:middle]]
+    share, near[0] = lax.optimization_barrier((share, near[0]))
+    far.append(lax.ppermute(near[0], "sub", around))
     observed = {0: share}
     step = blocks // 2
     while step:
@@ -504,12 +512,10 @@
     for b in range(batches):
         part = range(b, b + 1)
         if b == 0:
-            held = lax.optimization_barrier((*observed, *near[middle:]))
-            observed, near[middle:] = held[: len(observed)], held[len(observed) :]
-            far += [lax.ppermute(x, "sub", onward) for x in near[middle:]]
+            *observed, near[1] = lax.optimization_barrier((*observed, near[1]))
+            far.append(lax.ppermute(near[1], "sub", across))
         if b == 2:
-            held = lax.optimization_barrier((*observed, *far[:middle]))
-            observed, far[:middle] = held[: len(observed)], held[len(observed) :]
+            *observed, far[0] = lax.optimization_barrier((*observed, far[0]))
         outs = call(
             chain_kernel(part, batches, nobs, len(observed)),
             [(len(part), members, nobs)] * 2
@@ -520,7 +526,7 @@
         pairs += outs[:2]
         observed = outs[2:]
     (out,) = call(
-        update_kernel(width, comps, batches, members, cols_dev, count, blocks, comps),
+        update_kernel(width, comps, batches, members, cols_dev, count, blocks, bands, comps),
         [(members * comps, cols_dev)],
         "update",
         (*grid, *near, *far, courant_x, courant_y, diffusion, cell_taper, *pairs),

time: 65.5 us -> 62.2 us (0.950)
  starting transfers between devices: 26.7 us -> 14.1 us
  waiting for transfers between devices: 10.4 us -> 19.8 us
    ppermute x8 -> x4, starting transfers between devices: 16.7 us -> 4.05 us  [the longest x2 3.15 us: shards(): near.append(lax.ppermute(jnp.stack(grid[part]), 'sub', swap))]
    ppermute x8 -> x4, waiting for transfers between devices: 1.07 us -> 10.8 us  [the longest x2 8.12 us: shards(): near.append(lax.ppermute(jnp.stack(grid[part]), 'sub', swap))]
  transfers between devices with their start and end apart: 17 -> 13, of which waited for: 5 -> 8; matrix products, arithmetic and copies ran while one was open for 0% -> 0% of each run, Pallas kernels for 29% -> 31%
where the time goes in v8:
time: 62.2 us; the launch traced here: 62.1 us
  Pallas kernels  26 us (42%)
  waiting for transfers between devices  19.8 us (32%)
  starting transfers between devices  14.1 us (23%)
  local copies, waits for them, and re-layouts  1.85 us (3%)
    pallas_call x11, Pallas kernels, call(): pl.pallas_call(kernel, in_specs=specs, out_specs=[pl.BlockSpec(memory_spa...  26 us
    ppermute x2, waiting for transfers between devices, shards(): near.append(lax.ppermute(jnp.stack(grid[part]), 'sub', swap))  8.12 us
    ppermute x3, waiting for transfers between devices, shards(): other = lax.ppermute(share, 'sub', [(i, i ^ step) for i in range(bands)])  5.8 us
    ppermute x3, starting transfers between devices, shards(): other = lax.ppermute(share, 'sub', [(i, i ^ step) for i in range(bands)])  5.79 us
    ppermute x3, starting transfers between devices, shards(): lax.ppermute(sends[k], 'mem', [(i, i ^ k) for i in range(blocks)])  3.15 us
    ppermute x2, starting transfers between devices, shards(): near.append(lax.ppermute(jnp.stack(grid[part]), 'sub', swap))  3.15 us
    ppermute x3, waiting for transfers between devices, shards(): lax.ppermute(x, 'mem', to)  2.95 us
    ppermute x1, waiting for transfers between devices, shards(): far.append(lax.ppermute(near[0], 'sub', around))  2.72 us
  transfers between devices with their start and end apart: 13, of which 8 were waited for; matrix products, arithmetic and copies ran while one was open for 0% of the time, Pallas kernels for 31%

profile of v8, /device:TPU:0, one launch (start us, length us, event | category | flops | bytes accessed | tf_op | source)
XLA Modules:
  0.0 62.1 jit_solution(8965665700562750076)
XLA Ops:
  0.0 1.2 %copy-done = f32[20,1,24,512]{3,2,1,0:T(8,128)S(1)} copy-done((f32[20,1,24,512]{3,2,1,0:T(8,128)S(1)}, f32[20,1,24,512]{3,2,1,0:T(8,128)}, u32[]{:S(2)}) %copy-start) | copy-done | bytes 983064
  1.2 0.7 %send.1 = (f32[488,128]{1,0:T(8,128)S(1)}, f32[488,128]{1,0:T(8,128)S(1)}, f32[488,128]{1,0:T(8,128)S(1)}, f32[488,128]{1,0:T(8,128)S(1)}) custom-call(f32[480,512]{1,0:T(8,128)S(1)} %bitcast.9), custom_call_target="tpu_custom_call" | custom-call | tf_op jit(solution)/shard_map/send/pallas_call | solution.py:38
  2.4 2.6 %collective-permute-start.3 = (f32[488,128]{1,0:T(8,128)S(1)}, f32[488,128]{1,0:T(8,128)S(1)}, u32[]{:S(2)}, u32[]{:S(2)}) collective-permute-start(f32[488,128]{1,0:T(8,128)S(1)} %get-tuple-element.43), channel_id=1, source_target_pairs={{0,16},{8,24},{16,0},{24,8},{1,17},{9,25},{17,1},{25,9},{2,18},{10... | collective-permute-start | bytes 749576 | tf_op jit(solution)/shard_map/ppermute | solution.py:460
  5.0 0.6 copy-done.5
  5.7 2.4 %share.1.mine_ref = f32[24,512]{1,0:T(8,128)S(1)} custom-call(f32[480,512]{1,0:T(8,128)S(1)} %bitcast.10, f32[1,512]{1,0:T(1,128)S(1)} %copy-done.4, f32[1,512]{1,0:T(1,128)S(1)} %copy-done.5, f32[1,512]{1,0:T(1,128)S(1)} %copy-done.6, s32[4,128]{1,0:T(4,128)S(1)} %copy-done.7, f32[4,24,128]{2,1,0:T(8,128)S(1)} %bitcast.15), custom_call_target="tpu_custom_call" | custom-call | tf_op jit(solution)/shard_map/share/pallas_call | solution.py:38
  8.1 1.6 %collective-permute-start = (f32[24,512]{1,0:T(8,128)S(1)}, f32[24,512]{1,0:T(8,128)S(1)}, u32[]{:S(2)}, u32[]{:S(2)}) collective-permute-start(f32[24,512]{1,0:T(8,128)S(1)} %share.1.mine_ref), channel_id=1, source_target_pairs={{0,1},{1,0},{2,3},{3,2},{4,5},{5,4},{6,7},{7,6},{8,9},{9,8},{10,11... | collective-permute-start | bytes 147464 | tf_op jit(solution)/shard_map/ppermute | solution.py:487
  9.7 1.1 %tapers.1 = (f32[6,128,128]{2,1,0:T(8,128)S(1)}, f32[4,128,128]{2,1,0:T(8,128)S(1)}) custom-call(s32[4,128]{1,0:T(4,128)S(1)} %copy-done.7, f32[4,128]{1,0:T(4,128)S(1)} %copy-done.8), custom_call_target="tpu_custom_call" | custom-call | tf_op jit(solution)/shard_map/tapers/pallas_call | solution.py:38
  10.8 1.5 %collective-permute-done.other_ref = f32[24,512]{1,0:T(8,128)S(1)} collective-permute-done((f32[24,512]{1,0:T(8,128)S(1)}, f32[24,512]{1,0:T(8,128)S(1)}, u32[]{:S(2)}, u32[]{:S(2)}) %collective-permute-start) | collective-permute-done | bytes 49184 | tf_op jit(solution)/shard_map/ppermute | solution.py:487
  12.3 1.6 %collective-permute-start.2 = (f32[24,512]{1,0:T(8,128)S(1)}, f32[24,512]{1,0:T(8,128)S(1)}, u32[]{:S(2)}, u32[]{:S(2)}) collective-permute-start(f32[24,512]{1,0:T(8,128)S(1)} %join.3.mine_ref), channel_id=1, source_target_pairs={{0,2},{1,3},{2,0},{3,1},{4,6},{5,7},{6,4},{7,5},{8,10},{9,11},{10,... | collective-permute-start | bytes 147464 | tf_op jit(solution)/shard_map/ppermute | solution.py:487
  14.0 1.5 %collective-permute-start.6 = (f32[2,488,128]{2,1,0:T(8,128)S(1)}, f32[2,488,128]{2,1,0:T(8,128)S(1)}, u32[]{:S(2)}, u32[]{:S(2)}) collective-permute-start(f32[2,488,128]{2,1,0:T(8,128)S(1)} %pad_maximum_fusion), channel_id=1, source_target_pairs={{0,1},{1,0},{2,3},{3,2},{4,5},{5,4},{6,7},{7,6},{8,9},{9,8},{10,11... | collective-permute-start | bytes 1499144 | tf_op jit(solution)/shard_map/ppermute | solution.py:500
  15.5 0.9 %collective-permute-done.2.other_ref = f32[24,512]{1,0:T(8,128)S(1)} collective-permute-done((f32[24,512]{1,0:T(8,128)S(1)}, f32[24,512]{1,0:T(8,128)S(1)}, u32[]{:S(2)}, u32[]{:S(2)}) %collective-permute-start.2) | collective-permute-done | bytes 49184 | tf_op jit(solution)/shard_map/ppermute | solution.py:487
  16.8 1.6 %collective-permute-start.10 = (f32[2,488,128]{2,1,0:T(8,128)S(1)}, f32[2,488,128]{2,1,0:T(8,128)S(1)}, u32[]{:S(2)}, u32[]{:S(2)}) collective-permute-start(f32[2,488,128]{2,1,0:T(8,128)S(1)} %pad_maximum_fusion.1), channel_id=1, source_target_pairs={{0,1},{1,0},{2,3},{3,2},{4,5},{5,4},{6,7},{7,6},{8,9},{9,8},{10,11... | collective-permute-start | bytes 1499144 | tf_op jit(solution)/shard_map/ppermute | solution.py:500
  18.4 2.6 %collective-permute-start.5 = (f32[24,512]{1,0:T(8,128)S(1)}, f32[24,512]{1,0:T(8,128)S(1)}, u32[]{:S(2)}, u32[]{:S(2)}) collective-permute-start(f32[24,512]{1,0:T(8,128)S(1)} %join.4.mine_ref), channel_id=1, source_target_pairs={{0,4},{1,5},{2,6},{3,7},{4,0},{5,1},{6,2},{7,3},{8,12},{9,13},{10,... | collective-permute-start | bytes 147464 | tf_op jit(solution)/shard_map/ppermute | solution.py:487
  21.0 3.5 %collective-permute-done.5.other_ref = f32[24,512]{1,0:T(8,128)S(1)} collective-permute-done((f32[24,512]{1,0:T(8,128)S(1)}, f32[24,512]{1,0:T(8,128)S(1)}, u32[]{:S(2)}, u32[]{:S(2)}) %collective-permute-start.5) | collective-permute-done | bytes 49184 | tf_op jit(solution)/shard_map/ppermute | solution.py:487
  24.4 4.0 %collective-permute-done.6.refs_4_ = f32[2,488,128]{2,1,0:T(8,128)S(1)} collective-permute-done((f32[2,488,128]{2,1,0:T(8,128)S(1)}, f32[2,488,128]{2,1,0:T(8,128)S(1)}, u32[]{:S(2)}, u32[]{:S(2)}) %collective-permute-start.6) | collective-permute-done | bytes 499744 | tf_op jit(solution)/shard_map/ppermute | solution.py:500
  28.4 1.1 %collective-permute-start.8 = (f32[20,512]{1,0:T(8,128)S(1)}, f32[20,512]{1,0:T(8,128)S(1)}, u32[]{:S(2)}, u32[]{:S(2)}) collective-permute-start(f32[20,512]{1,0:T(8,128)S(1)} %join.5.refs_0_), channel_id=1, source_target_pairs={{0,16},{8,24},{16,0},{24,8},{1,17},{9,25},{17,1},{25,9},{2,18},{10... | collective-permute-start | bytes 122888 | tf_op jit(solution)/shard_map/ppermute | solution.py:508
  29.5 2.9 %collective-permute-done.8.refs_2_ = f32[20,512]{1,0:T(8,128)S(1)} collective-permute-done((f32[20,512]{1,0:T(8,128)S(1)}, f32[20,512]{1,0:T(8,128)S(1)}, u32[]{:S(2)}, u32[]{:S(2)}) %collective-permute-start.8) | collective-permute-done | bytes 40992 | tf_op jit(solution)/shard_map/ppermute | solution.py:508
  32.9 4.2 %collective-permute-done.10.refs_5_ = f32[2,488,128]{2,1,0:T(8,128)S(1)} collective-permute-done((f32[2,488,128]{2,1,0:T(8,128)S(1)}, f32[2,488,128]{2,1,0:T(8,128)S(1)}, u32[]{:S(2)}, u32[]{:S(2)}) %collective-permute-start.10) | collective-permute-done | bytes 499744 | tf_op jit(solution)/shard_map/ppermute | solution.py:500
  37.6 3.9 %chain.4 = (f32[1,80,128]{2,1,0:T(8,128)S(1)}, f32[1,80,128]{2,1,0:T(8,128)S(1)}, f32[80,384]{1,0:T(8,128)S(1)}) custom-call(f32[20,512]{1,0:T(8,128)S(1)} %join.5.refs_0_, f32[20,512]{1,0:T(8,128)S(1)} %collective-permute-done.7.refs_1_, f32[20,512]{1,0:T(8,128)S(1)} %collective-permute-done.8.refs_2_, f32[20,512]{1,0:T(8,128)S(1)} %collective-permute-done.9.refs_3_, ...), custom_call_target="tpu_custom_call" | custom-call | tf_op jit(solution)/shard_map/chain/pallas_call | solution.py:38
  41.5 3.9 %chain.5 = (f32[1,80,128]{2,1,0:T(8,128)S(1)}, f32[1,80,128]{2,1,0:T(8,128)S(1)}, f32[80,256]{1,0:T(8,128)S(1)}) custom-call(f32[80,384]{1,0:T(8,128)S(1)} %get-tuple-element.63.refs_0_, f32[4,128]{1,0:T(4,128)S(1)} %copy-done.2, f32[4,128]{1,0:T(4,128)S(1)} %copy-done.3, f32[6,128,128]{2,1,0:T(8,128)S(1)} %get-tuple-element.62.refs_6_.refs_3_), custom_call_target="tpu_custom_call" | custom-call | tf_op jit(solution)/shard_map/chain/pallas_call | solution.py:38
  45.4 2.7 %collective-permute-done.11.refs_6_ = f32[2,488,128]{2,1,0:T(8,128)S(1)} collective-permute-done((f32[2,488,128]{2,1,0:T(8,128)S(1)}, f32[2,488,128]{2,1,0:T(8,128)S(1)}, u32[]{:S(2)}, u32[]{:S(2)}) %collective-permute-start.11) | collective-permute-done | bytes 499744 | tf_op jit(solution)/shard_map/ppermute | solution.py:503
  48.1 3.9 %chain.6 = (f32[1,80,128]{2,1,0:T(8,128)S(1)}, f32[1,80,128]{2,1,0:T(8,128)S(1)}, f32[80,128]{1,0:T(8,128)S(1)}) custom-call(f32[80,256]{1,0:T(8,128)S(1)} %get-tuple-element.71.refs_0_, f32[4,128]{1,0:T(4,128)S(1)} %copy-done.2, f32[4,128]{1,0:T(4,128)S(1)} %copy-done.3, f32[6,128,128]{2,1,0:T(8,128)S(1)} %get-tuple-element.62.refs_6_.refs_3_), custom_call_target="tpu_custom_call" | custom-call | tf_op jit(solution)/shard_map/chain/pallas_call | solution.py:38
  51.9 3.7 %chain.7 = (f32[1,80,128]{2,1,0:T(8,128)S(1)}, f32[1,80,128]{2,1,0:T(8,128)S(1)}) custom-call(f32[80,128]{1,0:T(8,128)S(1)} %get-tuple-element.74.refs_0_, f32[4,128]{1,0:T(4,128)S(1)} %copy-done.2, f32[4,128]{1,0:T(4,128)S(1)} %copy-done.3, f32[6,128,128]{2,1,0:T(8,128)S(1)} %get-tuple-element.62.refs_6_.refs_3_), custom_call_target="tpu_custom_call" | custom-call | tf_op jit(solution)/shard_map/chain/pallas_call | solution.py:38
  55.7 6.4 %update.1 = f32[1920,128]{1,0:T(8,128)} custom-call(f32[488,128]{1,0:T(8,128)S(1)} %get-tuple-element.49.refs_0_, f32[488,128]{1,0:T(8,128)S(1)} %collective-permute-done.1.refs_1_, f32[488,128]{1,0:T(8,128)S(1)} %collective-permute-done.3.refs_2_, f32[488,128]{1,0:T(8,128)S(1)} %collective-permute-done.4.refs_3_, ...), custom_call_target="tpu_custom_call" | custom-call | tf_op jit(solution)/shard_map/update/pallas_call | solution.py:38
  (33 shorter events, 1.9 us)
Async XLA Ops:
  0.0 1.2 %copy-start = (f32[20,1,24,512]{3,2,1,0:T(8,128)S(1)}, f32[20,1,24,512]{3,2,1,0:T(8,128)}, u32[]{:S(2)}) copy-start(f32[20,1,24,512]{3,2,1,0:T(8,128)} %param.9) | copy-start | bytes 2949124
  1.2 3.8 %copy-start.1 = (f32[4,128,24]{1,2,0:T(8,128)S(1)}, f32[4,128,24]{1,2,0:T(8,128)}, u32[]{:S(2)}) copy-start(f32[4,128,24]{1,2,0:T(8,128)} %param.16) | copy-start | bytes 147460
  1.2 3.8 %copy-start.6 = (f32[1,512]{1,0:T(1,128)S(1)}, f32[1,512]{1,0:T(1,128)}, u32[]{:S(2)}) copy-start(f32[1,512]{1,0:T(1,128)} %refs_10_.1) | copy-start | bytes 6148
  1.2 3.8 %copy-start.7 = (s32[4,128]{1,0:T(4,128)S(1)}, s32[4,128]{1,0:T(4,128)}, u32[]{:S(2)}) copy-start(s32[4,128]{1,0:T(4,128)} %cell_ref.1) | copy-start | bytes 6148
  1.9 10.4 %collective-permute-start.1 = (f32[488,128]{1,0:T(8,128)S(1)}, f32[488,128]{1,0:T(8,128)S(1)}, u32[]{:S(2)}, u32[]{:S(2)}) collective-permute-start(f32[488,128]{1,0:T(8,128)S(1)} %get-tuple-element.42), channel_id=1, source_target_pairs={{0,8},{8,0},{16,24},{24,16},{1,9},{9,1},{17,25},{25,17},{2,10},{10... | collective-permute-start | bytes 749576 | tf_op jit(solution)/shard_map/ppermute | solution.py:460
  2.4 14.1 %collective-permute-start.3 = (f32[488,128]{1,0:T(8,128)S(1)}, f32[488,128]{1,0:T(8,128)S(1)}, u32[]{:S(2)}, u32[]{:S(2)}) collective-permute-start(f32[488,128]{1,0:T(8,128)S(1)} %get-tuple-element.43), channel_id=1, source_target_pairs={{0,16},{8,24},{16,0},{24,8},{1,17},{9,25},{17,1},{25,9},{2,18},{10... | collective-permute-start | bytes 749576 | tf_op jit(solution)/shard_map/ppermute | solution.py:460
  5.0 0.7 %copy-start.5 = (f32[1,512]{1,0:T(1,128)S(1)}, f32[1,512]{1,0:T(1,128)}, u32[]{:S(2)}) copy-start(f32[1,512]{1,0:T(1,128)} %refs_9_.1) | copy-start | bytes 6148
  5.0 0.7 %copy-start.4 = (f32[1,512]{1,0:T(1,128)S(1)}, f32[1,512]{1,0:T(1,128)}, u32[]{:S(2)}) copy-start(f32[1,512]{1,0:T(1,128)} %refs_8_.1) | copy-start | bytes 6148
  5.0 11.7 %collective-permute-start.4 = (f32[488,128]{1,0:T(8,128)S(1)}, f32[488,128]{1,0:T(8,128)S(1)}, u32[]{:S(2)}, u32[]{:S(2)}) collective-permute-start(f32[488,128]{1,0:T(8,128)S(1)} %get-tuple-element.44), channel_id=1, source_target_pairs={{0,24},{8,16},{16,8},{24,0},{1,25},{9,17},{17,9},{25,1},{2,26},{10... | collective-permute-start | bytes 749576 | tf_op jit(solution)/shard_map/ppermute | solution.py:460
  5.7 4.0 %copy-start.8 = (f32[4,128]{1,0:T(4,128)S(1)}, f32[4,128]{1,0:T(4,128)}, u32[]{:S(2)}) copy-start(f32[4,128]{1,0:T(4,128)} %radius_ref.1) | copy-start | bytes 6148
  8.1 4.2 %collective-permute-start = (f32[24,512]{1,0:T(8,128)S(1)}, f32[24,512]{1,0:T(8,128)S(1)}, u32[]{:S(2)}, u32[]{:S(2)}) collective-permute-start(f32[24,512]{1,0:T(8,128)S(1)} %share.1.mine_ref), channel_id=1, source_target_pairs={{0,1},{1,0},{2,3},{3,2},{4,5},{5,4},{6,7},{7,6},{8,9},{9,8},{10,11... | collective-permute-start | bytes 147464 | tf_op jit(solution)/shard_map/ppermute | solution.py:487
  12.3 4.2 %collective-permute-start.2 = (f32[24,512]{1,0:T(8,128)S(1)}, f32[24,512]{1,0:T(8,128)S(1)}, u32[]{:S(2)}, u32[]{:S(2)}) collective-permute-start(f32[24,512]{1,0:T(8,128)S(1)} %join.3.mine_ref), channel_id=1, source_target_pairs={{0,2},{1,3},{2,0},{3,1},{4,6},{5,7},{6,4},{7,5},{8,10},{9,11},{10,... | collective-permute-start | bytes 147464 | tf_op jit(solution)/shard_map/ppermute | solution.py:487
  14.0 14.4 %collective-permute-start.6 = (f32[2,488,128]{2,1,0:T(8,128)S(1)}, f32[2,488,128]{2,1,0:T(8,128)S(1)}, u32[]{:S(2)}, u32[]{:S(2)}) collective-permute-start(f32[2,488,128]{2,1,0:T(8,128)S(1)} %pad_maximum_fusion), channel_id=1, source_target_pairs={{0,1},{1,0},{2,3},{3,2},{4,5},{5,4},{6,7},{7,6},{8,9},{9,8},{10,11... | collective-permute-start | bytes 1499144 | tf_op jit(solution)/shard_map/ppermute | solution.py:500
  16.7 20.8 %copy-start.2 = (f32[4,128]{1,0:T(4,128)S(1)}, f32[4,128]{1,0:T(4,128)}, u32[]{:S(2)}) copy-start(f32[4,128]{1,0:T(4,128)} %refs_1_.6) | copy-start | bytes 6148
  16.8 20.8 %copy-start.3 = (f32[4,128]{1,0:T(4,128)S(1)}, f32[4,128]{1,0:T(4,128)}, u32[]{:S(2)}) copy-start(f32[4,128]{1,0:T(4,128)} %refs_2_.7) | copy-start | bytes 6148
  16.8 20.3 %collective-permute-start.10 = (f32[2,488,128]{2,1,0:T(8,128)S(1)}, f32[2,488,128]{2,1,0:T(8,128)S(1)}, u32[]{:S(2)}, u32[]{:S(2)}) collective-permute-start(f32[2,488,128]{2,1,0:T(8,128)S(1)} %pad_maximum_fusion.1), channel_id=1, source_target_pairs={{0,1},{1,0},{2,3},{3,2},{4,5},{5,4},{6,7},{7,6},{8,9},{9,8},{10,11... | collective-permute-start | bytes 1499144 | tf_op jit(solution)/shard_map/ppermute | solution.py:500
  18.4 6.0 %collective-permute-start.5 = (f32[24,512]{1,0:T(8,128)S(1)}, f32[24,512]{1,0:T(8,128)S(1)}, u32[]{:S(2)}, u32[]{:S(2)}) collective-permute-start(f32[24,512]{1,0:T(8,128)S(1)} %join.4.mine_ref), channel_id=1, source_target_pairs={{0,4},{1,5},{2,6},{3,7},{4,0},{5,1},{6,2},{7,3},{8,12},{9,13},{10,... | collective-permute-start | bytes 147464 | tf_op jit(solution)/shard_map/ppermute | solution.py:487
  28.4 4.1 %collective-permute-start.8 = (f32[20,512]{1,0:T(8,128)S(1)}, f32[20,512]{1,0:T(8,128)S(1)}, u32[]{:S(2)}, u32[]{:S(2)}) collective-permute-start(f32[20,512]{1,0:T(8,128)S(1)} %join.5.refs_0_), channel_id=1, source_target_pairs={{0,16},{8,24},{16,0},{24,8},{1,17},{9,25},{17,1},{25,9},{2,18},{10... | collective-permute-start | bytes 122888 | tf_op jit(solution)/shard_map/ppermute | solution.py:508
  29.5 3.4 %collective-permute-start.7 = (f32[20,512]{1,0:T(8,128)S(1)}, f32[20,512]{1,0:T(8,128)S(1)}, u32[]{:S(2)}, u32[]{:S(2)}) collective-permute-start(f32[20,512]{1,0:T(8,128)S(1)} %join.5.refs_0_), channel_id=1, source_target_pairs={{0,8},{8,0},{16,24},{24,16},{1,9},{9,1},{17,25},{25,17},{2,10},{10... | collective-permute-start | bytes 122888 | tf_op jit(solution)/shard_map/ppermute | solution.py:508
  32.5 4.6 %collective-permute-start.9 = (f32[20,512]{1,0:T(8,128)S(1)}, f32[20,512]{1,0:T(8,128)S(1)}, u32[]{:S(2)}, u32[]{:S(2)}) collective-permute-start(f32[20,512]{1,0:T(8,128)S(1)} %collective-permute-done.8.refs_2_), channel_id=1, source_target_pairs={{0,8},{8,0},{16,24},{24,16},{1,9},{9,1},{17,25},{25,17},{2,10},{10... | collective-permute-start | bytes 122888 | tf_op jit(solution)/shard_map/ppermute | solution.py:508
  32.5 15.6 %collective-permute-start.11 = (f32[2,488,128]{2,1,0:T(8,128)S(1)}, f32[2,488,128]{2,1,0:T(8,128)S(1)}, u32[]{:S(2)}, u32[]{:S(2)}) collective-permute-start(f32[2,488,128]{2,1,0:T(8,128)S(1)} %collective-permute-done.6.refs_4_), channel_id=1, source_target_pairs={{0,2},{2,4},{4,6},{3,1},{5,3},{7,5},{6,0},{1,7},{8,10},{10,12},{12... | collective-permute-start | bytes 1499144 | tf_op jit(solution)/shard_map/ppermute | solution.py:503
  37.1 18.6 %collective-permute-start.12 = (f32[2,488,128]{2,1,0:T(8,128)S(1)}, f32[2,488,128]{2,1,0:T(8,128)S(1)}, u32[]{:S(2)}, u32[]{:S(2)}) collective-permute-start(f32[2,488,128]{2,1,0:T(8,128)S(1)} %collective-permute-done.10.refs_5_), channel_id=1, source_target_pairs={{0,2},{2,4},{4,6},{3,1},{5,3},{7,5},{1,0},{6,7},{8,10},{10,12},{12... | collective-permute-start | bytes 1499144 | tf_op jit(solution)/shard_map/ppermute | solution.py:516

commit v9 on v8

--- a/solution.py
+++ b/solution.py
@@ -499,8 +499,6 @@
             share, *grid[part] = lax.optimization_barrier((share, *grid[part]))
             near.append(lax.ppermute(jnp.stack(grid[part]), "sub", swap))
         step *= 2
-    share, near[0] = lax.optimization_barrier((share, near[0]))
-    far.append(lax.ppermute(near[0], "sub", around))
     observed = {0: share}
     step = blocks // 2
     while step:
@@ -511,10 +509,10 @@
     pairs = []
     for b in range(batches):
         part = range(b, b + 1)
-        if b == 0:
-            *observed, near[1] = lax.optimization_barrier((*observed, near[1]))
-            far.append(lax.ppermute(near[1], "sub", across))
-        if b == 2:
+        if b < 2:
+            *observed, near[b] = lax.optimization_barrier((*observed, near[b]))
+            far.append(lax.ppermute(near[b], "sub", (around, across)[b]))
+        if b == 3:
             *observed, far[0] = lax.optimization_barrier((*observed, far[0]))
         outs = call(
             chain_kernel(part, batches, nobs, len(observed)),

time: 62.2 us -> 58.4 us (0.939)
  waiting for transfers between devices: 19.8 us -> 15.7 us
    ppermute x2, waiting for transfers between devices: 8.12 us -> 2.81 us  [shards(): near.append(lax.ppermute(jnp.stack(grid[part]), 'sub', swap))]
    ppermute x3, waiting for transfers between devices: 2.95 us -> 3.8 us  [shards(): lax.ppermute(x, 'mem', to)]
  transfers between devices with their start and end apart: 13 -> 13, of which waited for: 8 -> 8; matrix products, arithmetic and copies ran while one was open for 0% -> 0% of each run, Pallas kernels for 31% -> 33%
where the time goes in v9:
time: 58.4 us; the launch traced here: 58.2 us
  Pallas kernels  25.8 us (44%)
  waiting for transfers between devices  15.7 us (27%)
  starting transfers between devices  14.7 us (25%)
  local copies, waits for them, and re-layouts  1.85 us (3%)
    pallas_call x11, Pallas kernels, call(): pl.pallas_call(kernel, in_specs=specs, out_specs=[pl.BlockSpec(memory_spa...  25.8 us
    ppermute x3, waiting for transfers between devices, shards(): other = lax.ppermute(share, 'sub', [(i, i ^ step) for i in range(bands)])  5.8 us
    ppermute x3, starting transfers between devices, shards(): other = lax.ppermute(share, 'sub', [(i, i ^ step) for i in range(bands)])  5.79 us
    ppermute x3, waiting for transfers between devices, shards(): lax.ppermute(x, 'mem', to)  3.8 us
    ppermute x3, starting transfers between devices, shards(): lax.ppermute(sends[k], 'mem', [(i, i ^ k) for i in range(blocks)])  3.15 us
    ppermute x2, starting transfers between devices, shards(): near.append(lax.ppermute(jnp.stack(grid[part]), 'sub', swap))  3.15 us
    ppermute x2, waiting for transfers between devices, shards(): far.append(lax.ppermute(near[b], 'sub', (around, across)[b]))  3.06 us
    ppermute x2, waiting for transfers between devices, shards(): near.append(lax.ppermute(jnp.stack(grid[part]), 'sub', swap))  2.81 us
  transfers between devices with their start and end apart: 13, of which 8 were waited for; matrix products, arithmetic and copies ran while one was open for 0% of the time, Pallas kernels for 33%

profile of v9, /device:TPU:0, one launch (start us, length us, event | category | flops | bytes accessed | tf_op | source)
XLA Modules:
  0.0 58.2 jit_solution(12278901629736007700)
XLA Ops:
  0.0 1.2 %copy-done = f32[20,1,24,512]{3,2,1,0:T(8,128)S(1)} copy-done((f32[20,1,24,512]{3,2,1,0:T(8,128)S(1)}, f32[20,1,24,512]{3,2,1,0:T(8,128)}, u32[]{:S(2)}) %copy-start) | copy-done | bytes 983064
  1.2 0.7 %send.1 = (f32[488,128]{1,0:T(8,128)S(1)}, f32[488,128]{1,0:T(8,128)S(1)}, f32[488,128]{1,0:T(8,128)S(1)}, f32[488,128]{1,0:T(8,128)S(1)}) custom-call(f32[480,512]{1,0:T(8,128)S(1)} %bitcast.9), custom_call_target="tpu_custom_call" | custom-call | tf_op jit(solution)/shard_map/send/pallas_call | solution.py:38
  2.4 2.6 %collective-permute-start.3 = (f32[488,128]{1,0:T(8,128)S(1)}, f32[488,128]{1,0:T(8,128)S(1)}, u32[]{:S(2)}, u32[]{:S(2)}) collective-permute-start(f32[488,128]{1,0:T(8,128)S(1)} %get-tuple-element.43), channel_id=1, source_target_pairs={{0,16},{8,24},{16,0},{24,8},{1,17},{9,25},{17,1},{25,9},{2,18},{10... | collective-permute-start | bytes 749576 | tf_op jit(solution)/shard_map/ppermute | solution.py:460
  5.0 0.6 %copy-done.5 = f32[1,512]{1,0:T(1,128)S(1)} copy-done((f32[1,512]{1,0:T(1,128)S(1)}, f32[1,512]{1,0:T(1,128)}, u32[]{:S(2)}) %copy-start.5) | copy-done | bytes 2072
  5.7 2.4 %share.1.mine_ref = f32[24,512]{1,0:T(8,128)S(1)} custom-call(f32[480,512]{1,0:T(8,128)S(1)} %bitcast.10, f32[1,512]{1,0:T(1,128)S(1)} %copy-done.4, f32[1,512]{1,0:T(1,128)S(1)} %copy-done.5, f32[1,512]{1,0:T(1,128)S(1)} %copy-done.6, s32[4,128]{1,0:T(4,128)S(1)} %copy-done.7, f32[4,24,128]{2,1,0:T(8,128)S(1)} %bitcast.15), custom_call_target="tpu_custom_call" | custom-call | tf_op jit(solution)/shard_map/share/pallas_call | solution.py:38
  8.1 1.6 %collective-permute-start = (f32[24,512]{1,0:T(8,128)S(1)}, f32[24,512]{1,0:T(8,128)S(1)}, u32[]{:S(2)}, u32[]{:S(2)}) collective-permute-start(f32[24,512]{1,0:T(8,128)S(1)} %share.1.mine_ref), channel_id=1, source_target_pairs={{0,1},{1,0},{2,3},{3,2},{4,5},{5,4},{6,7},{7,6},{8,9},{9,8},{10,11... | collective-permute-start | bytes 147464 | tf_op jit(solution)/shard_map/ppermute | solution.py:487
  9.7 1.1 %tapers.1 = (f32[6,128,128]{2,1,0:T(8,128)S(1)}, f32[4,128,128]{2,1,0:T(8,128)S(1)}) custom-call(s32[4,128]{1,0:T(4,128)S(1)} %copy-done.7, f32[4,128]{1,0:T(4,128)S(1)} %copy-done.8), custom_call_target="tpu_custom_call" | custom-call | tf_op jit(solution)/shard_map/tapers/pallas_call | solution.py:38
  10.8 1.5 %collective-permute-done.other_ref = f32[24,512]{1,0:T(8,128)S(1)} collective-permute-done((f32[24,512]{1,0:T(8,128)S(1)}, f32[24,512]{1,0:T(8,128)S(1)}, u32[]{:S(2)}, u32[]{:S(2)}) %collective-permute-start) | collective-permute-done | bytes 49184 | tf_op jit(solution)/shard_map/ppermute | solution.py:487
  12.3 1.6 %collective-permute-start.2 = (f32[24,512]{1,0:T(8,128)S(1)}, f32[24,512]{1,0:T(8,128)S(1)}, u32[]{:S(2)}, u32[]{:S(2)}) collective-permute-start(f32[24,512]{1,0:T(8,128)S(1)} %join.3.mine_ref), channel_id=1, source_target_pairs={{0,2},{1,3},{2,0},{3,1},{4,6},{5,7},{6,4},{7,5},{8,10},{9,11},{10,... | collective-permute-start | bytes 147464 | tf_op jit(solution)/shard_map/ppermute | solution.py:487
  14.0 1.5 %collective-permute-start.9 = (f32[2,488,128]{2,1,0:T(8,128)S(1)}, f32[2,488,128]{2,1,0:T(8,128)S(1)}, u32[]{:S(2)}, u32[]{:S(2)}) collective-permute-start(f32[2,488,128]{2,1,0:T(8,128)S(1)} %pad_maximum_fusion), channel_id=1, source_target_pairs={{0,1},{1,0},{2,3},{3,2},{4,5},{5,4},{6,7},{7,6},{8,9},{9,8},{10,11... | collective-permute-start | bytes 1499144 | tf_op jit(solution)/shard_map/ppermute | solution.py:500
  15.5 0.9 %collective-permute-done.2.other_ref = f32[24,512]{1,0:T(8,128)S(1)} collective-permute-done((f32[24,512]{1,0:T(8,128)S(1)}, f32[24,512]{1,0:T(8,128)S(1)}, u32[]{:S(2)}, u32[]{:S(2)}) %collective-permute-start.2) | collective-permute-done | bytes 49184 | tf_op jit(solution)/shard_map/ppermute | solution.py:487
  16.8 1.6 %collective-permute-start.10 = (f32[2,488,128]{2,1,0:T(8,128)S(1)}, f32[2,488,128]{2,1,0:T(8,128)S(1)}, u32[]{:S(2)}, u32[]{:S(2)}) collective-permute-start(f32[2,488,128]{2,1,0:T(8,128)S(1)} %pad_maximum_fusion.1), channel_id=1, source_target_pairs={{0,1},{1,0},{2,3},{3,2},{4,5},{5,4},{6,7},{7,6},{8,9},{9,8},{10,11... | collective-permute-start | bytes 1499144 | tf_op jit(solution)/shard_map/ppermute | solution.py:500
  18.4 2.6 %collective-permute-start.5 = (f32[24,512]{1,0:T(8,128)S(1)}, f32[24,512]{1,0:T(8,128)S(1)}, u32[]{:S(2)}, u32[]{:S(2)}) collective-permute-start(f32[24,512]{1,0:T(8,128)S(1)} %join.4.mine_ref), channel_id=1, source_target_pairs={{0,4},{1,5},{2,6},{3,7},{4,0},{5,1},{6,2},{7,3},{8,12},{9,13},{10,... | collective-permute-start | bytes 147464 | tf_op jit(solution)/shard_map/ppermute | solution.py:487
  21.0 3.5 %collective-permute-done.5.other_ref = f32[24,512]{1,0:T(8,128)S(1)} collective-permute-done((f32[24,512]{1,0:T(8,128)S(1)}, f32[24,512]{1,0:T(8,128)S(1)}, u32[]{:S(2)}, u32[]{:S(2)}) %collective-permute-start.5) | collective-permute-done | bytes 49184 | tf_op jit(solution)/shard_map/ppermute | solution.py:487
  24.4 1.6 %collective-permute-start.7 = (f32[20,512]{1,0:T(8,128)S(1)}, f32[20,512]{1,0:T(8,128)S(1)}, u32[]{:S(2)}, u32[]{:S(2)}) collective-permute-start(f32[20,512]{1,0:T(8,128)S(1)} %join.5.refs_0_), channel_id=1, source_target_pairs={{0,16},{8,24},{16,0},{24,8},{1,17},{9,25},{17,1},{25,9},{2,18},{10... | collective-permute-start | bytes 122888 | tf_op jit(solution)/shard_map/ppermute | solution.py:506
  26.0 2.6 %collective-permute-done.7.refs_2_ = f32[20,512]{1,0:T(8,128)S(1)} collective-permute-done((f32[20,512]{1,0:T(8,128)S(1)}, f32[20,512]{1,0:T(8,128)S(1)}, u32[]{:S(2)}, u32[]{:S(2)}) %collective-permute-start.7) | collective-permute-done | bytes 40992 | tf_op jit(solution)/shard_map/ppermute | solution.py:506
  28.6 1.2 %collective-permute-done.8.refs_3_ = f32[20,512]{1,0:T(8,128)S(1)} collective-permute-done((f32[20,512]{1,0:T(8,128)S(1)}, f32[20,512]{1,0:T(8,128)S(1)}, u32[]{:S(2)}, u32[]{:S(2)}) %collective-permute-start.8) | collective-permute-done | bytes 40992 | tf_op jit(solution)/shard_map/ppermute | solution.py:506
  30.3 3.9 %chain.4 = (f32[1,80,128]{2,1,0:T(8,128)S(1)}, f32[1,80,128]{2,1,0:T(8,128)S(1)}, f32[80,384]{1,0:T(8,128)S(1)}) custom-call(f32[20,512]{1,0:T(8,128)S(1)} %join.5.refs_0_, f32[20,512]{1,0:T(8,128)S(1)} %collective-permute-done.6.refs_1_, f32[20,512]{1,0:T(8,128)S(1)} %collective-permute-done.7.refs_2_, f32[20,512]{1,0:T(8,128)S(1)} %collective-permute-done.8.refs_3_, ...), custom_call_target="tpu_custom_call" | custom-call | tf_op jit(solution)/shard_map/chain/pallas_call | solution.py:38
  34.3 2.8 %collective-permute-done.10.refs_5_ = f32[2,488,128]{2,1,0:T(8,128)S(1)} collective-permute-done((f32[2,488,128]{2,1,0:T(8,128)S(1)}, f32[2,488,128]{2,1,0:T(8,128)S(1)}, u32[]{:S(2)}, u32[]{:S(2)}) %collective-permute-start.10) | collective-permute-done | bytes 499744 | tf_op jit(solution)/shard_map/ppermute | solution.py:500
  37.5 3.9 %chain.5 = (f32[1,80,128]{2,1,0:T(8,128)S(1)}, f32[1,80,128]{2,1,0:T(8,128)S(1)}, f32[80,256]{1,0:T(8,128)S(1)}) custom-call(f32[80,384]{1,0:T(8,128)S(1)} %get-tuple-element.63.refs_0_, f32[4,128]{1,0:T(4,128)S(1)} %copy-done.2, f32[4,128]{1,0:T(4,128)S(1)} %copy-done.3, f32[6,128,128]{2,1,0:T(8,128)S(1)} %get-tuple-element.60.refs_6_.refs_3_), custom_call_target="tpu_custom_call" | custom-call | tf_op jit(solution)/shard_map/chain/pallas_call | solution.py:38
  41.4 3.9 %chain.6 = (f32[1,80,128]{2,1,0:T(8,128)S(1)}, f32[1,80,128]{2,1,0:T(8,128)S(1)}, f32[80,128]{1,0:T(8,128)S(1)}) custom-call(f32[80,256]{1,0:T(8,128)S(1)} %get-tuple-element.64.refs_0_, f32[4,128]{1,0:T(4,128)S(1)} %copy-done.2, f32[4,128]{1,0:T(4,128)S(1)} %copy-done.3, f32[6,128,128]{2,1,0:T(8,128)S(1)} %get-tuple-element.60.refs_6_.refs_3_), custom_call_target="tpu_custom_call" | custom-call | tf_op jit(solution)/shard_map/chain/pallas_call | solution.py:38
  45.3 3.7 %chain.7 = (f32[1,80,128]{2,1,0:T(8,128)S(1)}, f32[1,80,128]{2,1,0:T(8,128)S(1)}) custom-call(f32[80,128]{1,0:T(8,128)S(1)} %get-tuple-element.74.refs_0_, f32[4,128]{1,0:T(4,128)S(1)} %copy-done.2, f32[4,128]{1,0:T(4,128)S(1)} %copy-done.3, f32[6,128,128]{2,1,0:T(8,128)S(1)} %get-tuple-element.60.refs_6_.refs_3_), custom_call_target="tpu_custom_call" | custom-call | tf_op jit(solution)/shard_map/chain/pallas_call | solution.py:38
  49.0 3.1 %collective-permute-done.12.refs_7_ = f32[2,488,128]{2,1,0:T(8,128)S(1)} collective-permute-done((f32[2,488,128]{2,1,0:T(8,128)S(1)}, f32[2,488,128]{2,1,0:T(8,128)S(1)}, u32[]{:S(2)}, u32[]{:S(2)}) %collective-permute-start.12) | collective-permute-done | bytes 499744 | tf_op jit(solution)/shard_map/ppermute | solution.py:514
  52.0 6.2 %update.1 = f32[1920,128]{1,0:T(8,128)} custom-call(f32[488,128]{1,0:T(8,128)S(1)} %get-tuple-element.49.refs_0_, f32[488,128]{1,0:T(8,128)S(1)} %collective-permute-done.1.refs_1_, f32[488,128]{1,0:T(8,128)S(1)} %collective-permute-done.3.refs_2_, f32[488,128]{1,0:T(8,128)S(1)} %collective-permute-done.4.refs_3_, ...), custom_call_target="tpu_custom_call" | custom-call | tf_op jit(solution)/shard_map/update/pallas_call | solution.py:38
  (33 shorter events, 2.0 us)
Async XLA Ops:
  0.0 1.2 %copy-start = (f32[20,1,24,512]{3,2,1,0:T(8,128)S(1)}, f32[20,1,24,512]{3,2,1,0:T(8,128)}, u32[]{:S(2)}) copy-start(f32[20,1,24,512]{3,2,1,0:T(8,128)} %param.9) | copy-start | bytes 2949124
  1.2 3.8 %copy-start.1 = (f32[4,128,24]{1,2,0:T(8,128)S(1)}, f32[4,128,24]{1,2,0:T(8,128)}, u32[]{:S(2)}) copy-start(f32[4,128,24]{1,2,0:T(8,128)} %param.16) | copy-start | bytes 147460
  1.2 3.8 %copy-start.6 = (f32[1,512]{1,0:T(1,128)S(1)}, f32[1,512]{1,0:T(1,128)}, u32[]{:S(2)}) copy-start(f32[1,512]{1,0:T(1,128)} %refs_10_.1) | copy-start | bytes 6148
  1.2 3.8 %copy-start.7 = (s32[4,128]{1,0:T(4,128)S(1)}, s32[4,128]{1,0:T(4,128)}, u32[]{:S(2)}) copy-start(s32[4,128]{1,0:T(4,128)} %cell_ref.1) | copy-start | bytes 6148
  1.9 10.4 %collective-permute-start.1 = (f32[488,128]{1,0:T(8,128)S(1)}, f32[488,128]{1,0:T(8,128)S(1)}, u32[]{:S(2)}, u32[]{:S(2)}) collective-permute-start(f32[488,128]{1,0:T(8,128)S(1)} %get-tuple-element.42), channel_id=1, source_target_pairs={{0,8},{8,0},{16,24},{24,16},{1,9},{9,1},{17,25},{25,17},{2,10},{10... | collective-permute-start | bytes 749576 | tf_op jit(solution)/shard_map/ppermute | solution.py:460
  2.4 14.1 %collective-permute-start.3 = (f32[488,128]{1,0:T(8,128)S(1)}, f32[488,128]{1,0:T(8,128)S(1)}, u32[]{:S(2)}, u32[]{:S(2)}) collective-permute-start(f32[488,128]{1,0:T(8,128)S(1)} %get-tuple-element.43), channel_id=1, source_target_pairs={{0,16},{8,24},{16,0},{24,8},{1,17},{9,25},{17,1},{25,9},{2,18},{10... | collective-permute-start | bytes 749576 | tf_op jit(solution)/shard_map/ppermute | solution.py:460
  5.0 0.7 %copy-start.5 = (f32[1,512]{1,0:T(1,128)S(1)}, f32[1,512]{1,0:T(1,128)}, u32[]{:S(2)}) copy-start(f32[1,512]{1,0:T(1,128)} %refs_9_.1) | copy-start | bytes 6148
  5.0 0.7 %copy-start.4 = (f32[1,512]{1,0:T(1,128)S(1)}, f32[1,512]{1,0:T(1,128)}, u32[]{:S(2)}) copy-start(f32[1,512]{1,0:T(1,128)} %refs_8_.1) | copy-start | bytes 6148
  5.0 11.7 %collective-permute-start.4 = (f32[488,128]{1,0:T(8,128)S(1)}, f32[488,128]{1,0:T(8,128)S(1)}, u32[]{:S(2)}, u32[]{:S(2)}) collective-permute-start(f32[488,128]{1,0:T(8,128)S(1)} %get-tuple-element.44), channel_id=1, source_target_pairs={{0,24},{8,16},{16,8},{24,0},{1,25},{9,17},{17,9},{25,1},{2,26},{10... | collective-permute-start | bytes 749576 | tf_op jit(solution)/shard_map/ppermute | solution.py:460
  5.7 4.0 %copy-start.8 = (f32[4,128]{1,0:T(4,128)S(1)}, f32[4,128]{1,0:T(4,128)}, u32[]{:S(2)}) copy-start(f32[4,128]{1,0:T(4,128)} %radius_ref.1) | copy-start | bytes 6148
  8.1 4.2 %collective-permute-start = (f32[24,512]{1,0:T(8,128)S(1)}, f32[24,512]{1,0:T(8,128)S(1)}, u32[]{:S(2)}, u32[]{:S(2)}) collective-permute-start(f32[24,512]{1,0:T(8,128)S(1)} %share.1.mine_ref), channel_id=1, source_target_pairs={{0,1},{1,0},{2,3},{3,2},{4,5},{5,4},{6,7},{7,6},{8,9},{9,8},{10,11... | collective-permute-start | bytes 147464 | tf_op jit(solution)/shard_map/ppermute | solution.py:487
  12.3 4.2 %collective-permute-start.2 = (f32[24,512]{1,0:T(8,128)S(1)}, f32[24,512]{1,0:T(8,128)S(1)}, u32[]{:S(2)}, u32[]{:S(2)}) collective-permute-start(f32[24,512]{1,0:T(8,128)S(1)} %join.3.mine_ref), channel_id=1, source_target_pairs={{0,2},{1,3},{2,0},{3,1},{4,6},{5,7},{6,4},{7,5},{8,10},{9,11},{10,... | collective-permute-start | bytes 147464 | tf_op jit(solution)/shard_map/ppermute | solution.py:487
  14.0 15.8 %collective-permute-start.9 = (f32[2,488,128]{2,1,0:T(8,128)S(1)}, f32[2,488,128]{2,1,0:T(8,128)S(1)}, u32[]{:S(2)}, u32[]{:S(2)}) collective-permute-start(f32[2,488,128]{2,1,0:T(8,128)S(1)} %pad_maximum_fusion), channel_id=1, source_target_pairs={{0,1},{1,0},{2,3},{3,2},{4,5},{5,4},{6,7},{7,6},{8,9},{9,8},{10,11... | collective-permute-start | bytes 1499144 | tf_op jit(solution)/shard_map/ppermute | solution.py:500
  16.7 13.6 %copy-start.2 = (f32[4,128]{1,0:T(4,128)S(1)}, f32[4,128]{1,0:T(4,128)}, u32[]{:S(2)}) copy-start(f32[4,128]{1,0:T(4,128)} %refs_1_.6) | copy-start | bytes 6148
  16.8 13.6 %copy-start.3 = (f32[4,128]{1,0:T(4,128)S(1)}, f32[4,128]{1,0:T(4,128)}, u32[]{:S(2)}) copy-start(f32[4,128]{1,0:T(4,128)} %refs_2_.7) | copy-start | bytes 6148
  16.8 20.3 %collective-permute-start.10 = (f32[2,488,128]{2,1,0:T(8,128)S(1)}, f32[2,488,128]{2,1,0:T(8,128)S(1)}, u32[]{:S(2)}, u32[]{:S(2)}) collective-permute-start(f32[2,488,128]{2,1,0:T(8,128)S(1)} %pad_maximum_fusion.1), channel_id=1, source_target_pairs={{0,1},{1,0},{2,3},{3,2},{4,5},{5,4},{6,7},{7,6},{8,9},{9,8},{10,11... | collective-permute-start | bytes 1499144 | tf_op jit(solution)/shard_map/ppermute | solution.py:500
  18.4 6.0 %collective-permute-start.5 = (f32[24,512]{1,0:T(8,128)S(1)}, f32[24,512]{1,0:T(8,128)S(1)}, u32[]{:S(2)}, u32[]{:S(2)}) collective-permute-start(f32[24,512]{1,0:T(8,128)S(1)} %join.4.mine_ref), channel_id=1, source_target_pairs={{0,4},{1,5},{2,6},{3,7},{4,0},{5,1},{6,2},{7,3},{8,12},{9,13},{10,... | collective-permute-start | bytes 147464 | tf_op jit(solution)/shard_map/ppermute | solution.py:487
  24.4 4.2 %collective-permute-start.7 = (f32[20,512]{1,0:T(8,128)S(1)}, f32[20,512]{1,0:T(8,128)S(1)}, u32[]{:S(2)}, u32[]{:S(2)}) collective-permute-start(f32[20,512]{1,0:T(8,128)S(1)} %join.5.refs_0_), channel_id=1, source_target_pairs={{0,16},{8,24},{16,0},{24,8},{1,17},{9,25},{17,1},{25,9},{2,18},{10... | collective-permute-start | bytes 122888 | tf_op jit(solution)/shard_map/ppermute | solution.py:506
  26.0 2.6 %collective-permute-start.6 = (f32[20,512]{1,0:T(8,128)S(1)}, f32[20,512]{1,0:T(8,128)S(1)}, u32[]{:S(2)}, u32[]{:S(2)}) collective-permute-start(f32[20,512]{1,0:T(8,128)S(1)} %join.5.refs_0_), channel_id=1, source_target_pairs={{0,8},{8,0},{16,24},{24,16},{1,9},{9,1},{17,25},{25,17},{2,10},{10... | collective-permute-start | bytes 122888 | tf_op jit(solution)/shard_map/ppermute | solution.py:506
  28.6 1.2 %collective-permute-start.8 = (f32[20,512]{1,0:T(8,128)S(1)}, f32[20,512]{1,0:T(8,128)S(1)}, u32[]{:S(2)}, u32[]{:S(2)}) collective-permute-start(f32[20,512]{1,0:T(8,128)S(1)} %collective-permute-done.7.refs_2_), channel_id=1, source_target_pairs={{0,8},{8,0},{16,24},{24,16},{1,9},{9,1},{17,25},{25,17},{2,10},{10... | collective-permute-start | bytes 122888 | tf_op jit(solution)/shard_map/ppermute | solution.py:506
  29.8 15.5 %collective-permute-start.11 = (f32[2,488,128]{2,1,0:T(8,128)S(1)}, f32[2,488,128]{2,1,0:T(8,128)S(1)}, u32[]{:S(2)}, u32[]{:S(2)}) collective-permute-start(f32[2,488,128]{2,1,0:T(8,128)S(1)} %collective-permute-done.9.refs_4_), channel_id=1, source_target_pairs={{0,2},{2,4},{4,6},{3,1},{5,3},{7,5},{6,0},{1,7},{8,10},{10,12},{12... | collective-permute-start | bytes 1499144 | tf_op jit(solution)/shard_map/ppermute | solution.py:514
  37.1 14.9 %collective-permute-start.12 = (f32[2,488,128]{2,1,0:T(8,128)S(1)}, f32[2,488,128]{2,1,0:T(8,128)S(1)}, u32[]{:S(2)}, u32[]{:S(2)}) collective-permute-start(f32[2,488,128]{2,1,0:T(8,128)S(1)} %collective-permute-done.10.refs_5_), channel_id=1, source_target_pairs={{0,2},{2,4},{4,6},{3,1},{5,3},{7,5},{1,0},{6,7},{8,10},{10,12},{12... | collective-permute-start | bytes 1499144 | tf_op jit(solution)/shard_map/ppermute | solution.py:514

commit v10 on v9

--- a/solution.py
+++ b/solution.py
@@ -357,40 +357,35 @@
     return kernel
 
 
-def update_kernel(width, comps, batches, members, cols_dev, count, blocks, bands, group):
-    def kernel(
-        *refs,
-    ):
-        own_refs, halos, refs = refs[:blocks], refs[blocks : blocks + 4], refs[blocks + 4 :]
-        near_refs, far_refs = (
-            [ref.at[i] for ref in halos[at : at + 2] for i in range(ref.shape[0])] for at in (0, 2)
-        )
-        cx_ref, cy_ref, d_ref, taper_ref, *pair_refs, out_ref, grid_ref = refs
-        pairs = [
-            (pair_refs[i][k], pair_refs[i + 1][k])
-            for i in range(0, len(pair_refs), 2)
-            for k in range(pair_refs[i].shape[0])
-        ]
+def halo_scales(cy, bands):
+    band = jnp.full(cy.shape, lax.axis_index("sub"), jnp.int32)
+    even = band & 1 == 0
+    from_south, from_north = jnp.maximum(cy, 0.0), -jnp.minimum(cy, 0.0)
+    from_near = jnp.where(even, from_north, from_south)
+    from_far = jnp.where(even, from_south, from_north)
+    return from_near, from_far, (band == 0) | (band == bands - 1)
+
+
+def forecast_kernel(cols_dev, count, blocks, bands):
+    def kernel(*refs):
+        own_refs, halos, refs = refs[:blocks], refs[blocks : blocks + 3], refs[blocks + 3 :]
+        near_refs = [ref.at[i] for ref in halos[:2] for i in range(ref.shape[0])]
+        far_refs = [halos[2].at[i] for i in range(halos[2].shape[0])]
+        cx_ref, cy_ref, d_ref, grid_ref = refs
         start = pl.multiple_of(lax.axis_index("mem") * cols_dev, cols_dev)
         cx = cx_ref[:, pl.ds(start, cols_dev)]
         cy = cy_ref[:, pl.ds(start, cols_dev)]
         d = d_ref[:, pl.ds(start, cols_dev)]
         lane = lax.broadcasted_iota(jnp.int32, (1, cols_dev), 1)
-        band = jnp.full((1, cols_dev), lax.axis_index("sub"), jnp.int32)
-        even = band & 1 == 0
-        outermost = (band == 0) | (band == bands - 1)
-        from_south, from_north = jnp.maximum(cy, 0.0), -jnp.minimum(cy, 0.0)
-        from_near = jnp.where(even, from_north, from_south)
-        from_far = jnp.where(even, from_south, from_north)
+        from_near, from_far, outermost = halo_scales(cy, bands)
         from_west, from_east = jnp.maximum(cx, 0.0), -jnp.minimum(cx, 0.0)
-        for s, (own_ref, near_ref, far_ref) in enumerate(zip(own_refs, near_refs, far_refs)):
+        for s, (own_ref, near_ref) in enumerate(zip(own_refs, near_refs)):
             base = pl.multiple_of((lax.axis_index("mem") ^ s) * count, 8)
             outer = to_columns(own_ref[count:, :])
             for j in range(-(-count // 128)):
                 size = min(128, count - 128 * j)
                 at = slice(128 * j, 128 * j + size)
                 q, near = own_ref[at, :], near_ref[at, :]
-                far = jnp.where(outermost, 0.0, far_ref[at, :])
                 west = jnp.where(lane == 0, outer[:size, 2 * j : 2 * j + 1], pltpu.roll(q, 1, 1))
                 east = jnp.where(
                     lane == cols_dev - 1,
@@ -398,9 +393,34 @@
                     pltpu.roll(q, cols_dev - 1, 1),
                 )
                 x = q - from_west * (q - west) - from_east * (q - east)
-                x = x - from_near * (q - near) - from_far * (q - far)
-                x = x + d * (east + west + near + far - 4.0 * q)
+                if s < len(far_refs):
+                    far = jnp.where(outermost, 0.0, far_refs[s][at, :])
+                    x = x - from_near * (q - near) - from_far * (q - far)
+                    x = x + d * (east + west + near + far - 4.0 * q)
+                else:
+                    x = x - from_near * (q - near) - from_far * q
+                    x = x + d * (east + west + near - 4.0 * q)
                 grid_ref[pl.ds(base + 128 * j, size), :] = x
+
+    return kernel
+
+
+def update_kernel(comps, batches, members, cols_dev, count, bands, group):
+    def kernel(cells_ref, far_ref, cy_ref, d_ref, taper_ref, *refs):
+        *pair_refs, out_ref, grid_ref = refs
+        pairs = [
+            (pair_refs[i][k], pair_refs[i + 1][k])
+            for i in range(0, len(pair_refs), 2)
+            for k in range(pair_refs[i].shape[0])
+        ]
+        start = pl.multiple_of(lax.axis_index("mem") * cols_dev, cols_dev)
+        _, from_far, outermost = halo_scales(cy_ref[:, pl.ds(start, cols_dev)], bands)
+        scale = jnp.where(outermost, 0.0, from_far + d_ref[:, pl.ds(start, cols_dev)])
+        late = far_ref.shape[0]
+        for s in range(2 * late):
+            at = pl.ds(pl.multiple_of((lax.axis_index("mem") ^ s) * count, 8), count)
+            cells = cells_ref[at, :]
+            grid_ref[at, :] = cells if s < late else cells + scale * far_ref[s - late, :count, :]
         left, right, tapers = [], [], []
         nobs = taper_ref.shape[1]
         fill = -3 * members % 128
@@ -523,11 +543,17 @@
         )
         pairs += outs[:2]
         observed = outs[2:]
+    (cells,) = call(
+        forecast_kernel(cols_dev, count, blocks, bands),
+        [(members * comps, cols_dev)],
+        "forecast",
+        (*grid, *near, far[0], courant_x, courant_y, diffusion),
+    )
     (out,) = call(
-        update_kernel(width, comps, batches, members, cols_dev, count, blocks, bands, comps),
+        update_kernel(comps, batches, members, cols_dev, count, bands, comps),
         [(members * comps, cols_dev)],
         "update",
-        (*grid, *near, *far, courant_x, courant_y, diffusion, cell_taper, *pairs),
+        (cells, far[1], courant_y, diffusion, cell_taper, *pairs),
         (pltpu.VMEM((members * comps, cols_dev), f32),),
     )
     return out.reshape(members, rows_dev, comps, cols_dev)

time: 58.4 us -> 56.8 us (0.973)
  waiting for transfers between devices: 15.7 us -> 14.1 us
    ppermute x2, waiting for transfers between devices: 3.06 us -> 1.5 us  [shards(): far.append(lax.ppermute(near[b], 'sub', (around, across)[b]))]
    pallas_call x11 -> x12, Pallas kernels: 25.8 us -> 25.8 us  [call(): pl.pallas_call(kernel, in_specs=specs, out_specs=[pl.BlockSpec(memory_spa...]
  transfers between devices with their start and end apart: 13 -> 13, of which waited for: 8 -> 8; matrix products, arithmetic and copies ran while one was open for 0% -> 0% of each run, Pallas kernels for 33% -> 36%
where the time goes in v10:
time: 56.8 us; the launch traced here: 56.7 us
  Pallas kernels  25.8 us (45%)
  starting transfers between devices  14.7 us (26%)
  waiting for transfers between devices  14.1 us (25%)
  local copies, waits for them, and re-layouts  1.85 us (3%)
    pallas_call x12, Pallas kernels, call(): pl.pallas_call(kernel, in_specs=specs, out_specs=[pl.BlockSpec(memory_spa...  25.8 us
    ppermute x3, waiting for transfers between devices, shards(): other = lax.ppermute(share, 'sub', [(i, i ^ step) for i in range(bands)])  5.8 us
    ppermute x3, starting transfers between devices, shards(): other = lax.ppermute(share, 'sub', [(i, i ^ step) for i in range(bands)])  5.79 us
    ppermute x3, waiting for transfers between devices, shards(): lax.ppermute(x, 'mem', to)  3.8 us
    ppermute x3, starting transfers between devices, shards(): lax.ppermute(sends[k], 'mem', [(i, i ^ k) for i in range(blocks)])  3.15 us
    ppermute x2, starting transfers between devices, shards(): near.append(lax.ppermute(jnp.stack(grid[part]), 'sub', swap))  3.15 us
    ppermute x2, waiting for transfers between devices, shards(): near.append(lax.ppermute(jnp.stack(grid[part]), 'sub', swap))  2.81 us
    unnamed x18, local copies, waits for them, and re-layouts  1.85 us
  transfers between devices with their start and end apart: 13, of which 8 were waited for; matrix products, arithmetic and copies ran while one was open for 0% of the time, Pallas kernels for 36%

profile of v10, /device:TPU:0, one launch (start us, length us, event | category | flops | bytes accessed | tf_op | source)
XLA Modules:
  0.0 56.7 jit_solution(7829666977482586490)
XLA Ops:
  0.0 1.2 %copy-done = f32[20,1,24,512]{3,2,1,0:T(8,128)S(1)} copy-done((f32[20,1,24,512]{3,2,1,0:T(8,128)S(1)}, f32[20,1,24,512]{3,2,1,0:T(8,128)}, u32[]{:S(2)}) %copy-start) | copy-done | bytes 983064
  1.2 0.7 %send.1 = (f32[488,128]{1,0:T(8,128)S(1)}, f32[488,128]{1,0:T(8,128)S(1)}, f32[488,128]{1,0:T(8,128)S(1)}, f32[488,128]{1,0:T(8,128)S(1)}) custom-call(f32[480,512]{1,0:T(8,128)S(1)} %bitcast.9), custom_call_target="tpu_custom_call" | custom-call | tf_op jit(solution)/shard_map/send/pallas_call | solution.py:38
  2.4 2.6 %collective-permute-start.3 = (f32[488,128]{1,0:T(8,128)S(1)}, f32[488,128]{1,0:T(8,128)S(1)}, u32[]{:S(2)}, u32[]{:S(2)}) collective-permute-start(f32[488,128]{1,0:T(8,128)S(1)} %get-tuple-element.43), channel_id=1, source_target_pairs={{0,16},{8,24},{16,0},{24,8},{1,17},{9,25},{17,1},{25,9},{2,18},{10... | collective-permute-start | bytes 749576 | tf_op jit(solution)/shard_map/ppermute | solution.py:480
  5.7 2.4 %share.1.mine_ref = f32[24,512]{1,0:T(8,128)S(1)} custom-call(f32[480,512]{1,0:T(8,128)S(1)} %bitcast.10, f32[1,512]{1,0:T(1,128)S(1)} %copy-done.6, f32[1,512]{1,0:T(1,128)S(1)} %copy-done.4, f32[1,512]{1,0:T(1,128)S(1)} %copy-done.5, s32[4,128]{1,0:T(4,128)S(1)} %copy-done.7, f32[4,24,128]{2,1,0:T(8,128)S(1)} %bitcast.15), custom_call_target="tpu_custom_call" | custom-call | tf_op jit(solution)/shard_map/share/pallas_call | solution.py:38
  8.1 1.6 %collective-permute-start = (f32[24,512]{1,0:T(8,128)S(1)}, f32[24,512]{1,0:T(8,128)S(1)}, u32[]{:S(2)}, u32[]{:S(2)}) collective-permute-start(f32[24,512]{1,0:T(8,128)S(1)} %share.1.mine_ref), channel_id=1, source_target_pairs={{0,1},{1,0},{2,3},{3,2},{4,5},{5,4},{6,7},{7,6},{8,9},{9,8},{10,11... | collective-permute-start | bytes 147464 | tf_op jit(solution)/shard_map/ppermute | solution.py:507
  9.7 1.1 %tapers.1 = (f32[6,128,128]{2,1,0:T(8,128)S(1)}, f32[4,128,128]{2,1,0:T(8,128)S(1)}) custom-call(s32[4,128]{1,0:T(4,128)S(1)} %copy-done.7, f32[4,128]{1,0:T(4,128)S(1)} %copy-done.8), custom_call_target="tpu_custom_call" | custom-call | tf_op jit(solution)/shard_map/tapers/pallas_call | solution.py:38
  10.8 1.5 %collective-permute-done.other_ref = f32[24,512]{1,0:T(8,128)S(1)} collective-permute-done((f32[24,512]{1,0:T(8,128)S(1)}, f32[24,512]{1,0:T(8,128)S(1)}, u32[]{:S(2)}, u32[]{:S(2)}) %collective-permute-start) | collective-permute-done | bytes 49184 | tf_op jit(solution)/shard_map/ppermute | solution.py:507
  12.3 1.6 %collective-permute-start.2 = (f32[24,512]{1,0:T(8,128)S(1)}, f32[24,512]{1,0:T(8,128)S(1)}, u32[]{:S(2)}, u32[]{:S(2)}) collective-permute-start(f32[24,512]{1,0:T(8,128)S(1)} %join.3.mine_ref), channel_id=1, source_target_pairs={{0,2},{1,3},{2,0},{3,1},{4,6},{5,7},{6,4},{7,5},{8,10},{9,11},{10,... | collective-permute-start | bytes 147464 | tf_op jit(solution)/shard_map/ppermute | solution.py:507
  14.0 1.5 %collective-permute-start.9 = (f32[2,488,128]{2,1,0:T(8,128)S(1)}, f32[2,488,128]{2,1,0:T(8,128)S(1)}, u32[]{:S(2)}, u32[]{:S(2)}) collective-permute-start(f32[2,488,128]{2,1,0:T(8,128)S(1)} %pad_maximum_fusion), channel_id=1, source_target_pairs={{0,1},{1,0},{2,3},{3,2},{4,5},{5,4},{6,7},{7,6},{8,9},{9,8},{10,11... | collective-permute-start | bytes 1499144 | tf_op jit(solution)/shard_map/ppermute | solution.py:520
  15.5 0.9 %collective-permute-done.2.other_ref = f32[24,512]{1,0:T(8,128)S(1)} collective-permute-done((f32[24,512]{1,0:T(8,128)S(1)}, f32[24,512]{1,0:T(8,128)S(1)}, u32[]{:S(2)}, u32[]{:S(2)}) %collective-permute-start.2) | collective-permute-done | bytes 49184 | tf_op jit(solution)/shard_map/ppermute | solution.py:507
  16.8 1.6 %collective-permute-start.10 = (f32[2,488,128]{2,1,0:T(8,128)S(1)}, f32[2,488,128]{2,1,0:T(8,128)S(1)}, u32[]{:S(2)}, u32[]{:S(2)}) collective-permute-start(f32[2,488,128]{2,1,0:T(8,128)S(1)} %pad_maximum_fusion.1), channel_id=1, source_target_pairs={{0,1},{1,0},{2,3},{3,2},{4,5},{5,4},{6,7},{7,6},{8,9},{9,8},{10,11... | collective-permute-start | bytes 1499144 | tf_op jit(solution)/shard_map/ppermute | solution.py:520
  18.4 2.6 %collective-permute-start.5 = (f32[24,512]{1,0:T(8,128)S(1)}, f32[24,512]{1,0:T(8,128)S(1)}, u32[]{:S(2)}, u32[]{:S(2)}) collective-permute-start(f32[24,512]{1,0:T(8,128)S(1)} %join.4.mine_ref), channel_id=1, source_target_pairs={{0,4},{1,5},{2,6},{3,7},{4,0},{5,1},{6,2},{7,3},{8,12},{9,13},{10,... | collective-permute-start | bytes 147464 | tf_op jit(solution)/shard_map/ppermute | solution.py:507
  21.0 3.5 %collective-permute-done.5.other_ref = f32[24,512]{1,0:T(8,128)S(1)} collective-permute-done((f32[24,512]{1,0:T(8,128)S(1)}, f32[24,512]{1,0:T(8,128)S(1)}, u32[]{:S(2)}, u32[]{:S(2)}) %collective-permute-start.5) | collective-permute-done | bytes 49184 | tf_op jit(solution)/shard_map/ppermute | solution.py:507
  24.4 1.6 %collective-permute-start.7 = (f32[20,512]{1,0:T(8,128)S(1)}, f32[20,512]{1,0:T(8,128)S(1)}, u32[]{:S(2)}, u32[]{:S(2)}) collective-permute-start(f32[20,512]{1,0:T(8,128)S(1)} %join.5.refs_0_), channel_id=1, source_target_pairs={{0,16},{8,24},{16,0},{24,8},{1,17},{9,25},{17,1},{25,9},{2,18},{10... | collective-permute-start | bytes 122888 | tf_op jit(solution)/shard_map/ppermute | solution.py:526
  26.0 2.6 %collective-permute-done.7.refs_2_ = f32[20,512]{1,0:T(8,128)S(1)} collective-permute-done((f32[20,512]{1,0:T(8,128)S(1)}, f32[20,512]{1,0:T(8,128)S(1)}, u32[]{:S(2)}, u32[]{:S(2)}) %collective-permute-start.7) | collective-permute-done | bytes 40992 | tf_op jit(solution)/shard_map/ppermute | solution.py:526
  28.6 1.2 %collective-permute-done.8.refs_3_ = f32[20,512]{1,0:T(8,128)S(1)} collective-permute-done((f32[20,512]{1,0:T(8,128)S(1)}, f32[20,512]{1,0:T(8,128)S(1)}, u32[]{:S(2)}, u32[]{:S(2)}) %collective-permute-start.8) | collective-permute-done | bytes 40992 | tf_op jit(solution)/shard_map/ppermute | solution.py:526
  30.3 3.9 %chain.4 = (f32[1,80,128]{2,1,0:T(8,128)S(1)}, f32[1,80,128]{2,1,0:T(8,128)S(1)}, f32[80,384]{1,0:T(8,128)S(1)}) custom-call(f32[20,512]{1,0:T(8,128)S(1)} %join.5.refs_0_, f32[20,512]{1,0:T(8,128)S(1)} %collective-permute-done.6.refs_1_, f32[20,512]{1,0:T(8,128)S(1)} %collective-permute-done.7.refs_2_, f32[20,512]{1,0:T(8,128)S(1)} %collective-permute-done.8.refs_3_, ...), custom_call_target="tpu_custom_call" | custom-call | tf_op jit(solution)/shard_map/chain/pallas_call | solution.py:38
  34.3 2.8 %collective-permute-done.10.refs_5_ = f32[2,488,128]{2,1,0:T(8,128)S(1)} collective-permute-done((f32[2,488,128]{2,1,0:T(8,128)S(1)}, f32[2,488,128]{2,1,0:T(8,128)S(1)}, u32[]{:S(2)}, u32[]{:S(2)}) %collective-permute-start.10) | collective-permute-done | bytes 499744 | tf_op jit(solution)/shard_map/ppermute | solution.py:520
  37.5 3.9 %chain.5 = (f32[1,80,128]{2,1,0:T(8,128)S(1)}, f32[1,80,128]{2,1,0:T(8,128)S(1)}, f32[80,256]{1,0:T(8,128)S(1)}) custom-call(f32[80,384]{1,0:T(8,128)S(1)} %get-tuple-element.63.refs_0_, f32[4,128]{1,0:T(4,128)S(1)} %copy-done.2, f32[4,128]{1,0:T(4,128)S(1)} %copy-done.3, f32[6,128,128]{2,1,0:T(8,128)S(1)} %get-tuple-element.60.refs_6_.refs_3_), custom_call_target="tpu_custom_call" | custom-call | tf_op jit(solution)/shard_map/chain/pallas_call | solution.py:38
  41.4 3.9 %chain.6 = (f32[1,80,128]{2,1,0:T(8,128)S(1)}, f32[1,80,128]{2,1,0:T(8,128)S(1)}, f32[80,128]{1,0:T(8,128)S(1)}) custom-call(f32[80,256]{1,0:T(8,128)S(1)} %get-tuple-element.64.refs_0_, f32[4,128]{1,0:T(4,128)S(1)} %copy-done.2, f32[4,128]{1,0:T(4,128)S(1)} %copy-done.3, f32[6,128,128]{2,1,0:T(8,128)S(1)} %get-tuple-element.60.refs_6_.refs_3_), custom_call_target="tpu_custom_call" | custom-call | tf_op jit(solution)/shard_map/chain/pallas_call | solution.py:38
  45.3 3.7 %chain.7 = (f32[1,80,128]{2,1,0:T(8,128)S(1)}, f32[1,80,128]{2,1,0:T(8,128)S(1)}) custom-call(f32[80,128]{1,0:T(8,128)S(1)} %get-tuple-element.74.refs_0_, f32[4,128]{1,0:T(4,128)S(1)} %copy-done.2, f32[4,128]{1,0:T(4,128)S(1)} %copy-done.3, f32[6,128,128]{2,1,0:T(8,128)S(1)} %get-tuple-element.60.refs_6_.refs_3_), custom_call_target="tpu_custom_call" | custom-call | tf_op jit(solution)/shard_map/chain/pallas_call | solution.py:38
  49.0 1.6 %forecast.1.cells_ref = f32[1920,128]{1,0:T(8,128)S(1)} custom-call(f32[488,128]{1,0:T(8,128)S(1)} %get-tuple-element.49.refs_0_, f32[488,128]{1,0:T(8,128)S(1)} %collective-permute-done.1.refs_1_, f32[488,128]{1,0:T(8,128)S(1)} %collective-permute-done.3.refs_2_, f32[488,128]{1,0:T(8,128)S(1)} %collective-permute-done.4.refs_3_, ...), custom_call_target="tpu_custom_call" | custom-call | tf_op jit(solution)/shard_map/forecast/pallas_call | solution.py:38
  50.5 1.5 %collective-permute-done.12.far_ref = f32[2,488,128]{2,1,0:T(8,128)S(1)} collective-permute-done((f32[2,488,128]{2,1,0:T(8,128)S(1)}, f32[2,488,128]{2,1,0:T(8,128)S(1)}, u32[]{:S(2)}, u32[]{:S(2)}) %collective-permute-start.12) | collective-permute-done | bytes 499744 | tf_op jit(solution)/shard_map/ppermute | solution.py:534
  52.0 4.6 %update.1 = f32[1920,128]{1,0:T(8,128)} custom-call(f32[1920,128]{1,0:T(8,128)S(1)} %forecast.1.cells_ref, f32[2,488,128]{2,1,0:T(8,128)S(1)} %collective-permute-done.12.far_ref, f32[1,512]{1,0:T(1,128)S(1)} %copy-done.4, f32[1,512]{1,0:T(1,128)S(1)} %copy-done.5, f32[4,128,128]{2,1,0:T(8,128)S(1)} %get-tuple-element.67.taper_ref, ...), custom_call_target="tpu_custom_call" | custom-call | tf_op jit(solution)/shard_map/update/pallas_call | solution.py:38
  (34 shorter events, 2.6 us)
Async XLA Ops:
  0.0 1.2 %copy-start = (f32[20,1,24,512]{3,2,1,0:T(8,128)S(1)}, f32[20,1,24,512]{3,2,1,0:T(8,128)}, u32[]{:S(2)}) copy-start(f32[20,1,24,512]{3,2,1,0:T(8,128)} %param.9) | copy-start | bytes 2949124
  1.2 3.8 %copy-start.1 = (f32[4,128,24]{1,2,0:T(8,128)S(1)}, f32[4,128,24]{1,2,0:T(8,128)}, u32[]{:S(2)}) copy-start(f32[4,128,24]{1,2,0:T(8,128)} %param.16) | copy-start | bytes 147460
  1.2 3.8 %copy-start.6 = (f32[1,512]{1,0:T(1,128)S(1)}, f32[1,512]{1,0:T(1,128)}, u32[]{:S(2)}) copy-start(f32[1,512]{1,0:T(1,128)} %refs_7_.1) | copy-start | bytes 6148
  1.2 3.8 %copy-start.7 = (s32[4,128]{1,0:T(4,128)S(1)}, s32[4,128]{1,0:T(4,128)}, u32[]{:S(2)}) copy-start(s32[4,128]{1,0:T(4,128)} %cell_ref.1) | copy-start | bytes 6148
  1.9 10.4 %collective-permute-start.1 = (f32[488,128]{1,0:T(8,128)S(1)}, f32[488,128]{1,0:T(8,128)S(1)}, u32[]{:S(2)}, u32[]{:S(2)}) collective-permute-start(f32[488,128]{1,0:T(8,128)S(1)} %get-tuple-element.42), channel_id=1, source_target_pairs={{0,8},{8,0},{16,24},{24,16},{1,9},{9,1},{17,25},{25,17},{2,10},{10... | collective-permute-start | bytes 749576 | tf_op jit(solution)/shard_map/ppermute | solution.py:480
  2.4 14.1 %collective-permute-start.3 = (f32[488,128]{1,0:T(8,128)S(1)}, f32[488,128]{1,0:T(8,128)S(1)}, u32[]{:S(2)}, u32[]{:S(2)}) collective-permute-start(f32[488,128]{1,0:T(8,128)S(1)} %get-tuple-element.43), channel_id=1, source_target_pairs={{0,16},{8,24},{16,0},{24,8},{1,17},{9,25},{17,1},{25,9},{2,18},{10... | collective-permute-start | bytes 749576 | tf_op jit(solution)/shard_map/ppermute | solution.py:480
  5.0 0.7 %copy-start.5 = (f32[1,512]{1,0:T(1,128)S(1)}, f32[1,512]{1,0:T(1,128)}, u32[]{:S(2)}) copy-start(f32[1,512]{1,0:T(1,128)} %d_ref.1) | copy-start | bytes 6148
  5.0 0.7 %copy-start.4 = (f32[1,512]{1,0:T(1,128)S(1)}, f32[1,512]{1,0:T(1,128)}, u32[]{:S(2)}) copy-start(f32[1,512]{1,0:T(1,128)} %cy_ref.1) | copy-start | bytes 6148
  5.0 11.7 %collective-permute-start.4 = (f32[488,128]{1,0:T(8,128)S(1)}, f32[488,128]{1,0:T(8,128)S(1)}, u32[]{:S(2)}, u32[]{:S(2)}) collective-permute-start(f32[488,128]{1,0:T(8,128)S(1)} %get-tuple-element.44), channel_id=1, source_target_pairs={{0,24},{8,16},{16,8},{24,0},{1,25},{9,17},{17,9},{25,1},{2,26},{10... | collective-permute-start | bytes 749576 | tf_op jit(solution)/shard_map/ppermute | solution.py:480
  5.7 4.0 %copy-start.8 = (f32[4,128]{1,0:T(4,128)S(1)}, f32[4,128]{1,0:T(4,128)}, u32[]{:S(2)}) copy-start(f32[4,128]{1,0:T(4,128)} %radius_ref.1) | copy-start | bytes 6148
  8.1 4.2 %collective-permute-start = (f32[24,512]{1,0:T(8,128)S(1)}, f32[24,512]{1,0:T(8,128)S(1)}, u32[]{:S(2)}, u32[]{:S(2)}) collective-permute-start(f32[24,512]{1,0:T(8,128)S(1)} %share.1.mine_ref), channel_id=1, source_target_pairs={{0,1},{1,0},{2,3},{3,2},{4,5},{5,4},{6,7},{7,6},{8,9},{9,8},{10,11... | collective-permute-start | bytes 147464 | tf_op jit(solution)/shard_map/ppermute | solution.py:507
  12.3 4.2 %collective-permute-start.2 = (f32[24,512]{1,0:T(8,128)S(1)}, f32[24,512]{1,0:T(8,128)S(1)}, u32[]{:S(2)}, u32[]{:S(2)}) collective-permute-start(f32[24,512]{1,0:T(8,128)S(1)} %join.3.mine_ref), channel_id=1, source_target_pairs={{0,2},{1,3},{2,0},{3,1},{4,6},{5,7},{6,4},{7,5},{8,10},{9,11},{10,... | collective-permute-start | bytes 147464 | tf_op jit(solution)/shard_map/ppermute | solution.py:507
  14.0 15.8 %collective-permute-start.9 = (f32[2,488,128]{2,1,0:T(8,128)S(1)}, f32[2,488,128]{2,1,0:T(8,128)S(1)}, u32[]{:S(2)}, u32[]{:S(2)}) collective-permute-start(f32[2,488,128]{2,1,0:T(8,128)S(1)} %pad_maximum_fusion), channel_id=1, source_target_pairs={{0,1},{1,0},{2,3},{3,2},{4,5},{5,4},{6,7},{7,6},{8,9},{9,8},{10,11... | collective-permute-start | bytes 1499144 | tf_op jit(solution)/shard_map/ppermute | solution.py:520
  16.7 13.6 %copy-start.2 = (f32[4,128]{1,0:T(4,128)S(1)}, f32[4,128]{1,0:T(4,128)}, u32[]{:S(2)}) copy-start(f32[4,128]{1,0:T(4,128)} %refs_1_.6) | copy-start | bytes 6148
  16.8 13.6 %copy-start.3 = (f32[4,128]{1,0:T(4,128)S(1)}, f32[4,128]{1,0:T(4,128)}, u32[]{:S(2)}) copy-start(f32[4,128]{1,0:T(4,128)} %refs_2_.7) | copy-start | bytes 6148
  16.8 20.3 %collective-permute-start.10 = (f32[2,488,128]{2,1,0:T(8,128)S(1)}, f32[2,488,128]{2,1,0:T(8,128)S(1)}, u32[]{:S(2)}, u32[]{:S(2)}) collective-permute-start(f32[2,488,128]{2,1,0:T(8,128)S(1)} %pad_maximum_fusion.1), channel_id=1, source_target_pairs={{0,1},{1,0},{2,3},{3,2},{4,5},{5,4},{6,7},{7,6},{8,9},{9,8},{10,11... | collective-permute-start | bytes 1499144 | tf_op jit(solution)/shard_map/ppermute | solution.py:520
  18.4 6.0 %collective-permute-start.5 = (f32[24,512]{1,0:T(8,128)S(1)}, f32[24,512]{1,0:T(8,128)S(1)}, u32[]{:S(2)}, u32[]{:S(2)}) collective-permute-start(f32[24,512]{1,0:T(8,128)S(1)} %join.4.mine_ref), channel_id=1, source_target_pairs={{0,4},{1,5},{2,6},{3,7},{4,0},{5,1},{6,2},{7,3},{8,12},{9,13},{10,... | collective-permute-start | bytes 147464 | tf_op jit(solution)/shard_map/ppermute | solution.py:507
  24.4 4.2 %collective-permute-start.7 = (f32[20,512]{1,0:T(8,128)S(1)}, f32[20,512]{1,0:T(8,128)S(1)}, u32[]{:S(2)}, u32[]{:S(2)}) collective-permute-start(f32[20,512]{1,0:T(8,128)S(1)} %join.5.refs_0_), channel_id=1, source_target_pairs={{0,16},{8,24},{16,0},{24,8},{1,17},{9,25},{17,1},{25,9},{2,18},{10... | collective-permute-start | bytes 122888 | tf_op jit(solution)/shard_map/ppermute | solution.py:526
  26.0 2.6 %collective-permute-start.6 = (f32[20,512]{1,0:T(8,128)S(1)}, f32[20,512]{1,0:T(8,128)S(1)}, u32[]{:S(2)}, u32[]{:S(2)}) collective-permute-start(f32[20,512]{1,0:T(8,128)S(1)} %join.5.refs_0_), channel_id=1, source_target_pairs={{0,8},{8,0},{16,24},{24,16},{1,9},{9,1},{17,25},{25,17},{2,10},{10... | collective-permute-start | bytes 122888 | tf_op jit(solution)/shard_map/ppermute | solution.py:526
  28.6 1.2 %collective-permute-start.8 = (f32[20,512]{1,0:T(8,128)S(1)}, f32[20,512]{1,0:T(8,128)S(1)}, u32[]{:S(2)}, u32[]{:S(2)}) collective-permute-start(f32[20,512]{1,0:T(8,128)S(1)} %collective-permute-done.7.refs_2_), channel_id=1, source_target_pairs={{0,8},{8,0},{16,24},{24,16},{1,9},{9,1},{17,25},{25,17},{2,10},{10... | collective-permute-start | bytes 122888 | tf_op jit(solution)/shard_map/ppermute | solution.py:526
  29.8 15.5 %collective-permute-start.11 = (f32[2,488,128]{2,1,0:T(8,128)S(1)}, f32[2,488,128]{2,1,0:T(8,128)S(1)}, u32[]{:S(2)}, u32[]{:S(2)}) collective-permute-start(f32[2,488,128]{2,1,0:T(8,128)S(1)} %collective-permute-done.9.refs_4_), channel_id=1, source_target_pairs={{0,2},{2,4},{4,6},{3,1},{5,3},{7,5},{6,0},{1,7},{8,10},{10,12},{12... | collective-permute-start | bytes 1499144 | tf_op jit(solution)/shard_map/ppermute | solution.py:534
  37.1 14.9 %collective-permute-start.12 = (f32[2,488,128]{2,1,0:T(8,128)S(1)}, f32[2,488,128]{2,1,0:T(8,128)S(1)}, u32[]{:S(2)}, u32[]{:S(2)}) collective-permute-start(f32[2,488,128]{2,1,0:T(8,128)S(1)} %collective-permute-done.10.refs_5_), channel_id=1, source_target_pairs={{0,2},{2,4},{4,6},{3,1},{5,3},{7,5},{1,0},{6,7},{8,10},{10,12},{12... | collective-permute-start | bytes 1499144 | tf_op jit(solution)/shard_map/ppermute | solution.py:534

commit v11 on v10

--- a/solution.py
+++ b/solution.py
@@ -497,7 +497,6 @@
     )
     swap = [(i, i ^ 1) for i in range(bands)]
     onward = [(i, i + 2) for i in range(0, bands - 2, 2)] + [(i, i - 2) for i in range(3, bands, 2)]
-    around = onward + [(bands - 2, 0), (1, bands - 1)]
     across = onward + [(1, 0), (bands - 2, bands - 1)]
     middle = blocks // 2
     parts = (slice(0, middle), slice(middle, blocks))
@@ -531,7 +530,7 @@
         part = range(b, b + 1)
         if b < 2:
             *observed, near[b] = lax.optimization_barrier((*observed, near[b]))
-            far.append(lax.ppermute(near[b], "sub", (around, across)[b]))
+            far.append(lax.ppermute(near[b], "sub", (onward, across)[b]))
         if b == 3:
             *observed, far[0] = lax.optimization_barrier((*observed, far[0]))
         outs = call(

time: 56.8 us -> 58.7 us (1.033)
  starting transfers between devices: 14.7 us -> 17.1 us
    ppermute x2, starting transfers between devices: 0.98 us -> 3.39 us  [shards(): far.append(lax.ppermute(near[b], 'sub', (onward, across)[b]))]
    ppermute x2, waiting for transfers between devices: 2.81 us -> 0.86 us  [shards(): near.append(lax.ppermute(jnp.stack(grid[part]), 'sub', swap))]
    ppermute x2, waiting for transfers between devices: 1.5 us -> 2.89 us  [shards(): far.append(lax.ppermute(near[b], 'sub', (onward, across)[b]))]
  transfers between devices with their start and end apart: 13 -> 13, of which waited for: 8 -> 8; matrix products, arithmetic and copies ran while one was open for 0% -> 0% of each run, Pallas kernels for 36% -> 35%
where the time goes in v11:
time: 58.7 us; the launch traced here: 58.5 us
  Pallas kernels  25.8 us (44%)
  starting transfers between devices  17.1 us (29%)
  waiting for transfers between devices  13.6 us (23%)
  local copies, waits for them, and re-layouts  1.85 us (3%)
    pallas_call x12, Pallas kernels, call(): pl.pallas_call(kernel, in_specs=specs, out_specs=[pl.BlockSpec(memory_spa...  25.8 us
    ppermute x3, waiting for transfers between devices, shards(): other = lax.ppermute(share, 'sub', [(i, i ^ step) for i in range(bands)])  5.8 us
    ppermute x3, starting transfers between devices, shards(): other = lax.ppermute(share, 'sub', [(i, i ^ step) for i in range(bands)])  5.79 us
    ppermute x3, waiting for transfers between devices, shards(): lax.ppermute(x, 'mem', to)  3.8 us
    ppermute x2, starting transfers between devices, shards(): far.append(lax.ppermute(near[b], 'sub', (onward, across)[b]))  3.39 us
    ppermute x3, starting transfers between devices, shards(): lax.ppermute(sends[k], 'mem', [(i, i ^ k) for i in range(blocks)])  3.15 us
    ppermute x2, starting transfers between devices, shards(): near.append(lax.ppermute(jnp.stack(grid[part]), 'sub', swap))  3.15 us
    ppermute x2, waiting for transfers between devices, shards(): far.append(lax.ppermute(near[b], 'sub', (onward, across)[b]))  2.89 us
  transfers between devices with their start and end apart: 13, of which 8 were waited for; matrix products, arithmetic and copies ran while one was open for 0% of the time, Pallas kernels for 35%

profile of v11, /device:TPU:0, one launch (start us, length us, event | category | flops | bytes accessed | tf_op | source)
XLA Modules:
  0.0 58.5 jit_solution(14882918285156678750)
XLA Ops:
  0.0 1.2 %copy-done = f32[20,1,24,512]{3,2,1,0:T(8,128)S(1)} copy-done((f32[20,1,24,512]{3,2,1,0:T(8,128)S(1)}, f32[20,1,24,512]{3,2,1,0:T(8,128)}, u32[]{:S(2)}) %copy-start) | copy-done | bytes 983064
  2.4 2.6 %collective-permute-start.3 = (f32[488,128]{1,0:T(8,128)S(1)}, f32[488,128]{1,0:T(8,128)S(1)}, u32[]{:S(2)}, u32[]{:S(2)}) collective-permute-start(f32[488,128]{1,0:T(8,128)S(1)} %get-tuple-element.43), channel_id=1, source_target_pairs={{0,16},{8,24},{16,0},{24,8},{1,17},{9,25},{17,1},{25,9},{2,18},{10... | collective-permute-start | bytes 749576 | tf_op jit(solution)/shard_map/ppermute | solution.py:480
  5.7 2.4 %share.1.mine_ref = f32[24,512]{1,0:T(8,128)S(1)} custom-call(f32[480,512]{1,0:T(8,128)S(1)} %bitcast.10, f32[1,512]{1,0:T(1,128)S(1)} %copy-done.6, f32[1,512]{1,0:T(1,128)S(1)} %copy-done.4, f32[1,512]{1,0:T(1,128)S(1)} %copy-done.5, s32[4,128]{1,0:T(4,128)S(1)} %copy-done.7, f32[4,24,128]{2,1,0:T(8,128)S(1)} %bitcast.15), custom_call_target="tpu_custom_call" | custom-call | tf_op jit(solution)/shard_map/share/pallas_call | solution.py:38
  8.1 1.6 %collective-permute-start = (f32[24,512]{1,0:T(8,128)S(1)}, f32[24,512]{1,0:T(8,128)S(1)}, u32[]{:S(2)}, u32[]{:S(2)}) collective-permute-start(f32[24,512]{1,0:T(8,128)S(1)} %share.1.mine_ref), channel_id=1, source_target_pairs={{0,1},{1,0},{2,3},{3,2},{4,5},{5,4},{6,7},{7,6},{8,9},{9,8},{10,11... | collective-permute-start | bytes 147464 | tf_op jit(solution)/shard_map/ppermute | solution.py:506
  9.7 1.1 %tapers.1 = (f32[6,128,128]{2,1,0:T(8,128)S(1)}, f32[4,128,128]{2,1,0:T(8,128)S(1)}) custom-call(s32[4,128]{1,0:T(4,128)S(1)} %copy-done.7, f32[4,128]{1,0:T(4,128)S(1)} %copy-done.8), custom_call_target="tpu_custom_call" | custom-call | tf_op jit(solution)/shard_map/tapers/pallas_call | solution.py:38
  10.8 1.5 %collective-permute-done.other_ref = f32[24,512]{1,0:T(8,128)S(1)} collective-permute-done((f32[24,512]{1,0:T(8,128)S(1)}, f32[24,512]{1,0:T(8,128)S(1)}, u32[]{:S(2)}, u32[]{:S(2)}) %collective-permute-start) | collective-permute-done | bytes 49184 | tf_op jit(solution)/shard_map/ppermute | solution.py:506
  12.3 1.6 %collective-permute-start.2 = (f32[24,512]{1,0:T(8,128)S(1)}, f32[24,512]{1,0:T(8,128)S(1)}, u32[]{:S(2)}, u32[]{:S(2)}) collective-permute-start(f32[24,512]{1,0:T(8,128)S(1)} %join.3.mine_ref), channel_id=1, source_target_pairs={{0,2},{1,3},{2,0},{3,1},{4,6},{5,7},{6,4},{7,5},{8,10},{9,11},{10,... | collective-permute-start | bytes 147464 | tf_op jit(solution)/shard_map/ppermute | solution.py:506
  14.0 1.5 %collective-permute-start.9 = (f32[2,488,128]{2,1,0:T(8,128)S(1)}, f32[2,488,128]{2,1,0:T(8,128)S(1)}, u32[]{:S(2)}, u32[]{:S(2)}) collective-permute-start(f32[2,488,128]{2,1,0:T(8,128)S(1)} %pad_maximum_fusion), channel_id=1, source_target_pairs={{0,1},{1,0},{2,3},{3,2},{4,5},{5,4},{6,7},{7,6},{8,9},{9,8},{10,11... | collective-permute-start | bytes 1499144 | tf_op jit(solution)/shard_map/ppermute | solution.py:519
  15.5 0.9 %collective-permute-done.2.other_ref = f32[24,512]{1,0:T(8,128)S(1)} collective-permute-done((f32[24,512]{1,0:T(8,128)S(1)}, f32[24,512]{1,0:T(8,128)S(1)}, u32[]{:S(2)}, u32[]{:S(2)}) %collective-permute-start.2) | collective-permute-done | bytes 49184 | tf_op jit(solution)/shard_map/ppermute | solution.py:506
  16.8 1.6 %collective-permute-start.10 = (f32[2,488,128]{2,1,0:T(8,128)S(1)}, f32[2,488,128]{2,1,0:T(8,128)S(1)}, u32[]{:S(2)}, u32[]{:S(2)}) collective-permute-start(f32[2,488,128]{2,1,0:T(8,128)S(1)} %pad_maximum_fusion.1), channel_id=1, source_target_pairs={{0,1},{1,0},{2,3},{3,2},{4,5},{5,4},{6,7},{7,6},{8,9},{9,8},{10,11... | collective-permute-start | bytes 1499144 | tf_op jit(solution)/shard_map/ppermute | solution.py:519
  18.4 2.6 %collective-permute-start.5 = (f32[24,512]{1,0:T(8,128)S(1)}, f32[24,512]{1,0:T(8,128)S(1)}, u32[]{:S(2)}, u32[]{:S(2)}) collective-permute-start(f32[24,512]{1,0:T(8,128)S(1)} %join.4.mine_ref), channel_id=1, source_target_pairs={{0,4},{1,5},{2,6},{3,7},{4,0},{5,1},{6,2},{7,3},{8,12},{9,13},{10,... | collective-permute-start | bytes 147464 | tf_op jit(solution)/shard_map/ppermute | solution.py:506
  21.0 3.5 %collective-permute-done.5.other_ref = f32[24,512]{1,0:T(8,128)S(1)} collective-permute-done((f32[24,512]{1,0:T(8,128)S(1)}, f32[24,512]{1,0:T(8,128)S(1)}, u32[]{:S(2)}, u32[]{:S(2)}) %collective-permute-start.5) | collective-permute-done | bytes 49184 | tf_op jit(solution)/shard_map/ppermute | solution.py:506
  24.4 1.6 %collective-permute-start.7 = (f32[20,512]{1,0:T(8,128)S(1)}, f32[20,512]{1,0:T(8,128)S(1)}, u32[]{:S(2)}, u32[]{:S(2)}) collective-permute-start(f32[20,512]{1,0:T(8,128)S(1)} %join.5.refs_0_), channel_id=1, source_target_pairs={{0,16},{8,24},{16,0},{24,8},{1,17},{9,25},{17,1},{25,9},{2,18},{10... | collective-permute-start | bytes 122888 | tf_op jit(solution)/shard_map/ppermute | solution.py:525
  26.0 2.6 %collective-permute-done.7.refs_2_ = f32[20,512]{1,0:T(8,128)S(1)} collective-permute-done((f32[20,512]{1,0:T(8,128)S(1)}, f32[20,512]{1,0:T(8,128)S(1)}, u32[]{:S(2)}, u32[]{:S(2)}) %collective-permute-start.7) | collective-permute-done | bytes 40992 | tf_op jit(solution)/shard_map/ppermute | solution.py:525
  28.6 1.2 %collective-permute-done.8.refs_3_ = f32[20,512]{1,0:T(8,128)S(1)} collective-permute-done((f32[20,512]{1,0:T(8,128)S(1)}, f32[20,512]{1,0:T(8,128)S(1)}, u32[]{:S(2)}, u32[]{:S(2)}) %collective-permute-start.8) | collective-permute-done | bytes 40992 | tf_op jit(solution)/shard_map/ppermute | solution.py:525
  29.8 2.5 %collective-permute-start.11 = (f32[2,488,128]{2,1,0:T(8,128)S(1)}, f32[2,488,128]{2,1,0:T(8,128)S(1)}, u32[]{:S(2)}, u32[]{:S(2)}) collective-permute-start(f32[2,488,128]{2,1,0:T(8,128)S(1)} %collective-permute-done.9.refs_4_), channel_id=1, source_target_pairs={{0,2},{2,4},{4,6},{3,1},{5,3},{7,5},{8,10},{10,12},{12,14},{11,9},... | collective-permute-start | bytes 1499144 | tf_op jit(solution)/shard_map/ppermute | solution.py:533
  32.3 3.9 %chain.4 = (f32[1,80,128]{2,1,0:T(8,128)S(1)}, f32[1,80,128]{2,1,0:T(8,128)S(1)}, f32[80,384]{1,0:T(8,128)S(1)}) custom-call(f32[20,512]{1,0:T(8,128)S(1)} %join.5.refs_0_, f32[20,512]{1,0:T(8,128)S(1)} %collective-permute-done.6.refs_1_, f32[20,512]{1,0:T(8,128)S(1)} %collective-permute-done.7.refs_2_, f32[20,512]{1,0:T(8,128)S(1)} %collective-permute-done.8.refs_3_, ...), custom_call_target="tpu_custom_call" | custom-call | tf_op jit(solution)/shard_map/chain/pallas_call | solution.py:38
  37.1 0.9 %collective-permute-start.12 = (f32[2,488,128]{2,1,0:T(8,128)S(1)}, f32[2,488,128]{2,1,0:T(8,128)S(1)}, u32[]{:S(2)}, u32[]{:S(2)}) collective-permute-start(f32[2,488,128]{2,1,0:T(8,128)S(1)} %collective-permute-done.10.refs_5_), channel_id=1, source_target_pairs={{0,2},{2,4},{4,6},{3,1},{5,3},{7,5},{1,0},{6,7},{8,10},{10,12},{12... | collective-permute-start | bytes 1499144 | tf_op jit(solution)/shard_map/ppermute | solution.py:533
  38.0 3.9 %chain.5 = (f32[1,80,128]{2,1,0:T(8,128)S(1)}, f32[1,80,128]{2,1,0:T(8,128)S(1)}, f32[80,256]{1,0:T(8,128)S(1)}) custom-call(f32[80,384]{1,0:T(8,128)S(1)} %get-tuple-element.63.refs_0_, f32[4,128]{1,0:T(4,128)S(1)} %copy-done.2, f32[4,128]{1,0:T(4,128)S(1)} %copy-done.3, f32[6,128,128]{2,1,0:T(8,128)S(1)} %get-tuple-element.60.refs_6_.refs_3_), custom_call_target="tpu_custom_call" | custom-call | tf_op jit(solution)/shard_map/chain/pallas_call | solution.py:38
  41.9 3.9 %chain.6 = (f32[1,80,128]{2,1,0:T(8,128)S(1)}, f32[1,80,128]{2,1,0:T(8,128)S(1)}, f32[80,128]{1,0:T(8,128)S(1)}) custom-call(f32[80,256]{1,0:T(8,128)S(1)} %get-tuple-element.64.refs_0_, f32[4,128]{1,0:T(4,128)S(1)} %copy-done.2, f32[4,128]{1,0:T(4,128)S(1)} %copy-done.3, f32[6,128,128]{2,1,0:T(8,128)S(1)} %get-tuple-element.60.refs_6_.refs_3_), custom_call_target="tpu_custom_call" | custom-call | tf_op jit(solution)/shard_map/chain/pallas_call | solution.py:38
  45.8 3.7 %chain.7 = (f32[1,80,128]{2,1,0:T(8,128)S(1)}, f32[1,80,128]{2,1,0:T(8,128)S(1)}) custom-call(f32[80,128]{1,0:T(8,128)S(1)} %get-tuple-element.74.refs_0_, f32[4,128]{1,0:T(4,128)S(1)} %copy-done.2, f32[4,128]{1,0:T(4,128)S(1)} %copy-done.3, f32[6,128,128]{2,1,0:T(8,128)S(1)} %get-tuple-element.60.refs_6_.refs_3_), custom_call_target="tpu_custom_call" | custom-call | tf_op jit(solution)/shard_map/chain/pallas_call | solution.py:38
  49.5 1.6 %forecast.1.cells_ref = f32[1920,128]{1,0:T(8,128)S(1)} custom-call(f32[488,128]{1,0:T(8,128)S(1)} %get-tuple-element.49.refs_0_, f32[488,128]{1,0:T(8,128)S(1)} %collective-permute-done.1.refs_1_, f32[488,128]{1,0:T(8,128)S(1)} %collective-permute-done.3.refs_2_, f32[488,128]{1,0:T(8,128)S(1)} %collective-permute-done.4.refs_3_, ...), custom_call_target="tpu_custom_call" | custom-call | tf_op jit(solution)/shard_map/forecast/pallas_call | solution.py:38
  51.0 2.9 %collective-permute-done.12.far_ref = f32[2,488,128]{2,1,0:T(8,128)S(1)} collective-permute-done((f32[2,488,128]{2,1,0:T(8,128)S(1)}, f32[2,488,128]{2,1,0:T(8,128)S(1)}, u32[]{:S(2)}, u32[]{:S(2)}) %collective-permute-start.12) | collective-permute-done | bytes 499744 | tf_op jit(solution)/shard_map/ppermute | solution.py:533
  53.9 4.6 %update.1 = f32[1920,128]{1,0:T(8,128)} custom-call(f32[1920,128]{1,0:T(8,128)S(1)} %forecast.1.cells_ref, f32[2,488,128]{2,1,0:T(8,128)S(1)} %collective-permute-done.12.far_ref, f32[1,512]{1,0:T(1,128)S(1)} %copy-done.4, f32[1,512]{1,0:T(1,128)S(1)} %copy-done.5, f32[4,128,128]{2,1,0:T(8,128)S(1)} %get-tuple-element.67.taper_ref, ...), custom_call_target="tpu_custom_call" | custom-call | tf_op jit(solution)/shard_map/update/pallas_call | solution.py:38
  (34 shorter events, 3.1 us)
Async XLA Ops:
  0.0 1.2 %copy-start = (f32[20,1,24,512]{3,2,1,0:T(8,128)S(1)}, f32[20,1,24,512]{3,2,1,0:T(8,128)}, u32[]{:S(2)}) copy-start(f32[20,1,24,512]{3,2,1,0:T(8,128)} %param.9) | copy-start | bytes 2949124
  1.2 3.8 %copy-start.1 = (f32[4,128,24]{1,2,0:T(8,128)S(1)}, f32[4,128,24]{1,2,0:T(8,128)}, u32[]{:S(2)}) copy-start(f32[4,128,24]{1,2,0:T(8,128)} %param.16) | copy-start | bytes 147460
  1.2 3.8 %copy-start.6 = (f32[1,512]{1,0:T(1,128)S(1)}, f32[1,512]{1,0:T(1,128)}, u32[]{:S(2)}) copy-start(f32[1,512]{1,0:T(1,128)} %refs_7_.1) | copy-start | bytes 6148
  1.2 3.8 %copy-start.7 = (s32[4,128]{1,0:T(4,128)S(1)}, s32[4,128]{1,0:T(4,128)}, u32[]{:S(2)}) copy-start(s32[4,128]{1,0:T(4,128)} %cell_ref.1) | copy-start | bytes 6148
  1.9 10.4 %collective-permute-start.1 = (f32[488,128]{1,0:T(8,128)S(1)}, f32[488,128]{1,0:T(8,128)S(1)}, u32[]{:S(2)}, u32[]{:S(2)}) collective-permute-start(f32[488,128]{1,0:T(8,128)S(1)} %get-tuple-element.42), channel_id=1, source_target_pairs={{0,8},{8,0},{16,24},{24,16},{1,9},{9,1},{17,25},{25,17},{2,10},{10... | collective-permute-start | bytes 749576 | tf_op jit(solution)/shard_map/ppermute | solution.py:480
  2.4 14.1 %collective-permute-start.3 = (f32[488,128]{1,0:T(8,128)S(1)}, f32[488,128]{1,0:T(8,128)S(1)}, u32[]{:S(2)}, u32[]{:S(2)}) collective-permute-start(f32[488,128]{1,0:T(8,128)S(1)} %get-tuple-element.43), channel_id=1, source_target_pairs={{0,16},{8,24},{16,0},{24,8},{1,17},{9,25},{17,1},{25,9},{2,18},{10... | collective-permute-start | bytes 749576 | tf_op jit(solution)/shard_map/ppermute | solution.py:480
  5.0 0.7 %copy-start.5 = (f32[1,512]{1,0:T(1,128)S(1)}, f32[1,512]{1,0:T(1,128)}, u32[]{:S(2)}) copy-start(f32[1,512]{1,0:T(1,128)} %d_ref.1) | copy-start | bytes 6148
  5.0 0.7 %copy-start.4 = (f32[1,512]{1,0:T(1,128)S(1)}, f32[1,512]{1,0:T(1,128)}, u32[]{:S(2)}) copy-start(f32[1,512]{1,0:T(1,128)} %cy_ref.1) | copy-start | bytes 6148
  5.0 11.7 %collective-permute-start.4 = (f32[488,128]{1,0:T(8,128)S(1)}, f32[488,128]{1,0:T(8,128)S(1)}, u32[]{:S(2)}, u32[]{:S(2)}) collective-permute-start(f32[488,128]{1,0:T(8,128)S(1)} %get-tuple-element.44), channel_id=1, source_target_pairs={{0,24},{8,16},{16,8},{24,0},{1,25},{9,17},{17,9},{25,1},{2,26},{10... | collective-permute-start | bytes 749576 | tf_op jit(solution)/shard_map/ppermute | solution.py:480
  5.7 4.0 %copy-start.8 = (f32[4,128]{1,0:T(4,128)S(1)}, f32[4,128]{1,0:T(4,128)}, u32[]{:S(2)}) copy-start(f32[4,128]{1,0:T(4,128)} %radius_ref.1) | copy-start | bytes 6148
  8.1 4.2 %collective-permute-start = (f32[24,512]{1,0:T(8,128)S(1)}, f32[24,512]{1,0:T(8,128)S(1)}, u32[]{:S(2)}, u32[]{:S(2)}) collective-permute-start(f32[24,512]{1,0:T(8,128)S(1)} %share.1.mine_ref), channel_id=1, source_target_pairs={{0,1},{1,0},{2,3},{3,2},{4,5},{5,4},{6,7},{7,6},{8,9},{9,8},{10,11... | collective-permute-start | bytes 147464 | tf_op jit(solution)/shard_map/ppermute | solution.py:506
  12.3 4.2 %collective-permute-start.2 = (f32[24,512]{1,0:T(8,128)S(1)}, f32[24,512]{1,0:T(8,128)S(1)}, u32[]{:S(2)}, u32[]{:S(2)}) collective-permute-start(f32[24,512]{1,0:T(8,128)S(1)} %join.3.mine_ref), channel_id=1, source_target_pairs={{0,2},{1,3},{2,0},{3,1},{4,6},{5,7},{6,4},{7,5},{8,10},{9,11},{10,... | collective-permute-start | bytes 147464 | tf_op jit(solution)/shard_map/ppermute | solution.py:506
  14.0 15.8 %collective-permute-start.9 = (f32[2,488,128]{2,1,0:T(8,128)S(1)}, f32[2,488,128]{2,1,0:T(8,128)S(1)}, u32[]{:S(2)}, u32[]{:S(2)}) collective-permute-start(f32[2,488,128]{2,1,0:T(8,128)S(1)} %pad_maximum_fusion), channel_id=1, source_target_pairs={{0,1},{1,0},{2,3},{3,2},{4,5},{5,4},{6,7},{7,6},{8,9},{9,8},{10,11... | collective-permute-start | bytes 1499144 | tf_op jit(solution)/shard_map/ppermute | solution.py:519
  16.7 15.5 %copy-start.2 = (f32[4,128]{1,0:T(4,128)S(1)}, f32[4,128]{1,0:T(4,128)}, u32[]{:S(2)}) copy-start(f32[4,128]{1,0:T(4,128)} %refs_1_.6) | copy-start | bytes 6148
  16.8 15.5 %copy-start.3 = (f32[4,128]{1,0:T(4,128)S(1)}, f32[4,128]{1,0:T(4,128)}, u32[]{:S(2)}) copy-start(f32[4,128]{1,0:T(4,128)} %refs_2_.7) | copy-start | bytes 6148
  16.8 20.3 %collective-permute-start.10 = (f32[2,488,128]{2,1,0:T(8,128)S(1)}, f32[2,488,128]{2,1,0:T(8,128)S(1)}, u32[]{:S(2)}, u32[]{:S(2)}) collective-permute-start(f32[2,488,128]{2,1,0:T(8,128)S(1)} %pad_maximum_fusion.1), channel_id=1, source_target_pairs={{0,1},{1,0},{2,3},{3,2},{4,5},{5,4},{6,7},{7,6},{8,9},{9,8},{10,11... | collective-permute-start | bytes 1499144 | tf_op jit(solution)/shard_map/ppermute | solution.py:519
  18.4 6.0 %collective-permute-start.5 = (f32[24,512]{1,0:T(8,128)S(1)}, f32[24,512]{1,0:T(8,128)S(1)}, u32[]{:S(2)}, u32[]{:S(2)}) collective-permute-start(f32[24,512]{1,0:T(8,128)S(1)} %join.4.mine_ref), channel_id=1, source_target_pairs={{0,4},{1,5},{2,6},{3,7},{4,0},{5,1},{6,2},{7,3},{8,12},{9,13},{10,... | collective-permute-start | bytes 147464 | tf_op jit(solution)/shard_map/ppermute | solution.py:506
  24.4 4.2 %collective-permute-start.7 = (f32[20,512]{1,0:T(8,128)S(1)}, f32[20,512]{1,0:T(8,128)S(1)}, u32[]{:S(2)}, u32[]{:S(2)}) collective-permute-start(f32[20,512]{1,0:T(8,128)S(1)} %join.5.refs_0_), channel_id=1, source_target_pairs={{0,16},{8,24},{16,0},{24,8},{1,17},{9,25},{17,1},{25,9},{2,18},{10... | collective-permute-start | bytes 122888 | tf_op jit(solution)/shard_map/ppermute | solution.py:525
  26.0 2.6 %collective-permute-start.6 = (f32[20,512]{1,0:T(8,128)S(1)}, f32[20,512]{1,0:T(8,128)S(1)}, u32[]{:S(2)}, u32[]{:S(2)}) collective-permute-start(f32[20,512]{1,0:T(8,128)S(1)} %join.5.refs_0_), channel_id=1, source_target_pairs={{0,8},{8,0},{16,24},{24,16},{1,9},{9,1},{17,25},{25,17},{2,10},{10... | collective-permute-start | bytes 122888 | tf_op jit(solution)/shard_map/ppermute | solution.py:525
  28.6 1.2 %collective-permute-start.8 = (f32[20,512]{1,0:T(8,128)S(1)}, f32[20,512]{1,0:T(8,128)S(1)}, u32[]{:S(2)}, u32[]{:S(2)}) collective-permute-start(f32[20,512]{1,0:T(8,128)S(1)} %collective-permute-done.7.refs_2_), channel_id=1, source_target_pairs={{0,8},{8,0},{16,24},{24,16},{1,9},{9,1},{17,25},{25,17},{2,10},{10... | collective-permute-start | bytes 122888 | tf_op jit(solution)/shard_map/ppermute | solution.py:525
  29.8 15.9 %collective-permute-start.11 = (f32[2,488,128]{2,1,0:T(8,128)S(1)}, f32[2,488,128]{2,1,0:T(8,128)S(1)}, u32[]{:S(2)}, u32[]{:S(2)}) collective-permute-start(f32[2,488,128]{2,1,0:T(8,128)S(1)} %collective-permute-done.9.refs_4_), channel_id=1, source_target_pairs={{0,2},{2,4},{4,6},{3,1},{5,3},{7,5},{8,10},{10,12},{12,14},{11,9},... | collective-permute-start | bytes 1499144 | tf_op jit(solution)/shard_map/ppermute | solution.py:533
  37.1 16.8 %collective-permute-start.12 = (f32[2,488,128]{2,1,0:T(8,128)S(1)}, f32[2,488,128]{2,1,0:T(8,128)S(1)}, u32[]{:S(2)}, u32[]{:S(2)}) collective-permute-start(f32[2,488,128]{2,1,0:T(8,128)S(1)} %collective-permute-done.10.refs_5_), channel_id=1, source_target_pairs={{0,2},{2,4},{4,6},{3,1},{5,3},{7,5},{1,0},{6,7},{8,10},{10,12},{12... | collective-permute-start | bytes 1499144 | tf_op jit(solution)/shard_map/ppermute | solution.py:533

commit v12 on v10

--- a/solution.py
+++ b/solution.py
@@ -479,8 +479,8 @@
     grid = [sends[0]] + [
         lax.ppermute(sends[k], "mem", [(i, i ^ k) for i in range(blocks)]) for k in range(1, blocks)
     ]
-    held_x, *sends = lax.optimization_barrier((courant_x, *sends))
-    sources = (prior, held_x, courant_y, diffusion, obs_cell, obs_weight.transpose(0, 2, 1))
+    weight, *sends = lax.optimization_barrier((obs_weight, *sends))
+    sources = (prior, courant_x, courant_y, diffusion, obs_cell, weight.transpose(0, 2, 1))
     (share,) = call(
         share_kernel(width, comps, batches, nobs, local),
         [(share_rows, batches * nobs)],

time: 56.8 us -> 56.8 us (level)
  no operation moved by 1% of the time
where the time goes in v12:
time: 56.8 us; the launch traced here: 56.7 us
  Pallas kernels  25.8 us (45%)
  starting transfers between devices  14.7 us (26%)
  waiting for transfers between devices  14.1 us (25%)
  local copies, waits for them, and re-layouts  1.85 us (3%)
    pallas_call x12, Pallas kernels, call(): pl.pallas_call(kernel, in_specs=specs, out_specs=[pl.BlockSpec(memory_spa...  25.8 us
    ppermute x3, waiting for transfers between devices, shards(): other = lax.ppermute(share, 'sub', [(i, i ^ step) for i in range(bands)])  5.8 us
    ppermute x3, starting transfers between devices, shards(): other = lax.ppermute(share, 'sub', [(i, i ^ step) for i in range(bands)])  5.79 us
    ppermute x3, waiting for transfers between devices, shards(): lax.ppermute(x, 'mem', to)  3.8 us
    ppermute x3, starting transfers between devices, shards(): lax.ppermute(sends[k], 'mem', [(i, i ^ k) for i in range(blocks)])  3.15 us
    ppermute x2, starting transfers between devices, shards(): near.append(lax.ppermute(jnp.stack(grid[part]), 'sub', swap))  3.15 us
    ppermute x2, waiting for transfers between devices, shards(): near.append(lax.ppermute(jnp.stack(grid[part]), 'sub', swap))  2.81 us
    unnamed x18, local copies, waits for them, and re-layouts  1.85 us
  transfers between devices with their start and end apart: 13, of which 8 were waited for; matrix products, arithmetic and copies ran while one was open for 0% of the time, Pallas kernels for 36%

profile of v12, /device:TPU:0, one launch (start us, length us, event | category | flops | bytes accessed | tf_op | source)
XLA Modules:
  0.0 56.7 jit_solution(7829666977482586490)
XLA Ops:
  0.0 1.2 %copy-done = f32[20,1,24,512]{3,2,1,0:T(8,128)S(1)} copy-done((f32[20,1,24,512]{3,2,1,0:T(8,128)S(1)}, f32[20,1,24,512]{3,2,1,0:T(8,128)}, u32[]{:S(2)}) %copy-start) | copy-done | bytes 983064
  1.2 0.7 %send.1 = (f32[488,128]{1,0:T(8,128)S(1)}, f32[488,128]{1,0:T(8,128)S(1)}, f32[488,128]{1,0:T(8,128)S(1)}, f32[488,128]{1,0:T(8,128)S(1)}) custom-call(f32[480,512]{1,0:T(8,128)S(1)} %bitcast.9), custom_call_target="tpu_custom_call" | custom-call | tf_op jit(solution)/shard_map/send/pallas_call | solution.py:38
  2.4 2.6 %collective-permute-start.3 = (f32[488,128]{1,0:T(8,128)S(1)}, f32[488,128]{1,0:T(8,128)S(1)}, u32[]{:S(2)}, u32[]{:S(2)}) collective-permute-start(f32[488,128]{1,0:T(8,128)S(1)} %get-tuple-element.43), channel_id=1, source_target_pairs={{0,16},{8,24},{16,0},{24,8},{1,17},{9,25},{17,1},{25,9},{2,18},{10... | collective-permute-start | bytes 749576 | tf_op jit(solution)/shard_map/ppermute | solution.py:480
  5.7 2.4 %share.1.mine_ref = f32[24,512]{1,0:T(8,128)S(1)} custom-call(f32[480,512]{1,0:T(8,128)S(1)} %bitcast.10, f32[1,512]{1,0:T(1,128)S(1)} %copy-done.6, f32[1,512]{1,0:T(1,128)S(1)} %copy-done.4, f32[1,512]{1,0:T(1,128)S(1)} %copy-done.5, s32[4,128]{1,0:T(4,128)S(1)} %copy-done.7, f32[4,24,128]{2,1,0:T(8,128)S(1)} %bitcast.15), custom_call_target="tpu_custom_call" | custom-call | tf_op jit(solution)/shard_map/share/pallas_call | solution.py:38
  8.1 1.6 %collective-permute-start = (f32[24,512]{1,0:T(8,128)S(1)}, f32[24,512]{1,0:T(8,128)S(1)}, u32[]{:S(2)}, u32[]{:S(2)}) collective-permute-start(f32[24,512]{1,0:T(8,128)S(1)} %share.1.mine_ref), channel_id=1, source_target_pairs={{0,1},{1,0},{2,3},{3,2},{4,5},{5,4},{6,7},{7,6},{8,9},{9,8},{10,11... | collective-permute-start | bytes 147464 | tf_op jit(solution)/shard_map/ppermute | solution.py:507
  9.7 1.1 %tapers.1 = (f32[6,128,128]{2,1,0:T(8,128)S(1)}, f32[4,128,128]{2,1,0:T(8,128)S(1)}) custom-call(s32[4,128]{1,0:T(4,128)S(1)} %copy-done.7, f32[4,128]{1,0:T(4,128)S(1)} %copy-done.8), custom_call_target="tpu_custom_call" | custom-call | tf_op jit(solution)/shard_map/tapers/pallas_call | solution.py:38
  10.8 1.5 %collective-permute-done.other_ref = f32[24,512]{1,0:T(8,128)S(1)} collective-permute-done((f32[24,512]{1,0:T(8,128)S(1)}, f32[24,512]{1,0:T(8,128)S(1)}, u32[]{:S(2)}, u32[]{:S(2)}) %collective-permute-start) | collective-permute-done | bytes 49184 | tf_op jit(solution)/shard_map/ppermute | solution.py:507
  12.3 1.6 %collective-permute-start.2 = (f32[24,512]{1,0:T(8,128)S(1)}, f32[24,512]{1,0:T(8,128)S(1)}, u32[]{:S(2)}, u32[]{:S(2)}) collective-permute-start(f32[24,512]{1,0:T(8,128)S(1)} %join.3.mine_ref), channel_id=1, source_target_pairs={{0,2},{1,3},{2,0},{3,1},{4,6},{5,7},{6,4},{7,5},{8,10},{9,11},{10,... | collective-permute-start | bytes 147464 | tf_op jit(solution)/shard_map/ppermute | solution.py:507
  14.0 1.5 %collective-permute-start.9 = (f32[2,488,128]{2,1,0:T(8,128)S(1)}, f32[2,488,128]{2,1,0:T(8,128)S(1)}, u32[]{:S(2)}, u32[]{:S(2)}) collective-permute-start(f32[2,488,128]{2,1,0:T(8,128)S(1)} %pad_maximum_fusion), channel_id=1, source_target_pairs={{0,1},{1,0},{2,3},{3,2},{4,5},{5,4},{6,7},{7,6},{8,9},{9,8},{10,11... | collective-permute-start | bytes 1499144 | tf_op jit(solution)/shard_map/ppermute | solution.py:520
  15.5 0.9 %collective-permute-done.2.other_ref = f32[24,512]{1,0:T(8,128)S(1)} collective-permute-done((f32[24,512]{1,0:T(8,128)S(1)}, f32[24,512]{1,0:T(8,128)S(1)}, u32[]{:S(2)}, u32[]{:S(2)}) %collective-permute-start.2) | collective-permute-done | bytes 49184 | tf_op jit(solution)/shard_map/ppermute | solution.py:507
  16.8 1.6 %collective-permute-start.10 = (f32[2,488,128]{2,1,0:T(8,128)S(1)}, f32[2,488,128]{2,1,0:T(8,128)S(1)}, u32[]{:S(2)}, u32[]{:S(2)}) collective-permute-start(f32[2,488,128]{2,1,0:T(8,128)S(1)} %pad_maximum_fusion.1), channel_id=1, source_target_pairs={{0,1},{1,0},{2,3},{3,2},{4,5},{5,4},{6,7},{7,6},{8,9},{9,8},{10,11... | collective-permute-start | bytes 1499144 | tf_op jit(solution)/shard_map/ppermute | solution.py:520
  18.4 2.6 %collective-permute-start.5 = (f32[24,512]{1,0:T(8,128)S(1)}, f32[24,512]{1,0:T(8,128)S(1)}, u32[]{:S(2)}, u32[]{:S(2)}) collective-permute-start(f32[24,512]{1,0:T(8,128)S(1)} %join.4.mine_ref), channel_id=1, source_target_pairs={{0,4},{1,5},{2,6},{3,7},{4,0},{5,1},{6,2},{7,3},{8,12},{9,13},{10,... | collective-permute-start | bytes 147464 | tf_op jit(solution)/shard_map/ppermute | solution.py:507
  21.0 3.5 %collective-permute-done.5.other_ref = f32[24,512]{1,0:T(8,128)S(1)} collective-permute-done((f32[24,512]{1,0:T(8,128)S(1)}, f32[24,512]{1,0:T(8,128)S(1)}, u32[]{:S(2)}, u32[]{:S(2)}) %collective-permute-start.5) | collective-permute-done | bytes 49184 | tf_op jit(solution)/shard_map/ppermute | solution.py:507
  24.4 1.6 %collective-permute-start.7 = (f32[20,512]{1,0:T(8,128)S(1)}, f32[20,512]{1,0:T(8,128)S(1)}, u32[]{:S(2)}, u32[]{:S(2)}) collective-permute-start(f32[20,512]{1,0:T(8,128)S(1)} %join.5.refs_0_), channel_id=1, source_target_pairs={{0,16},{8,24},{16,0},{24,8},{1,17},{9,25},{17,1},{25,9},{2,18},{10... | collective-permute-start | bytes 122888 | tf_op jit(solution)/shard_map/ppermute | solution.py:526
  26.0 2.6 %collective-permute-done.7.refs_2_ = f32[20,512]{1,0:T(8,128)S(1)} collective-permute-done((f32[20,512]{1,0:T(8,128)S(1)}, f32[20,512]{1,0:T(8,128)S(1)}, u32[]{:S(2)}, u32[]{:S(2)}) %collective-permute-start.7) | collective-permute-done | bytes 40992 | tf_op jit(solution)/shard_map/ppermute | solution.py:526
  28.6 1.2 %collective-permute-done.8.refs_3_ = f32[20,512]{1,0:T(8,128)S(1)} collective-permute-done((f32[20,512]{1,0:T(8,128)S(1)}, f32[20,512]{1,0:T(8,128)S(1)}, u32[]{:S(2)}, u32[]{:S(2)}) %collective-permute-start.8) | collective-permute-done | bytes 40992 | tf_op jit(solution)/shard_map/ppermute | solution.py:526
  30.3 3.9 %chain.4 = (f32[1,80,128]{2,1,0:T(8,128)S(1)}, f32[1,80,128]{2,1,0:T(8,128)S(1)}, f32[80,384]{1,0:T(8,128)S(1)}) custom-call(f32[20,512]{1,0:T(8,128)S(1)} %join.5.refs_0_, f32[20,512]{1,0:T(8,128)S(1)} %collective-permute-done.6.refs_1_, f32[20,512]{1,0:T(8,128)S(1)} %collective-permute-done.7.refs_2_, f32[20,512]{1,0:T(8,128)S(1)} %collective-permute-done.8.refs_3_, ...), custom_call_target="tpu_custom_call" | custom-call | tf_op jit(solution)/shard_map/chain/pallas_call | solution.py:38
  34.3 2.8 %collective-permute-done.10.refs_5_ = f32[2,488,128]{2,1,0:T(8,128)S(1)} collective-permute-done((f32[2,488,128]{2,1,0:T(8,128)S(1)}, f32[2,488,128]{2,1,0:T(8,128)S(1)}, u32[]{:S(2)}, u32[]{:S(2)}) %collective-permute-start.10) | collective-permute-done | bytes 499744 | tf_op jit(solution)/shard_map/ppermute | solution.py:520
  37.5 3.9 %chain.5 = (f32[1,80,128]{2,1,0:T(8,128)S(1)}, f32[1,80,128]{2,1,0:T(8,128)S(1)}, f32[80,256]{1,0:T(8,128)S(1)}) custom-call(f32[80,384]{1,0:T(8,128)S(1)} %get-tuple-element.63.refs_0_, f32[4,128]{1,0:T(4,128)S(1)} %copy-done.2, f32[4,128]{1,0:T(4,128)S(1)} %copy-done.3, f32[6,128,128]{2,1,0:T(8,128)S(1)} %get-tuple-element.60.refs_6_.refs_3_), custom_call_target="tpu_custom_call" | custom-call | tf_op jit(solution)/shard_map/chain/pallas_call | solution.py:38
  41.4 3.9 %chain.6 = (f32[1,80,128]{2,1,0:T(8,128)S(1)}, f32[1,80,128]{2,1,0:T(8,128)S(1)}, f32[80,128]{1,0:T(8,128)S(1)}) custom-call(f32[80,256]{1,0:T(8,128)S(1)} %get-tuple-element.64.refs_0_, f32[4,128]{1,0:T(4,128)S(1)} %copy-done.2, f32[4,128]{1,0:T(4,128)S(1)} %copy-done.3, f32[6,128,128]{2,1,0:T(8,128)S(1)} %get-tuple-element.60.refs_6_.refs_3_), custom_call_target="tpu_custom_call" | custom-call | tf_op jit(solution)/shard_map/chain/pallas_call | solution.py:38
  45.3 3.7 %chain.7 = (f32[1,80,128]{2,1,0:T(8,128)S(1)}, f32[1,80,128]{2,1,0:T(8,128)S(1)}) custom-call(f32[80,128]{1,0:T(8,128)S(1)} %get-tuple-element.74.refs_0_, f32[4,128]{1,0:T(4,128)S(1)} %copy-done.2, f32[4,128]{1,0:T(4,128)S(1)} %copy-done.3, f32[6,128,128]{2,1,0:T(8,128)S(1)} %get-tuple-element.60.refs_6_.refs_3_), custom_call_target="tpu_custom_call" | custom-call | tf_op jit(solution)/shard_map/chain/pallas_call | solution.py:38
  49.0 1.6 %forecast.1.cells_ref = f32[1920,128]{1,0:T(8,128)S(1)} custom-call(f32[488,128]{1,0:T(8,128)S(1)} %get-tuple-element.49.refs_0_, f32[488,128]{1,0:T(8,128)S(1)} %collective-permute-done.1.refs_1_, f32[488,128]{1,0:T(8,128)S(1)} %collective-permute-done.3.refs_2_, f32[488,128]{1,0:T(8,128)S(1)} %collective-permute-done.4.refs_3_, ...), custom_call_target="tpu_custom_call" | custom-call | tf_op jit(solution)/shard_map/forecast/pallas_call | solution.py:38
  50.5 1.5 %collective-permute-done.12.far_ref = f32[2,488,128]{2,1,0:T(8,128)S(1)} collective-permute-done((f32[2,488,128]{2,1,0:T(8,128)S(1)}, f32[2,488,128]{2,1,0:T(8,128)S(1)}, u32[]{:S(2)}, u32[]{:S(2)}) %collective-permute-start.12) | collective-permute-done | bytes 499744 | tf_op jit(solution)/shard_map/ppermute | solution.py:534
  52.0 4.6 %update.1 = f32[1920,128]{1,0:T(8,128)} custom-call(f32[1920,128]{1,0:T(8,128)S(1)} %forecast.1.cells_ref, f32[2,488,128]{2,1,0:T(8,128)S(1)} %collective-permute-done.12.far_ref, f32[1,512]{1,0:T(1,128)S(1)} %copy-done.4, f32[1,512]{1,0:T(1,128)S(1)} %copy-done.5, f32[4,128,128]{2,1,0:T(8,128)S(1)} %get-tuple-element.67.taper_ref, ...), custom_call_target="tpu_custom_call" | custom-call | tf_op jit(solution)/shard_map/update/pallas_call | solution.py:38
  (34 shorter events, 2.6 us)
Async XLA Ops:
  0.0 1.2 %copy-start = (f32[20,1,24,512]{3,2,1,0:T(8,128)S(1)}, f32[20,1,24,512]{3,2,1,0:T(8,128)}, u32[]{:S(2)}) copy-start(f32[20,1,24,512]{3,2,1,0:T(8,128)} %param.9) | copy-start | bytes 2949124
  1.2 3.8 %copy-start.1 = (f32[4,128,24]{1,2,0:T(8,128)S(1)}, f32[4,128,24]{1,2,0:T(8,128)}, u32[]{:S(2)}) copy-start(f32[4,128,24]{1,2,0:T(8,128)} %param.16) | copy-start | bytes 147460
  1.2 3.8 %copy-start.6 = (f32[1,512]{1,0:T(1,128)S(1)}, f32[1,512]{1,0:T(1,128)}, u32[]{:S(2)}) copy-start(f32[1,512]{1,0:T(1,128)} %refs_7_.1) | copy-start | bytes 6148
  1.2 3.8 %copy-start.7 = (s32[4,128]{1,0:T(4,128)S(1)}, s32[4,128]{1,0:T(4,128)}, u32[]{:S(2)}) copy-start(s32[4,128]{1,0:T(4,128)} %cell_ref.1) | copy-start | bytes 6148
  1.9 10.4 %collective-permute-start.1 = (f32[488,128]{1,0:T(8,128)S(1)}, f32[488,128]{1,0:T(8,128)S(1)}, u32[]{:S(2)}, u32[]{:S(2)}) collective-permute-start(f32[488,128]{1,0:T(8,128)S(1)} %get-tuple-element.42), channel_id=1, source_target_pairs={{0,8},{8,0},{16,24},{24,16},{1,9},{9,1},{17,25},{25,17},{2,10},{10... | collective-permute-start | bytes 749576 | tf_op jit(solution)/shard_map/ppermute | solution.py:480
  2.4 14.1 %collective-permute-start.3 = (f32[488,128]{1,0:T(8,128)S(1)}, f32[488,128]{1,0:T(8,128)S(1)}, u32[]{:S(2)}, u32[]{:S(2)}) collective-permute-start(f32[488,128]{1,0:T(8,128)S(1)} %get-tuple-element.43), channel_id=1, source_target_pairs={{0,16},{8,24},{16,0},{24,8},{1,17},{9,25},{17,1},{25,9},{2,18},{10... | collective-permute-start | bytes 749576 | tf_op jit(solution)/shard_map/ppermute | solution.py:480
  5.0 0.7 %copy-start.5 = (f32[1,512]{1,0:T(1,128)S(1)}, f32[1,512]{1,0:T(1,128)}, u32[]{:S(2)}) copy-start(f32[1,512]{1,0:T(1,128)} %d_ref.1) | copy-start | bytes 6148
  5.0 0.7 %copy-start.4 = (f32[1,512]{1,0:T(1,128)S(1)}, f32[1,512]{1,0:T(1,128)}, u32[]{:S(2)}) copy-start(f32[1,512]{1,0:T(1,128)} %cy_ref.1) | copy-start | bytes 6148
  5.0 11.7 %collective-permute-start.4 = (f32[488,128]{1,0:T(8,128)S(1)}, f32[488,128]{1,0:T(8,128)S(1)}, u32[]{:S(2)}, u32[]{:S(2)}) collective-permute-start(f32[488,128]{1,0:T(8,128)S(1)} %get-tuple-element.44), channel_id=1, source_target_pairs={{0,24},{8,16},{16,8},{24,0},{1,25},{9,17},{17,9},{25,1},{2,26},{10... | collective-permute-start | bytes 749576 | tf_op jit(solution)/shard_map/ppermute | solution.py:480
  5.7 4.0 %copy-start.8 = (f32[4,128]{1,0:T(4,128)S(1)}, f32[4,128]{1,0:T(4,128)}, u32[]{:S(2)}) copy-start(f32[4,128]{1,0:T(4,128)} %radius_ref.1) | copy-start | bytes 6148
  8.1 4.2 %collective-permute-start = (f32[24,512]{1,0:T(8,128)S(1)}, f32[24,512]{1,0:T(8,128)S(1)}, u32[]{:S(2)}, u32[]{:S(2)}) collective-permute-start(f32[24,512]{1,0:T(8,128)S(1)} %share.1.mine_ref), channel_id=1, source_target_pairs={{0,1},{1,0},{2,3},{3,2},{4,5},{5,4},{6,7},{7,6},{8,9},{9,8},{10,11... | collective-permute-start | bytes 147464 | tf_op jit(solution)/shard_map/ppermute | solution.py:507
  12.3 4.2 %collective-permute-start.2 = (f32[24,512]{1,0:T(8,128)S(1)}, f32[24,512]{1,0:T(8,128)S(1)}, u32[]{:S(2)}, u32[]{:S(2)}) collective-permute-start(f32[24,512]{1,0:T(8,128)S(1)} %join.3.mine_ref), channel_id=1, source_target_pairs={{0,2},{1,3},{2,0},{3,1},{4,6},{5,7},{6,4},{7,5},{8,10},{9,11},{10,... | collective-permute-start | bytes 147464 | tf_op jit(solution)/shard_map/ppermute | solution.py:507
  14.0 15.8 %collective-permute-start.9 = (f32[2,488,128]{2,1,0:T(8,128)S(1)}, f32[2,488,128]{2,1,0:T(8,128)S(1)}, u32[]{:S(2)}, u32[]{:S(2)}) collective-permute-start(f32[2,488,128]{2,1,0:T(8,128)S(1)} %pad_maximum_fusion), channel_id=1, source_target_pairs={{0,1},{1,0},{2,3},{3,2},{4,5},{5,4},{6,7},{7,6},{8,9},{9,8},{10,11... | collective-permute-start | bytes 1499144 | tf_op jit(solution)/shard_map/ppermute | solution.py:520
  16.7 13.6 %copy-start.2 = (f32[4,128]{1,0:T(4,128)S(1)}, f32[4,128]{1,0:T(4,128)}, u32[]{:S(2)}) copy-start(f32[4,128]{1,0:T(4,128)} %refs_1_.7) | copy-start | bytes 6148
  16.8 13.6 %copy-start.3 = (f32[4,128]{1,0:T(4,128)S(1)}, f32[4,128]{1,0:T(4,128)}, u32[]{:S(2)}) copy-start(f32[4,128]{1,0:T(4,128)} %refs_2_.7) | copy-start | bytes 6148
  16.8 20.3 %collective-permute-start.10 = (f32[2,488,128]{2,1,0:T(8,128)S(1)}, f32[2,488,128]{2,1,0:T(8,128)S(1)}, u32[]{:S(2)}, u32[]{:S(2)}) collective-permute-start(f32[2,488,128]{2,1,0:T(8,128)S(1)} %pad_maximum_fusion.1), channel_id=1, source_target_pairs={{0,1},{1,0},{2,3},{3,2},{4,5},{5,4},{6,7},{7,6},{8,9},{9,8},{10,11... | collective-permute-start | bytes 1499144 | tf_op jit(solution)/shard_map/ppermute | solution.py:520
  18.4 6.0 %collective-permute-start.5 = (f32[24,512]{1,0:T(8,128)S(1)}, f32[24,512]{1,0:T(8,128)S(1)}, u32[]{:S(2)}, u32[]{:S(2)}) collective-permute-start(f32[24,512]{1,0:T(8,128)S(1)} %join.4.mine_ref), channel_id=1, source_target_pairs={{0,4},{1,5},{2,6},{3,7},{4,0},{5,1},{6,2},{7,3},{8,12},{9,13},{10,... | collective-permute-start | bytes 147464 | tf_op jit(solution)/shard_map/ppermute | solution.py:507
  24.4 4.2 %collective-permute-start.7 = (f32[20,512]{1,0:T(8,128)S(1)}, f32[20,512]{1,0:T(8,128)S(1)}, u32[]{:S(2)}, u32[]{:S(2)}) collective-permute-start(f32[20,512]{1,0:T(8,128)S(1)} %join.5.refs_0_), channel_id=1, source_target_pairs={{0,16},{8,24},{16,0},{24,8},{1,17},{9,25},{17,1},{25,9},{2,18},{10... | collective-permute-start | bytes 122888 | tf_op jit(solution)/shard_map/ppermute | solution.py:526
  26.0 2.6 %collective-permute-start.6 = (f32[20,512]{1,0:T(8,128)S(1)}, f32[20,512]{1,0:T(8,128)S(1)}, u32[]{:S(2)}, u32[]{:S(2)}) collective-permute-start(f32[20,512]{1,0:T(8,128)S(1)} %join.5.refs_0_), channel_id=1, source_target_pairs={{0,8},{8,0},{16,24},{24,16},{1,9},{9,1},{17,25},{25,17},{2,10},{10... | collective-permute-start | bytes 122888 | tf_op jit(solution)/shard_map/ppermute | solution.py:526
  28.6 1.2 %collective-permute-start.8 = (f32[20,512]{1,0:T(8,128)S(1)}, f32[20,512]{1,0:T(8,128)S(1)}, u32[]{:S(2)}, u32[]{:S(2)}) collective-permute-start(f32[20,512]{1,0:T(8,128)S(1)} %collective-permute-done.7.refs_2_), channel_id=1, source_target_pairs={{0,8},{8,0},{16,24},{24,16},{1,9},{9,1},{17,25},{25,17},{2,10},{10... | collective-permute-start | bytes 122888 | tf_op jit(solution)/shard_map/ppermute | solution.py:526
  29.8 15.5 %collective-permute-start.11 = (f32[2,488,128]{2,1,0:T(8,128)S(1)}, f32[2,488,128]{2,1,0:T(8,128)S(1)}, u32[]{:S(2)}, u32[]{:S(2)}) collective-permute-start(f32[2,488,128]{2,1,0:T(8,128)S(1)} %collective-permute-done.9.refs_4_), channel_id=1, source_target_pairs={{0,2},{2,4},{4,6},{3,1},{5,3},{7,5},{6,0},{1,7},{8,10},{10,12},{12... | collective-permute-start | bytes 1499144 | tf_op jit(solution)/shard_map/ppermute | solution.py:534
  37.1 14.9 %collective-permute-start.12 = (f32[2,488,128]{2,1,0:T(8,128)S(1)}, f32[2,488,128]{2,1,0:T(8,128)S(1)}, u32[]{:S(2)}, u32[]{:S(2)}) collective-permute-start(f32[2,488,128]{2,1,0:T(8,128)S(1)} %collective-permute-done.10.refs_5_), channel_id=1, source_target_pairs={{0,2},{2,4},{4,6},{3,1},{5,3},{7,5},{1,0},{6,7},{8,10},{10,12},{12... | collective-permute-start | bytes 1499144 | tf_op jit(solution)/shard_map/ppermute | solution.py:534
